TPU v7x, 32 devices: a whole 2x2x4 slice. The times are simulated.
32 devices in a mesh: groups: 2 (over y), region: 4 (over z), member: 2 (over x), tile: 2 (over core).
Axes of the slice: x: 2, y: 2, z: 4, core: 2. Of those that a mesh axis runs over, the one named last changes fastest.
Arguments:
- anomalies: bfloat16 [32768, 1024], P(('groups', 'region'), ('member', 'tile')), parts along dimension 0, may hold values from -12 to 12
- tapering: float32 [256, 9], P(('groups', 'region')), parts along dimension 0, may hold values from 0 to 1, as said below
Outputs:
- analysis: bfloat16 [32768, 1024], P(('groups', 'region'), ('member', 'tile')), parts along dimension 0
There are 2 independent parts, one for each index of `groups`. A program takes and returns all parts, laid end to end along the dimension named above; each array names one. Nothing has to cross between parts.
Inputs may be any that keep to these rules, and one draw needn't show every extreme that they name: tapering[b, o + 4] is 1 at o = 0, and 0 exactly where block b + o lies outside the grid or beyond the cutoff of block b.
All inputs are finite; a program needn't handle non-finite values.
Results may differ from a plain program's by a relative error of at most 0.005.
Values may be sent and summed in bfloat16 or wider, within the bound.
No kernel may reach another device: no remote copies, remote signals or barrier semaphores. Data moves between devices by JAX's collectives and lax.ppermute only.
A program may use at most 64 MiB of HBM per device.

v0:
```python
import jax
import jax.numpy as jnp
from jax import lax
from jax.sharding import PartitionSpec as P

MEMBERS = 1024
BLOCK = 128
REACH = 4
SLOTS = 9
OWN_BLOCKS = 8


def extended_2(cells, sides, width):
    for axis, dim in sides:
        count = lax.axis_size(axis)
        ends = count - 1
        head = lax.slice_in_dim(cells, 0, width, axis=dim)
        tail = lax.slice_in_dim(cells, cells.shape[dim] - width, cells.shape[dim], axis=dim)
        cells = jnp.concatenate(
            [
                lax.ppermute(tail, axis, [(i, (i + 1) % count) for i in range(ends)]),
                cells,
                lax.ppermute(head, axis, [((i + 1) % count, i) for i in range(ends)]),
            ],
            axis=dim,
        )
    return cells


def keep_same(current):
    return current


def tile_rows(extended, weights, starts):
    owned_count = weights.shape[0]
    members = extended.shape[1]
    factor = 1.0 / (MEMBERS - 1)

    def one_block(number, result):
        anchor = starts[number] * BLOCK
        own = lax.dynamic_slice_in_dim(extended, anchor, BLOCK, 0)
        update = jnp.zeros((BLOCK, members), jnp.float32)
        for offset in range(SLOTS):
            partner = lax.dynamic_slice_in_dim(
                extended, anchor + (offset - REACH) * BLOCK, BLOCK, 0
            )
            weight = weights[number, offset]

            def add_tile(current, partner=partner, weight=weight):
                covariance = lax.dot_general(
                    own, partner, (((1,), (1,)), ((), ())), preferred_element_type=jnp.float32
                )
                weighted = (covariance * (weight * factor)).astype(jnp.bfloat16)
                return current + jnp.dot(weighted, partner, preferred_element_type=jnp.float32)

            update = lax.cond(weight != 0, add_tile, keep_same, update)
        analysis = (own.astype(jnp.float32) - 0.5 * update).astype(jnp.bfloat16)
        return lax.dynamic_update_slice_in_dim(result, analysis, number * BLOCK, 0)

    empty = jnp.zeros((owned_count * BLOCK, members), jnp.bfloat16)
    return lax.fori_loop(0, owned_count, one_block, empty)


def per_device(anomalies, tapering):
    position = lax.axis_index(("member", "tile"))
    owned_rows = lax.all_to_all(
        anomalies, ("member", "tile"), split_axis=0, concat_axis=1, tiled=True
    )
    extended = extended_2(owned_rows, ((("region", "member", "tile"), 0),), REACH * BLOCK)
    weights = lax.dynamic_slice_in_dim(tapering, position * OWN_BLOCKS, OWN_BLOCKS, 0)
    starts = jnp.arange(OWN_BLOCKS, dtype=jnp.int32) + REACH
    analysis = tile_rows(extended, weights, starts)
    return lax.all_to_all(analysis, ("member", "tile"), split_axis=1, concat_axis=0, tiled=True)


def solution(mesh):
    in_specs = (P(("groups", "region"), ("member", "tile")), P(("groups", "region"), None))
    out_specs = P(("groups", "region"), ("member", "tile"))
    return jax.shard_map(
        per_device, mesh=mesh, in_specs=in_specs, out_specs=out_specs, check_vma=False
    )
```

profile of v0, /device:TPU:12, one launch (start us, length us, event | category | flops | bytes accessed | tf_op | source)
XLA Modules:
  0.0 334.4 jit_solution(13558777671811211718)
XLA Ops:
  0.0 30.3 %all_to_all.38 = bf16[4,1024,256]{2,1,0:T(8,128)(2,1)} all-to-all(bf16[4,1024,256]{2,1,0:T(8,128)(2,1)} %bitcast.59), channel_id=1, replica_groups=mesh['groups'=2,'region'=4,'member'=2,'tile'=2] {'member','tile'}, dimensions={0} | all-to-all | bytes 4194304 | tf_op jit(solution)/shard_map/all_to_all | solution.py:66
  30.3 3.0 copy.8
  34.4 1.9 collective-permute-start
  36.4 4.5 %collective-permute-start.1 = (bf16[512,1024]{0,1:T(8,128)(2,1)S(1)}, bf16[512,1024]{0,1:T(8,128)(2,1)}, u32[]{:S(2)}, u32[]{:S(2)}) collective-permute-start(bf16[512,1024]{0,1:T(8,128)(2,1)S(1)} %bitcast.60), channel_id=1, source_target_pairs={{1,0},{2,1},{3,2},{4,3},{5,4},{6,5},{7,6},{8,7},{9,8},{10,9},{11,1... | collective-permute-start | bytes 3145736 | tf_op jit(solution)/shard_map/ppermute | solution.py:23
  41.1 10.8 %collective-permute-done = bf16[512,1024]{0,1:T(8,128)(2,1)} collective-permute-done((bf16[512,1024]{0,1:T(8,128)(2,1)}, bf16[512,1024]{0,1:T(8,128)(2,1)}, u32[]{:S(2)}, u32[]{:S(2)}) %collective-permute-start) | collective-permute-done | bytes 1048608 | tf_op jit(solution)/shard_map/ppermute | solution.py:21
  53.2 3.4 %pad_maximum_fusion = bf16[2048,1024]{0,1:T(8,128)(2,1)} fusion(bf16[512,1024]{0,1:T(8,128)(2,1)} %collective-permute-done.1, bf16[1024,1024]{0,1:T(8,128)(2,1)S(1)} %bitcast.55, bf16[512,1024]{0,1:T(8,128)(2,1)} %collective-permute-done), kind=kLoop, calls=%fused_computation.64 | loop fusion | flops 12582912 | bytes 8388608 | tf_op jit(solution)/shard_map/concatenate | solution.py:19
  56.7 6.4 %copy.10 = bf16[2048,1024]{1,0:T(8,128)(2,1)} copy(bf16[2048,1024]{0,1:T(8,128)(2,1)} %pad_maximum_fusion) | data formatting | bytes 8388608 | tf_op jit(solution)/shard_map/while | solution.py:61
  63.3 124.6 %while.15 = (s32[]{:T(128)}, bf16[1024,1024]{1,0:T(8,128)(2,1)S(1)}, s32[8]{0:T(128)S(1)}, bf16[2048,1024]{1,0:T(8,128)(2,1)}, f32[8,9]{1,0:T(8,128)S(1)}, /*ind...) while((s32[]{:T(128)}, ...), condition=%wide.region_19.0_spmd, body=%wide.region_0.0_spmd.sunk | while | flops 605847616 | bytes 17053092 | solution.py:61
  68.9 2.3 conditional.21
  73.7 2.3 conditional.23
  74.4 1.6 convolution_add_fusion.2
  84.5 2.3 conditional.21
  85.1 1.6 convolution_add_fusion.5
  89.2 2.3 conditional.23
  89.9 1.6 convolution_add_fusion.2
  100.0 2.3 conditional.21
  104.8 2.3 conditional.23
  105.5 1.6 convolution_add_fusion.2
  115.6 2.3 conditional.21
  120.4 2.3 conditional.23
  121.1 1.6 convolution_add_fusion.2
  131.2 2.3 conditional.21
  131.8 1.6 convolution_add_fusion.5
  136.0 2.3 conditional.23
  146.8 2.3 conditional.21
  151.6 2.3 conditional.23
  152.3 1.6 convolution_add_fusion.2
  162.4 2.3 conditional.21
  167.2 2.3 conditional.23
  177.9 2.3 conditional.21
  182.7 2.3 conditional.23
  188.1 145.0 %all_to_all.39 = bf16[1024,4,256]{2,0,1:T(8,128)(2,1)S(1)} all-to-all(bf16[1024,4,256]{2,0,1:T(8,128)(2,1)S(1)} %bitcast.57), channel_id=1, replica_groups=mesh['groups'=2,'region'=4,'member'=2,'tile'=2] {'member','tile'}, dimensions={1} | all-to-all | bytes 4194304 | tf_op jit(solution)/shard_map/all_to_all | solution.py:73
  (123 shorter events, 60.0 us)
Async XLA Ops:
  0.0 40.9 %copy-start = (f32[32,9]{0,1:T(8,128)S(1)}, f32[32,9]{0,1:T(8,128)}, u32[]{:S(2)}) copy-start(f32[32,9]{0,1:T(8,128)} %param.23) | copy-start | bytes 3460
  34.4 17.4 %collective-permute-start = (bf16[512,1024]{0,1:T(8,128)(2,1)}, bf16[512,1024]{0,1:T(8,128)(2,1)}, u32[]{:S(2)}, u32[]{:S(2)}) collective-permute-start(bf16[512,1024]{0,1:T(8,128)(2,1)} %bitcast.12), channel_id=1, source_target_pairs={{0,1},{1,2},{2,3},{3,4},{4,5},{5,6},{6,7},{7,8},{8,9},{9,10},{10,1... | collective-permute-start | bytes 3145736 | tf_op jit(solution)/shard_map/ppermute | solution.py:21
  36.4 16.9 %collective-permute-start.1 = (bf16[512,1024]{0,1:T(8,128)(2,1)S(1)}, bf16[512,1024]{0,1:T(8,128)(2,1)}, u32[]{:S(2)}, u32[]{:S(2)}) collective-permute-start(bf16[512,1024]{0,1:T(8,128)(2,1)S(1)} %bitcast.60), channel_id=1, source_target_pairs={{1,0},{2,1},{3,2},{4,3},{5,4},{6,5},{7,6},{8,7},{9,8},{10,9},{11,1... | collective-permute-start | bytes 3145736 | tf_op jit(solution)/shard_map/ppermute | solution.py:23
where the time goes:
time: 338 us; the launch traced here: 334 us
  blocking collectives  175 us (52%)
  loops' own time  67.7 us (20%)
  local copies, waits for them, and re-layouts  30.7 us (9%)
  matrix products  30.4 us (9%)
  waiting for transfers between devices  12.2 us (4%)
  other arithmetic  11.7 us (3%)
  starting transfers between devices  6.45 us (2%)
    all_to_all x1, blocking collectives, per_device(): lax.all_to_all(analysis, ('member', 'tile'), split_axis=1, concat_axis=0,...  145 us
    another operation x1, loops' own time, tile_rows(): return lax.fori_loop(0, owned_count, one_block, empty)  51.2 us
    dot_general x24, matrix products, add_tile(): jnp.dot(weighted, partner, preferred_element_type=jnp.float32)  30.4 us
    all_to_all x1, blocking collectives, per_device(): lax.all_to_all(anomalies, ('member', 'tile'), split_axis=0, concat_axis=1...  30.3 us
    another operation x72, loops' own time, one_block(): update = lax.cond(weight != 0, add_tile, keep_same, update)  16.4 us
    ppermute x1, waiting for transfers between devices, extended_2(): lax.ppermute(tail, axis, [(i, (i + 1) % count) for i in range(ends)])  10.8 us
    dynamic_update_slice x8, other arithmetic, one_block(): return lax.dynamic_update_slice_in_dim(result, analysis, number * BLOCK, 0)  8.27 us
    dynamic_slice x8, local copies, waits for them, and re-layouts, one_block(): own = lax.dynamic_slice_in_dim(extended, anchor, BLOCK, 0)  7.8 us
  transfers between devices with their start and end apart: 2, of which 2 were waited for; matrix products, arithmetic and copies ran while one was open for 0% of the time, Pallas kernels for 0%

commit v1 on v0

v1 whole, which is shorter than its diff:
```python
import functools

import jax
import jax.numpy as jnp
from jax import lax
from jax.experimental import pallas as pl
from jax.experimental.pallas import tpu as pltpu
from jax.sharding import PartitionSpec as P


MEMBERS = 1024
BLOCK = 128
REACH = 4
SLOTS = 9
FACTOR = 1.0 / (MEMBERS - 1)
PAIR = 2
ROWS = PAIR * BLOCK
NEAR = REACH // PAIR


def shifted(value, axis):
    count = lax.axis_size(axis)
    return [
        lax.ppermute(value, axis, [(i, (i + s) % count) for i in range(count)])
        for s in range(1, count)
    ]


def tile_rows(start, count=1):
    return pl.ds(start * ROWS, count * ROWS)


def update_kernel(job, *refs):
    slots, parts = job["slots"], job["parts"]
    plan, steps, owned = job["plan"], job["steps"], job["owned"]
    acc_in, acc_out, finished = job["acc_in"], job["acc_out"], job["finished"]
    arrays = job["arrays"]
    taper = refs[0]
    sources = refs[1 : 1 + arrays]
    inputs = refs[1 + arrays : 1 + arrays + len(acc_in)]
    outs = refs[1 + arrays + len(acc_in) + job["aliased"] :]
    if finished:
        out, outs = outs[0], outs[1:]
    carried, outs = outs[: len(acc_out)], outs[len(acc_out) :]
    ybuf, acc, wcol, wrow, obuf, in_sem, acc_sem, out_sem = outs

    def fetch(n):
        array, part, start, slot = plan[n]
        return pltpu.make_async_copy(
            sources[array].at[tile_rows(start)], ybuf.at[part, slot], in_sem.at[n]
        )

    def take(n):
        return pltpu.make_async_copy(inputs[n], acc.at[slots[acc_in[n]]], acc_sem.at[n])

    for n in range(len(plan)):
        fetch(n).start()
    for n in range(len(acc_in)):
        take(n).start()
    here, begun = set(), set()

    def arrive(pair):
        if pair not in here:
            here.add(pair)
            for n in range(len(plan)):
                if plan[n][3] == slots[pair]:
                    fetch(n).wait()

    def add(pair, value):
        slot = slots[pair]
        if pair in begun:
            acc[slot] = acc[slot] + value
        elif pair in acc_in:
            take(acc_in.index(pair)).wait()
            acc[slot] = acc[slot] + value
        else:
            acc[slot] = value
        begun.add(pair)

    def weighted(c, i_pair, j_pair, base, flip):
        rows = []
        for ii in range(PAIR):
            row = []
            for jj in range(PAIR):
                i, j = i_pair * PAIR + ii, j_pair * PAIR + jj
                slot = (i - j if flip else j - i) + REACH
                if 0 <= slot < SLOTS:
                    weight = taper[j if flip else i, slot] * FACTOR
                    tile = c[
                        base + ii * BLOCK : base + (ii + 1) * BLOCK,
                        jj * BLOCK : (jj + 1) * BLOCK,
                    ]
                    row.append((tile * weight).astype(jnp.bfloat16))
                else:
                    row.append(jnp.zeros((BLOCK, BLOCK), jnp.bfloat16))
            rows.append(jnp.concatenate(row, axis=1))
        return jnp.concatenate(rows, axis=0)

    for j, first, count in steps:
        near = list(range(first, first + count))
        for pair in near + [j]:
            arrive(pair)
        total = None
        for part in range(parts):
            left = ybuf[part, pl.ds(slots[first], count)].reshape(count * ROWS, -1)
            term = lax.dot_general(
                left,
                ybuf[part, slots[j]],
                (((1,), (1,)), ((), ())),
                preferred_element_type=jnp.float32,
            )
            total = term if total is None else total + term
        others = [i for i in near if i != j]
        for k, i in enumerate(near):
            if i in owned:
                wcol[tile_rows(k)] = weighted(total, i, j, k * ROWS, False)
            if j in owned and i != j:
                wrow[tile_rows(others.index(i))] = weighted(total, i, j, k * ROWS, True)
        for k, i in enumerate(near):
            if i in owned:
                add(
                    i,
                    jnp.dot(
                        wcol[tile_rows(k)],
                        ybuf[0, slots[j]],
                        preferred_element_type=jnp.float32,
                    ),
                )
        if j in owned and others:
            value = None
            for k, i in enumerate(others):
                term = lax.dot_general(
                    wrow[tile_rows(k)],
                    ybuf[0, slots[i]],
                    (((0,), (0,)), ((), ())),
                    preferred_element_type=jnp.float32,
                )
                value = term if value is None else value + term
            add(j, value)

    def store(n):
        return pltpu.make_async_copy(
            obuf.at[n], out.at[tile_rows(finished[n])], out_sem.at[n]
        )

    def hand_on(n):
        return pltpu.make_async_copy(
            acc.at[slots[acc_out[n]]], carried[n], out_sem.at[len(finished) + n]
        )

    for n, pair in enumerate(acc_out):
        if pair in acc_in and pair not in begun:
            take(acc_in.index(pair)).wait()
        hand_on(n).start()
    for n, pair in enumerate(finished):
        if pair in acc_in and pair not in begun:
            take(acc_in.index(pair)).wait()
        own = ybuf[0, slots[pair]].astype(jnp.float32)
        obuf[n] = (own - 0.5 * acc[slots[pair]]).astype(jnp.bfloat16)
        store(n).start()
    for n in range(len(acc_out)):
        hand_on(n).wait()
    for n in range(len(finished)):
        store(n).wait()


def run_steps(taper, pieces, steps, owned, state, finished, result, rows, members):
    parts = len(pieces)
    needed = set()
    for j, first, count in steps:
        needed |= {j} | set(range(first, first + count))
    needed |= set(finished)
    slots = {pair: n for n, pair in enumerate(sorted(needed))}
    touched = set()
    for j, first, count in steps:
        near = set(range(first, first + count))
        touched |= near & owned
        if j in owned and near - {j}:
            touched.add(j)
    acc_in = [pair for pair in sorted(touched | set(finished)) if pair in state]
    acc_out = sorted(touched - set(finished))
    order = []
    for j, first, count in steps:
        for pair in [j] + list(range(first, first + count)):
            if pair not in order:
                order.append(pair)
    order += [pair for pair in finished if pair not in order]
    arrays, plan = [], []
    for pair in order:
        for part in range(parts):
            array, start = pieces[part][pair]
            known = [n for n, other in enumerate(arrays) if other is array]
            if not known:
                arrays.append(array)
                known = [len(arrays) - 1]
            plan.append((known[0], part, start, slots[pair]))
    aliased = int(bool(finished) and result is not None)
    job = dict(
        slots=slots, parts=parts, plan=plan, steps=steps, owned=owned, acc_in=acc_in,
        acc_out=acc_out, finished=finished, arrays=len(arrays), aliased=aliased,
    )
    operands = [taper] + arrays + [state[pair] for pair in acc_in]
    anywhere = pl.BlockSpec(memory_space=pl.ANY)
    specs = [pl.BlockSpec(memory_space=pltpu.SMEM)] + [anywhere] * (len(operands) - 1)
    aliases = {}
    shapes = []
    if finished:
        shapes.append(jax.ShapeDtypeStruct((rows, members), jnp.bfloat16))
        if aliased:
            aliases = {len(operands): 0}
            operands.append(result)
            specs.append(anywhere)
    shapes += [jax.ShapeDtypeStruct((ROWS, members), jnp.float32)] * len(acc_out)
    widest = max(count for _, _, count in steps)
    count = len(needed)
    products = sum(n for _, _, n in steps)
    outputs = pl.pallas_call(
        functools.partial(update_kernel, job),
        out_shape=shapes,
        in_specs=specs,
        out_specs=[anywhere] * len(shapes),
        input_output_aliases=aliases,
        scratch_shapes=[
            pltpu.VMEM((parts, count, ROWS, members), jnp.bfloat16),
            pltpu.VMEM((count, ROWS, members), jnp.float32),
            pltpu.VMEM((widest * ROWS, ROWS), jnp.bfloat16),
            pltpu.VMEM((widest * ROWS, ROWS), jnp.bfloat16),
            pltpu.VMEM((max(len(finished), 1), ROWS, members), jnp.bfloat16),
            pltpu.SemaphoreType.DMA((len(plan),)),
            pltpu.SemaphoreType.DMA((max(len(acc_in), 1),)),
            pltpu.SemaphoreType.DMA((len(finished) + len(acc_out),)),
        ],
        compiler_params=pltpu.CompilerParams(vmem_limit_bytes=32 * 2**20),
        cost_estimate=pl.CostEstimate(
            flops=2 * products * ROWS * ROWS * members * (parts + 2),
            bytes_accessed=2 * ROWS * members * (len(plan) + 3 * len(finished)),
            transcendentals=0,
        ),
    )(*operands)
    if finished:
        result, outputs = outputs[0], outputs[1:]
    state = {pair: value for pair, value in state.items() if pair not in touched}
    state.update(zip(acc_out, outputs))
    for pair in finished:
        state.pop(pair, None)
    return result, state


def chunk_bounds(pairs):
    first, last = NEAR, pairs - NEAR
    tail = [2, 2]
    bulk = last - first - sum(tail)
    sizes = [(bulk + 1) // 2, bulk // 2] + tail
    bounds = [first]
    for size in sizes:
        if size:
            bounds.append(bounds[-1] + size)
    return list(zip(bounds, bounds[1:]))


def per_device(anomalies, taper):
    rows, members = anomalies.shape
    pairs = rows // ROWS
    ring = lax.axis_size("region")
    down = [(i, i + 1) for i in range(ring - 1)]
    up = [(i + 1, i) for i in range(ring - 1)]
    chunks = chunk_bounds(pairs)

    def cut(first, last):
        return lax.slice_in_dim(anomalies, first * ROWS, last * ROWS, axis=0)

    top, bottom = cut(0, NEAR), cut(pairs - NEAR, pairs)
    tops = shifted(top, "member")
    bottoms = shifted(bottom, "member")
    middles = []
    for first, last in chunks:
        middles.append(shifted(cut(first, last), "member"))

    sets = [([(anomalies, 0, pairs)], top, bottom)]
    for s in range(len(tops)):
        listed = [(tops[s], 0, NEAR)]
        for (first, last), middle in zip(chunks, middles):
            listed.append((middle[s], first, last - first))
        listed.append((bottoms[s], pairs - NEAR, NEAR))
        sets.append((listed, tops[s], bottoms[s]))
    held = []
    for listed, head, tail in sets:
        before = (lax.ppermute(tail, "region", down), -NEAR, NEAR)
        after = (lax.ppermute(head, "region", up), pairs, NEAR)
        held.append([before, after] + listed)
    for turn in range(lax.axis_size("tile") - 1):
        held += [
            [(shifted(array, "tile")[turn], first, count) for array, first, count in listed]
            for listed in list(held)
        ]
    pieces = [
        {first + n: (array, n) for array, first, count in listed for n in range(count)}
        for listed in held
    ]

    owned = set(range(pairs))
    state, result = {}, None

    def steps_for(fresh, before):
        there, steps = set(before), []
        for j in fresh:
            there.add(j)
            near = [i for i in range(j - NEAR, j + NEAR + 1) if i in there and (i in owned or j in owned)]
            while near:
                run = [near[0]]
                while run[-1] + 1 in near:
                    run.append(run[-1] + 1)
                steps.append((j, run[0], len(run)))
                near = near[len(run) :]
        return steps, there

    low = list(range(-NEAR, NEAR))
    high = list(range(pairs - NEAR, pairs + NEAR))
    there, done = set(), set()
    batches = [high, low + list(range(*chunks[0]))] + [list(range(*c)) for c in chunks[1:]]
    for fresh in batches:
        steps, there = steps_for(fresh, there)
        ready = [
            i for i in range(pairs)
            if i not in done and all(k in there for k in range(i - NEAR, i + NEAR + 1))
        ]
        done |= set(ready)
        result, state = run_steps(taper, pieces, steps, owned, state, ready, result, rows, members)
    return result


def solution(mesh):
    in_specs = (P(("groups", "region"), ("member", "tile")), P(("groups", "region"), None))
    out_specs = P(("groups", "region"), ("member", "tile"))

    return jax.shard_map(
        per_device, mesh=mesh, in_specs=in_specs, out_specs=out_specs, check_vma=False
    )
```

time: 338 us -> 95.4 us (0.28)
  blocking collectives: 175 us -> 0 us
  loops' own time: 67.7 us -> 0 us
  Pallas kernels: 0 us -> 41.1 us
  matrix products: 30.4 us -> 0 us
  local copies, waits for them, and re-layouts: 30.7 us -> 7.21 us
  starting transfers between devices: 6.45 us -> 20.6 us
  waiting for transfers between devices: 12.2 us -> 24.3 us
  other arithmetic: 11.7 us -> 0 us
    all_to_all x2 -> x0, blocking collectives: 175 us -> none  [the longest x1 145 us: per_device(): lax.all_to_all(analysis, ('member', 'tile'), split_axis=1, concat_axis=0,...]
    another operation x73 -> x0, loops' own time: 67.7 us -> none  [the longest x1 51.2 us: tile_rows(): return lax.fori_loop(0, owned_count, one_block, empty)]
    pallas_call x0 -> x5, Pallas kernels: none -> 41.1 us  [run_steps(): pl.pallas_call(functools.partial(update_kernel, job), out_shape=shapes, i...]
    dot_general x24 -> x0, matrix products: 30.4 us -> none  [add_tile(): jnp.dot(weighted, partner, preferred_element_type=jnp.float32)]
    dynamic_slice x25 -> x0, local copies, waits for them, and re-layouts: 18 us -> none  [the longest x8 7.8 us: one_block(): own = lax.dynamic_slice_in_dim(extended, anchor, BLOCK, 0)]
    ppermute x2 -> x21, starting transfers between devices: 6.45 us -> 20.6 us  [the longest x17 8.95 us: shifted(): lax.ppermute(value, axis, [(i, (i + s) % count) for i in range(count)])]
    ppermute x2 -> x21, waiting for transfers between devices: 12.2 us -> 24.3 us  [the longest x17 23.3 us: shifted(): lax.ppermute(value, axis, [(i, (i + s) % count) for i in range(count)])]
    dynamic_update_slice x8 -> x0, other arithmetic: 8.27 us -> none  [one_block(): return lax.dynamic_update_slice_in_dim(result, analysis, number * BLOCK, 0)]
  transfers between devices with their start and end apart: 2 -> 21, of which waited for: 2 -> 6; matrix products, arithmetic and copies ran while one was open for 0% -> 2% of each run, Pallas kernels for 0% -> 34%
where the time goes in v1:
time: 95.4 us; the launch traced here: 93.6 us
  Pallas kernels  41.1 us (43%)
  waiting for transfers between devices  24.3 us (25%)
  starting transfers between devices  20.6 us (22%)
  local copies, waits for them, and re-layouts  7.21 us (8%)
    pallas_call x5, Pallas kernels, run_steps(): pl.pallas_call(functools.partial(update_kernel, job), out_shape=shapes, i...  41.1 us
    ppermute x17, waiting for transfers between devices, shifted(): lax.ppermute(value, axis, [(i, (i + s) % count) for i in range(count)])  23.3 us
    ppermute x17, starting transfers between devices, shifted(): lax.ppermute(value, axis, [(i, (i + s) % count) for i in range(count)])  8.95 us
    ppermute x2, starting transfers between devices, per_device(): before = (lax.ppermute(tail, 'region', down), -NEAR, NEAR)  6.96 us
    unnamed x17, local copies, waits for them, and re-layouts  5.05 us
    ppermute x2, starting transfers between devices, per_device(): after = (lax.ppermute(head, 'region', up), pairs, NEAR)  4.69 us
    slice x2, local copies, waits for them, and re-layouts, cut(): return lax.slice_in_dim(anomalies, first * ROWS, last * ROWS, axis=0)  2.16 us
  transfers between devices with their start and end apart: 21, of which 6 were waited for; matrix products, arithmetic and copies ran while one was open for 2% of the time, Pallas kernels for 34%

profile of v1, /device:TPU:12, one launch (start us, length us, event | category | flops | bytes accessed | tf_op | source)
XLA Modules:
  0.0 93.6 jit_solution(1089573221393067642)
XLA Ops:
  0.0 2.1 %fusion = (bf16[512,256]{1,0:T(8,128)(2,1)S(1)}, bf16[512,256]{1,0:T(8,128)(2,1)S(1)}, bf16[512,256]{1,0:T(8,128)(2,1)S(1)}, bf16[512,256]{1,0:T(8,128)(2,1)}) fusion(bf16[4096,256]{1,0:T(8,128)(2,1)} %refs_1_.9), kind=kLoop, calls=%fused_computation | loop fusion | bytes 2097152 | tf_op jit(solution)/shard_map/slice | solution.py:270
  2.1 1.5 %collective-permute-start.5 = (bf16[512,256]{1,0:T(8,128)(2,1)S(1)}, bf16[512,256]{1,0:T(8,128)(2,1)S(1)}, u32[]{:S(2)}, u32[]{:S(2)}) collective-permute-start(bf16[512,256]{1,0:T(8,128)(2,1)S(1)} %get-tuple-element.28), channel_id=1, source_target_pairs={{0,2},{2,0},{1,3},{3,1},{4,6},{6,4},{5,7},{7,5},{8,10},{10,8},{9,1... | collective-permute-start | bytes 786440 | tf_op jit(solution)/shard_map/ppermute | solution.py:24
  3.6 3.5 %collective-permute-start.13 = (bf16[512,256]{1,0:T(8,128)(2,1)S(1)}, bf16[512,256]{1,0:T(8,128)(2,1)S(1)}, u32[]{:S(2)}, u32[]{:S(2)}) collective-permute-start(bf16[512,256]{1,0:T(8,128)(2,1)S(1)} %get-tuple-element.28), channel_id=1, source_target_pairs={{0,4},{4,8},{8,12},{1,5},{5,9},{9,13},{2,6},{6,10},{10,14},{3,7},{... | collective-permute-start | bytes 786440 | tf_op jit(solution)/shard_map/ppermute | solution.py:288
  7.1 0.6 collective-permute-start.11
  7.8 1.6 %collective-permute-start.9 = (bf16[1024,256]{1,0:T(8,128)(2,1)S(1)}, bf16[1024,256]{1,0:T(8,128)(2,1)}, u32[]{:S(2)}, u32[]{:S(2)}) collective-permute-start(bf16[1024,256]{1,0:T(8,128)(2,1)S(1)} %get-tuple-element.31), channel_id=1, source_target_pairs={{0,2},{2,0},{1,3},{3,1},{4,6},{6,4},{5,7},{7,5},{8,10},{10,8},{9,1... | collective-permute-start | bytes 1572872 | tf_op jit(solution)/shard_map/ppermute | solution.py:24
  9.3 2.0 %collective-permute-done.5.refs_2_.refs_7_ = bf16[512,256]{1,0:T(8,128)(2,1)S(1)} collective-permute-done((bf16[512,256]{1,0:T(8,128)(2,1)S(1)}, bf16[512,256]{1,0:T(8,128)(2,1)S(1)}, u32[]{:S(2)}, u32[]{:S(2)}) %collective-permute-start.5) | collective-permute-done | bytes 262176 | tf_op jit(solution)/shard_map/ppermute | solution.py:24
  11.3 1.5 %collective-permute-start.3 = (bf16[512,256]{1,0:T(8,128)(2,1)S(1)}, bf16[512,256]{1,0:T(8,128)(2,1)S(1)}, u32[]{:S(2)}, u32[]{:S(2)}) collective-permute-start(bf16[512,256]{1,0:T(8,128)(2,1)S(1)} %get-tuple-element.29), channel_id=1, source_target_pairs={{0,2},{2,0},{1,3},{3,1},{4,6},{6,4},{5,7},{7,5},{8,10},{10,8},{9,1... | collective-permute-start | bytes 786440 | tf_op jit(solution)/shard_map/ppermute | solution.py:24
  12.8 4.2 %collective-permute-done.11.refs_2_ = bf16[512,256]{1,0:T(8,128)(2,1)} collective-permute-done((bf16[512,256]{1,0:T(8,128)(2,1)S(1)}, bf16[512,256]{1,0:T(8,128)(2,1)}, u32[]{:S(2)}, u32[]{:S(2)}) %collective-permute-start.11) | collective-permute-done | bytes 262176 | tf_op jit(solution)/shard_map/ppermute | solution.py:24
  17.0 2.3 %collective-permute-start.17 = (bf16[512,256]{1,0:T(8,128)(2,1)S(1)}, bf16[512,256]{1,0:T(8,128)(2,1)S(1)}, u32[]{:S(2)}, u32[]{:S(2)}) collective-permute-start(bf16[512,256]{1,0:T(8,128)(2,1)S(1)} %get-tuple-element.27), channel_id=1, source_target_pairs={{4,0},{8,4},{12,8},{5,1},{9,5},{13,9},{6,2},{10,6},{14,10},{7,3},{... | collective-permute-start | bytes 786440 | tf_op jit(solution)/shard_map/ppermute | solution.py:289
  19.4 3.5 %collective-permute-start.14 = (bf16[512,256]{1,0:T(8,128)(2,1)S(1)}, bf16[512,256]{1,0:T(8,128)(2,1)}, u32[]{:S(2)}, u32[]{:S(2)}) collective-permute-start(bf16[512,256]{1,0:T(8,128)(2,1)S(1)} %collective-permute-done.5.refs_2_.refs_7_), channel_id=1, source_target_pairs={{0,4},{4,8},{8,12},{1,5},{5,9},{9,13},{2,6},{6,10},{10,14},{3,7},{... | collective-permute-start | bytes 786440 | tf_op jit(solution)/shard_map/ppermute | solution.py:288
  22.9 10.3 %collective-permute-done.3.refs_2_.refs_5_ = bf16[512,256]{1,0:T(8,128)(2,1)S(1)} collective-permute-done((bf16[512,256]{1,0:T(8,128)(2,1)S(1)}, bf16[512,256]{1,0:T(8,128)(2,1)S(1)}, u32[]{:S(2)}, u32[]{:S(2)}) %collective-permute-start.3) | collective-permute-done | bytes 262176 | tf_op jit(solution)/shard_map/ppermute | solution.py:24
  33.1 1.5 %collective-permute-start.7 = (bf16[1024,256]{1,0:T(8,128)(2,1)S(1)}, bf16[1024,256]{1,0:T(8,128)(2,1)S(1)}, u32[]{:S(2)}, u32[]{:S(2)}) collective-permute-start(bf16[1024,256]{1,0:T(8,128)(2,1)S(1)} %get-tuple-element.32), channel_id=1, source_target_pairs={{0,2},{2,0},{1,3},{3,1},{4,6},{6,4},{5,7},{7,5},{8,10},{10,8},{9,1... | collective-permute-start | bytes 1572872 | tf_op jit(solution)/shard_map/ppermute | solution.py:24
  34.6 0.5 collective-permute-start.15
  35.2 0.7 copy-done.1
  35.9 0.5 collective-permute-done.12.refs_4_
  36.4 0.7 copy-done.3
  37.1 2.3 %collective-permute-start.18 = (bf16[512,256]{1,0:T(8,128)(2,1)}, bf16[512,256]{1,0:T(8,128)(2,1)}, u32[]{:S(2)}, u32[]{:S(2)}) collective-permute-start(bf16[512,256]{1,0:T(8,128)(2,1)} %collective-permute-done.11.refs_2_), channel_id=1, source_target_pairs={{4,0},{8,4},{12,8},{5,1},{9,5},{13,9},{6,2},{10,6},{14,10},{7,3},{... | collective-permute-start | bytes 786440 | tf_op jit(solution)/shard_map/ppermute | solution.py:289
  39.5 0.7 copy-done.5
  40.2 6.3 %collective-permute-done.7.refs_2_.refs_5_ = bf16[1024,256]{1,0:T(8,128)(2,1)S(1)} collective-permute-done((bf16[1024,256]{1,0:T(8,128)(2,1)S(1)}, bf16[1024,256]{1,0:T(8,128)(2,1)S(1)}, u32[]{:S(2)}, u32[]{:S(2)}) %collective-permute-start.7) | collective-permute-done | bytes 524320 | tf_op jit(solution)/shard_map/ppermute | solution.py:24
  46.6 1.1 %collective-permute-done.18.refs_6_ = bf16[512,256]{1,0:T(8,128)(2,1)} collective-permute-done((bf16[512,256]{1,0:T(8,128)(2,1)}, bf16[512,256]{1,0:T(8,128)(2,1)}, u32[]{:S(2)}, u32[]{:S(2)}) %collective-permute-start.18) | collective-permute-done | bytes 262176 | tf_op jit(solution)/shard_map/ppermute | solution.py:289
  47.6 0.5 collective-permute-start
  48.2 0.1 collective-permute-start.6
  48.3 0.4 collective-permute-start.19
  48.8 0.9 %copy-done.2 = bf16[512,256]{1,0:T(8,128)(2,1)S(1)} copy-done((bf16[512,256]{1,0:T(8,128)(2,1)S(1)}, bf16[512,256]{1,0:T(8,128)(2,1)}, u32[]{:S(2)}) %copy-start.2) | copy-done | bytes 262168
  49.8 0.9 %copy-done.4 = bf16[512,256]{1,0:T(8,128)(2,1)S(1)} copy-done((bf16[512,256]{1,0:T(8,128)(2,1)S(1)}, bf16[512,256]{1,0:T(8,128)(2,1)}, u32[]{:S(2)}) %copy-start.4) | copy-done | bytes 262168
  50.7 0.9 %copy-done.6 = bf16[512,256]{1,0:T(8,128)(2,1)S(1)} copy-done((bf16[512,256]{1,0:T(8,128)(2,1)S(1)}, bf16[512,256]{1,0:T(8,128)(2,1)}, u32[]{:S(2)}) %copy-start.6) | copy-done | bytes 262168
  51.7 11.0 %shard_map.28 = (bf16[4096,256]{1,0:T(8,128)(2,1)}, f32[256,256]{1,0:T(8,128)S(1)}, f32[256,256]{1,0:T(8,128)S(1)}) custom-call(f32[32,9]{1,0:T(8,128)S(1)} %copy.10.refs_0_, bf16[4096,256]{1,0:T(8,128)(2,1)S(1)} %copy-done, bf16[512,256]{1,0:T(8,128)(2,1)} %collective-permute-done.11.refs_2_, bf16[4096,256]{1,0:T(8,128)(2,1)} %collective-permute-done.1.refs_3_, ...), custom_call_target="tpu_custom_call" | custom-call | flops 3623878656 | bytes 5767168 | tf_op jit(solution)/shard_map/pallas_call | solution.py:217
  62.7 0.5 collective-permute-start.4
  63.3 8.6 %shard_map.29 = (bf16[4096,256]{1,0:T(8,128)(2,1)}, f32[256,256]{1,0:T(8,128)S(1)}, f32[256,256]{1,0:T(8,128)S(1)}) custom-call(f32[32,9]{1,0:T(8,128)S(1)} %copy.10.refs_0_, bf16[4096,256]{1,0:T(8,128)(2,1)S(1)} %copy-done, bf16[1024,256]{1,0:T(8,128)(2,1)S(1)} %collective-permute-done.7.refs_2_.refs_5_, ...), custom_call_target="tpu_custom_call", output_to_operand_aliasing={{0}: (9, {})} | custom-call | flops 2415919104 | bytes 4718592 | tf_op jit(solution)/shard_map/pallas_call | solution.py:217
  71.9 5.6 %shard_map.31 = (f32[256,256]{1,0:T(8,128)S(1)}, f32[256,256]{1,0:T(8,128)S(1)}) custom-call(f32[32,9]{1,0:T(8,128)S(1)} %copy.10.refs_0_, bf16[4096,256]{1,0:T(8,128)(2,1)S(1)} %copy-done, bf16[512,256]{1,0:T(8,128)(2,1)S(1)} %collective-permute-done.5.refs_2_.refs_7_, bf16[4096,256]{1,0:T(8,128)(2,1)} %collective-permute-done.1.refs_3_, ...), custom_call_target="tpu_custom_call" | custom-call | flops 1207959552 | bytes 2097152 | tf_op jit(solution)/shard_map/pallas_call | solution.py:217
  77.5 6.6 %shard_map.30 = (bf16[4096,256]{1,0:T(8,128)(2,1)}, f32[256,256]{1,0:T(8,128)S(1)}, f32[256,256]{1,0:T(8,128)S(1)}) custom-call(f32[32,9]{1,0:T(8,128)S(1)} %copy.10.refs_0_, bf16[4096,256]{1,0:T(8,128)(2,1)S(1)} %copy-done, bf16[512,256]{1,0:T(8,128)(2,1)S(1)} %collective-permute-done.3.refs_2_.refs_5_, ...), custom_call_target="tpu_custom_call", output_to_operand_aliasing={{0}: (9, {})} | custom-call | flops 1207959552 | bytes 2883584 | tf_op jit(solution)/shard_map/pallas_call | solution.py:217
  84.2 9.3 %shard_map.32 = bf16[4096,256]{1,0:T(8,128)(2,1)} custom-call(f32[32,9]{1,0:T(8,128)S(1)} %copy.10.refs_0_, bf16[4096,256]{1,0:T(8,128)(2,1)S(1)} %copy-done, bf16[512,256]{1,0:T(8,128)(2,1)S(1)} %collective-permute-done.refs_2_, bf16[4096,256]{1,0:T(8,128)(2,1)} %collective-permute-done.1.refs_3_, ...), custom_call_target="tpu_custom_call", output_to_operand_aliasing={{}: (13, {})} | custom-call | flops 1811939328 | bytes 5505024 | tf_op jit(solution)/shard_map/pallas_call | solution.py:217
  (34 shorter events, 0.5 us)
Async XLA Ops:
  0.0 7.7 %copy-start = (bf16[4096,256]{1,0:T(8,128)(2,1)S(1)}, bf16[4096,256]{1,0:T(8,128)(2,1)}, u32[]{:S(2)}) copy-start(bf16[4096,256]{1,0:T(8,128)(2,1)} %refs_1_.9) | copy-start | bytes 6291460
  0.0 46.5 %copy-start.7 = (f32[32,9]{0,1:T(8,128)S(1)}, f32[32,9]{0,1:T(8,128)}, u32[]{:S(2)}) copy-start(f32[32,9]{0,1:T(8,128)} %param.3) | copy-start | bytes 3460
  0.0 48.7 %collective-permute-start.1 = (bf16[4096,256]{1,0:T(8,128)(2,1)}, bf16[4096,256]{1,0:T(8,128)(2,1)}, u32[]{:S(2)}, u32[]{:S(2)}) collective-permute-start(bf16[4096,256]{1,0:T(8,128)(2,1)} %refs_1_.9), channel_id=1, source_target_pairs={{0,1},{1,0},{2,3},{3,2},{4,5},{5,4},{6,7},{7,6},{8,9},{9,8},{10,11... | collective-permute-start | bytes 6291464 | tf_op jit(solution)/shard_map/ppermute | solution.py:24
  2.1 9.2 %collective-permute-start.5 = (bf16[512,256]{1,0:T(8,128)(2,1)S(1)}, bf16[512,256]{1,0:T(8,128)(2,1)S(1)}, u32[]{:S(2)}, u32[]{:S(2)}) collective-permute-start(bf16[512,256]{1,0:T(8,128)(2,1)S(1)} %get-tuple-element.28), channel_id=1, source_target_pairs={{0,2},{2,0},{1,3},{3,1},{4,6},{6,4},{5,7},{7,5},{8,10},{10,8},{9,1... | collective-permute-start | bytes 786440 | tf_op jit(solution)/shard_map/ppermute | solution.py:24
  3.6 15.8 %collective-permute-start.13 = (bf16[512,256]{1,0:T(8,128)(2,1)S(1)}, bf16[512,256]{1,0:T(8,128)(2,1)S(1)}, u32[]{:S(2)}, u32[]{:S(2)}) collective-permute-start(bf16[512,256]{1,0:T(8,128)(2,1)S(1)} %get-tuple-element.28), channel_id=1, source_target_pairs={{0,4},{4,8},{8,12},{1,5},{5,9},{9,13},{2,6},{6,10},{10,14},{3,7},{... | collective-permute-start | bytes 786440 | tf_op jit(solution)/shard_map/ppermute | solution.py:288
  7.1 9.9 %collective-permute-start.11 = (bf16[512,256]{1,0:T(8,128)(2,1)S(1)}, bf16[512,256]{1,0:T(8,128)(2,1)}, u32[]{:S(2)}, u32[]{:S(2)}) collective-permute-start(bf16[512,256]{1,0:T(8,128)(2,1)S(1)} %get-tuple-element.27), channel_id=1, source_target_pairs={{0,2},{2,0},{1,3},{3,1},{4,6},{6,4},{5,7},{7,5},{8,10},{10,8},{9,1... | collective-permute-start | bytes 786440 | tf_op jit(solution)/shard_map/ppermute | solution.py:24
  7.8 28.1 %collective-permute-start.9 = (bf16[1024,256]{1,0:T(8,128)(2,1)S(1)}, bf16[1024,256]{1,0:T(8,128)(2,1)}, u32[]{:S(2)}, u32[]{:S(2)}) collective-permute-start(bf16[1024,256]{1,0:T(8,128)(2,1)S(1)} %get-tuple-element.31), channel_id=1, source_target_pairs={{0,2},{2,0},{1,3},{3,1},{4,6},{6,4},{5,7},{7,5},{8,10},{10,8},{9,1... | collective-permute-start | bytes 1572872 | tf_op jit(solution)/shard_map/ppermute | solution.py:24
  11.3 21.9 %collective-permute-start.3 = (bf16[512,256]{1,0:T(8,128)(2,1)S(1)}, bf16[512,256]{1,0:T(8,128)(2,1)S(1)}, u32[]{:S(2)}, u32[]{:S(2)}) collective-permute-start(bf16[512,256]{1,0:T(8,128)(2,1)S(1)} %get-tuple-element.29), channel_id=1, source_target_pairs={{0,2},{2,0},{1,3},{3,1},{4,6},{6,4},{5,7},{7,5},{8,10},{10,8},{9,1... | collective-permute-start | bytes 786440 | tf_op jit(solution)/shard_map/ppermute | solution.py:24
  17.0 17.6 %collective-permute-start.17 = (bf16[512,256]{1,0:T(8,128)(2,1)S(1)}, bf16[512,256]{1,0:T(8,128)(2,1)S(1)}, u32[]{:S(2)}, u32[]{:S(2)}) collective-permute-start(bf16[512,256]{1,0:T(8,128)(2,1)S(1)} %get-tuple-element.27), channel_id=1, source_target_pairs={{4,0},{8,4},{12,8},{5,1},{9,5},{13,9},{6,2},{10,6},{14,10},{7,3},{... | collective-permute-start | bytes 786440 | tf_op jit(solution)/shard_map/ppermute | solution.py:289
  19.4 15.3 %collective-permute-start.14 = (bf16[512,256]{1,0:T(8,128)(2,1)S(1)}, bf16[512,256]{1,0:T(8,128)(2,1)}, u32[]{:S(2)}, u32[]{:S(2)}) collective-permute-start(bf16[512,256]{1,0:T(8,128)(2,1)S(1)} %collective-permute-done.5.refs_2_.refs_7_), channel_id=1, source_target_pairs={{0,4},{4,8},{8,12},{1,5},{5,9},{9,13},{2,6},{6,10},{10,14},{3,7},{... | collective-permute-start | bytes 786440 | tf_op jit(solution)/shard_map/ppermute | solution.py:288
  33.1 13.3 %collective-permute-start.7 = (bf16[1024,256]{1,0:T(8,128)(2,1)S(1)}, bf16[1024,256]{1,0:T(8,128)(2,1)S(1)}, u32[]{:S(2)}, u32[]{:S(2)}) collective-permute-start(bf16[1024,256]{1,0:T(8,128)(2,1)S(1)} %get-tuple-element.32), channel_id=1, source_target_pairs={{0,2},{2,0},{1,3},{3,1},{4,6},{6,4},{5,7},{7,5},{8,10},{10,8},{9,1... | collective-permute-start | bytes 1572872 | tf_op jit(solution)/shard_map/ppermute | solution.py:24
  34.6 1.7 %collective-permute-start.12 = (bf16[512,256]{1,0:T(8,128)(2,1)}, bf16[512,256]{1,0:T(8,128)(2,1)S(1)}, u32[]{:S(2)}, u32[]{:S(2)}) collective-permute-start(bf16[512,256]{1,0:T(8,128)(2,1)} %collective-permute-done.11.refs_2_), channel_id=1, source_target_pairs={{0,1},{1,0},{2,3},{3,2},{4,5},{5,4},{6,7},{7,6},{8,9},{9,8},{10,11... | collective-permute-start | bytes 786440 | tf_op jit(solution)/shard_map/ppermute | solution.py:24
  34.6 4.8 %collective-permute-start.15 = (bf16[512,256]{1,0:T(8,128)(2,1)S(1)}, bf16[512,256]{1,0:T(8,128)(2,1)S(1)}, u32[]{:S(2)}, u32[]{:S(2)}) collective-permute-start(bf16[512,256]{1,0:T(8,128)(2,1)S(1)} %collective-permute-done.13.refs_5_), channel_id=1, source_target_pairs={{0,1},{1,0},{2,3},{3,2},{4,5},{5,4},{6,7},{7,6},{8,9},{9,8},{10,11... | collective-permute-start | bytes 786440 | tf_op jit(solution)/shard_map/ppermute | solution.py:24
  35.2 0.7 copy-start.1
  35.9 12.4 %collective-permute-start.10 = (bf16[1024,256]{1,0:T(8,128)(2,1)}, bf16[1024,256]{1,0:T(8,128)(2,1)}, u32[]{:S(2)}, u32[]{:S(2)}) collective-permute-start(bf16[1024,256]{1,0:T(8,128)(2,1)} %collective-permute-done.9.refs_9_.refs_5_), channel_id=1, source_target_pairs={{0,1},{1,0},{2,3},{3,2},{4,5},{5,4},{6,7},{7,6},{8,9},{9,8},{10,11... | collective-permute-start | bytes 1572872 | tf_op jit(solution)/shard_map/ppermute | solution.py:24
  36.4 0.7 copy-start.3
  37.1 10.5 %collective-permute-start.18 = (bf16[512,256]{1,0:T(8,128)(2,1)}, bf16[512,256]{1,0:T(8,128)(2,1)}, u32[]{:S(2)}, u32[]{:S(2)}) collective-permute-start(bf16[512,256]{1,0:T(8,128)(2,1)} %collective-permute-done.11.refs_2_), channel_id=1, source_target_pairs={{4,0},{8,4},{12,8},{5,1},{9,5},{13,9},{6,2},{10,6},{14,10},{7,3},{... | collective-permute-start | bytes 786440 | tf_op jit(solution)/shard_map/ppermute | solution.py:289
  39.5 0.7 copy-start.5
  40.2 8.0 %collective-permute-start.16 = (bf16[512,256]{1,0:T(8,128)(2,1)}, bf16[512,256]{1,0:T(8,128)(2,1)}, u32[]{:S(2)}, u32[]{:S(2)}) collective-permute-start(bf16[512,256]{1,0:T(8,128)(2,1)} %collective-permute-done.14.refs_6_), channel_id=1, source_target_pairs={{0,1},{1,0},{2,3},{3,2},{4,5},{5,4},{6,7},{7,6},{8,9},{9,8},{10,11... | collective-permute-start | bytes 786440 | tf_op jit(solution)/shard_map/ppermute | solution.py:24
  46.5 16.7 %collective-permute-start.8 = (bf16[1024,256]{1,0:T(8,128)(2,1)S(1)}, bf16[1024,256]{1,0:T(8,128)(2,1)}, u32[]{:S(2)}, u32[]{:S(2)}) collective-permute-start(bf16[1024,256]{1,0:T(8,128)(2,1)S(1)} %collective-permute-done.7.refs_2_.refs_5_), channel_id=1, source_target_pairs={{0,1},{1,0},{2,3},{3,2},{4,5},{5,4},{6,7},{7,6},{8,9},{9,8},{10,11... | collective-permute-start | bytes 1572872 | tf_op jit(solution)/shard_map/ppermute | solution.py:24
  47.6 15.1 %collective-permute-start = (bf16[512,256]{1,0:T(8,128)(2,1)}, bf16[512,256]{1,0:T(8,128)(2,1)S(1)}, u32[]{:S(2)}, u32[]{:S(2)}) collective-permute-start(bf16[512,256]{1,0:T(8,128)(2,1)} %get-tuple-element.30), channel_id=1, source_target_pairs={{0,2},{2,0},{1,3},{3,1},{4,6},{6,4},{5,7},{7,5},{8,10},{10,8},{9,1... | collective-permute-start | bytes 786440 | tf_op jit(solution)/shard_map/ppermute | solution.py:24
  48.2 23.7 %collective-permute-start.6 = (bf16[512,256]{1,0:T(8,128)(2,1)S(1)}, bf16[512,256]{1,0:T(8,128)(2,1)S(1)}, u32[]{:S(2)}, u32[]{:S(2)}) collective-permute-start(bf16[512,256]{1,0:T(8,128)(2,1)S(1)} %collective-permute-done.5.refs_2_.refs_7_), channel_id=1, source_target_pairs={{0,1},{1,0},{2,3},{3,2},{4,5},{5,4},{6,7},{7,6},{8,9},{9,8},{10,11... | collective-permute-start | bytes 786440 | tf_op jit(solution)/shard_map/ppermute | solution.py:24
  48.3 23.6 %collective-permute-start.19 = (bf16[512,256]{1,0:T(8,128)(2,1)S(1)}, bf16[512,256]{1,0:T(8,128)(2,1)S(1)}, u32[]{:S(2)}, u32[]{:S(2)}) collective-permute-start(bf16[512,256]{1,0:T(8,128)(2,1)S(1)} %collective-permute-done.17.refs_5_), channel_id=1, source_target_pairs={{0,1},{1,0},{2,3},{3,2},{4,5},{5,4},{6,7},{7,6},{8,9},{9,8},{10,11... | collective-permute-start | bytes 786440 | tf_op jit(solution)/shard_map/ppermute | solution.py:24
  48.7 23.2 %collective-permute-start.20 = (bf16[512,256]{1,0:T(8,128)(2,1)}, bf16[512,256]{1,0:T(8,128)(2,1)S(1)}, u32[]{:S(2)}, u32[]{:S(2)}) collective-permute-start(bf16[512,256]{1,0:T(8,128)(2,1)} %collective-permute-done.18.refs_6_), channel_id=1, source_target_pairs={{0,1},{1,0},{2,3},{3,2},{4,5},{5,4},{6,7},{7,6},{8,9},{9,8},{10,11... | collective-permute-start | bytes 786440 | tf_op jit(solution)/shard_map/ppermute | solution.py:24
  48.8 0.9 %copy-start.2 = (bf16[512,256]{1,0:T(8,128)(2,1)S(1)}, bf16[512,256]{1,0:T(8,128)(2,1)}, u32[]{:S(2)}) copy-start(bf16[512,256]{1,0:T(8,128)(2,1)} %copy-done.1) | copy-start | bytes 786436
  49.8 0.9 %copy-start.4 = (bf16[512,256]{1,0:T(8,128)(2,1)S(1)}, bf16[512,256]{1,0:T(8,128)(2,1)}, u32[]{:S(2)}) copy-start(bf16[512,256]{1,0:T(8,128)(2,1)} %copy-done.3) | copy-start | bytes 786436
  50.7 0.9 %copy-start.6 = (bf16[512,256]{1,0:T(8,128)(2,1)S(1)}, bf16[512,256]{1,0:T(8,128)(2,1)}, u32[]{:S(2)}) copy-start(bf16[512,256]{1,0:T(8,128)(2,1)} %copy-done.5) | copy-start | bytes 786436
  62.7 14.8 %collective-permute-start.4 = (bf16[512,256]{1,0:T(8,128)(2,1)S(1)}, bf16[512,256]{1,0:T(8,128)(2,1)S(1)}, u32[]{:S(2)}, u32[]{:S(2)}) collective-permute-start(bf16[512,256]{1,0:T(8,128)(2,1)S(1)} %collective-permute-done.3.refs_2_.refs_5_), channel_id=1, source_target_pairs={{0,1},{1,0},{2,3},{3,2},{4,5},{5,4},{6,7},{7,6},{8,9},{9,8},{10,11... | collective-permute-start | bytes 786440 | tf_op jit(solution)/shard_map/ppermute | solution.py:24
  63.2 21.0 %collective-permute-start.2 = (bf16[512,256]{1,0:T(8,128)(2,1)S(1)}, bf16[512,256]{1,0:T(8,128)(2,1)S(1)}, u32[]{:S(2)}, u32[]{:S(2)}) collective-permute-start(bf16[512,256]{1,0:T(8,128)(2,1)S(1)} %collective-permute-done.refs_2_), channel_id=1, source_target_pairs={{0,1},{1,0},{2,3},{3,2},{4,5},{5,4},{6,7},{7,6},{8,9},{9,8},{10,11... | collective-permute-start | bytes 786440 | tf_op jit(solution)/shard_map/ppermute | solution.py:24

commit v2 on v1

--- a/solution.py
+++ b/solution.py
@@ -31,10 +31,10 @@
 
 
 def update_kernel(job, *refs):
-    slots, parts = job["slots"], job["parts"]
+    slots = job["slots"]
     plan, steps, owned = job["plan"], job["steps"], job["owned"]
     acc_in, acc_out, finished = job["acc_in"], job["acc_out"], job["finished"]
-    arrays = job["arrays"]
+    arrays, members = job["arrays"], job["members"]
     taper = refs[0]
     sources = refs[1 : 1 + arrays]
     inputs = refs[1 + arrays : 1 + arrays + len(acc_in)]
@@ -42,12 +42,14 @@
     if finished:
         out, outs = outs[0], outs[1:]
     carried, outs = outs[: len(acc_out)], outs[len(acc_out) :]
-    ybuf, acc, wcol, wrow, obuf, in_sem, acc_sem, out_sem = outs
+    ybuf, acc, obuf, in_sem, acc_sem, out_sem = outs
 
     def fetch(n):
         array, part, start, slot = plan[n]
         return pltpu.make_async_copy(
-            sources[array].at[tile_rows(start)], ybuf.at[part, slot], in_sem.at[n]
+            sources[array].at[tile_rows(start)],
+            ybuf.at[slot, :, pl.ds(part * members, members)],
+            in_sem.at[n],
         )
 
     def take(n):
@@ -77,7 +79,10 @@
             acc[slot] = value
         begun.add(pair)
 
-    def weighted(c, i_pair, j_pair, base, flip):
+    def own(pair):
+        return ybuf[slots[pair], :, :members]
+
+    def weighted(c, i_pair, j_pair, flip):
         rows = []
         for ii in range(PAIR):
             row = []
@@ -86,10 +91,7 @@
                 slot = (i - j if flip else j - i) + REACH
                 if 0 <= slot < SLOTS:
                     weight = taper[j if flip else i, slot] * FACTOR
-                    tile = c[
-                        base + ii * BLOCK : base + (ii + 1) * BLOCK,
-                        jj * BLOCK : (jj + 1) * BLOCK,
-                    ]
+                    tile = c[ii * BLOCK : (ii + 1) * BLOCK, jj * BLOCK : (jj + 1) * BLOCK]
                     row.append((tile * weight).astype(jnp.bfloat16))
                 else:
                     row.append(jnp.zeros((BLOCK, BLOCK), jnp.bfloat16))
@@ -98,42 +100,30 @@
 
     for j, first, count in steps:
         near = list(range(first, first + count))
-        for pair in near + [j]:
+        for pair in [j] + near:
             arrive(pair)
-        total = None
-        for part in range(parts):
-            left = ybuf[part, pl.ds(slots[first], count)].reshape(count * ROWS, -1)
-            term = lax.dot_general(
-                left,
-                ybuf[part, slots[j]],
-                (((1,), (1,)), ((), ())),
+        gram = lax.dot_general(
+            ybuf[pl.ds(slots[first], count)].reshape(count * ROWS, -1),
+            ybuf[slots[j]],
+            (((1,), (1,)), ((), ())),
+            preferred_element_type=jnp.float32,
+        )
+        tiles = {i: gram[n * ROWS : (n + 1) * ROWS] for n, i in enumerate(near)}
+        mine = [i for i in near if i in owned]
+        if mine:
+            value = jnp.dot(
+                jnp.concatenate([weighted(tiles[i], i, j, False) for i in mine], axis=0),
+                own(j),
                 preferred_element_type=jnp.float32,
             )
-            total = term if total is None else total + term
+            for n, i in enumerate(mine):
+                add(i, value[n * ROWS : (n + 1) * ROWS])
         others = [i for i in near if i != j]
-        for k, i in enumerate(near):
-            if i in owned:
-                wcol[tile_rows(k)] = weighted(total, i, j, k * ROWS, False)
-            if j in owned and i != j:
-                wrow[tile_rows(others.index(i))] = weighted(total, i, j, k * ROWS, True)
-        for k, i in enumerate(near):
-            if i in owned:
-                add(
-                    i,
-                    jnp.dot(
-                        wcol[tile_rows(k)],
-                        ybuf[0, slots[j]],
-                        preferred_element_type=jnp.float32,
-                    ),
-                )
         if j in owned and others:
             value = None
-            for k, i in enumerate(others):
-                term = lax.dot_general(
-                    wrow[tile_rows(k)],
-                    ybuf[0, slots[i]],
-                    (((0,), (0,)), ((), ())),
-                    preferred_element_type=jnp.float32,
+            for i in others:
+                term = jnp.dot(
+                    weighted(tiles[i], i, j, True).T, own(i), preferred_element_type=jnp.float32
                 )
                 value = term if value is None else value + term
             add(j, value)
@@ -155,8 +145,7 @@
     for n, pair in enumerate(finished):
         if pair in acc_in and pair not in begun:
             take(acc_in.index(pair)).wait()
-        own = ybuf[0, slots[pair]].astype(jnp.float32)
-        obuf[n] = (own - 0.5 * acc[slots[pair]]).astype(jnp.bfloat16)
+        obuf[n] = (own(pair).astype(jnp.float32) - 0.5 * acc[slots[pair]]).astype(jnp.bfloat16)
         store(n).start()
     for n in range(len(acc_out)):
         hand_on(n).wait()
@@ -198,6 +187,7 @@
     job = dict(
         slots=slots, parts=parts, plan=plan, steps=steps, owned=owned, acc_in=acc_in,
         acc_out=acc_out, finished=finished, arrays=len(arrays), aliased=aliased,
+        members=members,
     )
     operands = [taper] + arrays + [state[pair] for pair in acc_in]
     anywhere = pl.BlockSpec(memory_space=pl.ANY)
@@ -211,7 +201,6 @@
             operands.append(result)
             specs.append(anywhere)
     shapes += [jax.ShapeDtypeStruct((ROWS, members), jnp.float32)] * len(acc_out)
-    widest = max(count for _, _, count in steps)
     count = len(needed)
     products = sum(n for _, _, n in steps)
     outputs = pl.pallas_call(
@@ -221,10 +210,8 @@
         out_specs=[anywhere] * len(shapes),
         input_output_aliases=aliases,
         scratch_shapes=[
-            pltpu.VMEM((parts, count, ROWS, members), jnp.bfloat16),
+            pltpu.VMEM((count, ROWS, parts * members), jnp.bfloat16),
             pltpu.VMEM((count, ROWS, members), jnp.float32),
-            pltpu.VMEM((widest * ROWS, ROWS), jnp.bfloat16),
-            pltpu.VMEM((widest * ROWS, ROWS), jnp.bfloat16),
             pltpu.VMEM((max(len(finished), 1), ROWS, members), jnp.bfloat16),
             pltpu.SemaphoreType.DMA((len(plan),)),
             pltpu.SemaphoreType.DMA((max(len(acc_in), 1),)),

time: 95.4 us -> 90 us (0.943)
  the two profiles are of different devices: /device:TPU:12 before, /device:TPU:0 now
where the time goes in v2:
time: 90 us; the launch traced here: 89.6 us
  Pallas kernels  35.6 us (40%)
  waiting for transfers between devices  23.7 us (26%)
  starting transfers between devices  22.8 us (25%)
  local copies, waits for them, and re-layouts  7.21 us (8%)
    pallas_call x5, Pallas kernels, run_steps(): pl.pallas_call(functools.partial(update_kernel, job), out_shape=shapes, i...  35.6 us
    ppermute x17, waiting for transfers between devices, shifted(): lax.ppermute(value, axis, [(i, (i + s) % count) for i in range(count)])  22.6 us
    ppermute x17, starting transfers between devices, shifted(): lax.ppermute(value, axis, [(i, (i + s) % count) for i in range(count)])  11.4 us
    ppermute x2, starting transfers between devices, per_device(): before = (lax.ppermute(tail, 'region', down), -NEAR, NEAR)  8.84 us
    unnamed x17, local copies, waits for them, and re-layouts  5.05 us
    ppermute x2, starting transfers between devices, per_device(): after = (lax.ppermute(head, 'region', up), pairs, NEAR)  2.56 us
    slice x2, local copies, waits for them, and re-layouts, cut(): return lax.slice_in_dim(anomalies, first * ROWS, last * ROWS, axis=0)  2.16 us
  transfers between devices with their start and end apart: 21, of which 6 were waited for; matrix products, arithmetic and copies ran while one was open for 3% of the time, Pallas kernels for 32%

profile of v2, /device:TPU:0, one launch (start us, length us, event | category | flops | bytes accessed | tf_op | source)
XLA Modules:
  0.0 89.6 jit_solution(13470288998728762207)
XLA Ops:
  0.0 0.5 collective-permute-start.1
  0.5 2.1 %fusion = (bf16[512,256]{1,0:T(8,128)(2,1)S(1)}, bf16[512,256]{1,0:T(8,128)(2,1)S(1)}, bf16[512,256]{1,0:T(8,128)(2,1)S(1)}, bf16[512,256]{1,0:T(8,128)(2,1)}) fusion(bf16[4096,256]{1,0:T(8,128)(2,1)} %refs_1_.9), kind=kLoop, calls=%fused_computation | loop fusion | bytes 2097152 | tf_op jit(solution)/shard_map/slice | solution.py:257
  2.6 2.5 %collective-permute-start.5 = (bf16[512,256]{1,0:T(8,128)(2,1)S(1)}, bf16[512,256]{1,0:T(8,128)(2,1)S(1)}, u32[]{:S(2)}, u32[]{:S(2)}) collective-permute-start(bf16[512,256]{1,0:T(8,128)(2,1)S(1)} %get-tuple-element.28), channel_id=1, source_target_pairs={{0,2},{2,0},{1,3},{3,1},{4,6},{6,4},{5,7},{7,5},{8,10},{10,8},{9,1... | collective-permute-start | bytes 786440 | tf_op jit(solution)/shard_map/ppermute | solution.py:24
  5.1 3.5 %collective-permute-start.13 = (bf16[512,256]{1,0:T(8,128)(2,1)S(1)}, bf16[512,256]{1,0:T(8,128)(2,1)S(1)}, u32[]{:S(2)}, u32[]{:S(2)}) collective-permute-start(bf16[512,256]{1,0:T(8,128)(2,1)S(1)} %get-tuple-element.28), channel_id=1, source_target_pairs={{0,4},{4,8},{8,12},{1,5},{5,9},{9,13},{2,6},{6,10},{10,14},{3,7},{... | collective-permute-start | bytes 786440 | tf_op jit(solution)/shard_map/ppermute | solution.py:275
  8.6 0.6 collective-permute-start.11
  9.2 1.6 %collective-permute-start.9 = (bf16[1024,256]{1,0:T(8,128)(2,1)S(1)}, bf16[1024,256]{1,0:T(8,128)(2,1)}, u32[]{:S(2)}, u32[]{:S(2)}) collective-permute-start(bf16[1024,256]{1,0:T(8,128)(2,1)S(1)} %get-tuple-element.31), channel_id=1, source_target_pairs={{0,2},{2,0},{1,3},{3,1},{4,6},{6,4},{5,7},{7,5},{8,10},{10,8},{9,1... | collective-permute-start | bytes 1572872 | tf_op jit(solution)/shard_map/ppermute | solution.py:24
  10.8 1.4 %collective-permute-done.5.refs_2_.refs_7_ = bf16[512,256]{1,0:T(8,128)(2,1)S(1)} collective-permute-done((bf16[512,256]{1,0:T(8,128)(2,1)S(1)}, bf16[512,256]{1,0:T(8,128)(2,1)S(1)}, u32[]{:S(2)}, u32[]{:S(2)}) %collective-permute-start.5) | collective-permute-done | bytes 262176 | tf_op jit(solution)/shard_map/ppermute | solution.py:24
  12.2 2.0 %collective-permute-start.3 = (bf16[512,256]{1,0:T(8,128)(2,1)S(1)}, bf16[512,256]{1,0:T(8,128)(2,1)S(1)}, u32[]{:S(2)}, u32[]{:S(2)}) collective-permute-start(bf16[512,256]{1,0:T(8,128)(2,1)S(1)} %get-tuple-element.29), channel_id=1, source_target_pairs={{0,2},{2,0},{1,3},{3,1},{4,6},{6,4},{5,7},{7,5},{8,10},{10,8},{9,1... | collective-permute-start | bytes 786440 | tf_op jit(solution)/shard_map/ppermute | solution.py:24
  14.3 3.7 %collective-permute-done.11.refs_2_ = bf16[512,256]{1,0:T(8,128)(2,1)} collective-permute-done((bf16[512,256]{1,0:T(8,128)(2,1)S(1)}, bf16[512,256]{1,0:T(8,128)(2,1)}, u32[]{:S(2)}, u32[]{:S(2)}) %collective-permute-start.11) | collective-permute-done | bytes 262176 | tf_op jit(solution)/shard_map/ppermute | solution.py:24
  18.0 1.3 %collective-permute-start.17 = (bf16[512,256]{1,0:T(8,128)(2,1)S(1)}, bf16[512,256]{1,0:T(8,128)(2,1)S(1)}, u32[]{:S(2)}, u32[]{:S(2)}) collective-permute-start(bf16[512,256]{1,0:T(8,128)(2,1)S(1)} %get-tuple-element.27), channel_id=1, source_target_pairs={{4,0},{8,4},{12,8},{5,1},{9,5},{13,9},{6,2},{10,6},{14,10},{7,3},{... | collective-permute-start | bytes 786440 | tf_op jit(solution)/shard_map/ppermute | solution.py:276
  19.3 5.4 %collective-permute-start.14 = (bf16[512,256]{1,0:T(8,128)(2,1)S(1)}, bf16[512,256]{1,0:T(8,128)(2,1)}, u32[]{:S(2)}, u32[]{:S(2)}) collective-permute-start(bf16[512,256]{1,0:T(8,128)(2,1)S(1)} %collective-permute-done.5.refs_2_.refs_7_), channel_id=1, source_target_pairs={{0,4},{4,8},{8,12},{1,5},{5,9},{9,13},{2,6},{6,10},{10,14},{3,7},{... | collective-permute-start | bytes 786440 | tf_op jit(solution)/shard_map/ppermute | solution.py:275
  24.6 9.8 %collective-permute-done.3.refs_2_.refs_5_ = bf16[512,256]{1,0:T(8,128)(2,1)S(1)} collective-permute-done((bf16[512,256]{1,0:T(8,128)(2,1)S(1)}, bf16[512,256]{1,0:T(8,128)(2,1)S(1)}, u32[]{:S(2)}, u32[]{:S(2)}) %collective-permute-start.3) | collective-permute-done | bytes 262176 | tf_op jit(solution)/shard_map/ppermute | solution.py:24
  34.4 1.7 %collective-permute-start.7 = (bf16[1024,256]{1,0:T(8,128)(2,1)S(1)}, bf16[1024,256]{1,0:T(8,128)(2,1)S(1)}, u32[]{:S(2)}, u32[]{:S(2)}) collective-permute-start(bf16[1024,256]{1,0:T(8,128)(2,1)S(1)} %get-tuple-element.32), channel_id=1, source_target_pairs={{0,2},{2,0},{1,3},{3,1},{4,6},{6,4},{5,7},{7,5},{8,10},{10,8},{9,1... | collective-permute-start | bytes 1572872 | tf_op jit(solution)/shard_map/ppermute | solution.py:24
  36.1 0.5 collective-permute-start.15
  36.6 0.7 copy-done.1
  37.4 0.5 collective-permute-done.12.refs_4_
  37.9 0.7 copy-done.3
  38.6 1.3 %collective-permute-start.18 = (bf16[512,256]{1,0:T(8,128)(2,1)}, bf16[512,256]{1,0:T(8,128)(2,1)}, u32[]{:S(2)}, u32[]{:S(2)}) collective-permute-start(bf16[512,256]{1,0:T(8,128)(2,1)} %collective-permute-done.11.refs_2_), channel_id=1, source_target_pairs={{4,0},{8,4},{12,8},{5,1},{9,5},{13,9},{6,2},{10,6},{14,10},{7,3},{... | collective-permute-start | bytes 786440 | tf_op jit(solution)/shard_map/ppermute | solution.py:276
  39.9 0.7 copy-done.5
  40.7 7.3 %collective-permute-done.7.refs_2_.refs_5_ = bf16[1024,256]{1,0:T(8,128)(2,1)S(1)} collective-permute-done((bf16[1024,256]{1,0:T(8,128)(2,1)S(1)}, bf16[1024,256]{1,0:T(8,128)(2,1)S(1)}, u32[]{:S(2)}, u32[]{:S(2)}) %collective-permute-start.7) | collective-permute-done | bytes 524320 | tf_op jit(solution)/shard_map/ppermute | solution.py:24
  48.1 1.0 %collective-permute-done.18.refs_6_ = bf16[512,256]{1,0:T(8,128)(2,1)} collective-permute-done((bf16[512,256]{1,0:T(8,128)(2,1)}, bf16[512,256]{1,0:T(8,128)(2,1)}, u32[]{:S(2)}, u32[]{:S(2)}) %collective-permute-start.18) | collective-permute-done | bytes 262176 | tf_op jit(solution)/shard_map/ppermute | solution.py:276
  49.1 0.4 collective-permute-start
  49.8 0.3 collective-permute-start.19
  50.3 0.9 %copy-done.2 = bf16[512,256]{1,0:T(8,128)(2,1)S(1)} copy-done((bf16[512,256]{1,0:T(8,128)(2,1)S(1)}, bf16[512,256]{1,0:T(8,128)(2,1)}, u32[]{:S(2)}) %copy-start.2) | copy-done | bytes 262168
  51.2 0.9 %copy-done.4 = bf16[512,256]{1,0:T(8,128)(2,1)S(1)} copy-done((bf16[512,256]{1,0:T(8,128)(2,1)S(1)}, bf16[512,256]{1,0:T(8,128)(2,1)}, u32[]{:S(2)}) %copy-start.4) | copy-done | bytes 262168
  52.2 0.9 %copy-done.6 = bf16[512,256]{1,0:T(8,128)(2,1)S(1)} copy-done((bf16[512,256]{1,0:T(8,128)(2,1)S(1)}, bf16[512,256]{1,0:T(8,128)(2,1)}, u32[]{:S(2)}) %copy-start.6) | copy-done | bytes 262168
  53.1 10.3 %shard_map.28 = (bf16[4096,256]{1,0:T(8,128)(2,1)}, f32[256,256]{1,0:T(8,128)S(1)}, f32[256,256]{1,0:T(8,128)S(1)}) custom-call(f32[32,9]{1,0:T(8,128)S(1)} %copy.10.refs_0_, bf16[4096,256]{1,0:T(8,128)(2,1)S(1)} %copy-done, bf16[512,256]{1,0:T(8,128)(2,1)} %collective-permute-done.11.refs_2_, bf16[4096,256]{1,0:T(8,128)(2,1)} %collective-permute-done.1.refs_3_, ...), custom_call_target="tpu_custom_call" | custom-call | flops 3623878656 | bytes 5767168 | tf_op jit(solution)/shard_map/pallas_call | solution.py:206
  63.5 0.3 collective-permute-start.4
  64.0 8.2 %shard_map.29 = (bf16[4096,256]{1,0:T(8,128)(2,1)}, f32[256,256]{1,0:T(8,128)S(1)}, f32[256,256]{1,0:T(8,128)S(1)}) custom-call(f32[32,9]{1,0:T(8,128)S(1)} %copy.10.refs_0_, bf16[4096,256]{1,0:T(8,128)(2,1)S(1)} %copy-done, bf16[1024,256]{1,0:T(8,128)(2,1)S(1)} %collective-permute-done.7.refs_2_.refs_5_, ...), custom_call_target="tpu_custom_call", output_to_operand_aliasing={{0}: (9, {})} | custom-call | flops 2415919104 | bytes 4718592 | tf_op jit(solution)/shard_map/pallas_call | solution.py:206
  72.3 4.5 %shard_map.31 = (f32[256,256]{1,0:T(8,128)S(1)}, f32[256,256]{1,0:T(8,128)S(1)}) custom-call(f32[32,9]{1,0:T(8,128)S(1)} %copy.10.refs_0_, bf16[4096,256]{1,0:T(8,128)(2,1)S(1)} %copy-done, bf16[512,256]{1,0:T(8,128)(2,1)S(1)} %collective-permute-done.5.refs_2_.refs_7_, bf16[4096,256]{1,0:T(8,128)(2,1)} %collective-permute-done.1.refs_3_, ...), custom_call_target="tpu_custom_call" | custom-call | flops 1207959552 | bytes 2097152 | tf_op jit(solution)/shard_map/pallas_call | solution.py:206
  76.9 5.7 %shard_map.30 = (bf16[4096,256]{1,0:T(8,128)(2,1)}, f32[256,256]{1,0:T(8,128)S(1)}, f32[256,256]{1,0:T(8,128)S(1)}) custom-call(f32[32,9]{1,0:T(8,128)S(1)} %copy.10.refs_0_, bf16[4096,256]{1,0:T(8,128)(2,1)S(1)} %copy-done, bf16[512,256]{1,0:T(8,128)(2,1)S(1)} %collective-permute-done.3.refs_2_.refs_5_, ...), custom_call_target="tpu_custom_call", output_to_operand_aliasing={{0}: (9, {})} | custom-call | flops 1207959552 | bytes 2883584 | tf_op jit(solution)/shard_map/pallas_call | solution.py:206
  82.5 6.9 %shard_map.32 = bf16[4096,256]{1,0:T(8,128)(2,1)} custom-call(f32[32,9]{1,0:T(8,128)S(1)} %copy.10.refs_0_, bf16[4096,256]{1,0:T(8,128)(2,1)S(1)} %copy-done, bf16[512,256]{1,0:T(8,128)(2,1)S(1)} %collective-permute-done.refs_2_, bf16[4096,256]{1,0:T(8,128)(2,1)} %collective-permute-done.1.refs_3_, ...), custom_call_target="tpu_custom_call", output_to_operand_aliasing={{}: (13, {})} | custom-call | flops 1811939328 | bytes 5505024 | tf_op jit(solution)/shard_map/pallas_call | solution.py:206
  (34 shorter events, 1.1 us)
Async XLA Ops:
  0.0 9.2 %copy-start = (bf16[4096,256]{1,0:T(8,128)(2,1)S(1)}, bf16[4096,256]{1,0:T(8,128)(2,1)}, u32[]{:S(2)}) copy-start(bf16[4096,256]{1,0:T(8,128)(2,1)} %refs_1_.9) | copy-start | bytes 6291460
  0.0 48.0 %copy-start.7 = (f32[32,9]{0,1:T(8,128)S(1)}, f32[32,9]{0,1:T(8,128)}, u32[]{:S(2)}) copy-start(f32[32,9]{0,1:T(8,128)} %param.3) | copy-start | bytes 3460
  0.0 50.0 %collective-permute-start.1 = (bf16[4096,256]{1,0:T(8,128)(2,1)}, bf16[4096,256]{1,0:T(8,128)(2,1)}, u32[]{:S(2)}, u32[]{:S(2)}) collective-permute-start(bf16[4096,256]{1,0:T(8,128)(2,1)} %refs_1_.9), channel_id=1, source_target_pairs={{0,1},{1,0},{2,3},{3,2},{4,5},{5,4},{6,7},{7,6},{8,9},{9,8},{10,11... | collective-permute-start | bytes 6291464 | tf_op jit(solution)/shard_map/ppermute | solution.py:24
  2.6 9.6 %collective-permute-start.5 = (bf16[512,256]{1,0:T(8,128)(2,1)S(1)}, bf16[512,256]{1,0:T(8,128)(2,1)S(1)}, u32[]{:S(2)}, u32[]{:S(2)}) collective-permute-start(bf16[512,256]{1,0:T(8,128)(2,1)S(1)} %get-tuple-element.28), channel_id=1, source_target_pairs={{0,2},{2,0},{1,3},{3,1},{4,6},{6,4},{5,7},{7,5},{8,10},{10,8},{9,1... | collective-permute-start | bytes 786440 | tf_op jit(solution)/shard_map/ppermute | solution.py:24
  5.1 14.2 %collective-permute-start.13 = (bf16[512,256]{1,0:T(8,128)(2,1)S(1)}, bf16[512,256]{1,0:T(8,128)(2,1)S(1)}, u32[]{:S(2)}, u32[]{:S(2)}) collective-permute-start(bf16[512,256]{1,0:T(8,128)(2,1)S(1)} %get-tuple-element.28), channel_id=1, source_target_pairs={{0,4},{4,8},{8,12},{1,5},{5,9},{9,13},{2,6},{6,10},{10,14},{3,7},{... | collective-permute-start | bytes 786440 | tf_op jit(solution)/shard_map/ppermute | solution.py:275
  8.6 9.4 %collective-permute-start.11 = (bf16[512,256]{1,0:T(8,128)(2,1)S(1)}, bf16[512,256]{1,0:T(8,128)(2,1)}, u32[]{:S(2)}, u32[]{:S(2)}) collective-permute-start(bf16[512,256]{1,0:T(8,128)(2,1)S(1)} %get-tuple-element.27), channel_id=1, source_target_pairs={{0,2},{2,0},{1,3},{3,1},{4,6},{6,4},{5,7},{7,5},{8,10},{10,8},{9,1... | collective-permute-start | bytes 786440 | tf_op jit(solution)/shard_map/ppermute | solution.py:24
  9.2 28.1 %collective-permute-start.9 = (bf16[1024,256]{1,0:T(8,128)(2,1)S(1)}, bf16[1024,256]{1,0:T(8,128)(2,1)}, u32[]{:S(2)}, u32[]{:S(2)}) collective-permute-start(bf16[1024,256]{1,0:T(8,128)(2,1)S(1)} %get-tuple-element.31), channel_id=1, source_target_pairs={{0,2},{2,0},{1,3},{3,1},{4,6},{6,4},{5,7},{7,5},{8,10},{10,8},{9,1... | collective-permute-start | bytes 1572872 | tf_op jit(solution)/shard_map/ppermute | solution.py:24
  12.2 22.1 %collective-permute-start.3 = (bf16[512,256]{1,0:T(8,128)(2,1)S(1)}, bf16[512,256]{1,0:T(8,128)(2,1)S(1)}, u32[]{:S(2)}, u32[]{:S(2)}) collective-permute-start(bf16[512,256]{1,0:T(8,128)(2,1)S(1)} %get-tuple-element.29), channel_id=1, source_target_pairs={{0,2},{2,0},{1,3},{3,1},{4,6},{6,4},{5,7},{7,5},{8,10},{10,8},{9,1... | collective-permute-start | bytes 786440 | tf_op jit(solution)/shard_map/ppermute | solution.py:24
  18.0 18.2 %collective-permute-start.17 = (bf16[512,256]{1,0:T(8,128)(2,1)S(1)}, bf16[512,256]{1,0:T(8,128)(2,1)S(1)}, u32[]{:S(2)}, u32[]{:S(2)}) collective-permute-start(bf16[512,256]{1,0:T(8,128)(2,1)S(1)} %get-tuple-element.27), channel_id=1, source_target_pairs={{4,0},{8,4},{12,8},{5,1},{9,5},{13,9},{6,2},{10,6},{14,10},{7,3},{... | collective-permute-start | bytes 786440 | tf_op jit(solution)/shard_map/ppermute | solution.py:276
  19.3 16.9 %collective-permute-start.14 = (bf16[512,256]{1,0:T(8,128)(2,1)S(1)}, bf16[512,256]{1,0:T(8,128)(2,1)}, u32[]{:S(2)}, u32[]{:S(2)}) collective-permute-start(bf16[512,256]{1,0:T(8,128)(2,1)S(1)} %collective-permute-done.5.refs_2_.refs_7_), channel_id=1, source_target_pairs={{0,4},{4,8},{8,12},{1,5},{5,9},{9,13},{2,6},{6,10},{10,14},{3,7},{... | collective-permute-start | bytes 786440 | tf_op jit(solution)/shard_map/ppermute | solution.py:275
  34.4 13.6 %collective-permute-start.7 = (bf16[1024,256]{1,0:T(8,128)(2,1)S(1)}, bf16[1024,256]{1,0:T(8,128)(2,1)S(1)}, u32[]{:S(2)}, u32[]{:S(2)}) collective-permute-start(bf16[1024,256]{1,0:T(8,128)(2,1)S(1)} %get-tuple-element.32), channel_id=1, source_target_pairs={{0,2},{2,0},{1,3},{3,1},{4,6},{6,4},{5,7},{7,5},{8,10},{10,8},{9,1... | collective-permute-start | bytes 1572872 | tf_op jit(solution)/shard_map/ppermute | solution.py:24
  36.1 1.7 %collective-permute-start.12 = (bf16[512,256]{1,0:T(8,128)(2,1)}, bf16[512,256]{1,0:T(8,128)(2,1)S(1)}, u32[]{:S(2)}, u32[]{:S(2)}) collective-permute-start(bf16[512,256]{1,0:T(8,128)(2,1)} %collective-permute-done.11.refs_2_), channel_id=1, source_target_pairs={{0,1},{1,0},{2,3},{3,2},{4,5},{5,4},{6,7},{7,6},{8,9},{9,8},{10,11... | collective-permute-start | bytes 786440 | tf_op jit(solution)/shard_map/ppermute | solution.py:24
  36.1 3.7 %collective-permute-start.15 = (bf16[512,256]{1,0:T(8,128)(2,1)S(1)}, bf16[512,256]{1,0:T(8,128)(2,1)S(1)}, u32[]{:S(2)}, u32[]{:S(2)}) collective-permute-start(bf16[512,256]{1,0:T(8,128)(2,1)S(1)} %collective-permute-done.13.refs_5_), channel_id=1, source_target_pairs={{0,1},{1,0},{2,3},{3,2},{4,5},{5,4},{6,7},{7,6},{8,9},{9,8},{10,11... | collective-permute-start | bytes 786440 | tf_op jit(solution)/shard_map/ppermute | solution.py:24
  36.6 0.7 copy-start.1
  37.3 12.4 %collective-permute-start.10 = (bf16[1024,256]{1,0:T(8,128)(2,1)}, bf16[1024,256]{1,0:T(8,128)(2,1)}, u32[]{:S(2)}, u32[]{:S(2)}) collective-permute-start(bf16[1024,256]{1,0:T(8,128)(2,1)} %collective-permute-done.9.refs_9_.refs_5_), channel_id=1, source_target_pairs={{0,1},{1,0},{2,3},{3,2},{4,5},{5,4},{6,7},{7,6},{8,9},{9,8},{10,11... | collective-permute-start | bytes 1572872 | tf_op jit(solution)/shard_map/ppermute | solution.py:24
  37.9 0.7 copy-start.3
  38.6 10.5 %collective-permute-start.18 = (bf16[512,256]{1,0:T(8,128)(2,1)}, bf16[512,256]{1,0:T(8,128)(2,1)}, u32[]{:S(2)}, u32[]{:S(2)}) collective-permute-start(bf16[512,256]{1,0:T(8,128)(2,1)} %collective-permute-done.11.refs_2_), channel_id=1, source_target_pairs={{4,0},{8,4},{12,8},{5,1},{9,5},{13,9},{6,2},{10,6},{14,10},{7,3},{... | collective-permute-start | bytes 786440 | tf_op jit(solution)/shard_map/ppermute | solution.py:276
  39.9 0.7 copy-start.5
  40.6 9.0 %collective-permute-start.16 = (bf16[512,256]{1,0:T(8,128)(2,1)}, bf16[512,256]{1,0:T(8,128)(2,1)}, u32[]{:S(2)}, u32[]{:S(2)}) collective-permute-start(bf16[512,256]{1,0:T(8,128)(2,1)} %collective-permute-done.14.refs_6_), channel_id=1, source_target_pairs={{0,1},{1,0},{2,3},{3,2},{4,5},{5,4},{6,7},{7,6},{8,9},{9,8},{10,11... | collective-permute-start | bytes 786440 | tf_op jit(solution)/shard_map/ppermute | solution.py:24
  48.0 15.8 %collective-permute-start.8 = (bf16[1024,256]{1,0:T(8,128)(2,1)S(1)}, bf16[1024,256]{1,0:T(8,128)(2,1)}, u32[]{:S(2)}, u32[]{:S(2)}) collective-permute-start(bf16[1024,256]{1,0:T(8,128)(2,1)S(1)} %collective-permute-done.7.refs_2_.refs_5_), channel_id=1, source_target_pairs={{0,1},{1,0},{2,3},{3,2},{4,5},{5,4},{6,7},{7,6},{8,9},{9,8},{10,11... | collective-permute-start | bytes 1572872 | tf_op jit(solution)/shard_map/ppermute | solution.py:24
  49.1 14.3 %collective-permute-start = (bf16[512,256]{1,0:T(8,128)(2,1)}, bf16[512,256]{1,0:T(8,128)(2,1)S(1)}, u32[]{:S(2)}, u32[]{:S(2)}) collective-permute-start(bf16[512,256]{1,0:T(8,128)(2,1)} %get-tuple-element.30), channel_id=1, source_target_pairs={{0,2},{2,0},{1,3},{3,1},{4,6},{6,4},{5,7},{7,5},{8,10},{10,8},{9,1... | collective-permute-start | bytes 786440 | tf_op jit(solution)/shard_map/ppermute | solution.py:24
  49.5 22.7 %collective-permute-start.6 = (bf16[512,256]{1,0:T(8,128)(2,1)S(1)}, bf16[512,256]{1,0:T(8,128)(2,1)S(1)}, u32[]{:S(2)}, u32[]{:S(2)}) collective-permute-start(bf16[512,256]{1,0:T(8,128)(2,1)S(1)} %collective-permute-done.5.refs_2_.refs_7_), channel_id=1, source_target_pairs={{0,1},{1,0},{2,3},{3,2},{4,5},{5,4},{6,7},{7,6},{8,9},{9,8},{10,11... | collective-permute-start | bytes 786440 | tf_op jit(solution)/shard_map/ppermute | solution.py:24
  49.8 22.5 %collective-permute-start.19 = (bf16[512,256]{1,0:T(8,128)(2,1)S(1)}, bf16[512,256]{1,0:T(8,128)(2,1)S(1)}, u32[]{:S(2)}, u32[]{:S(2)}) collective-permute-start(bf16[512,256]{1,0:T(8,128)(2,1)S(1)} %collective-permute-done.17.refs_5_), channel_id=1, source_target_pairs={{0,1},{1,0},{2,3},{3,2},{4,5},{5,4},{6,7},{7,6},{8,9},{9,8},{10,11... | collective-permute-start | bytes 786440 | tf_op jit(solution)/shard_map/ppermute | solution.py:24
  50.1 22.2 %collective-permute-start.20 = (bf16[512,256]{1,0:T(8,128)(2,1)}, bf16[512,256]{1,0:T(8,128)(2,1)S(1)}, u32[]{:S(2)}, u32[]{:S(2)}) collective-permute-start(bf16[512,256]{1,0:T(8,128)(2,1)} %collective-permute-done.18.refs_6_), channel_id=1, source_target_pairs={{0,1},{1,0},{2,3},{3,2},{4,5},{5,4},{6,7},{7,6},{8,9},{9,8},{10,11... | collective-permute-start | bytes 786440 | tf_op jit(solution)/shard_map/ppermute | solution.py:24
  50.3 0.9 %copy-start.2 = (bf16[512,256]{1,0:T(8,128)(2,1)S(1)}, bf16[512,256]{1,0:T(8,128)(2,1)}, u32[]{:S(2)}) copy-start(bf16[512,256]{1,0:T(8,128)(2,1)} %copy-done.1) | copy-start | bytes 786436
  51.2 0.9 %copy-start.4 = (bf16[512,256]{1,0:T(8,128)(2,1)S(1)}, bf16[512,256]{1,0:T(8,128)(2,1)}, u32[]{:S(2)}) copy-start(bf16[512,256]{1,0:T(8,128)(2,1)} %copy-done.3) | copy-start | bytes 786436
  52.2 0.9 %copy-start.6 = (bf16[512,256]{1,0:T(8,128)(2,1)S(1)}, bf16[512,256]{1,0:T(8,128)(2,1)}, u32[]{:S(2)}) copy-start(bf16[512,256]{1,0:T(8,128)(2,1)} %copy-done.5) | copy-start | bytes 786436
  63.5 13.4 %collective-permute-start.4 = (bf16[512,256]{1,0:T(8,128)(2,1)S(1)}, bf16[512,256]{1,0:T(8,128)(2,1)S(1)}, u32[]{:S(2)}, u32[]{:S(2)}) collective-permute-start(bf16[512,256]{1,0:T(8,128)(2,1)S(1)} %collective-permute-done.3.refs_2_.refs_5_), channel_id=1, source_target_pairs={{0,1},{1,0},{2,3},{3,2},{4,5},{5,4},{6,7},{7,6},{8,9},{9,8},{10,11... | collective-permute-start | bytes 786440 | tf_op jit(solution)/shard_map/ppermute | solution.py:24
  63.8 18.7 %collective-permute-start.2 = (bf16[512,256]{1,0:T(8,128)(2,1)S(1)}, bf16[512,256]{1,0:T(8,128)(2,1)S(1)}, u32[]{:S(2)}, u32[]{:S(2)}) collective-permute-start(bf16[512,256]{1,0:T(8,128)(2,1)S(1)} %collective-permute-done.refs_2_), channel_id=1, source_target_pairs={{0,1},{1,0},{2,3},{3,2},{4,5},{5,4},{6,7},{7,6},{8,9},{9,8},{10,11... | collective-permute-start | bytes 786440 | tf_op jit(solution)/shard_map/ppermute | solution.py:24

commit v3 on v2

--- a/solution.py
+++ b/solution.py
@@ -31,56 +31,39 @@
 
 
 def update_kernel(job, *refs):
-    slots = job["slots"]
+    parts = job["parts"]
     plan, steps, owned = job["plan"], job["steps"], job["owned"]
     acc_in, acc_out, finished = job["acc_in"], job["acc_out"], job["finished"]
-    arrays, members = job["arrays"], job["members"]
+    arrays = job["arrays"]
     taper = refs[0]
     sources = refs[1 : 1 + arrays]
-    inputs = refs[1 + arrays : 1 + arrays + len(acc_in)]
+    inputs = dict(zip(acc_in, refs[1 + arrays : 1 + arrays + len(acc_in)]))
     outs = refs[1 + arrays + len(acc_in) + job["aliased"] :]
     if finished:
         out, outs = outs[0], outs[1:]
     carried, outs = outs[: len(acc_out)], outs[len(acc_out) :]
-    ybuf, acc, obuf, in_sem, acc_sem, out_sem = outs
-
-    def fetch(n):
-        array, part, start, slot = plan[n]
-        return pltpu.make_async_copy(
-            sources[array].at[tile_rows(start)],
-            ybuf.at[slot, :, pl.ds(part * members, members)],
-            in_sem.at[n],
-        )
-
-    def take(n):
-        return pltpu.make_async_copy(inputs[n], acc.at[slots[acc_in[n]]], acc_sem.at[n])
-
-    for n in range(len(plan)):
-        fetch(n).start()
-    for n in range(len(acc_in)):
-        take(n).start()
-    here, begun = set(), set()
-
-    def arrive(pair):
-        if pair not in here:
-            here.add(pair)
-            for n in range(len(plan)):
-                if plan[n][3] == slots[pair]:
-                    fetch(n).wait()
+    acc, obuf, out_sem = outs
+    sums = {pair: carried[n] for n, pair in enumerate(acc_out)}
+    sums |= {pair: acc.at[n] for n, pair in enumerate(finished)}
+    begun = set()
+
+    def piece(pair, part):
+        array, start = plan[pair, part]
+        return sources[array][tile_rows(start), :]
+
+    def held(pair):
+        return jnp.concatenate([piece(pair, part) for part in range(parts)], axis=1)
+
+    def own(pair):
+        return piece(pair, 0)
 
     def add(pair, value):
-        slot = slots[pair]
         if pair in begun:
-            acc[slot] = acc[slot] + value
+            value = sums[pair][...] + value
         elif pair in acc_in:
-            take(acc_in.index(pair)).wait()
-            acc[slot] = acc[slot] + value
-        else:
-            acc[slot] = value
+            value = inputs[pair][...] + value
+        sums[pair][...] = value
         begun.add(pair)
-
-    def own(pair):
-        return ybuf[slots[pair], :, :members]
 
     def weighted(c, i_pair, j_pair, flip):
         rows = []
@@ -100,11 +83,9 @@
 
     for j, first, count in steps:
         near = list(range(first, first + count))
-        for pair in [j] + near:
-            arrive(pair)
         gram = lax.dot_general(
-            ybuf[pl.ds(slots[first], count)].reshape(count * ROWS, -1),
-            ybuf[slots[j]],
+            jnp.concatenate([held(i) for i in near], axis=0),
+            held(j),
             (((1,), (1,)), ((), ())),
             preferred_element_type=jnp.float32,
         )
@@ -133,22 +114,10 @@
             obuf.at[n], out.at[tile_rows(finished[n])], out_sem.at[n]
         )
 
-    def hand_on(n):
-        return pltpu.make_async_copy(
-            acc.at[slots[acc_out[n]]], carried[n], out_sem.at[len(finished) + n]
-        )
-
-    for n, pair in enumerate(acc_out):
-        if pair in acc_in and pair not in begun:
-            take(acc_in.index(pair)).wait()
-        hand_on(n).start()
     for n, pair in enumerate(finished):
-        if pair in acc_in and pair not in begun:
-            take(acc_in.index(pair)).wait()
-        obuf[n] = (own(pair).astype(jnp.float32) - 0.5 * acc[slots[pair]]).astype(jnp.bfloat16)
+        update = (sums if pair in begun else inputs)[pair][...]
+        obuf[n] = (own(pair).astype(jnp.float32) - 0.5 * update).astype(jnp.bfloat16)
         store(n).start()
-    for n in range(len(acc_out)):
-        hand_on(n).wait()
     for n in range(len(finished)):
         store(n).wait()
 
@@ -159,7 +128,6 @@
     for j, first, count in steps:
         needed |= {j} | set(range(first, first + count))
     needed |= set(finished)
-    slots = {pair: n for n, pair in enumerate(sorted(needed))}
     touched = set()
     for j, first, count in steps:
         near = set(range(first, first + count))
@@ -168,30 +136,24 @@
             touched.add(j)
     acc_in = [pair for pair in sorted(touched | set(finished)) if pair in state]
     acc_out = sorted(touched - set(finished))
-    order = []
-    for j, first, count in steps:
-        for pair in [j] + list(range(first, first + count)):
-            if pair not in order:
-                order.append(pair)
-    order += [pair for pair in finished if pair not in order]
-    arrays, plan = [], []
-    for pair in order:
+    arrays, plan = [], {}
+    for pair in sorted(needed):
         for part in range(parts):
             array, start = pieces[part][pair]
             known = [n for n, other in enumerate(arrays) if other is array]
             if not known:
                 arrays.append(array)
                 known = [len(arrays) - 1]
-            plan.append((known[0], part, start, slots[pair]))
+            plan[pair, part] = (known[0], start)
     aliased = int(bool(finished) and result is not None)
     job = dict(
-        slots=slots, parts=parts, plan=plan, steps=steps, owned=owned, acc_in=acc_in,
+        parts=parts, plan=plan, steps=steps, owned=owned, acc_in=acc_in,
         acc_out=acc_out, finished=finished, arrays=len(arrays), aliased=aliased,
-        members=members,
     )
     operands = [taper] + arrays + [state[pair] for pair in acc_in]
     anywhere = pl.BlockSpec(memory_space=pl.ANY)
-    specs = [pl.BlockSpec(memory_space=pltpu.SMEM)] + [anywhere] * (len(operands) - 1)
+    inside = pl.BlockSpec(memory_space=pltpu.VMEM)
+    specs = [pl.BlockSpec(memory_space=pltpu.SMEM)] + [inside] * (len(operands) - 1)
     aliases = {}
     shapes = []
     if finished:
@@ -201,21 +163,17 @@
             operands.append(result)
             specs.append(anywhere)
     shapes += [jax.ShapeDtypeStruct((ROWS, members), jnp.float32)] * len(acc_out)
-    count = len(needed)
     products = sum(n for _, _, n in steps)
     outputs = pl.pallas_call(
         functools.partial(update_kernel, job),
         out_shape=shapes,
         in_specs=specs,
-        out_specs=[anywhere] * len(shapes),
+        out_specs=[anywhere] * int(bool(finished)) + [inside] * len(acc_out),
         input_output_aliases=aliases,
         scratch_shapes=[
-            pltpu.VMEM((count, ROWS, parts * members), jnp.bfloat16),
-            pltpu.VMEM((count, ROWS, members), jnp.float32),
+            pltpu.VMEM((max(len(finished), 1), ROWS, members), jnp.float32),
             pltpu.VMEM((max(len(finished), 1), ROWS, members), jnp.bfloat16),
-            pltpu.SemaphoreType.DMA((len(plan),)),
-            pltpu.SemaphoreType.DMA((max(len(acc_in), 1),)),
-            pltpu.SemaphoreType.DMA((len(finished) + len(acc_out),)),
+            pltpu.SemaphoreType.DMA((max(len(finished), 1),)),
         ],
         compiler_params=pltpu.CompilerParams(vmem_limit_bytes=32 * 2**20),
         cost_estimate=pl.CostEstimate(

time: 90 us -> 79.7 us (0.89)
  Pallas kernels: 35.6 us -> 25.5 us
    pallas_call x5, Pallas kernels: 35.6 us -> 25.5 us  [run_steps(): pl.pallas_call(functools.partial(update_kernel, job), out_shape=shapes, i...]
  transfers between devices with their start and end apart: 21 -> 21, of which waited for: 6 -> 6; matrix products, arithmetic and copies ran while one was open for 3% -> 3% of each run, Pallas kernels for 32% -> 26%
where the time goes in v3:
time: 79.7 us; the launch traced here: 79.3 us
  Pallas kernels  25.5 us (32%)
  waiting for transfers between devices  23.7 us (30%)
  starting transfers between devices  22.7 us (28%)
  local copies, waits for them, and re-layouts  7.25 us (9%)
    pallas_call x5, Pallas kernels, run_steps(): pl.pallas_call(functools.partial(update_kernel, job), out_shape=shapes, i...  25.5 us
    ppermute x17, waiting for transfers between devices, shifted(): lax.ppermute(value, axis, [(i, (i + s) % count) for i in range(count)])  22.6 us
    ppermute x17, starting transfers between devices, shifted(): lax.ppermute(value, axis, [(i, (i + s) % count) for i in range(count)])  11.3 us
    ppermute x2, starting transfers between devices, per_device(): before = (lax.ppermute(tail, 'region', down), -NEAR, NEAR)  8.84 us
    unnamed x17, local copies, waits for them, and re-layouts  5.09 us
    ppermute x2, starting transfers between devices, per_device(): after = (lax.ppermute(head, 'region', up), pairs, NEAR)  2.56 us
    slice x2, local copies, waits for them, and re-layouts, cut(): return lax.slice_in_dim(anomalies, first * ROWS, last * ROWS, axis=0)  2.16 us
  transfers between devices with their start and end apart: 21, of which 6 were waited for; matrix products, arithmetic and copies ran while one was open for 3% of the time, Pallas kernels for 26%

profile of v3, /device:TPU:0, one launch (start us, length us, event | category | flops | bytes accessed | tf_op | source)
XLA Modules:
  0.0 79.3 jit_solution(6989325665291701549)
XLA Ops:
  0.0 0.5 collective-permute-start.1
  0.5 2.1 %fusion = (bf16[512,256]{1,0:T(8,128)(2,1)S(1)}, bf16[512,256]{1,0:T(8,128)(2,1)S(1)}, bf16[512,256]{1,0:T(8,128)(2,1)}, bf16[512,256]{1,0:T(8,128)(2,1)S(1)}) fusion(bf16[4096,256]{1,0:T(8,128)(2,1)} %refs_1_.7), kind=kLoop, calls=%fused_computation | loop fusion | bytes 2097152 | tf_op jit(solution)/shard_map/slice | solution.py:215
  2.6 2.5 %collective-permute-start.5 = (bf16[512,256]{1,0:T(8,128)(2,1)S(1)}, bf16[512,256]{1,0:T(8,128)(2,1)S(1)}, u32[]{:S(2)}, u32[]{:S(2)}) collective-permute-start(bf16[512,256]{1,0:T(8,128)(2,1)S(1)} %get-tuple-element.28), channel_id=1, source_target_pairs={{0,2},{2,0},{1,3},{3,1},{4,6},{6,4},{5,7},{7,5},{8,10},{10,8},{9,1... | collective-permute-start | bytes 786440 | tf_op jit(solution)/shard_map/ppermute | solution.py:24
  5.1 3.5 %collective-permute-start.11 = (bf16[512,256]{1,0:T(8,128)(2,1)S(1)}, bf16[512,256]{1,0:T(8,128)(2,1)S(1)}, u32[]{:S(2)}, u32[]{:S(2)}) collective-permute-start(bf16[512,256]{1,0:T(8,128)(2,1)S(1)} %get-tuple-element.28), channel_id=1, source_target_pairs={{0,4},{4,8},{8,12},{1,5},{5,9},{9,13},{2,6},{6,10},{10,14},{3,7},{... | collective-permute-start | bytes 786440 | tf_op jit(solution)/shard_map/ppermute | solution.py:233
  8.6 0.6 collective-permute-start.15
  9.2 1.6 %collective-permute-start.9 = (bf16[1024,256]{1,0:T(8,128)(2,1)S(1)}, bf16[1024,256]{1,0:T(8,128)(2,1)}, u32[]{:S(2)}, u32[]{:S(2)}) collective-permute-start(bf16[1024,256]{1,0:T(8,128)(2,1)S(1)} %get-tuple-element.31), channel_id=1, source_target_pairs={{0,2},{2,0},{1,3},{3,1},{4,6},{6,4},{5,7},{7,5},{8,10},{10,8},{9,1... | collective-permute-start | bytes 1572872 | tf_op jit(solution)/shard_map/ppermute | solution.py:24
  10.8 1.4 %collective-permute-done.5.refs_2_.refs_7_ = bf16[512,256]{1,0:T(8,128)(2,1)S(1)} collective-permute-done((bf16[512,256]{1,0:T(8,128)(2,1)S(1)}, bf16[512,256]{1,0:T(8,128)(2,1)S(1)}, u32[]{:S(2)}, u32[]{:S(2)}) %collective-permute-start.5) | collective-permute-done | bytes 262176 | tf_op jit(solution)/shard_map/ppermute | solution.py:24
  12.2 2.0 %collective-permute-start = (bf16[512,256]{1,0:T(8,128)(2,1)S(1)}, bf16[512,256]{1,0:T(8,128)(2,1)S(1)}, u32[]{:S(2)}, u32[]{:S(2)}) collective-permute-start(bf16[512,256]{1,0:T(8,128)(2,1)S(1)} %get-tuple-element.30), channel_id=1, source_target_pairs={{0,2},{2,0},{1,3},{3,1},{4,6},{6,4},{5,7},{7,5},{8,10},{10,8},{9,1... | collective-permute-start | bytes 786440 | tf_op jit(solution)/shard_map/ppermute | solution.py:24
  14.3 3.7 %collective-permute-done.15.refs_6_ = bf16[512,256]{1,0:T(8,128)(2,1)} collective-permute-done((bf16[512,256]{1,0:T(8,128)(2,1)S(1)}, bf16[512,256]{1,0:T(8,128)(2,1)}, u32[]{:S(2)}, u32[]{:S(2)}) %collective-permute-start.15) | collective-permute-done | bytes 262176 | tf_op jit(solution)/shard_map/ppermute | solution.py:24
  18.0 1.3 %collective-permute-start.17 = (bf16[512,256]{1,0:T(8,128)(2,1)S(1)}, bf16[512,256]{1,0:T(8,128)(2,1)S(1)}, u32[]{:S(2)}, u32[]{:S(2)}) collective-permute-start(bf16[512,256]{1,0:T(8,128)(2,1)S(1)} %get-tuple-element.27), channel_id=1, source_target_pairs={{4,0},{8,4},{12,8},{5,1},{9,5},{13,9},{6,2},{10,6},{14,10},{7,3},{... | collective-permute-start | bytes 786440 | tf_op jit(solution)/shard_map/ppermute | solution.py:234
  19.3 5.4 %collective-permute-start.12 = (bf16[512,256]{1,0:T(8,128)(2,1)S(1)}, bf16[512,256]{1,0:T(8,128)(2,1)}, u32[]{:S(2)}, u32[]{:S(2)}) collective-permute-start(bf16[512,256]{1,0:T(8,128)(2,1)S(1)} %collective-permute-done.5.refs_2_.refs_7_), channel_id=1, source_target_pairs={{0,4},{4,8},{8,12},{1,5},{5,9},{9,13},{2,6},{6,10},{10,14},{3,7},{... | collective-permute-start | bytes 786440 | tf_op jit(solution)/shard_map/ppermute | solution.py:233
  24.6 9.8 %collective-permute-done.refs_5_.refs_2_ = bf16[512,256]{1,0:T(8,128)(2,1)S(1)} collective-permute-done((bf16[512,256]{1,0:T(8,128)(2,1)S(1)}, bf16[512,256]{1,0:T(8,128)(2,1)S(1)}, u32[]{:S(2)}, u32[]{:S(2)}) %collective-permute-start) | collective-permute-done | bytes 262176 | tf_op jit(solution)/shard_map/ppermute | solution.py:24
  34.4 1.7 %collective-permute-start.7 = (bf16[1024,256]{1,0:T(8,128)(2,1)S(1)}, bf16[1024,256]{1,0:T(8,128)(2,1)S(1)}, u32[]{:S(2)}, u32[]{:S(2)}) collective-permute-start(bf16[1024,256]{1,0:T(8,128)(2,1)S(1)} %get-tuple-element.32), channel_id=1, source_target_pairs={{0,2},{2,0},{1,3},{3,1},{4,6},{6,4},{5,7},{7,5},{8,10},{10,8},{9,1... | collective-permute-start | bytes 1572872 | tf_op jit(solution)/shard_map/ppermute | solution.py:24
  36.1 0.5 collective-permute-start.13
  36.6 0.7 copy-done.1
  37.4 0.5 collective-permute-done.16.refs_8_
  37.9 0.7 copy-done.3
  38.6 1.3 %collective-permute-start.18 = (bf16[512,256]{1,0:T(8,128)(2,1)}, bf16[512,256]{1,0:T(8,128)(2,1)}, u32[]{:S(2)}, u32[]{:S(2)}) collective-permute-start(bf16[512,256]{1,0:T(8,128)(2,1)} %collective-permute-done.15.refs_6_), channel_id=1, source_target_pairs={{4,0},{8,4},{12,8},{5,1},{9,5},{13,9},{6,2},{10,6},{14,10},{7,3},{... | collective-permute-start | bytes 786440 | tf_op jit(solution)/shard_map/ppermute | solution.py:234
  39.9 0.7 copy-done.5
  40.7 7.2 %collective-permute-done.7.refs_5_.refs_2_ = bf16[1024,256]{1,0:T(8,128)(2,1)S(1)} collective-permute-done((bf16[1024,256]{1,0:T(8,128)(2,1)S(1)}, bf16[1024,256]{1,0:T(8,128)(2,1)S(1)}, u32[]{:S(2)}, u32[]{:S(2)}) %collective-permute-start.7) | collective-permute-done | bytes 524320 | tf_op jit(solution)/shard_map/ppermute | solution.py:24
  48.1 1.1 %collective-permute-done.18.refs_6_ = bf16[512,256]{1,0:T(8,128)(2,1)} collective-permute-done((bf16[512,256]{1,0:T(8,128)(2,1)}, bf16[512,256]{1,0:T(8,128)(2,1)}, u32[]{:S(2)}, u32[]{:S(2)}) %collective-permute-start.18) | collective-permute-done | bytes 262176 | tf_op jit(solution)/shard_map/ppermute | solution.py:234
  49.1 0.4 collective-permute-start.3
  49.8 0.3 collective-permute-start.19
  50.3 0.9 %copy-done.2 = bf16[512,256]{1,0:T(8,128)(2,1)S(1)} copy-done((bf16[512,256]{1,0:T(8,128)(2,1)S(1)}, bf16[512,256]{1,0:T(8,128)(2,1)}, u32[]{:S(2)}) %copy-start.2) | copy-done | bytes 262168
  51.2 0.9 %copy-done.4 = bf16[512,256]{1,0:T(8,128)(2,1)S(1)} copy-done((bf16[512,256]{1,0:T(8,128)(2,1)S(1)}, bf16[512,256]{1,0:T(8,128)(2,1)}, u32[]{:S(2)}) %copy-start.4) | copy-done | bytes 262168
  52.2 0.9 %copy-done.6 = bf16[512,256]{1,0:T(8,128)(2,1)S(1)} copy-done((bf16[512,256]{1,0:T(8,128)(2,1)S(1)}, bf16[512,256]{1,0:T(8,128)(2,1)}, u32[]{:S(2)}) %copy-start.6) | copy-done | bytes 262168
  53.1 7.0 %shard_map.28 = (bf16[4096,256]{1,0:T(8,128)(2,1)}, f32[256,256]{1,0:T(8,128)S(1)}, f32[256,256]{1,0:T(8,128)S(1)}) custom-call(f32[32,9]{1,0:T(8,128)S(1)} %copy.10.refs_0_, bf16[512,256]{1,0:T(8,128)(2,1)S(1)} %copy-done.2, bf16[512,256]{1,0:T(8,128)(2,1)} %collective-permute-done.12.refs_2_, bf16[512,256]{1,0:T(8,128)(2,1)S(1)} %copy-done.6, ...), custom_call_target="tpu_custom_call" | custom-call | flops 3623878656 | bytes 5767168 | tf_op jit(solution)/shard_map/pallas_call | solution.py:167
  60.1 0.3 collective-permute-start.2
  60.7 5.7 %shard_map.29 = (bf16[4096,256]{1,0:T(8,128)(2,1)}, f32[256,256]{1,0:T(8,128)S(1)}, f32[256,256]{1,0:T(8,128)S(1)}) custom-call(f32[32,9]{1,0:T(8,128)S(1)} %copy.10.refs_0_, bf16[4096,256]{1,0:T(8,128)(2,1)S(1)} %copy-done, bf16[1024,256]{1,0:T(8,128)(2,1)} %collective-permute-done.9.refs_9_.refs_2_, ...), custom_call_target="tpu_custom_call", output_to_operand_aliasing={{0}: (9, {})} | custom-call | flops 2415919104 | bytes 4718592 | tf_op jit(solution)/shard_map/pallas_call | solution.py:167
  66.5 3.2 %shard_map.31 = (f32[256,256]{1,0:T(8,128)S(1)}, f32[256,256]{1,0:T(8,128)S(1)}) custom-call(f32[32,9]{1,0:T(8,128)S(1)} %copy.10.refs_0_, bf16[4096,256]{1,0:T(8,128)(2,1)S(1)} %copy-done, bf16[512,256]{1,0:T(8,128)(2,1)S(1)} %collective-permute-done.5.refs_2_.refs_7_, bf16[4096,256]{1,0:T(8,128)(2,1)} %collective-permute-done.1.refs_7_.refs_3_, ...), custom_call_target="tpu_custom_call" | custom-call | flops 1207959552 | bytes 2097152 | tf_op jit(solution)/shard_map/pallas_call | solution.py:167
  69.7 4.4 %shard_map.30 = (bf16[4096,256]{1,0:T(8,128)(2,1)}, f32[256,256]{1,0:T(8,128)S(1)}, f32[256,256]{1,0:T(8,128)S(1)}) custom-call(f32[32,9]{1,0:T(8,128)S(1)} %copy.10.refs_0_, bf16[4096,256]{1,0:T(8,128)(2,1)S(1)} %copy-done, bf16[1024,256]{1,0:T(8,128)(2,1)S(1)} %collective-permute-done.7.refs_5_.refs_2_, ...), custom_call_target="tpu_custom_call", output_to_operand_aliasing={{0}: (9, {})} | custom-call | flops 1207959552 | bytes 2883584 | tf_op jit(solution)/shard_map/pallas_call | solution.py:167
  74.1 5.2 %shard_map.32 = bf16[4096,256]{1,0:T(8,128)(2,1)} custom-call(f32[32,9]{1,0:T(8,128)S(1)} %copy.10.refs_0_, bf16[4096,256]{1,0:T(8,128)(2,1)S(1)} %copy-done, bf16[512,256]{1,0:T(8,128)(2,1)S(1)} %collective-permute-done.refs_5_.refs_2_, bf16[4096,256]{1,0:T(8,128)(2,1)} %collective-permute-done.1.refs_7_.refs_3_, ...), custom_call_target="tpu_custom_call", output_to_operand_aliasing={{}: (13, {})} | custom-call | flops 1811939328 | bytes 5505024 | tf_op jit(solution)/shard_map/pallas_call | solution.py:167
  (34 shorter events, 1.1 us)
Async XLA Ops:
  0.0 9.2 %copy-start = (bf16[4096,256]{1,0:T(8,128)(2,1)S(1)}, bf16[4096,256]{1,0:T(8,128)(2,1)}, u32[]{:S(2)}) copy-start(bf16[4096,256]{1,0:T(8,128)(2,1)} %refs_1_.7) | copy-start | bytes 6291460
  0.0 48.0 %copy-start.7 = (f32[32,9]{0,1:T(8,128)S(1)}, f32[32,9]{0,1:T(8,128)}, u32[]{:S(2)}) copy-start(f32[32,9]{0,1:T(8,128)} %param.3) | copy-start | bytes 3460
  0.0 50.0 %collective-permute-start.1 = (bf16[4096,256]{1,0:T(8,128)(2,1)}, bf16[4096,256]{1,0:T(8,128)(2,1)}, u32[]{:S(2)}, u32[]{:S(2)}) collective-permute-start(bf16[4096,256]{1,0:T(8,128)(2,1)} %refs_1_.7), channel_id=1, source_target_pairs={{0,1},{1,0},{2,3},{3,2},{4,5},{5,4},{6,7},{7,6},{8,9},{9,8},{10,11... | collective-permute-start | bytes 6291464 | tf_op jit(solution)/shard_map/ppermute | solution.py:24
  2.6 9.6 %collective-permute-start.5 = (bf16[512,256]{1,0:T(8,128)(2,1)S(1)}, bf16[512,256]{1,0:T(8,128)(2,1)S(1)}, u32[]{:S(2)}, u32[]{:S(2)}) collective-permute-start(bf16[512,256]{1,0:T(8,128)(2,1)S(1)} %get-tuple-element.28), channel_id=1, source_target_pairs={{0,2},{2,0},{1,3},{3,1},{4,6},{6,4},{5,7},{7,5},{8,10},{10,8},{9,1... | collective-permute-start | bytes 786440 | tf_op jit(solution)/shard_map/ppermute | solution.py:24
  5.1 14.2 %collective-permute-start.11 = (bf16[512,256]{1,0:T(8,128)(2,1)S(1)}, bf16[512,256]{1,0:T(8,128)(2,1)S(1)}, u32[]{:S(2)}, u32[]{:S(2)}) collective-permute-start(bf16[512,256]{1,0:T(8,128)(2,1)S(1)} %get-tuple-element.28), channel_id=1, source_target_pairs={{0,4},{4,8},{8,12},{1,5},{5,9},{9,13},{2,6},{6,10},{10,14},{3,7},{... | collective-permute-start | bytes 786440 | tf_op jit(solution)/shard_map/ppermute | solution.py:233
  8.6 9.4 %collective-permute-start.15 = (bf16[512,256]{1,0:T(8,128)(2,1)S(1)}, bf16[512,256]{1,0:T(8,128)(2,1)}, u32[]{:S(2)}, u32[]{:S(2)}) collective-permute-start(bf16[512,256]{1,0:T(8,128)(2,1)S(1)} %get-tuple-element.27), channel_id=1, source_target_pairs={{0,2},{2,0},{1,3},{3,1},{4,6},{6,4},{5,7},{7,5},{8,10},{10,8},{9,1... | collective-permute-start | bytes 786440 | tf_op jit(solution)/shard_map/ppermute | solution.py:24
  9.2 28.1 %collective-permute-start.9 = (bf16[1024,256]{1,0:T(8,128)(2,1)S(1)}, bf16[1024,256]{1,0:T(8,128)(2,1)}, u32[]{:S(2)}, u32[]{:S(2)}) collective-permute-start(bf16[1024,256]{1,0:T(8,128)(2,1)S(1)} %get-tuple-element.31), channel_id=1, source_target_pairs={{0,2},{2,0},{1,3},{3,1},{4,6},{6,4},{5,7},{7,5},{8,10},{10,8},{9,1... | collective-permute-start | bytes 1572872 | tf_op jit(solution)/shard_map/ppermute | solution.py:24
  12.2 22.1 %collective-permute-start = (bf16[512,256]{1,0:T(8,128)(2,1)S(1)}, bf16[512,256]{1,0:T(8,128)(2,1)S(1)}, u32[]{:S(2)}, u32[]{:S(2)}) collective-permute-start(bf16[512,256]{1,0:T(8,128)(2,1)S(1)} %get-tuple-element.30), channel_id=1, source_target_pairs={{0,2},{2,0},{1,3},{3,1},{4,6},{6,4},{5,7},{7,5},{8,10},{10,8},{9,1... | collective-permute-start | bytes 786440 | tf_op jit(solution)/shard_map/ppermute | solution.py:24
  18.0 18.2 %collective-permute-start.17 = (bf16[512,256]{1,0:T(8,128)(2,1)S(1)}, bf16[512,256]{1,0:T(8,128)(2,1)S(1)}, u32[]{:S(2)}, u32[]{:S(2)}) collective-permute-start(bf16[512,256]{1,0:T(8,128)(2,1)S(1)} %get-tuple-element.27), channel_id=1, source_target_pairs={{4,0},{8,4},{12,8},{5,1},{9,5},{13,9},{6,2},{10,6},{14,10},{7,3},{... | collective-permute-start | bytes 786440 | tf_op jit(solution)/shard_map/ppermute | solution.py:234
  19.3 16.9 %collective-permute-start.12 = (bf16[512,256]{1,0:T(8,128)(2,1)S(1)}, bf16[512,256]{1,0:T(8,128)(2,1)}, u32[]{:S(2)}, u32[]{:S(2)}) collective-permute-start(bf16[512,256]{1,0:T(8,128)(2,1)S(1)} %collective-permute-done.5.refs_2_.refs_7_), channel_id=1, source_target_pairs={{0,4},{4,8},{8,12},{1,5},{5,9},{9,13},{2,6},{6,10},{10,14},{3,7},{... | collective-permute-start | bytes 786440 | tf_op jit(solution)/shard_map/ppermute | solution.py:233
  34.4 13.6 %collective-permute-start.7 = (bf16[1024,256]{1,0:T(8,128)(2,1)S(1)}, bf16[1024,256]{1,0:T(8,128)(2,1)S(1)}, u32[]{:S(2)}, u32[]{:S(2)}) collective-permute-start(bf16[1024,256]{1,0:T(8,128)(2,1)S(1)} %get-tuple-element.32), channel_id=1, source_target_pairs={{0,2},{2,0},{1,3},{3,1},{4,6},{6,4},{5,7},{7,5},{8,10},{10,8},{9,1... | collective-permute-start | bytes 1572872 | tf_op jit(solution)/shard_map/ppermute | solution.py:24
  36.1 1.7 %collective-permute-start.16 = (bf16[512,256]{1,0:T(8,128)(2,1)}, bf16[512,256]{1,0:T(8,128)(2,1)S(1)}, u32[]{:S(2)}, u32[]{:S(2)}) collective-permute-start(bf16[512,256]{1,0:T(8,128)(2,1)} %collective-permute-done.15.refs_6_), channel_id=1, source_target_pairs={{0,1},{1,0},{2,3},{3,2},{4,5},{5,4},{6,7},{7,6},{8,9},{9,8},{10,11... | collective-permute-start | bytes 786440 | tf_op jit(solution)/shard_map/ppermute | solution.py:24
  36.1 3.8 %collective-permute-start.13 = (bf16[512,256]{1,0:T(8,128)(2,1)S(1)}, bf16[512,256]{1,0:T(8,128)(2,1)S(1)}, u32[]{:S(2)}, u32[]{:S(2)}) collective-permute-start(bf16[512,256]{1,0:T(8,128)(2,1)S(1)} %collective-permute-done.11.refs_1_), channel_id=1, source_target_pairs={{0,1},{1,0},{2,3},{3,2},{4,5},{5,4},{6,7},{7,6},{8,9},{9,8},{10,11... | collective-permute-start | bytes 786440 | tf_op jit(solution)/shard_map/ppermute | solution.py:24
  36.6 0.7 copy-start.1
  37.3 12.4 %collective-permute-start.10 = (bf16[1024,256]{1,0:T(8,128)(2,1)}, bf16[1024,256]{1,0:T(8,128)(2,1)}, u32[]{:S(2)}, u32[]{:S(2)}) collective-permute-start(bf16[1024,256]{1,0:T(8,128)(2,1)} %collective-permute-done.9.refs_9_.refs_2_), channel_id=1, source_target_pairs={{0,1},{1,0},{2,3},{3,2},{4,5},{5,4},{6,7},{7,6},{8,9},{9,8},{10,11... | collective-permute-start | bytes 1572872 | tf_op jit(solution)/shard_map/ppermute | solution.py:24
  37.9 0.7 copy-start.3
  38.6 10.5 %collective-permute-start.18 = (bf16[512,256]{1,0:T(8,128)(2,1)}, bf16[512,256]{1,0:T(8,128)(2,1)}, u32[]{:S(2)}, u32[]{:S(2)}) collective-permute-start(bf16[512,256]{1,0:T(8,128)(2,1)} %collective-permute-done.15.refs_6_), channel_id=1, source_target_pairs={{4,0},{8,4},{12,8},{5,1},{9,5},{13,9},{6,2},{10,6},{14,10},{7,3},{... | collective-permute-start | bytes 786440 | tf_op jit(solution)/shard_map/ppermute | solution.py:234
  39.9 0.7 copy-start.5
  40.6 8.9 %collective-permute-start.14 = (bf16[512,256]{1,0:T(8,128)(2,1)}, bf16[512,256]{1,0:T(8,128)(2,1)}, u32[]{:S(2)}, u32[]{:S(2)}) collective-permute-start(bf16[512,256]{1,0:T(8,128)(2,1)} %collective-permute-done.12.refs_2_), channel_id=1, source_target_pairs={{0,1},{1,0},{2,3},{3,2},{4,5},{5,4},{6,7},{7,6},{8,9},{9,8},{10,11... | collective-permute-start | bytes 786440 | tf_op jit(solution)/shard_map/ppermute | solution.py:24
  48.0 12.5 %collective-permute-start.8 = (bf16[1024,256]{1,0:T(8,128)(2,1)S(1)}, bf16[1024,256]{1,0:T(8,128)(2,1)}, u32[]{:S(2)}, u32[]{:S(2)}) collective-permute-start(bf16[1024,256]{1,0:T(8,128)(2,1)S(1)} %collective-permute-done.7.refs_5_.refs_2_), channel_id=1, source_target_pairs={{0,1},{1,0},{2,3},{3,2},{4,5},{5,4},{6,7},{7,6},{8,9},{9,8},{10,11... | collective-permute-start | bytes 1572872 | tf_op jit(solution)/shard_map/ppermute | solution.py:24
  49.1 11.0 %collective-permute-start.3 = (bf16[512,256]{1,0:T(8,128)(2,1)}, bf16[512,256]{1,0:T(8,128)(2,1)S(1)}, u32[]{:S(2)}, u32[]{:S(2)}) collective-permute-start(bf16[512,256]{1,0:T(8,128)(2,1)} %get-tuple-element.29), channel_id=1, source_target_pairs={{0,2},{2,0},{1,3},{3,1},{4,6},{6,4},{5,7},{7,5},{8,10},{10,8},{9,1... | collective-permute-start | bytes 786440 | tf_op jit(solution)/shard_map/ppermute | solution.py:24
  49.5 16.9 %collective-permute-start.6 = (bf16[512,256]{1,0:T(8,128)(2,1)S(1)}, bf16[512,256]{1,0:T(8,128)(2,1)S(1)}, u32[]{:S(2)}, u32[]{:S(2)}) collective-permute-start(bf16[512,256]{1,0:T(8,128)(2,1)S(1)} %collective-permute-done.5.refs_2_.refs_7_), channel_id=1, source_target_pairs={{0,1},{1,0},{2,3},{3,2},{4,5},{5,4},{6,7},{7,6},{8,9},{9,8},{10,11... | collective-permute-start | bytes 786440 | tf_op jit(solution)/shard_map/ppermute | solution.py:24
  49.8 16.7 %collective-permute-start.19 = (bf16[512,256]{1,0:T(8,128)(2,1)S(1)}, bf16[512,256]{1,0:T(8,128)(2,1)S(1)}, u32[]{:S(2)}, u32[]{:S(2)}) collective-permute-start(bf16[512,256]{1,0:T(8,128)(2,1)S(1)} %collective-permute-done.17.refs_5_), channel_id=1, source_target_pairs={{0,1},{1,0},{2,3},{3,2},{4,5},{5,4},{6,7},{7,6},{8,9},{9,8},{10,11... | collective-permute-start | bytes 786440 | tf_op jit(solution)/shard_map/ppermute | solution.py:24
  50.1 16.4 %collective-permute-start.20 = (bf16[512,256]{1,0:T(8,128)(2,1)}, bf16[512,256]{1,0:T(8,128)(2,1)S(1)}, u32[]{:S(2)}, u32[]{:S(2)}) collective-permute-start(bf16[512,256]{1,0:T(8,128)(2,1)} %collective-permute-done.18.refs_6_), channel_id=1, source_target_pairs={{0,1},{1,0},{2,3},{3,2},{4,5},{5,4},{6,7},{7,6},{8,9},{9,8},{10,11... | collective-permute-start | bytes 786440 | tf_op jit(solution)/shard_map/ppermute | solution.py:24
  50.3 0.9 %copy-start.2 = (bf16[512,256]{1,0:T(8,128)(2,1)S(1)}, bf16[512,256]{1,0:T(8,128)(2,1)}, u32[]{:S(2)}) copy-start(bf16[512,256]{1,0:T(8,128)(2,1)} %copy-done.1) | copy-start | bytes 786436
  51.2 0.9 %copy-start.4 = (bf16[512,256]{1,0:T(8,128)(2,1)S(1)}, bf16[512,256]{1,0:T(8,128)(2,1)}, u32[]{:S(2)}) copy-start(bf16[512,256]{1,0:T(8,128)(2,1)} %copy-done.3) | copy-start | bytes 786436
  52.2 0.9 %copy-start.6 = (bf16[512,256]{1,0:T(8,128)(2,1)S(1)}, bf16[512,256]{1,0:T(8,128)(2,1)}, u32[]{:S(2)}) copy-start(bf16[512,256]{1,0:T(8,128)(2,1)} %copy-done.5) | copy-start | bytes 786436
  60.1 9.5 %collective-permute-start.2 = (bf16[512,256]{1,0:T(8,128)(2,1)S(1)}, bf16[512,256]{1,0:T(8,128)(2,1)S(1)}, u32[]{:S(2)}, u32[]{:S(2)}) collective-permute-start(bf16[512,256]{1,0:T(8,128)(2,1)S(1)} %collective-permute-done.refs_5_.refs_2_), channel_id=1, source_target_pairs={{0,1},{1,0},{2,3},{3,2},{4,5},{5,4},{6,7},{7,6},{8,9},{9,8},{10,11... | collective-permute-start | bytes 786440 | tf_op jit(solution)/shard_map/ppermute | solution.py:24
  60.5 13.6 %collective-permute-start.4 = (bf16[512,256]{1,0:T(8,128)(2,1)S(1)}, bf16[512,256]{1,0:T(8,128)(2,1)S(1)}, u32[]{:S(2)}, u32[]{:S(2)}) collective-permute-start(bf16[512,256]{1,0:T(8,128)(2,1)S(1)} %collective-permute-done.3.refs_5_), channel_id=1, source_target_pairs={{0,1},{1,0},{2,3},{3,2},{4,5},{5,4},{6,7},{7,6},{8,9},{9,8},{10,11... | collective-permute-start | bytes 786440 | tf_op jit(solution)/shard_map/ppermute | solution.py:24

commit v4 on v3

--- a/solution.py
+++ b/solution.py
@@ -16,6 +16,7 @@
 PAIR = 2
 ROWS = PAIR * BLOCK
 NEAR = REACH // PAIR
+VMEM_LIMIT = 24 * 2**20
 
 
 def shifted(value, axis):
@@ -34,15 +35,28 @@
     parts = job["parts"]
     plan, steps, owned = job["plan"], job["steps"], job["owned"]
     acc_in, acc_out, finished = job["acc_in"], job["acc_out"], job["finished"]
+    writes = job["writes"]
     arrays = job["arrays"]
     taper = refs[0]
     sources = refs[1 : 1 + arrays]
     inputs = dict(zip(acc_in, refs[1 + arrays : 1 + arrays + len(acc_in)]))
-    outs = refs[1 + arrays + len(acc_in) + job["aliased"] :]
-    if finished:
-        out, outs = outs[0], outs[1:]
-    carried, outs = outs[: len(acc_out)], outs[len(acc_out) :]
-    acc, obuf, out_sem = outs
+    earlier = refs[1 + arrays + len(acc_in) : job["operands"]]
+    outs = refs[job["operands"] :]
+    if writes:
+        out, acc, obuf, out_sem = outs[0], *outs[-3:]
+        sent = [
+            pltpu.make_async_copy(
+                earlier[array].at[n], out.at[tile_rows(pair)], out_sem.at[len(finished) + k]
+            )
+            for k, (array, n, pair) in enumerate(writes)
+        ]
+        for copy in sent:
+            copy.start()
+    else:
+        outs, acc = outs[:-1], outs[-1]
+        if finished:
+            obuf, outs = outs[0], outs[1:]
+    carried = outs
     sums = {pair: carried[n] for n, pair in enumerate(acc_out)}
     sums |= {pair: acc.at[n] for n, pair in enumerate(finished)}
     begun = set()
@@ -109,20 +123,40 @@
                 value = term if value is None else value + term
             add(j, value)
 
-    def store(n):
-        return pltpu.make_async_copy(
-            obuf.at[n], out.at[tile_rows(finished[n])], out_sem.at[n]
-        )
-
     for n, pair in enumerate(finished):
         update = (sums if pair in begun else inputs)[pair][...]
         obuf[n] = (own(pair).astype(jnp.float32) - 0.5 * update).astype(jnp.bfloat16)
-        store(n).start()
-    for n in range(len(finished)):
-        store(n).wait()
-
-
-def run_steps(taper, pieces, steps, owned, state, finished, result, rows, members):
+        if writes:
+            sent.append(
+                pltpu.make_async_copy(obuf.at[n], out.at[tile_rows(pair)], out_sem.at[n])
+            )
+            sent[-1].start()
+    if writes:
+        for copy in sent:
+            copy.wait()
+
+
+def stage_kernel(source, target, sem):
+    copy = pltpu.make_async_copy(source, target, sem)
+    copy.start()
+    copy.wait()
+
+
+def staged(array):
+    return pl.pallas_call(
+        stage_kernel,
+        out_shape=jax.ShapeDtypeStruct(array.shape, array.dtype),
+        in_specs=[pl.BlockSpec(memory_space=pl.ANY)],
+        out_specs=pl.BlockSpec(memory_space=pltpu.VMEM),
+        scratch_shapes=[pltpu.SemaphoreType.DMA],
+        compiler_params=pltpu.CompilerParams(vmem_limit_bytes=VMEM_LIMIT),
+        cost_estimate=pl.CostEstimate(
+            flops=0, bytes_accessed=2 * array.size, transcendentals=0
+        ),
+    )(array)
+
+
+def run_steps(taper, pieces, steps, owned, state, finished, stored, rows, members, last):
     parts = len(pieces)
     needed = set()
     for j, first, count in steps:
@@ -145,61 +179,66 @@
                 arrays.append(array)
                 known = [len(arrays) - 1]
             plan[pair, part] = (known[0], start)
-    aliased = int(bool(finished) and result is not None)
+    writes = []
+    if last:
+        for array, (pairs, _) in enumerate(stored):
+            writes += [(array, n, pair) for n, pair in enumerate(pairs)]
+    operands = [taper] + arrays + [state[pair] for pair in acc_in]
+    if last:
+        operands += [block for _, block in stored]
     job = dict(
-        parts=parts, plan=plan, steps=steps, owned=owned, acc_in=acc_in,
-        acc_out=acc_out, finished=finished, arrays=len(arrays), aliased=aliased,
+        parts=parts, plan=plan, steps=steps, owned=owned, acc_in=acc_in, acc_out=acc_out,
+        finished=finished, arrays=len(arrays), writes=writes, operands=len(operands),
     )
-    operands = [taper] + arrays + [state[pair] for pair in acc_in]
-    anywhere = pl.BlockSpec(memory_space=pl.ANY)
     inside = pl.BlockSpec(memory_space=pltpu.VMEM)
     specs = [pl.BlockSpec(memory_space=pltpu.SMEM)] + [inside] * (len(operands) - 1)
-    aliases = {}
-    shapes = []
-    if finished:
-        shapes.append(jax.ShapeDtypeStruct((rows, members), jnp.bfloat16))
-        if aliased:
-            aliases = {len(operands): 0}
-            operands.append(result)
-            specs.append(anywhere)
-    shapes += [jax.ShapeDtypeStruct((ROWS, members), jnp.float32)] * len(acc_out)
     products = sum(n for _, _, n in steps)
+    count = max(len(finished), 1)
+    carries = [jax.ShapeDtypeStruct((ROWS, members), jnp.float32)] * len(acc_out)
+    block = (len(finished), ROWS, members)
+    scratch = [pltpu.VMEM((count, ROWS, members), jnp.float32)]
+    if last:
+        shapes = [jax.ShapeDtypeStruct((rows, members), jnp.bfloat16)]
+        out_specs = [pl.BlockSpec(memory_space=pl.ANY)]
+        scratch += [
+            pltpu.VMEM(block, jnp.bfloat16),
+            pltpu.SemaphoreType.DMA((len(finished) + len(writes),)),
+        ]
+    else:
+        shapes = [jax.ShapeDtypeStruct(block, jnp.bfloat16)] * int(bool(finished)) + carries
+        out_specs = [inside] * len(shapes)
     outputs = pl.pallas_call(
         functools.partial(update_kernel, job),
         out_shape=shapes,
         in_specs=specs,
-        out_specs=[anywhere] * int(bool(finished)) + [inside] * len(acc_out),
-        input_output_aliases=aliases,
-        scratch_shapes=[
-            pltpu.VMEM((max(len(finished), 1), ROWS, members), jnp.float32),
-            pltpu.VMEM((max(len(finished), 1), ROWS, members), jnp.bfloat16),
-            pltpu.SemaphoreType.DMA((max(len(finished), 1),)),
-        ],
-        compiler_params=pltpu.CompilerParams(vmem_limit_bytes=32 * 2**20),
+        out_specs=out_specs,
+        scratch_shapes=scratch,
+        compiler_params=pltpu.CompilerParams(vmem_limit_bytes=VMEM_LIMIT),
         cost_estimate=pl.CostEstimate(
             flops=2 * products * ROWS * ROWS * members * (parts + 2),
             bytes_accessed=2 * ROWS * members * (len(plan) + 3 * len(finished)),
             transcendentals=0,
         ),
     )(*operands)
+    if last:
+        return outputs[0], state
     if finished:
-        result, outputs = outputs[0], outputs[1:]
+        stored.append((finished, outputs[0]))
+        outputs = outputs[1:]
     state = {pair: value for pair, value in state.items() if pair not in touched}
     state.update(zip(acc_out, outputs))
     for pair in finished:
         state.pop(pair, None)
-    return result, state
+    return None, state
 
 
 def chunk_bounds(pairs):
     first, last = NEAR, pairs - NEAR
-    tail = [2, 2]
-    bulk = last - first - sum(tail)
-    sizes = [(bulk + 1) // 2, bulk // 2] + tail
+    bulk = last - first - 6
+    sizes = [2, bulk // 2, bulk - bulk // 2, 2, 2]
     bounds = [first]
     for size in sizes:
-        if size:
-            bounds.append(bounds[-1] + size)
+        bounds.append(bounds[-1] + size)
     return list(zip(bounds, bounds[1:]))
 
 
@@ -214,7 +253,9 @@
     def cut(first, last):
         return lax.slice_in_dim(anomalies, first * ROWS, last * ROWS, axis=0)
 
-    top, bottom = cut(0, NEAR), cut(pairs - NEAR, pairs)
+    top = cut(0, NEAR)
+    anomalies, top = lax.optimization_barrier((anomalies, top))
+    bottom = cut(pairs - NEAR, pairs)
     tops = shifted(top, "member")
     bottoms = shifted(bottom, "member")
     middles = []
@@ -234,17 +275,21 @@
         after = (lax.ppermute(head, "region", up), pairs, NEAR)
         held.append([before, after] + listed)
     for turn in range(lax.axis_size("tile") - 1):
-        held += [
-            [(shifted(array, "tile")[turn], first, count) for array, first, count in listed]
-            for listed in list(held)
-        ]
+        for listed in list(held):
+            there = [(shifted(array, "tile")[turn], first, count) for array, first, count in listed]
+            held.append(
+                [
+                    (staged(array) if count == pairs else array, first, count)
+                    for array, first, count in there
+                ]
+            )
     pieces = [
         {first + n: (array, n) for array, first, count in listed for n in range(count)}
         for listed in held
     ]
 
     owned = set(range(pairs))
-    state, result = {}, None
+    state, stored = {}, []
 
     def steps_for(fresh, before):
         there, steps = set(before), []
@@ -259,18 +304,21 @@
                 near = near[len(run) :]
         return steps, there
 
-    low = list(range(-NEAR, NEAR))
-    high = list(range(pairs - NEAR, pairs + NEAR))
     there, done = set(), set()
-    batches = [high, low + list(range(*chunks[0]))] + [list(range(*c)) for c in chunks[1:]]
-    for fresh in batches:
+    low, high = list(range(NEAR)), list(range(pairs - NEAR, pairs))
+    around = list(range(-NEAR, 0)) + list(range(pairs, pairs + NEAR))
+    batches = [low + list(range(*chunks[0])), high + around] + [list(range(*c)) for c in chunks[1:]]
+    for n, fresh in enumerate(batches):
         steps, there = steps_for(fresh, there)
         ready = [
             i for i in range(pairs)
             if i not in done and all(k in there for k in range(i - NEAR, i + NEAR + 1))
         ]
         done |= set(ready)
-        result, state = run_steps(taper, pieces, steps, owned, state, ready, result, rows, members)
+        result, state = run_steps(
+            taper, pieces, steps, owned, state, ready, stored, rows, members,
+            n == len(batches) - 1,
+        )
     return result
 
 

time: 79.7 us -> 82.8 us (1.039)
  the two profiles are of different devices: /device:TPU:0 before, /device:TPU:12 now
where the time goes in v4:
time: 82.8 us; the launch traced here: 81.2 us
  waiting for transfers between devices  29.8 us (36%)
  Pallas kernels  22.2 us (27%)
  starting transfers between devices  22.1 us (27%)
  local copies, waits for them, and re-layouts  6.83 us (8%)
    ppermute x19, waiting for transfers between devices, shifted(): lax.ppermute(value, axis, [(i, (i + s) % count) for i in range(count)])  24.4 us
    pallas_call x6, Pallas kernels, run_steps(): pl.pallas_call(functools.partial(update_kernel, job), out_shape=shapes, i...  22.1 us
    ppermute x19, starting transfers between devices, shifted(): lax.ppermute(value, axis, [(i, (i + s) % count) for i in range(count)])  10.5 us
    ppermute x2, starting transfers between devices, per_device(): before = (lax.ppermute(tail, 'region', down), -NEAR, NEAR)  6.95 us
    ppermute x2, waiting for transfers between devices, per_device(): after = (lax.ppermute(head, 'region', up), pairs, NEAR)  5.42 us
    ppermute x2, starting transfers between devices, per_device(): after = (lax.ppermute(head, 'region', up), pairs, NEAR)  4.72 us
    unnamed x17, local copies, waits for them, and re-layouts  3.71 us
    slice x3, local copies, waits for them, and re-layouts, cut(): return lax.slice_in_dim(anomalies, first * ROWS, last * ROWS, axis=0)  3.12 us
  transfers between devices with their start and end apart: 23, of which 6 were waited for; matrix products, arithmetic and copies ran while one was open for 3% of the time, Pallas kernels for 22%

profile of v4, /device:TPU:12, one launch (start us, length us, event | category | flops | bytes accessed | tf_op | source)
XLA Modules:
  0.0 81.2 jit_solution(15854659675767391959)
XLA Ops:
  0.0 1.1 %slice.21 = bf16[512,256]{1,0:T(8,128)(2,1)S(1)} slice(bf16[4096,256]{1,0:T(8,128)(2,1)} %refs_1_.4), slice={[0:512], [0:256]} | slice | bytes 524288 | tf_op jit(solution)/shard_map/slice | solution.py:254
  1.2 1.9 %fusion = (bf16[512,256]{1,0:T(8,128)(2,1)S(1)}, bf16[512,256]{1,0:T(8,128)(2,1)S(1)}, bf16[512,256]{1,0:T(8,128)(2,1)}, bf16[512,256]{1,0:T(8,128)(2,1)S(1)}) fusion(bf16[4096,256]{1,0:T(8,128)(2,1)} %refs_1_.4), kind=kLoop, calls=%fused_computation | loop fusion | bytes 2097152 | tf_op jit(solution)/shard_map/slice | solution.py:254
  3.2 1.5 %collective-permute-start.11 = (bf16[512,256]{1,0:T(8,128)(2,1)S(1)}, bf16[512,256]{1,0:T(8,128)(2,1)}, u32[]{:S(2)}, u32[]{:S(2)}) collective-permute-start(bf16[512,256]{1,0:T(8,128)(2,1)S(1)} %get-tuple-element.41), channel_id=1, source_target_pairs={{0,2},{2,0},{1,3},{3,1},{4,6},{6,4},{5,7},{7,5},{8,10},{10,8},{9,1... | collective-permute-start | bytes 786440 | tf_op jit(solution)/shard_map/ppermute | solution.py:25
  4.6 0.5 collective-permute-start.5
  5.2 3.5 %collective-permute-start.15 = (bf16[512,256]{1,0:T(8,128)(2,1)S(1)}, bf16[512,256]{1,0:T(8,128)(2,1)S(1)}, u32[]{:S(2)}, u32[]{:S(2)}) collective-permute-start(bf16[512,256]{1,0:T(8,128)(2,1)S(1)} %get-tuple-element.42), channel_id=1, source_target_pairs={{0,4},{4,8},{8,12},{1,5},{5,9},{9,13},{2,6},{6,10},{10,14},{3,7},{... | collective-permute-start | bytes 786440 | tf_op jit(solution)/shard_map/ppermute | solution.py:274
  8.7 1.6 %collective-permute-start.13 = (bf16[512,256]{1,0:T(8,128)(2,1)S(1)}, bf16[512,256]{1,0:T(8,128)(2,1)}, u32[]{:S(2)}, u32[]{:S(2)}) collective-permute-start(bf16[512,256]{1,0:T(8,128)(2,1)S(1)} %slice.21), channel_id=1, source_target_pairs={{0,2},{2,0},{1,3},{3,1},{4,6},{6,4},{5,7},{7,5},{8,10},{10,8},{9,1... | collective-permute-start | bytes 786440 | tf_op jit(solution)/shard_map/ppermute | solution.py:25
  10.3 2.2 %collective-permute-done.11.refs_5_.refs_2_ = bf16[512,256]{1,0:T(8,128)(2,1)} collective-permute-done((bf16[512,256]{1,0:T(8,128)(2,1)S(1)}, bf16[512,256]{1,0:T(8,128)(2,1)}, u32[]{:S(2)}, u32[]{:S(2)}) %collective-permute-start.11) | collective-permute-done | bytes 262176 | tf_op jit(solution)/shard_map/ppermute | solution.py:25
  12.4 1.5 %collective-permute-start.9 = (bf16[768,256]{1,0:T(8,128)(2,1)S(1)}, bf16[768,256]{1,0:T(8,128)(2,1)}, u32[]{:S(2)}, u32[]{:S(2)}) collective-permute-start(bf16[768,256]{1,0:T(8,128)(2,1)S(1)} %get-tuple-element.45), channel_id=1, source_target_pairs={{0,2},{2,0},{1,3},{3,1},{4,6},{6,4},{5,7},{7,5},{8,10},{10,8},{9,1... | collective-permute-start | bytes 1179656 | tf_op jit(solution)/shard_map/ppermute | solution.py:25
  13.9 9.7 %collective-permute-done.13.refs_2_.refs_6_ = bf16[512,256]{1,0:T(8,128)(2,1)} collective-permute-done((bf16[512,256]{1,0:T(8,128)(2,1)S(1)}, bf16[512,256]{1,0:T(8,128)(2,1)}, u32[]{:S(2)}, u32[]{:S(2)}) %collective-permute-start.13) | collective-permute-done | bytes 262176 | tf_op jit(solution)/shard_map/ppermute | solution.py:25
  23.7 1.5 %collective-permute-start.7 = (bf16[768,256]{1,0:T(8,128)(2,1)S(1)}, bf16[768,256]{1,0:T(8,128)(2,1)S(1)}, u32[]{:S(2)}, u32[]{:S(2)}) collective-permute-start(bf16[768,256]{1,0:T(8,128)(2,1)S(1)} %get-tuple-element.46), channel_id=1, source_target_pairs={{0,2},{2,0},{1,3},{3,1},{4,6},{6,4},{5,7},{7,5},{8,10},{10,8},{9,1... | collective-permute-start | bytes 1179656 | tf_op jit(solution)/shard_map/ppermute | solution.py:25
  25.2 2.3 %collective-permute-start.19 = (bf16[512,256]{1,0:T(8,128)(2,1)S(1)}, bf16[512,256]{1,0:T(8,128)(2,1)S(1)}, u32[]{:S(2)}, u32[]{:S(2)}) collective-permute-start(bf16[512,256]{1,0:T(8,128)(2,1)S(1)} %slice.21), channel_id=1, source_target_pairs={{4,0},{8,4},{12,8},{5,1},{9,5},{13,9},{6,2},{10,6},{14,10},{7,3},{... | collective-permute-start | bytes 786440 | tf_op jit(solution)/shard_map/ppermute | solution.py:275
  27.5 0.7 copy-done.3
  28.2 0.5 collective-permute-start
  28.8 5.4 %collective-permute-done.19.refs_11_ = bf16[512,256]{1,0:T(8,128)(2,1)S(1)} collective-permute-done((bf16[512,256]{1,0:T(8,128)(2,1)S(1)}, bf16[512,256]{1,0:T(8,128)(2,1)S(1)}, u32[]{:S(2)}, u32[]{:S(2)}) %collective-permute-start.19) | collective-permute-done | bytes 262176 | tf_op jit(solution)/shard_map/ppermute | solution.py:275
  34.1 0.5 collective-permute-start.3
  34.7 11.4 %collective-permute-done.refs_5_.refs_2_ = bf16[512,256]{1,0:T(8,128)(2,1)S(1)} collective-permute-done((bf16[512,256]{1,0:T(8,128)(2,1)S(1)}, bf16[512,256]{1,0:T(8,128)(2,1)S(1)}, u32[]{:S(2)}, u32[]{:S(2)}) %collective-permute-start) | collective-permute-done | bytes 262176 | tf_op jit(solution)/shard_map/ppermute | solution.py:25
  46.0 0.5 collective-permute-start.14
  46.6 1.3 %copy-done.1 = bf16[4096,256]{1,0:T(8,128)(2,1)} copy-done((bf16[4096,256]{1,0:T(8,128)(2,1)}, bf16[4096,256]{1,0:T(8,128)(2,1)S(1)}, u32[]{:S(2)}) %copy-start.1) | copy-done | bytes 2097176
  48.0 0.4 collective-permute-start.8
  48.5 1.6 %copy-done.2 = bf16[4096,256]{1,0:T(8,128)(2,1)S(1)} copy-done((bf16[4096,256]{1,0:T(8,128)(2,1)S(1)}, bf16[4096,256]{1,0:T(8,128)(2,1)}, u32[]{:S(2)}) %copy-start.2) | copy-done | bytes 2097176
  50.2 1.1 %collective-permute-done.3.refs_5_ = bf16[512,256]{1,0:T(8,128)(2,1)} collective-permute-done((bf16[512,256]{1,0:T(8,128)(2,1)}, bf16[512,256]{1,0:T(8,128)(2,1)}, u32[]{:S(2)}, u32[]{:S(2)}) %collective-permute-start.3) | collective-permute-done | bytes 262176 | tf_op jit(solution)/shard_map/ppermute | solution.py:25
  51.3 3.5 %collective-permute-start.16 = (bf16[512,256]{1,0:T(8,128)(2,1)S(1)}, bf16[512,256]{1,0:T(8,128)(2,1)S(1)}, u32[]{:S(2)}, u32[]{:S(2)}) collective-permute-start(bf16[512,256]{1,0:T(8,128)(2,1)S(1)} %collective-permute-done.5.refs_9_.refs_7_), channel_id=1, source_target_pairs={{0,4},{4,8},{8,12},{1,5},{5,9},{9,13},{2,6},{6,10},{10,14},{3,7},{... | collective-permute-start | bytes 786440 | tf_op jit(solution)/shard_map/ppermute | solution.py:274
  54.9 2.4 %collective-permute-start.20 = (bf16[512,256]{1,0:T(8,128)(2,1)}, bf16[512,256]{1,0:T(8,128)(2,1)S(1)}, u32[]{:S(2)}, u32[]{:S(2)}) collective-permute-start(bf16[512,256]{1,0:T(8,128)(2,1)} %collective-permute-done.13.refs_2_.refs_6_), channel_id=1, source_target_pairs={{4,0},{8,4},{12,8},{5,1},{9,5},{13,9},{6,2},{10,6},{14,10},{7,3},{... | collective-permute-start | bytes 786440 | tf_op jit(solution)/shard_map/ppermute | solution.py:275
  57.2 3.4 %shard_map.29 = (f32[256,256]{1,0:T(8,128)S(1)}, f32[256,256]{1,0:T(8,128)S(1)}, f32[256,256]{1,0:T(8,128)S(1)}, f32[256,256]{1,0:T(8,128)S(1)}) custom-call(f32[32,9]{1,0:T(8,128)S(1)} %copy.8.refs_0_, bf16[4096,256]{1,0:T(8,128)(2,1)S(1)} %copy-done, bf16[512,256]{1,0:T(8,128)(2,1)} %collective-permute-done.13.refs_2_.refs_6_, ...), custom_call_target="tpu_custom_call" | custom-call | flops 1811939328 | bytes 2097152 | tf_op jit(solution)/shard_map/pallas_call | solution.py:210
  60.7 0.3 collective-permute-start.2
  60.9 4.1 %shard_map.30 = (bf16[3,256,256]{2,1,0:T(8,128)(2,1)S(1)}, f32[256,256]{1,0:T(8,128)S(1)}, f32[256,256]{1,0:T(8,128)S(1)}) custom-call(f32[32,9]{1,0:T(8,128)S(1)} %copy.8.refs_0_, bf16[4096,256]{1,0:T(8,128)(2,1)S(1)} %copy-done, bf16[512,256]{1,0:T(8,128)(2,1)} %collective-permute-done.11.refs_5_.refs_2_, bf16[4096,256]{1,0:T(8,128)(2,1)S(1)} %shard_map.28.refs_3_.refs_7_, ...), custom_call_target="tpu_custom_call" | custom-call | flops 1811939328 | bytes 3801088 | tf_op jit(solution)/shard_map/pallas_call | solution.py:210
  65.0 0.4 collective-permute-start.17
  66.2 3.9 %shard_map.31 = (bf16[3,256,256]{2,1,0:T(8,128)(2,1)S(1)}, f32[256,256]{1,0:T(8,128)S(1)}, f32[256,256]{1,0:T(8,128)S(1)}) custom-call(f32[32,9]{1,0:T(8,128)S(1)} %copy.8.refs_0_, bf16[4096,256]{1,0:T(8,128)(2,1)S(1)} %copy-done, bf16[768,256]{1,0:T(8,128)(2,1)} %collective-permute-done.9.refs_5_.refs_2_, bf16[4096,256]{1,0:T(8,128)(2,1)S(1)} %shard_map.28.refs_3_.refs_7_, ...), custom_call_target="tpu_custom_call" | custom-call | flops 1811939328 | bytes 3801088 | tf_op jit(solution)/shard_map/pallas_call | solution.py:210
  70.0 0.3 collective-permute-start.4
  70.4 3.0 %shard_map.32 = (bf16[2,256,256]{2,1,0:T(8,128)(2,1)S(1)}, f32[256,256]{1,0:T(8,128)S(1)}, f32[256,256]{1,0:T(8,128)S(1)}) custom-call(f32[32,9]{1,0:T(8,128)S(1)} %copy.8.refs_0_, bf16[4096,256]{1,0:T(8,128)(2,1)S(1)} %copy-done, bf16[768,256]{1,0:T(8,128)(2,1)S(1)} %collective-permute-done.7.refs_5_.refs_2_, ...), custom_call_target="tpu_custom_call" | custom-call | flops 1207959552 | bytes 2883584 | tf_op jit(solution)/shard_map/pallas_call | solution.py:210
  73.5 3.1 %shard_map.33 = (bf16[2,256,256]{2,1,0:T(8,128)(2,1)S(1)}, f32[256,256]{1,0:T(8,128)S(1)}, f32[256,256]{1,0:T(8,128)S(1)}) custom-call(f32[32,9]{1,0:T(8,128)S(1)} %copy.8.refs_0_, bf16[512,256]{1,0:T(8,128)(2,1)S(1)} %copy-done.4, bf16[512,256]{1,0:T(8,128)(2,1)S(1)} %collective-permute-done.16.refs_2_, ...), custom_call_target="tpu_custom_call" | custom-call | flops 1811939328 | bytes 4980736 | tf_op jit(solution)/shard_map/pallas_call | solution.py:210
  76.6 4.6 %shard_map.34 = bf16[4096,256]{1,0:T(8,128)(2,1)} custom-call(f32[32,9]{1,0:T(8,128)S(1)} %copy.8.refs_0_, bf16[4096,256]{1,0:T(8,128)(2,1)S(1)} %copy-done, bf16[512,256]{1,0:T(8,128)(2,1)S(1)} %collective-permute-done.refs_5_.refs_2_, bf16[4096,256]{1,0:T(8,128)(2,1)S(1)} %shard_map.28.refs_3_.refs_7_, ...), custom_call_target="tpu_custom_call" | custom-call | flops 1811939328 | bytes 5505024 | tf_op jit(solution)/shard_map/pallas_call | solution.py:210
  (41 shorter events, 1.3 us)
Async XLA Ops:
  0.0 10.2 %copy-start = (bf16[4096,256]{1,0:T(8,128)(2,1)S(1)}, bf16[4096,256]{1,0:T(8,128)(2,1)}, u32[]{:S(2)}) copy-start(bf16[4096,256]{1,0:T(8,128)(2,1)} %refs_1_.4) | copy-start | bytes 6291460
  0.0 48.4 %copy-start.7 = (f32[32,9]{0,1:T(8,128)S(1)}, f32[32,9]{0,1:T(8,128)}, u32[]{:S(2)}) copy-start(f32[32,9]{0,1:T(8,128)} %param.3) | copy-start | bytes 3460
  1.1 45.5 %collective-permute-start.1 = (bf16[4096,256]{1,0:T(8,128)(2,1)}, bf16[4096,256]{1,0:T(8,128)(2,1)S(1)}, u32[]{:S(2)}, u32[]{:S(2)}) collective-permute-start(bf16[4096,256]{1,0:T(8,128)(2,1)} %refs_1_.4), channel_id=1, source_target_pairs={{0,1},{1,0},{2,3},{3,2},{4,5},{5,4},{6,7},{7,6},{8,9},{9,8},{10,11... | collective-permute-start | bytes 6291464 | tf_op jit(solution)/shard_map/ppermute | solution.py:25
  3.2 9.3 %collective-permute-start.11 = (bf16[512,256]{1,0:T(8,128)(2,1)S(1)}, bf16[512,256]{1,0:T(8,128)(2,1)}, u32[]{:S(2)}, u32[]{:S(2)}) collective-permute-start(bf16[512,256]{1,0:T(8,128)(2,1)S(1)} %get-tuple-element.41), channel_id=1, source_target_pairs={{0,2},{2,0},{1,3},{3,1},{4,6},{6,4},{5,7},{7,5},{8,10},{10,8},{9,1... | collective-permute-start | bytes 786440 | tf_op jit(solution)/shard_map/ppermute | solution.py:25
  4.6 20.5 %collective-permute-start.5 = (bf16[512,256]{1,0:T(8,128)(2,1)S(1)}, bf16[512,256]{1,0:T(8,128)(2,1)S(1)}, u32[]{:S(2)}, u32[]{:S(2)}) collective-permute-start(bf16[512,256]{1,0:T(8,128)(2,1)S(1)} %get-tuple-element.42), channel_id=1, source_target_pairs={{0,2},{2,0},{1,3},{3,1},{4,6},{6,4},{5,7},{7,5},{8,10},{10,8},{9,1... | collective-permute-start | bytes 786440 | tf_op jit(solution)/shard_map/ppermute | solution.py:25
  5.2 22.3 %collective-permute-start.15 = (bf16[512,256]{1,0:T(8,128)(2,1)S(1)}, bf16[512,256]{1,0:T(8,128)(2,1)S(1)}, u32[]{:S(2)}, u32[]{:S(2)}) collective-permute-start(bf16[512,256]{1,0:T(8,128)(2,1)S(1)} %get-tuple-element.42), channel_id=1, source_target_pairs={{0,4},{4,8},{8,12},{1,5},{5,9},{9,13},{2,6},{6,10},{10,14},{3,7},{... | collective-permute-start | bytes 786440 | tf_op jit(solution)/shard_map/ppermute | solution.py:274
  8.7 15.0 %collective-permute-start.13 = (bf16[512,256]{1,0:T(8,128)(2,1)S(1)}, bf16[512,256]{1,0:T(8,128)(2,1)}, u32[]{:S(2)}, u32[]{:S(2)}) collective-permute-start(bf16[512,256]{1,0:T(8,128)(2,1)S(1)} %slice.21), channel_id=1, source_target_pairs={{0,2},{2,0},{1,3},{3,1},{4,6},{6,4},{5,7},{7,5},{8,10},{10,8},{9,1... | collective-permute-start | bytes 786440 | tf_op jit(solution)/shard_map/ppermute | solution.py:25
  12.4 33.6 %collective-permute-start.9 = (bf16[768,256]{1,0:T(8,128)(2,1)S(1)}, bf16[768,256]{1,0:T(8,128)(2,1)}, u32[]{:S(2)}, u32[]{:S(2)}) collective-permute-start(bf16[768,256]{1,0:T(8,128)(2,1)S(1)} %get-tuple-element.45), channel_id=1, source_target_pairs={{0,2},{2,0},{1,3},{3,1},{4,6},{6,4},{5,7},{7,5},{8,10},{10,8},{9,1... | collective-permute-start | bytes 1179656 | tf_op jit(solution)/shard_map/ppermute | solution.py:25
  23.7 22.9 %collective-permute-start.7 = (bf16[768,256]{1,0:T(8,128)(2,1)S(1)}, bf16[768,256]{1,0:T(8,128)(2,1)S(1)}, u32[]{:S(2)}, u32[]{:S(2)}) collective-permute-start(bf16[768,256]{1,0:T(8,128)(2,1)S(1)} %get-tuple-element.46), channel_id=1, source_target_pairs={{0,2},{2,0},{1,3},{3,1},{4,6},{6,4},{5,7},{7,5},{8,10},{10,8},{9,1... | collective-permute-start | bytes 1179656 | tf_op jit(solution)/shard_map/ppermute | solution.py:25
  25.2 9.0 %collective-permute-start.19 = (bf16[512,256]{1,0:T(8,128)(2,1)S(1)}, bf16[512,256]{1,0:T(8,128)(2,1)S(1)}, u32[]{:S(2)}, u32[]{:S(2)}) collective-permute-start(bf16[512,256]{1,0:T(8,128)(2,1)S(1)} %slice.21), channel_id=1, source_target_pairs={{4,0},{8,4},{12,8},{5,1},{9,5},{13,9},{6,2},{10,6},{14,10},{7,3},{... | collective-permute-start | bytes 786440 | tf_op jit(solution)/shard_map/ppermute | solution.py:275
  27.5 0.7 copy-start.3
  28.2 17.8 %collective-permute-start = (bf16[512,256]{1,0:T(8,128)(2,1)S(1)}, bf16[512,256]{1,0:T(8,128)(2,1)S(1)}, u32[]{:S(2)}, u32[]{:S(2)}) collective-permute-start(bf16[512,256]{1,0:T(8,128)(2,1)S(1)} %get-tuple-element.44), channel_id=1, source_target_pairs={{0,2},{2,0},{1,3},{3,1},{4,6},{6,4},{5,7},{7,5},{8,10},{10,8},{9,1... | collective-permute-start | bytes 786440 | tf_op jit(solution)/shard_map/ppermute | solution.py:25
  34.1 12.5 %copy-start.5 = (bf16[512,256]{1,0:T(8,128)(2,1)}, bf16[512,256]{1,0:T(8,128)(2,1)S(1)}, u32[]{:S(2)}) copy-start(bf16[512,256]{1,0:T(8,128)(2,1)S(1)} %collective-permute-done.19.refs_11_) | copy-start | bytes 786436
  34.1 17.1 %collective-permute-start.3 = (bf16[512,256]{1,0:T(8,128)(2,1)}, bf16[512,256]{1,0:T(8,128)(2,1)}, u32[]{:S(2)}, u32[]{:S(2)}) collective-permute-start(bf16[512,256]{1,0:T(8,128)(2,1)} %get-tuple-element.43), channel_id=1, source_target_pairs={{0,2},{2,0},{1,3},{3,1},{4,6},{6,4},{5,7},{7,5},{8,10},{10,8},{9,1... | collective-permute-start | bytes 786440 | tf_op jit(solution)/shard_map/ppermute | solution.py:25
  46.0 8.7 %collective-permute-start.12 = (bf16[512,256]{1,0:T(8,128)(2,1)}, bf16[512,256]{1,0:T(8,128)(2,1)}, u32[]{:S(2)}, u32[]{:S(2)}) collective-permute-start(bf16[512,256]{1,0:T(8,128)(2,1)} %collective-permute-done.11.refs_5_.refs_2_), channel_id=1, source_target_pairs={{0,1},{1,0},{2,3},{3,2},{4,5},{5,4},{6,7},{7,6},{8,9},{9,8},{10,11... | collective-permute-start | bytes 786440 | tf_op jit(solution)/shard_map/ppermute | solution.py:25
  46.0 8.8 %collective-permute-start.14 = (bf16[512,256]{1,0:T(8,128)(2,1)}, bf16[512,256]{1,0:T(8,128)(2,1)}, u32[]{:S(2)}, u32[]{:S(2)}) collective-permute-start(bf16[512,256]{1,0:T(8,128)(2,1)} %collective-permute-done.13.refs_2_.refs_6_), channel_id=1, source_target_pairs={{0,1},{1,0},{2,3},{3,2},{4,5},{5,4},{6,7},{7,6},{8,9},{9,8},{10,11... | collective-permute-start | bytes 786440 | tf_op jit(solution)/shard_map/ppermute | solution.py:25
  46.6 14.1 %collective-permute-start.10 = (bf16[768,256]{1,0:T(8,128)(2,1)}, bf16[768,256]{1,0:T(8,128)(2,1)}, u32[]{:S(2)}, u32[]{:S(2)}) collective-permute-start(bf16[768,256]{1,0:T(8,128)(2,1)} %collective-permute-done.9.refs_5_.refs_2_), channel_id=1, source_target_pairs={{0,1},{1,0},{2,3},{3,2},{4,5},{5,4},{6,7},{7,6},{8,9},{9,8},{10,11... | collective-permute-start | bytes 1179656 | tf_op jit(solution)/shard_map/ppermute | solution.py:25
  46.6 1.3 %copy-start.1 = (bf16[4096,256]{1,0:T(8,128)(2,1)}, bf16[4096,256]{1,0:T(8,128)(2,1)S(1)}, u32[]{:S(2)}) copy-start(bf16[4096,256]{1,0:T(8,128)(2,1)S(1)} %collective-permute-done.1.source) | copy-start | bytes 6291460
  48.0 18.0 %collective-permute-start.8 = (bf16[768,256]{1,0:T(8,128)(2,1)S(1)}, bf16[768,256]{1,0:T(8,128)(2,1)S(1)}, u32[]{:S(2)}, u32[]{:S(2)}) collective-permute-start(bf16[768,256]{1,0:T(8,128)(2,1)S(1)} %collective-permute-done.7.refs_5_.refs_2_), channel_id=1, source_target_pairs={{0,1},{1,0},{2,3},{3,2},{4,5},{5,4},{6,7},{7,6},{8,9},{9,8},{10,11... | collective-permute-start | bytes 1179656 | tf_op jit(solution)/shard_map/ppermute | solution.py:25
  48.5 1.6 %copy-start.2 = (bf16[4096,256]{1,0:T(8,128)(2,1)S(1)}, bf16[4096,256]{1,0:T(8,128)(2,1)}, u32[]{:S(2)}) copy-start(bf16[4096,256]{1,0:T(8,128)(2,1)} %copy-done.1) | copy-start | bytes 6291460
  51.3 13.7 %collective-permute-start.16 = (bf16[512,256]{1,0:T(8,128)(2,1)S(1)}, bf16[512,256]{1,0:T(8,128)(2,1)S(1)}, u32[]{:S(2)}, u32[]{:S(2)}) collective-permute-start(bf16[512,256]{1,0:T(8,128)(2,1)S(1)} %collective-permute-done.5.refs_9_.refs_7_), channel_id=1, source_target_pairs={{0,4},{4,8},{8,12},{1,5},{5,9},{9,13},{2,6},{6,10},{10,14},{3,7},{... | collective-permute-start | bytes 786440 | tf_op jit(solution)/shard_map/ppermute | solution.py:274
  54.8 10.6 %collective-permute-start.6 = (bf16[512,256]{1,0:T(8,128)(2,1)S(1)}, bf16[512,256]{1,0:T(8,128)(2,1)S(1)}, u32[]{:S(2)}, u32[]{:S(2)}) collective-permute-start(bf16[512,256]{1,0:T(8,128)(2,1)S(1)} %collective-permute-done.5.refs_9_.refs_7_), channel_id=1, source_target_pairs={{0,1},{1,0},{2,3},{3,2},{4,5},{5,4},{6,7},{7,6},{8,9},{9,8},{10,11... | collective-permute-start | bytes 786440 | tf_op jit(solution)/shard_map/ppermute | solution.py:25
  54.9 10.8 %collective-permute-start.20 = (bf16[512,256]{1,0:T(8,128)(2,1)}, bf16[512,256]{1,0:T(8,128)(2,1)S(1)}, u32[]{:S(2)}, u32[]{:S(2)}) collective-permute-start(bf16[512,256]{1,0:T(8,128)(2,1)} %collective-permute-done.13.refs_2_.refs_6_), channel_id=1, source_target_pairs={{4,0},{8,4},{12,8},{5,1},{9,5},{13,9},{6,2},{10,6},{14,10},{7,3},{... | collective-permute-start | bytes 786440 | tf_op jit(solution)/shard_map/ppermute | solution.py:275
  60.7 9.4 %collective-permute-start.2 = (bf16[512,256]{1,0:T(8,128)(2,1)S(1)}, bf16[512,256]{1,0:T(8,128)(2,1)S(1)}, u32[]{:S(2)}, u32[]{:S(2)}) collective-permute-start(bf16[512,256]{1,0:T(8,128)(2,1)S(1)} %collective-permute-done.refs_5_.refs_2_), channel_id=1, source_target_pairs={{0,1},{1,0},{2,3},{3,2},{4,5},{5,4},{6,7},{7,6},{8,9},{9,8},{10,11... | collective-permute-start | bytes 786440 | tf_op jit(solution)/shard_map/ppermute | solution.py:25
  60.9 4.1 %copy-start.4 = (bf16[512,256]{1,0:T(8,128)(2,1)S(1)}, bf16[512,256]{1,0:T(8,128)(2,1)}, u32[]{:S(2)}) copy-start(bf16[512,256]{1,0:T(8,128)(2,1)} %copy-done.3) | copy-start | bytes 786436
  60.9 4.5 %copy-start.6 = (bf16[512,256]{1,0:T(8,128)(2,1)S(1)}, bf16[512,256]{1,0:T(8,128)(2,1)}, u32[]{:S(2)}) copy-start(bf16[512,256]{1,0:T(8,128)(2,1)} %copy-done.5) | copy-start | bytes 786436
  65.0 8.4 %collective-permute-start.17 = (bf16[512,256]{1,0:T(8,128)(2,1)S(1)}, bf16[512,256]{1,0:T(8,128)(2,1)S(1)}, u32[]{:S(2)}, u32[]{:S(2)}) collective-permute-start(bf16[512,256]{1,0:T(8,128)(2,1)S(1)} %copy-done.4), channel_id=1, source_target_pairs={{0,1},{1,0},{2,3},{3,2},{4,5},{5,4},{6,7},{7,6},{8,9},{9,8},{10,11... | collective-permute-start | bytes 786440 | tf_op jit(solution)/shard_map/ppermute | solution.py:25
  65.4 8.0 %collective-permute-start.21 = (bf16[512,256]{1,0:T(8,128)(2,1)S(1)}, bf16[512,256]{1,0:T(8,128)(2,1)S(1)}, u32[]{:S(2)}, u32[]{:S(2)}) collective-permute-start(bf16[512,256]{1,0:T(8,128)(2,1)S(1)} %copy-done.6), channel_id=1, source_target_pairs={{0,1},{1,0},{2,3},{3,2},{4,5},{5,4},{6,7},{7,6},{8,9},{9,8},{10,11... | collective-permute-start | bytes 786440 | tf_op jit(solution)/shard_map/ppermute | solution.py:25
  65.7 7.8 %collective-permute-start.18 = (bf16[512,256]{1,0:T(8,128)(2,1)S(1)}, bf16[512,256]{1,0:T(8,128)(2,1)S(1)}, u32[]{:S(2)}, u32[]{:S(2)}) collective-permute-start(bf16[512,256]{1,0:T(8,128)(2,1)S(1)} %collective-permute-done.16.refs_2_), channel_id=1, source_target_pairs={{0,1},{1,0},{2,3},{3,2},{4,5},{5,4},{6,7},{7,6},{8,9},{9,8},{10,11... | collective-permute-start | bytes 786440 | tf_op jit(solution)/shard_map/ppermute | solution.py:25
  65.9 7.5 %collective-permute-start.22 = (bf16[512,256]{1,0:T(8,128)(2,1)S(1)}, bf16[512,256]{1,0:T(8,128)(2,1)S(1)}, u32[]{:S(2)}, u32[]{:S(2)}) collective-permute-start(bf16[512,256]{1,0:T(8,128)(2,1)S(1)} %collective-permute-done.20.refs_12_), channel_id=1, source_target_pairs={{0,1},{1,0},{2,3},{3,2},{4,5},{5,4},{6,7},{7,6},{8,9},{9,8},{10,11... | collective-permute-start | bytes 786440 | tf_op jit(solution)/shard_map/ppermute | solution.py:25
  70.0 6.5 %collective-permute-start.4 = (bf16[512,256]{1,0:T(8,128)(2,1)}, bf16[512,256]{1,0:T(8,128)(2,1)S(1)}, u32[]{:S(2)}, u32[]{:S(2)}) collective-permute-start(bf16[512,256]{1,0:T(8,128)(2,1)} %collective-permute-done.3.refs_5_), channel_id=1, source_target_pairs={{0,1},{1,0},{2,3},{3,2},{4,5},{5,4},{6,7},{7,6},{8,9},{9,8},{10,11... | collective-permute-start | bytes 786440 | tf_op jit(solution)/shard_map/ppermute | solution.py:25

commit v5 on v4

--- a/solution.py
+++ b/solution.py
@@ -140,6 +140,36 @@
     copy = pltpu.make_async_copy(source, target, sem)
     copy.start()
     copy.wait()
+
+
+def cut_kernel(starts, source, *refs):
+    targets, sems = refs[:-1], refs[-1]
+    copies = [
+        pltpu.make_async_copy(source.at[pl.ds(start, target.shape[0])], target, sems.at[n])
+        for n, (start, target) in enumerate(zip(starts, targets))
+    ]
+    for copy in copies:
+        copy.start()
+    for copy in copies:
+        copy.wait()
+
+
+def cut_rows(array, ranges):
+    shapes = [
+        jax.ShapeDtypeStruct(((last - first) * ROWS, array.shape[1]), array.dtype)
+        for first, last in ranges
+    ]
+    return pl.pallas_call(
+        functools.partial(cut_kernel, tuple(first * ROWS for first, _ in ranges)),
+        out_shape=shapes,
+        in_specs=[pl.BlockSpec(memory_space=pl.ANY)],
+        out_specs=[pl.BlockSpec(memory_space=pltpu.VMEM)] * len(shapes),
+        scratch_shapes=[pltpu.SemaphoreType.DMA((len(shapes),))],
+        compiler_params=pltpu.CompilerParams(vmem_limit_bytes=VMEM_LIMIT),
+        cost_estimate=pl.CostEstimate(
+            flops=0, bytes_accessed=sum(4 * shape.size for shape in shapes), transcendentals=0
+        ),
+    )(array)
 
 
 def staged(array):
@@ -250,17 +280,14 @@
     up = [(i + 1, i) for i in range(ring - 1)]
     chunks = chunk_bounds(pairs)
 
-    def cut(first, last):
-        return lax.slice_in_dim(anomalies, first * ROWS, last * ROWS, axis=0)
-
-    top = cut(0, NEAR)
-    anomalies, top = lax.optimization_barrier((anomalies, top))
-    bottom = cut(pairs - NEAR, pairs)
+    top, bottom, start = cut_rows(anomalies, [(0, NEAR), (pairs - NEAR, pairs), chunks[0]])
+    *cuts, inside = cut_rows(anomalies, chunks[1:] + [(0, pairs)])
+    cuts = [start] + cuts
     tops = shifted(top, "member")
     bottoms = shifted(bottom, "member")
     middles = []
-    for first, last in chunks:
-        middles.append(shifted(cut(first, last), "member"))
+    for piece in cuts:
+        middles.append(shifted(piece, "member"))
 
     sets = [([(anomalies, 0, pairs)], top, bottom)]
     for s in range(len(tops)):
@@ -283,6 +310,7 @@
                     for array, first, count in there
                 ]
             )
+    held[0] = [(inside if array is anomalies else array, *run) for array, *run in held[0]]
     pieces = [
         {first + n: (array, n) for array, first, count in listed for n in range(count)}
         for listed in held

time: 82.8 us -> 81.5 us (0.984)
  waiting for transfers between devices: 29.8 us -> 26.6 us
  starting transfers between devices: 22.1 us -> 24.1 us
  local copies, waits for them, and re-layouts: 6.83 us -> 5.29 us
  Pallas kernels: 22.2 us -> 23.6 us
    slice x3 -> x0, local copies, waits for them, and re-layouts: 3.12 us -> none  [cut(): return lax.slice_in_dim(anomalies, first * ROWS, last * ROWS, axis=0)]
    ppermute x19, waiting for transfers between devices: 24.4 us -> 21.9 us  [shifted(): lax.ppermute(value, axis, [(i, (i + s) % count) for i in range(count)])]
    ppermute x19, starting transfers between devices: 10.5 us -> 12.4 us  [shifted(): lax.ppermute(value, axis, [(i, (i + s) % count) for i in range(count)])]
    unnamed x17, local copies, waits for them, and re-layouts: 3.71 us -> 5.29 us
    pallas_call x0 -> x2, Pallas kernels: none -> 1.4 us  [cut_rows(): pl.pallas_call(functools.partial(cut_kernel, tuple((first * ROWS for firs...]
  transfers between devices with their start and end apart: 23 -> 23, of which waited for: 6 -> 6; matrix products, arithmetic and copies ran while one was open for 3% -> 0% of each run, Pallas kernels for 22% -> 24%
where the time goes in v5:
time: 81.5 us; the launch traced here: 79.9 us
  waiting for transfers between devices  26.6 us (33%)
  starting transfers between devices  24.1 us (30%)
  Pallas kernels  23.6 us (29%)
  local copies, waits for them, and re-layouts  5.29 us (6%)
    pallas_call x6, Pallas kernels, run_steps(): pl.pallas_call(functools.partial(update_kernel, job), out_shape=shapes, i...  22.1 us
    ppermute x19, waiting for transfers between devices, shifted(): lax.ppermute(value, axis, [(i, (i + s) % count) for i in range(count)])  21.9 us
    ppermute x19, starting transfers between devices, shifted(): lax.ppermute(value, axis, [(i, (i + s) % count) for i in range(count)])  12.4 us
    ppermute x2, starting transfers between devices, per_device(): before = (lax.ppermute(tail, 'region', down), -NEAR, NEAR)  6.96 us
    unnamed x17, local copies, waits for them, and re-layouts  5.29 us
    ppermute x2, waiting for transfers between devices, per_device(): after = (lax.ppermute(head, 'region', up), pairs, NEAR)  4.73 us
    ppermute x2, starting transfers between devices, per_device(): after = (lax.ppermute(head, 'region', up), pairs, NEAR)  4.69 us
  transfers between devices with their start and end apart: 23, of which 6 were waited for; matrix products, arithmetic and copies ran while one was open for 0% of the time, Pallas kernels for 24%

profile of v5, /device:TPU:12, one launch (start us, length us, event | category | flops | bytes accessed | tf_op | source)
XLA Modules:
  0.0 79.9 jit_solution(15406791861026917464)
XLA Ops:
  0.0 1.6 %copy-done = bf16[4096,256]{1,0:T(8,128)(2,1)S(1)} copy-done((bf16[4096,256]{1,0:T(8,128)(2,1)S(1)}, bf16[4096,256]{1,0:T(8,128)(2,1)}, u32[]{:S(2)}) %copy-start) | copy-done | bytes 2097176
  1.7 1.6 %collective-permute-start.13 = (bf16[512,256]{1,0:T(8,128)(2,1)S(1)}, bf16[512,256]{1,0:T(8,128)(2,1)}, u32[]{:S(2)}, u32[]{:S(2)}) collective-permute-start(bf16[512,256]{1,0:T(8,128)(2,1)S(1)} %get-tuple-element.36), channel_id=1, source_target_pairs={{0,2},{2,0},{1,3},{3,1},{4,6},{6,4},{5,7},{7,5},{8,10},{10,8},{9,1... | collective-permute-start | bytes 786440 | tf_op jit(solution)/shard_map/ppermute | solution.py:25
  3.2 0.5 collective-permute-start.11
  3.8 1.5 %collective-permute-start.5 = (bf16[512,256]{1,0:T(8,128)(2,1)S(1)}, bf16[512,256]{1,0:T(8,128)(2,1)S(1)}, u32[]{:S(2)}, u32[]{:S(2)}) collective-permute-start(bf16[512,256]{1,0:T(8,128)(2,1)S(1)} %get-tuple-element.32), channel_id=1, source_target_pairs={{0,2},{2,0},{1,3},{3,1},{4,6},{6,4},{5,7},{7,5},{8,10},{10,8},{9,1... | collective-permute-start | bytes 786440 | tf_op jit(solution)/shard_map/ppermute | solution.py:25
  5.3 3.5 %collective-permute-start.15 = (bf16[512,256]{1,0:T(8,128)(2,1)S(1)}, bf16[512,256]{1,0:T(8,128)(2,1)S(1)}, u32[]{:S(2)}, u32[]{:S(2)}) collective-permute-start(bf16[512,256]{1,0:T(8,128)(2,1)S(1)} %get-tuple-element.32), channel_id=1, source_target_pairs={{0,4},{4,8},{8,12},{1,5},{5,9},{9,13},{2,6},{6,10},{10,14},{3,7},{... | collective-permute-start | bytes 786440 | tf_op jit(solution)/shard_map/ppermute | solution.py:301
  8.8 1.3 %shard_map.28 = (bf16[768,256]{1,0:T(8,128)(2,1)S(1)}, bf16[768,256]{1,0:T(8,128)(2,1)S(1)}, bf16[512,256]{1,0:T(8,128)(2,1)S(1)}, bf16[512,256]{1,0:T(8,128)(2,1)}, bf16[4096,256]{1,0:T(8,128)(2,1)S(1)}) custom-call(bf16[4096,256]{1,0:T(8,128)(2,1)S(1)} %copy-done), custom_call_target="tpu_custom_call" | custom-call | bytes 6815744 | tf_op jit(solution)/shard_map/pallas_call | solution.py:162
  10.1 1.0 %collective-permute-done.13.refs_2_.refs_6_ = bf16[512,256]{1,0:T(8,128)(2,1)} collective-permute-done((bf16[512,256]{1,0:T(8,128)(2,1)S(1)}, bf16[512,256]{1,0:T(8,128)(2,1)}, u32[]{:S(2)}, u32[]{:S(2)}) %collective-permute-start.13) | collective-permute-done | bytes 262176 | tf_op jit(solution)/shard_map/ppermute | solution.py:25
  11.0 1.5 %collective-permute-start.9 = (bf16[768,256]{1,0:T(8,128)(2,1)S(1)}, bf16[768,256]{1,0:T(8,128)(2,1)}, u32[]{:S(2)}, u32[]{:S(2)}) collective-permute-start(bf16[768,256]{1,0:T(8,128)(2,1)S(1)} %get-tuple-element.34), channel_id=1, source_target_pairs={{0,2},{2,0},{1,3},{3,1},{4,6},{6,4},{5,7},{7,5},{8,10},{10,8},{9,1... | collective-permute-start | bytes 1179656 | tf_op jit(solution)/shard_map/ppermute | solution.py:25
  12.5 4.1 %collective-permute-done.11.refs_5_.refs_2_ = bf16[512,256]{1,0:T(8,128)(2,1)} collective-permute-done((bf16[512,256]{1,0:T(8,128)(2,1)S(1)}, bf16[512,256]{1,0:T(8,128)(2,1)}, u32[]{:S(2)}, u32[]{:S(2)}) %collective-permute-start.11) | collective-permute-done | bytes 262176 | tf_op jit(solution)/shard_map/ppermute | solution.py:25
  16.7 1.5 %collective-permute-start.7 = (bf16[768,256]{1,0:T(8,128)(2,1)S(1)}, bf16[768,256]{1,0:T(8,128)(2,1)S(1)}, u32[]{:S(2)}, u32[]{:S(2)}) collective-permute-start(bf16[768,256]{1,0:T(8,128)(2,1)S(1)} %get-tuple-element.33), channel_id=1, source_target_pairs={{0,2},{2,0},{1,3},{3,1},{4,6},{6,4},{5,7},{7,5},{8,10},{10,8},{9,1... | collective-permute-start | bytes 1179656 | tf_op jit(solution)/shard_map/ppermute | solution.py:25
  18.1 4.0 %collective-permute-done.5.refs_9_.refs_7_ = bf16[512,256]{1,0:T(8,128)(2,1)S(1)} collective-permute-done((bf16[512,256]{1,0:T(8,128)(2,1)S(1)}, bf16[512,256]{1,0:T(8,128)(2,1)S(1)}, u32[]{:S(2)}, u32[]{:S(2)}) %collective-permute-start.5) | collective-permute-done | bytes 262176 | tf_op jit(solution)/shard_map/ppermute | solution.py:25
  22.2 2.3 %collective-permute-start.19 = (bf16[512,256]{1,0:T(8,128)(2,1)S(1)}, bf16[512,256]{1,0:T(8,128)(2,1)S(1)}, u32[]{:S(2)}, u32[]{:S(2)}) collective-permute-start(bf16[512,256]{1,0:T(8,128)(2,1)S(1)} %get-tuple-element.36), channel_id=1, source_target_pairs={{4,0},{8,4},{12,8},{5,1},{9,5},{13,9},{6,2},{10,6},{14,10},{7,3},{... | collective-permute-start | bytes 786440 | tf_op jit(solution)/shard_map/ppermute | solution.py:302
  24.5 0.7 copy-done.3
  25.2 1.5 %collective-permute-start = (bf16[512,256]{1,0:T(8,128)(2,1)S(1)}, bf16[512,256]{1,0:T(8,128)(2,1)S(1)}, u32[]{:S(2)}, u32[]{:S(2)}) collective-permute-start(bf16[512,256]{1,0:T(8,128)(2,1)S(1)} %get-tuple-element.30), channel_id=1, source_target_pairs={{0,2},{2,0},{1,3},{3,1},{4,6},{6,4},{5,7},{7,5},{8,10},{10,8},{9,1... | collective-permute-start | bytes 786440 | tf_op jit(solution)/shard_map/ppermute | solution.py:25
  26.7 4.7 %collective-permute-done.19.refs_11_ = bf16[512,256]{1,0:T(8,128)(2,1)S(1)} collective-permute-done((bf16[512,256]{1,0:T(8,128)(2,1)S(1)}, bf16[512,256]{1,0:T(8,128)(2,1)S(1)}, u32[]{:S(2)}, u32[]{:S(2)}) %collective-permute-start.19) | collective-permute-done | bytes 262176 | tf_op jit(solution)/shard_map/ppermute | solution.py:302
  31.5 1.5 %collective-permute-start.3 = (bf16[512,256]{1,0:T(8,128)(2,1)}, bf16[512,256]{1,0:T(8,128)(2,1)}, u32[]{:S(2)}, u32[]{:S(2)}) collective-permute-start(bf16[512,256]{1,0:T(8,128)(2,1)} %get-tuple-element.31), channel_id=1, source_target_pairs={{0,2},{2,0},{1,3},{3,1},{4,6},{6,4},{5,7},{7,5},{8,10},{10,8},{9,1... | collective-permute-start | bytes 786440 | tf_op jit(solution)/shard_map/ppermute | solution.py:25
  32.9 11.7 %collective-permute-done.refs_5_.refs_2_ = bf16[512,256]{1,0:T(8,128)(2,1)S(1)} collective-permute-done((bf16[512,256]{1,0:T(8,128)(2,1)S(1)}, bf16[512,256]{1,0:T(8,128)(2,1)S(1)}, u32[]{:S(2)}, u32[]{:S(2)}) %collective-permute-start) | collective-permute-done | bytes 262176 | tf_op jit(solution)/shard_map/ppermute | solution.py:25
  44.6 0.5 collective-permute-start.12
  45.2 1.3 %copy-done.1 = bf16[4096,256]{1,0:T(8,128)(2,1)} copy-done((bf16[4096,256]{1,0:T(8,128)(2,1)}, bf16[4096,256]{1,0:T(8,128)(2,1)S(1)}, u32[]{:S(2)}) %copy-start.1) | copy-done | bytes 2097176
  46.6 0.4 collective-permute-start.8
  47.1 1.6 %copy-done.2 = bf16[4096,256]{1,0:T(8,128)(2,1)S(1)} copy-done((bf16[4096,256]{1,0:T(8,128)(2,1)S(1)}, bf16[4096,256]{1,0:T(8,128)(2,1)}, u32[]{:S(2)}) %copy-start.2) | copy-done | bytes 2097176
  48.8 1.1 %collective-permute-done.3.refs_5_ = bf16[512,256]{1,0:T(8,128)(2,1)} collective-permute-done((bf16[512,256]{1,0:T(8,128)(2,1)}, bf16[512,256]{1,0:T(8,128)(2,1)}, u32[]{:S(2)}, u32[]{:S(2)}) %collective-permute-start.3) | collective-permute-done | bytes 262176 | tf_op jit(solution)/shard_map/ppermute | solution.py:25
  49.9 2.3 %collective-permute-start.20 = (bf16[512,256]{1,0:T(8,128)(2,1)}, bf16[512,256]{1,0:T(8,128)(2,1)S(1)}, u32[]{:S(2)}, u32[]{:S(2)}) collective-permute-start(bf16[512,256]{1,0:T(8,128)(2,1)} %collective-permute-done.13.refs_2_.refs_6_), channel_id=1, source_target_pairs={{4,0},{8,4},{12,8},{5,1},{9,5},{13,9},{6,2},{10,6},{14,10},{7,3},{... | collective-permute-start | bytes 786440 | tf_op jit(solution)/shard_map/ppermute | solution.py:302
  52.3 3.5 %collective-permute-start.16 = (bf16[512,256]{1,0:T(8,128)(2,1)S(1)}, bf16[512,256]{1,0:T(8,128)(2,1)S(1)}, u32[]{:S(2)}, u32[]{:S(2)}) collective-permute-start(bf16[512,256]{1,0:T(8,128)(2,1)S(1)} %collective-permute-done.5.refs_9_.refs_7_), channel_id=1, source_target_pairs={{0,4},{4,8},{8,12},{1,5},{5,9},{9,13},{2,6},{6,10},{10,14},{3,7},{... | collective-permute-start | bytes 786440 | tf_op jit(solution)/shard_map/ppermute | solution.py:301
  55.9 3.4 %shard_map.31 = (f32[256,256]{1,0:T(8,128)S(1)}, f32[256,256]{1,0:T(8,128)S(1)}, f32[256,256]{1,0:T(8,128)S(1)}, f32[256,256]{1,0:T(8,128)S(1)}) custom-call(f32[32,9]{1,0:T(8,128)S(1)} %copy.8.refs_0_, bf16[4096,256]{1,0:T(8,128)(2,1)S(1)} %get-tuple-element.29.refs_1_.refs_5_, bf16[512,256]{1,0:T(8,128)(2,1)} %collective-permute-done.13.refs_2_.refs_6_, ...), custom_call_target="tpu_custom_call" | custom-call | flops 1811939328 | bytes 2097152 | tf_op jit(solution)/shard_map/pallas_call | solution.py:240
  59.3 0.6 collective-permute-start.2
  59.8 4.1 %shard_map.32 = (bf16[3,256,256]{2,1,0:T(8,128)(2,1)S(1)}, f32[256,256]{1,0:T(8,128)S(1)}, f32[256,256]{1,0:T(8,128)S(1)}) custom-call(f32[32,9]{1,0:T(8,128)S(1)} %copy.8.refs_0_, bf16[4096,256]{1,0:T(8,128)(2,1)S(1)} %get-tuple-element.29.refs_1_.refs_5_, bf16[512,256]{1,0:T(8,128)(2,1)} %collective-permute-done.11.refs_5_.refs_2_, ...), custom_call_target="tpu_custom_call" | custom-call | flops 1811939328 | bytes 3801088 | tf_op jit(solution)/shard_map/pallas_call | solution.py:240
  64.0 0.5 collective-permute-start.21
  65.0 3.9 %shard_map.33 = (bf16[3,256,256]{2,1,0:T(8,128)(2,1)S(1)}, f32[256,256]{1,0:T(8,128)S(1)}, f32[256,256]{1,0:T(8,128)S(1)}) custom-call(f32[32,9]{1,0:T(8,128)S(1)} %copy.8.refs_0_, bf16[4096,256]{1,0:T(8,128)(2,1)S(1)} %get-tuple-element.29.refs_1_.refs_5_, bf16[768,256]{1,0:T(8,128)(2,1)} %collective-permute-done.9.refs_5_.refs_2_, ...), custom_call_target="tpu_custom_call" | custom-call | flops 1811939328 | bytes 3801088 | tf_op jit(solution)/shard_map/pallas_call | solution.py:240
  69.1 3.0 %shard_map.34 = (bf16[2,256,256]{2,1,0:T(8,128)(2,1)S(1)}, f32[256,256]{1,0:T(8,128)S(1)}, f32[256,256]{1,0:T(8,128)S(1)}) custom-call(f32[32,9]{1,0:T(8,128)S(1)} %copy.8.refs_0_, bf16[4096,256]{1,0:T(8,128)(2,1)S(1)} %get-tuple-element.29.refs_1_.refs_5_, bf16[768,256]{1,0:T(8,128)(2,1)S(1)} %collective-permute-done.7.refs_5_.refs_2_, ...), custom_call_target="tpu_custom_call" | custom-call | flops 1207959552 | bytes 2883584 | tf_op jit(solution)/shard_map/pallas_call | solution.py:240
  72.2 3.1 %shard_map.35 = (bf16[2,256,256]{2,1,0:T(8,128)(2,1)S(1)}, f32[256,256]{1,0:T(8,128)S(1)}, f32[256,256]{1,0:T(8,128)S(1)}) custom-call(f32[32,9]{1,0:T(8,128)S(1)} %copy.8.refs_0_, bf16[512,256]{1,0:T(8,128)(2,1)S(1)} %copy-done.4, bf16[512,256]{1,0:T(8,128)(2,1)S(1)} %collective-permute-done.16.refs_2_, ...), custom_call_target="tpu_custom_call" | custom-call | flops 1811939328 | bytes 4980736 | tf_op jit(solution)/shard_map/pallas_call | solution.py:240
  75.3 4.6 %shard_map.36 = bf16[4096,256]{1,0:T(8,128)(2,1)} custom-call(f32[32,9]{1,0:T(8,128)S(1)} %copy.8.refs_0_, bf16[4096,256]{1,0:T(8,128)(2,1)S(1)} %get-tuple-element.29.refs_1_.refs_5_, bf16[512,256]{1,0:T(8,128)(2,1)S(1)} %collective-permute-done.refs_5_.refs_2_, bf16[4096,256]{1,0:T(8,128)(2,1)S(1)} %shard_map.29.refs_3_.refs_7_, ...), custom_call_target="tpu_custom_call" | custom-call | flops 1811939328 | bytes 5505024 | tf_op jit(solution)/shard_map/pallas_call | solution.py:240
  (40 shorter events, 1.3 us)
Async XLA Ops:
  0.0 45.2 %collective-permute-start.1 = (bf16[4096,256]{1,0:T(8,128)(2,1)}, bf16[4096,256]{1,0:T(8,128)(2,1)S(1)}, u32[]{:S(2)}, u32[]{:S(2)}) collective-permute-start(bf16[4096,256]{1,0:T(8,128)(2,1)} %source.3), channel_id=1, source_target_pairs={{0,1},{1,0},{2,3},{3,2},{4,5},{5,4},{6,7},{7,6},{8,9},{9,8},{10,11... | collective-permute-start | bytes 6291464 | tf_op jit(solution)/shard_map/ppermute | solution.py:25
  0.0 1.6 %copy-start = (bf16[4096,256]{1,0:T(8,128)(2,1)S(1)}, bf16[4096,256]{1,0:T(8,128)(2,1)}, u32[]{:S(2)}) copy-start(bf16[4096,256]{1,0:T(8,128)(2,1)} %source.3) | copy-start | bytes 6291460
  1.6 45.4 %copy-start.7 = (f32[32,9]{0,1:T(8,128)S(1)}, f32[32,9]{0,1:T(8,128)}, u32[]{:S(2)}) copy-start(f32[32,9]{0,1:T(8,128)} %param.3) | copy-start | bytes 3460
  1.7 9.3 %collective-permute-start.13 = (bf16[512,256]{1,0:T(8,128)(2,1)S(1)}, bf16[512,256]{1,0:T(8,128)(2,1)}, u32[]{:S(2)}, u32[]{:S(2)}) collective-permute-start(bf16[512,256]{1,0:T(8,128)(2,1)S(1)} %get-tuple-element.36), channel_id=1, source_target_pairs={{0,2},{2,0},{1,3},{3,1},{4,6},{6,4},{5,7},{7,5},{8,10},{10,8},{9,1... | collective-permute-start | bytes 786440 | tf_op jit(solution)/shard_map/ppermute | solution.py:25
  3.2 13.4 %collective-permute-start.11 = (bf16[512,256]{1,0:T(8,128)(2,1)S(1)}, bf16[512,256]{1,0:T(8,128)(2,1)}, u32[]{:S(2)}, u32[]{:S(2)}) collective-permute-start(bf16[512,256]{1,0:T(8,128)(2,1)S(1)} %get-tuple-element.35), channel_id=1, source_target_pairs={{0,2},{2,0},{1,3},{3,1},{4,6},{6,4},{5,7},{7,5},{8,10},{10,8},{9,1... | collective-permute-start | bytes 786440 | tf_op jit(solution)/shard_map/ppermute | solution.py:25
  3.8 18.4 %collective-permute-start.5 = (bf16[512,256]{1,0:T(8,128)(2,1)S(1)}, bf16[512,256]{1,0:T(8,128)(2,1)S(1)}, u32[]{:S(2)}, u32[]{:S(2)}) collective-permute-start(bf16[512,256]{1,0:T(8,128)(2,1)S(1)} %get-tuple-element.32), channel_id=1, source_target_pairs={{0,2},{2,0},{1,3},{3,1},{4,6},{6,4},{5,7},{7,5},{8,10},{10,8},{9,1... | collective-permute-start | bytes 786440 | tf_op jit(solution)/shard_map/ppermute | solution.py:25
  5.3 19.3 %collective-permute-start.15 = (bf16[512,256]{1,0:T(8,128)(2,1)S(1)}, bf16[512,256]{1,0:T(8,128)(2,1)S(1)}, u32[]{:S(2)}, u32[]{:S(2)}) collective-permute-start(bf16[512,256]{1,0:T(8,128)(2,1)S(1)} %get-tuple-element.32), channel_id=1, source_target_pairs={{0,4},{4,8},{8,12},{1,5},{5,9},{9,13},{2,6},{6,10},{10,14},{3,7},{... | collective-permute-start | bytes 786440 | tf_op jit(solution)/shard_map/ppermute | solution.py:301
  11.0 33.6 %collective-permute-start.9 = (bf16[768,256]{1,0:T(8,128)(2,1)S(1)}, bf16[768,256]{1,0:T(8,128)(2,1)}, u32[]{:S(2)}, u32[]{:S(2)}) collective-permute-start(bf16[768,256]{1,0:T(8,128)(2,1)S(1)} %get-tuple-element.34), channel_id=1, source_target_pairs={{0,2},{2,0},{1,3},{3,1},{4,6},{6,4},{5,7},{7,5},{8,10},{10,8},{9,1... | collective-permute-start | bytes 1179656 | tf_op jit(solution)/shard_map/ppermute | solution.py:25
  16.7 28.5 %collective-permute-start.7 = (bf16[768,256]{1,0:T(8,128)(2,1)S(1)}, bf16[768,256]{1,0:T(8,128)(2,1)S(1)}, u32[]{:S(2)}, u32[]{:S(2)}) collective-permute-start(bf16[768,256]{1,0:T(8,128)(2,1)S(1)} %get-tuple-element.33), channel_id=1, source_target_pairs={{0,2},{2,0},{1,3},{3,1},{4,6},{6,4},{5,7},{7,5},{8,10},{10,8},{9,1... | collective-permute-start | bytes 1179656 | tf_op jit(solution)/shard_map/ppermute | solution.py:25
  22.2 9.3 %collective-permute-start.19 = (bf16[512,256]{1,0:T(8,128)(2,1)S(1)}, bf16[512,256]{1,0:T(8,128)(2,1)S(1)}, u32[]{:S(2)}, u32[]{:S(2)}) collective-permute-start(bf16[512,256]{1,0:T(8,128)(2,1)S(1)} %get-tuple-element.36), channel_id=1, source_target_pairs={{4,0},{8,4},{12,8},{5,1},{9,5},{13,9},{6,2},{10,6},{14,10},{7,3},{... | collective-permute-start | bytes 786440 | tf_op jit(solution)/shard_map/ppermute | solution.py:302
  24.5 0.7 copy-start.3
  25.2 19.4 %collective-permute-start = (bf16[512,256]{1,0:T(8,128)(2,1)S(1)}, bf16[512,256]{1,0:T(8,128)(2,1)S(1)}, u32[]{:S(2)}, u32[]{:S(2)}) collective-permute-start(bf16[512,256]{1,0:T(8,128)(2,1)S(1)} %get-tuple-element.30), channel_id=1, source_target_pairs={{0,2},{2,0},{1,3},{3,1},{4,6},{6,4},{5,7},{7,5},{8,10},{10,8},{9,1... | collective-permute-start | bytes 786440 | tf_op jit(solution)/shard_map/ppermute | solution.py:25
  31.5 13.8 %copy-start.5 = (bf16[512,256]{1,0:T(8,128)(2,1)}, bf16[512,256]{1,0:T(8,128)(2,1)S(1)}, u32[]{:S(2)}) copy-start(bf16[512,256]{1,0:T(8,128)(2,1)S(1)} %collective-permute-done.19.refs_11_) | copy-start | bytes 786436
  31.5 18.4 %collective-permute-start.3 = (bf16[512,256]{1,0:T(8,128)(2,1)}, bf16[512,256]{1,0:T(8,128)(2,1)}, u32[]{:S(2)}, u32[]{:S(2)}) collective-permute-start(bf16[512,256]{1,0:T(8,128)(2,1)} %get-tuple-element.31), channel_id=1, source_target_pairs={{0,2},{2,0},{1,3},{3,1},{4,6},{6,4},{5,7},{7,5},{8,10},{10,8},{9,1... | collective-permute-start | bytes 786440 | tf_op jit(solution)/shard_map/ppermute | solution.py:25
  44.6 7.6 %collective-permute-start.14 = (bf16[512,256]{1,0:T(8,128)(2,1)}, bf16[512,256]{1,0:T(8,128)(2,1)}, u32[]{:S(2)}, u32[]{:S(2)}) collective-permute-start(bf16[512,256]{1,0:T(8,128)(2,1)} %collective-permute-done.13.refs_2_.refs_6_), channel_id=1, source_target_pairs={{0,1},{1,0},{2,3},{3,2},{4,5},{5,4},{6,7},{7,6},{8,9},{9,8},{10,11... | collective-permute-start | bytes 786440 | tf_op jit(solution)/shard_map/ppermute | solution.py:25
  44.6 11.1 %collective-permute-start.12 = (bf16[512,256]{1,0:T(8,128)(2,1)}, bf16[512,256]{1,0:T(8,128)(2,1)}, u32[]{:S(2)}, u32[]{:S(2)}) collective-permute-start(bf16[512,256]{1,0:T(8,128)(2,1)} %collective-permute-done.11.refs_5_.refs_2_), channel_id=1, source_target_pairs={{0,1},{1,0},{2,3},{3,2},{4,5},{5,4},{6,7},{7,6},{8,9},{9,8},{10,11... | collective-permute-start | bytes 786440 | tf_op jit(solution)/shard_map/ppermute | solution.py:25
  45.2 14.1 %collective-permute-start.10 = (bf16[768,256]{1,0:T(8,128)(2,1)}, bf16[768,256]{1,0:T(8,128)(2,1)}, u32[]{:S(2)}, u32[]{:S(2)}) collective-permute-start(bf16[768,256]{1,0:T(8,128)(2,1)} %collective-permute-done.9.refs_5_.refs_2_), channel_id=1, source_target_pairs={{0,1},{1,0},{2,3},{3,2},{4,5},{5,4},{6,7},{7,6},{8,9},{9,8},{10,11... | collective-permute-start | bytes 1179656 | tf_op jit(solution)/shard_map/ppermute | solution.py:25
  45.2 1.3 %copy-start.1 = (bf16[4096,256]{1,0:T(8,128)(2,1)}, bf16[4096,256]{1,0:T(8,128)(2,1)S(1)}, u32[]{:S(2)}) copy-start(bf16[4096,256]{1,0:T(8,128)(2,1)S(1)} %collective-permute-done.1.source) | copy-start | bytes 6291460
  46.6 18.0 %collective-permute-start.8 = (bf16[768,256]{1,0:T(8,128)(2,1)S(1)}, bf16[768,256]{1,0:T(8,128)(2,1)S(1)}, u32[]{:S(2)}, u32[]{:S(2)}) collective-permute-start(bf16[768,256]{1,0:T(8,128)(2,1)S(1)} %collective-permute-done.7.refs_5_.refs_2_), channel_id=1, source_target_pairs={{0,1},{1,0},{2,3},{3,2},{4,5},{5,4},{6,7},{7,6},{8,9},{9,8},{10,11... | collective-permute-start | bytes 1179656 | tf_op jit(solution)/shard_map/ppermute | solution.py:25
  47.1 1.6 %copy-start.2 = (bf16[4096,256]{1,0:T(8,128)(2,1)S(1)}, bf16[4096,256]{1,0:T(8,128)(2,1)}, u32[]{:S(2)}) copy-start(bf16[4096,256]{1,0:T(8,128)(2,1)} %copy-done.1) | copy-start | bytes 6291460
  49.9 14.1 %collective-permute-start.20 = (bf16[512,256]{1,0:T(8,128)(2,1)}, bf16[512,256]{1,0:T(8,128)(2,1)S(1)}, u32[]{:S(2)}, u32[]{:S(2)}) collective-permute-start(bf16[512,256]{1,0:T(8,128)(2,1)} %collective-permute-done.13.refs_2_.refs_6_), channel_id=1, source_target_pairs={{4,0},{8,4},{12,8},{5,1},{9,5},{13,9},{6,2},{10,6},{14,10},{7,3},{... | collective-permute-start | bytes 786440 | tf_op jit(solution)/shard_map/ppermute | solution.py:302
  52.3 11.6 %collective-permute-start.16 = (bf16[512,256]{1,0:T(8,128)(2,1)S(1)}, bf16[512,256]{1,0:T(8,128)(2,1)S(1)}, u32[]{:S(2)}, u32[]{:S(2)}) collective-permute-start(bf16[512,256]{1,0:T(8,128)(2,1)S(1)} %collective-permute-done.5.refs_9_.refs_7_), channel_id=1, source_target_pairs={{0,4},{4,8},{8,12},{1,5},{5,9},{9,13},{2,6},{6,10},{10,14},{3,7},{... | collective-permute-start | bytes 786440 | tf_op jit(solution)/shard_map/ppermute | solution.py:301
  55.8 8.7 %collective-permute-start.6 = (bf16[512,256]{1,0:T(8,128)(2,1)S(1)}, bf16[512,256]{1,0:T(8,128)(2,1)S(1)}, u32[]{:S(2)}, u32[]{:S(2)}) collective-permute-start(bf16[512,256]{1,0:T(8,128)(2,1)S(1)} %collective-permute-done.5.refs_9_.refs_7_), channel_id=1, source_target_pairs={{0,1},{1,0},{2,3},{3,2},{4,5},{5,4},{6,7},{7,6},{8,9},{9,8},{10,11... | collective-permute-start | bytes 786440 | tf_op jit(solution)/shard_map/ppermute | solution.py:25
  59.3 9.6 %collective-permute-start.2 = (bf16[512,256]{1,0:T(8,128)(2,1)S(1)}, bf16[512,256]{1,0:T(8,128)(2,1)S(1)}, u32[]{:S(2)}, u32[]{:S(2)}) collective-permute-start(bf16[512,256]{1,0:T(8,128)(2,1)S(1)} %collective-permute-done.refs_5_.refs_2_), channel_id=1, source_target_pairs={{0,1},{1,0},{2,3},{3,2},{4,5},{5,4},{6,7},{7,6},{8,9},{9,8},{10,11... | collective-permute-start | bytes 786440 | tf_op jit(solution)/shard_map/ppermute | solution.py:25
  59.8 4.1 %copy-start.4 = (bf16[512,256]{1,0:T(8,128)(2,1)S(1)}, bf16[512,256]{1,0:T(8,128)(2,1)}, u32[]{:S(2)}) copy-start(bf16[512,256]{1,0:T(8,128)(2,1)} %copy-done.3) | copy-start | bytes 786436
  59.8 4.2 %copy-start.6 = (bf16[512,256]{1,0:T(8,128)(2,1)S(1)}, bf16[512,256]{1,0:T(8,128)(2,1)}, u32[]{:S(2)}) copy-start(bf16[512,256]{1,0:T(8,128)(2,1)} %copy-done.5) | copy-start | bytes 786436
  63.9 8.2 %collective-permute-start.17 = (bf16[512,256]{1,0:T(8,128)(2,1)S(1)}, bf16[512,256]{1,0:T(8,128)(2,1)S(1)}, u32[]{:S(2)}, u32[]{:S(2)}) collective-permute-start(bf16[512,256]{1,0:T(8,128)(2,1)S(1)} %copy-done.4), channel_id=1, source_target_pairs={{0,1},{1,0},{2,3},{3,2},{4,5},{5,4},{6,7},{7,6},{8,9},{9,8},{10,11... | collective-permute-start | bytes 786440 | tf_op jit(solution)/shard_map/ppermute | solution.py:25
  64.0 8.1 %collective-permute-start.21 = (bf16[512,256]{1,0:T(8,128)(2,1)S(1)}, bf16[512,256]{1,0:T(8,128)(2,1)S(1)}, u32[]{:S(2)}, u32[]{:S(2)}) collective-permute-start(bf16[512,256]{1,0:T(8,128)(2,1)S(1)} %copy-done.6), channel_id=1, source_target_pairs={{0,1},{1,0},{2,3},{3,2},{4,5},{5,4},{6,7},{7,6},{8,9},{9,8},{10,11... | collective-permute-start | bytes 786440 | tf_op jit(solution)/shard_map/ppermute | solution.py:25
  64.5 7.6 %collective-permute-start.18 = (bf16[512,256]{1,0:T(8,128)(2,1)S(1)}, bf16[512,256]{1,0:T(8,128)(2,1)S(1)}, u32[]{:S(2)}, u32[]{:S(2)}) collective-permute-start(bf16[512,256]{1,0:T(8,128)(2,1)S(1)} %collective-permute-done.16.refs_2_), channel_id=1, source_target_pairs={{0,1},{1,0},{2,3},{3,2},{4,5},{5,4},{6,7},{7,6},{8,9},{9,8},{10,11... | collective-permute-start | bytes 786440 | tf_op jit(solution)/shard_map/ppermute | solution.py:25
  64.6 7.5 %collective-permute-start.22 = (bf16[512,256]{1,0:T(8,128)(2,1)S(1)}, bf16[512,256]{1,0:T(8,128)(2,1)S(1)}, u32[]{:S(2)}, u32[]{:S(2)}) collective-permute-start(bf16[512,256]{1,0:T(8,128)(2,1)S(1)} %collective-permute-done.20.refs_12_), channel_id=1, source_target_pairs={{0,1},{1,0},{2,3},{3,2},{4,5},{5,4},{6,7},{7,6},{8,9},{9,8},{10,11... | collective-permute-start | bytes 786440 | tf_op jit(solution)/shard_map/ppermute | solution.py:25
  68.9 6.4 %collective-permute-start.4 = (bf16[512,256]{1,0:T(8,128)(2,1)}, bf16[512,256]{1,0:T(8,128)(2,1)S(1)}, u32[]{:S(2)}, u32[]{:S(2)}) collective-permute-start(bf16[512,256]{1,0:T(8,128)(2,1)} %collective-permute-done.3.refs_5_), channel_id=1, source_target_pairs={{0,1},{1,0},{2,3},{3,2},{4,5},{5,4},{6,7},{7,6},{8,9},{9,8},{10,11... | collective-permute-start | bytes 786440 | tf_op jit(solution)/shard_map/ppermute | solution.py:25

commit v6 on v5

--- a/solution.py
+++ b/solution.py
@@ -42,7 +42,7 @@
     inputs = dict(zip(acc_in, refs[1 + arrays : 1 + arrays + len(acc_in)]))
     earlier = refs[1 + arrays + len(acc_in) : job["operands"]]
     outs = refs[job["operands"] :]
-    if writes:
+    if job["last"]:
         out, acc, obuf, out_sem = outs[0], *outs[-3:]
         sent = [
             pltpu.make_async_copy(
@@ -87,7 +87,7 @@
                 i, j = i_pair * PAIR + ii, j_pair * PAIR + jj
                 slot = (i - j if flip else j - i) + REACH
                 if 0 <= slot < SLOTS:
-                    weight = taper[j if flip else i, slot] * FACTOR
+                    weight = taper[slot, j if flip else i] * FACTOR
                     tile = c[ii * BLOCK : (ii + 1) * BLOCK, jj * BLOCK : (jj + 1) * BLOCK]
                     row.append((tile * weight).astype(jnp.bfloat16))
                 else:
@@ -97,11 +97,19 @@
 
     for j, first, count in steps:
         near = list(range(first, first + count))
-        gram = lax.dot_general(
-            jnp.concatenate([held(i) for i in near], axis=0),
-            held(j),
-            (((1,), (1,)), ((), ())),
-            preferred_element_type=jnp.float32,
+        left = jnp.concatenate([held(i) for i in near], axis=0)
+        half = count * ROWS // 2
+        gram = jnp.concatenate(
+            [
+                lax.dot_general(
+                    part,
+                    held(j),
+                    (((1,), (1,)), ((), ())),
+                    preferred_element_type=jnp.float32,
+                )
+                for part in (left[:half], left[half:])
+            ],
+            axis=0,
         )
         tiles = {i: gram[n * ROWS : (n + 1) * ROWS] for n, i in enumerate(near)}
         mine = [i for i in near if i in owned]
@@ -126,12 +134,12 @@
     for n, pair in enumerate(finished):
         update = (sums if pair in begun else inputs)[pair][...]
         obuf[n] = (own(pair).astype(jnp.float32) - 0.5 * update).astype(jnp.bfloat16)
-        if writes:
+        if job["last"]:
             sent.append(
                 pltpu.make_async_copy(obuf.at[n], out.at[tile_rows(pair)], out_sem.at[n])
             )
             sent[-1].start()
-    if writes:
+    if job["last"]:
         for copy in sent:
             copy.wait()
 
@@ -154,7 +162,7 @@
         copy.wait()
 
 
-def cut_rows(array, ranges):
+def cut_rows(array, ranges, limit=VMEM_LIMIT):
     shapes = [
         jax.ShapeDtypeStruct(((last - first) * ROWS, array.shape[1]), array.dtype)
         for first, last in ranges
@@ -162,10 +170,10 @@
     return pl.pallas_call(
         functools.partial(cut_kernel, tuple(first * ROWS for first, _ in ranges)),
         out_shape=shapes,
-        in_specs=[pl.BlockSpec(memory_space=pl.ANY)],
+        in_specs=[pl.BlockSpec(memory_space=pltpu.HBM)],
         out_specs=[pl.BlockSpec(memory_space=pltpu.VMEM)] * len(shapes),
         scratch_shapes=[pltpu.SemaphoreType.DMA((len(shapes),))],
-        compiler_params=pltpu.CompilerParams(vmem_limit_bytes=VMEM_LIMIT),
+        compiler_params=pltpu.CompilerParams(vmem_limit_bytes=limit),
         cost_estimate=pl.CostEstimate(
             flops=0, bytes_accessed=sum(4 * shape.size for shape in shapes), transcendentals=0
         ),
@@ -184,6 +192,35 @@
             flops=0, bytes_accessed=2 * array.size, transcendentals=0
         ),
     )(array)
+
+
+def join_kernel(*refs):
+    sources, target, sems = refs[:-2], refs[-2], refs[-1]
+    copies, at = [], 0
+    for n, source in enumerate(sources):
+        copies.append(
+            pltpu.make_async_copy(source, target.at[pl.ds(at, source.shape[0])], sems.at[n])
+        )
+        at += source.shape[0]
+    for copy in copies:
+        copy.start()
+    for copy in copies:
+        copy.wait()
+
+
+def joined(arrays):
+    rows = sum(array.shape[0] for array in arrays)
+    return pl.pallas_call(
+        join_kernel,
+        out_shape=jax.ShapeDtypeStruct((rows, arrays[0].shape[1]), arrays[0].dtype),
+        in_specs=[pl.BlockSpec(memory_space=pl.ANY)] * len(arrays),
+        out_specs=pl.BlockSpec(memory_space=pltpu.VMEM),
+        scratch_shapes=[pltpu.SemaphoreType.DMA((len(arrays),))],
+        compiler_params=pltpu.CompilerParams(vmem_limit_bytes=VMEM_LIMIT),
+        cost_estimate=pl.CostEstimate(
+            flops=0, bytes_accessed=4 * rows * arrays[0].shape[1], transcendentals=0
+        ),
+    )(*arrays)
 
 
 def run_steps(taper, pieces, steps, owned, state, finished, stored, rows, members, last):
@@ -213,12 +250,13 @@
     if last:
         for array, (pairs, _) in enumerate(stored):
             writes += [(array, n, pair) for n, pair in enumerate(pairs)]
-    operands = [taper] + arrays + [state[pair] for pair in acc_in]
+    operands = [taper.T] + arrays + [state[pair] for pair in acc_in]
     if last:
         operands += [block for _, block in stored]
     job = dict(
         parts=parts, plan=plan, steps=steps, owned=owned, acc_in=acc_in, acc_out=acc_out,
         finished=finished, arrays=len(arrays), writes=writes, operands=len(operands),
+        last=last,
     )
     inside = pl.BlockSpec(memory_space=pltpu.VMEM)
     specs = [pl.BlockSpec(memory_space=pltpu.SMEM)] + [inside] * (len(operands) - 1)
@@ -280,7 +318,9 @@
     up = [(i + 1, i) for i in range(ring - 1)]
     chunks = chunk_bounds(pairs)
 
-    top, bottom, start = cut_rows(anomalies, [(0, NEAR), (pairs - NEAR, pairs), chunks[0]])
+    top, bottom, start = cut_rows(
+        anomalies, [(0, NEAR), (pairs - NEAR, pairs), chunks[0]], 60 * 2**20
+    )
     *cuts, inside = cut_rows(anomalies, chunks[1:] + [(0, pairs)])
     cuts = [start] + cuts
     tops = shifted(top, "member")
@@ -289,32 +329,37 @@
     for piece in cuts:
         middles.append(shifted(piece, "member"))
 
-    sets = [([(anomalies, 0, pairs)], top, bottom)]
+    heads, tails = joined([top] + tops), joined([bottom] + bottoms)
+    before = lax.ppermute(tails, "region", down)
+    after = lax.ppermute(heads, "region", up)
+
+    def run(array, first, count, start=0):
+        return {first + n: (array, start + n) for n in range(count)}
+
+    held = [run(inside, 0, pairs)]
     for s in range(len(tops)):
-        listed = [(tops[s], 0, NEAR)]
+        listed = run(tops[s], 0, NEAR) | run(bottoms[s], pairs - NEAR, NEAR)
         for (first, last), middle in zip(chunks, middles):
-            listed.append((middle[s], first, last - first))
-        listed.append((bottoms[s], pairs - NEAR, NEAR))
-        sets.append((listed, tops[s], bottoms[s]))
-    held = []
-    for listed, head, tail in sets:
-        before = (lax.ppermute(tail, "region", down), -NEAR, NEAR)
-        after = (lax.ppermute(head, "region", up), pairs, NEAR)
-        held.append([before, after] + listed)
+            listed |= run(middle[s], first, last - first)
+        held.append(listed)
+    for n, listed in enumerate(held):
+        listed |= run(before, -NEAR, NEAR, n * NEAR) | run(after, pairs, NEAR, n * NEAR)
+
+    pieces = list(held)
     for turn in range(lax.axis_size("tile") - 1):
-        for listed in list(held):
-            there = [(shifted(array, "tile")[turn], first, count) for array, first, count in listed]
-            held.append(
-                [
-                    (staged(array) if count == pairs else array, first, count)
-                    for array, first, count in there
-                ]
-            )
-    held[0] = [(inside if array is anomalies else array, *run) for array, *run in held[0]]
-    pieces = [
-        {first + n: (array, n) for array, first, count in listed for n in range(count)}
-        for listed in held
-    ]
+        sent = {}
+
+        def passed(array):
+            if id(array) not in sent:
+                if array is inside:
+                    moved = shifted(anomalies, "tile")[turn]
+                    sent[id(array)] = staged(moved)
+                else:
+                    sent[id(array)] = shifted(array, "tile")[turn]
+            return sent[id(array)]
+
+        for listed in held:
+            pieces.append({pair: (passed(array), n) for pair, (array, n) in listed.items()})
 
     owned = set(range(pairs))
     state, stored = {}, []
@@ -335,7 +380,8 @@
     there, done = set(), set()
     low, high = list(range(NEAR)), list(range(pairs - NEAR, pairs))
     around = list(range(-NEAR, 0)) + list(range(pairs, pairs + NEAR))
-    batches = [low + list(range(*chunks[0])), high + around] + [list(range(*c)) for c in chunks[1:]]
+    batches = [low + list(range(*chunks[0])), list(range(*chunks[1])), high + around]
+    batches += [list(range(*c)) for c in chunks[2:]]
     for n, fresh in enumerate(batches):
         steps, there = steps_for(fresh, there)
         ready = [

time: 81.5 us -> 72.9 us (0.89)
  the two profiles are of different devices: /device:TPU:12 before, /device:TPU:0 now
where the time goes in v6:
time: 72.9 us; the launch traced here: 72.7 us
  waiting for transfers between devices  31.3 us (43%)
  Pallas kernels  22.9 us (31%)
  starting transfers between devices  18.3 us (25%)
    ppermute x17, waiting for transfers between devices, shifted(): lax.ppermute(value, axis, [(i, (i + s) % count) for i in range(count)])  28.4 us
    pallas_call x6, Pallas kernels, run_steps(): pl.pallas_call(functools.partial(update_kernel, job), out_shape=shapes, i...  18.4 us
    ppermute x17, starting transfers between devices, shifted(): lax.ppermute(value, axis, [(i, (i + s) % count) for i in range(count)])  13 us
    ppermute x1, starting transfers between devices, per_device(): before = lax.ppermute(tails, 'region', down)  4.03 us
    ppermute x1, waiting for transfers between devices, per_device(): after = lax.ppermute(heads, 'region', up)  2.89 us
    pallas_call x2, Pallas kernels, cut_rows(): pl.pallas_call(functools.partial(cut_kernel, tuple((first * ROWS for firs...  2.74 us
    pallas_call x1, Pallas kernels, staged(): pl.pallas_call(stage_kernel, out_shape=jax.ShapeDtypeStruct(array.shape,...  1.6 us
  transfers between devices with their start and end apart: 19, of which 6 were waited for; matrix products, arithmetic and copies ran while one was open for 0% of the time, Pallas kernels for 26%

profile of v6, /device:TPU:0, one launch (start us, length us, event | category | flops | bytes accessed | tf_op | source)
XLA Modules:
  0.0 72.7 jit_solution(13780345913247400762)
XLA Ops:
  0.0 0.5 collective-permute-start.1
  0.5 2.1 %shard_map.30 = (bf16[512,256]{1,0:T(8,128)(2,1)}, bf16[512,256]{1,0:T(8,128)(2,1)}, bf16[512,256]{1,0:T(8,128)(2,1)}) custom-call(bf16[4096,256]{1,0:T(8,128)(2,1)} %source.3), custom_call_target="tpu_custom_call" | custom-call | bytes 1572864 | tf_op jit(solution)/shard_map/pallas_call | solution.py:170
  2.7 2.6 %collective-permute-start.13 = (bf16[512,256]{1,0:T(8,128)(2,1)}, bf16[512,256]{1,0:T(8,128)(2,1)S(1)}, u32[]{:S(2)}, u32[]{:S(2)}) collective-permute-start(bf16[512,256]{1,0:T(8,128)(2,1)} %get-tuple-element.36.refs_0_), channel_id=1, source_target_pairs={{0,2},{2,0},{1,3},{3,1},{4,6},{6,4},{5,7},{7,5},{8,10},{10,8},{9,1... | collective-permute-start | bytes 786440 | tf_op jit(solution)/shard_map/ppermute | solution.py:25
  5.2 0.1 collective-permute-start.5
  5.3 0.6 shard_map.28
  5.9 2.0 %collective-permute-start.9 = (bf16[768,256]{1,0:T(8,128)(2,1)S(1)}, bf16[768,256]{1,0:T(8,128)(2,1)S(1)}, u32[]{:S(2)}, u32[]{:S(2)}) collective-permute-start(bf16[768,256]{1,0:T(8,128)(2,1)S(1)} %get-tuple-element.34), channel_id=1, source_target_pairs={{0,2},{2,0},{1,3},{3,1},{4,6},{6,4},{5,7},{7,5},{8,10},{10,8},{9,1... | collective-permute-start | bytes 1179656 | tf_op jit(solution)/shard_map/ppermute | solution.py:25
  7.9 0.1 collective-permute-start.11
  8.0 4.6 %collective-permute-done.13.refs_2_.refs_1_.refs_4_ = bf16[512,256]{1,0:T(8,128)(2,1)S(1)} collective-permute-done((bf16[512,256]{1,0:T(8,128)(2,1)}, bf16[512,256]{1,0:T(8,128)(2,1)S(1)}, u32[]{:S(2)}, u32[]{:S(2)}) %collective-permute-start.13) | collective-permute-done | bytes 262176 | tf_op jit(solution)/shard_map/ppermute | solution.py:25
  12.6 2.0 %collective-permute-start = (bf16[512,256]{1,0:T(8,128)(2,1)S(1)}, bf16[512,256]{1,0:T(8,128)(2,1)S(1)}, u32[]{:S(2)}, u32[]{:S(2)}) collective-permute-start(bf16[512,256]{1,0:T(8,128)(2,1)S(1)} %get-tuple-element.30), channel_id=1, source_target_pairs={{0,2},{2,0},{1,3},{3,1},{4,6},{6,4},{5,7},{7,5},{8,10},{10,8},{9,1... | collective-permute-start | bytes 786440 | tf_op jit(solution)/shard_map/ppermute | solution.py:25
  14.6 3.6 %collective-permute-done.5.refs_1_.refs_7_ = bf16[512,256]{1,0:T(8,128)(2,1)S(1)} collective-permute-done((bf16[512,256]{1,0:T(8,128)(2,1)}, bf16[512,256]{1,0:T(8,128)(2,1)S(1)}, u32[]{:S(2)}, u32[]{:S(2)}) %collective-permute-start.5) | collective-permute-done | bytes 262176 | tf_op jit(solution)/shard_map/ppermute | solution.py:25
  18.2 2.0 %collective-permute-start.7 = (bf16[768,256]{1,0:T(8,128)(2,1)S(1)}, bf16[768,256]{1,0:T(8,128)(2,1)S(1)}, u32[]{:S(2)}, u32[]{:S(2)}) collective-permute-start(bf16[768,256]{1,0:T(8,128)(2,1)S(1)} %get-tuple-element.33), channel_id=1, source_target_pairs={{0,2},{2,0},{1,3},{3,1},{4,6},{6,4},{5,7},{7,5},{8,10},{10,8},{9,1... | collective-permute-start | bytes 1179656 | tf_op jit(solution)/shard_map/ppermute | solution.py:25
  20.4 11.9 %collective-permute-done.11.refs_5_.refs_2_ = bf16[512,256]{1,0:T(8,128)(2,1)S(1)} collective-permute-done((bf16[512,256]{1,0:T(8,128)(2,1)S(1)}, bf16[512,256]{1,0:T(8,128)(2,1)S(1)}, u32[]{:S(2)}, u32[]{:S(2)}) %collective-permute-start.11) | collective-permute-done | bytes 262176 | tf_op jit(solution)/shard_map/ppermute | solution.py:25
  32.3 4.0 %collective-permute-start.15 = (bf16[1024,256]{1,0:T(8,128)(2,1)S(1)}, bf16[1024,256]{1,0:T(8,128)(2,1)S(1)}, u32[]{:S(2)}, u32[]{:S(2)}) collective-permute-start(bf16[1024,256]{1,0:T(8,128)(2,1)S(1)} %shard_map.35), channel_id=1, source_target_pairs={{0,4},{4,8},{8,12},{1,5},{5,9},{9,13},{2,6},{6,10},{10,14},{3,7},{... | collective-permute-start | bytes 1572872 | tf_op jit(solution)/shard_map/ppermute | solution.py:333
  36.3 1.6 %collective-permute-done.refs_5_.refs_2_ = bf16[512,256]{1,0:T(8,128)(2,1)S(1)} collective-permute-done((bf16[512,256]{1,0:T(8,128)(2,1)S(1)}, bf16[512,256]{1,0:T(8,128)(2,1)S(1)}, u32[]{:S(2)}, u32[]{:S(2)}) %collective-permute-start) | collective-permute-done | bytes 262176 | tf_op jit(solution)/shard_map/ppermute | solution.py:25
  37.9 1.3 %collective-permute-start.17 = (bf16[1024,256]{1,0:T(8,128)(2,1)S(1)}, bf16[1024,256]{1,0:T(8,128)(2,1)S(1)}, u32[]{:S(2)}, u32[]{:S(2)}) collective-permute-start(bf16[1024,256]{1,0:T(8,128)(2,1)S(1)} %shard_map.36), channel_id=1, source_target_pairs={{4,0},{8,4},{12,8},{5,1},{9,5},{13,9},{6,2},{10,6},{14,10},{7,3},{... | collective-permute-start | bytes 1572872 | tf_op jit(solution)/shard_map/ppermute | solution.py:334
  39.2 0.1 collective-permute-start.14
  39.3 6.7 %collective-permute-done.7.refs_5_.refs_2_ = bf16[768,256]{1,0:T(8,128)(2,1)S(1)} collective-permute-done((bf16[768,256]{1,0:T(8,128)(2,1)S(1)}, bf16[768,256]{1,0:T(8,128)(2,1)S(1)}, u32[]{:S(2)}, u32[]{:S(2)}) %collective-permute-start.7) | collective-permute-done | bytes 393248 | tf_op jit(solution)/shard_map/ppermute | solution.py:25
  46.0 0.5 collective-permute-start.10
  46.5 0.1 collective-permute-start.8
  46.6 1.6 %shard_map.29.refs_3_.refs_5_ = bf16[4096,256]{1,0:T(8,128)(2,1)S(1)} custom-call(bf16[4096,256]{1,0:T(8,128)(2,1)} %collective-permute-done.1.source), custom_call_target="tpu_custom_call" | custom-call | bytes 2097152 | tf_op jit(solution)/shard_map/pallas_call | solution.py:184
  48.2 1.8 %collective-permute-start.3 = (bf16[512,256]{1,0:T(8,128)(2,1)S(1)}, bf16[512,256]{1,0:T(8,128)(2,1)S(1)}, u32[]{:S(2)}, u32[]{:S(2)}) collective-permute-start(bf16[512,256]{1,0:T(8,128)(2,1)S(1)} %get-tuple-element.31), channel_id=1, source_target_pairs={{0,2},{2,0},{1,3},{3,1},{4,6},{6,4},{5,7},{7,5},{8,10},{10,8},{9,1... | collective-permute-start | bytes 786440 | tf_op jit(solution)/shard_map/ppermute | solution.py:25
  50.0 0.2 collective-permute-start.16
  50.2 2.9 %collective-permute-done.17.refs_9_ = bf16[1024,256]{1,0:T(8,128)(2,1)S(1)} collective-permute-done((bf16[1024,256]{1,0:T(8,128)(2,1)S(1)}, bf16[1024,256]{1,0:T(8,128)(2,1)S(1)}, u32[]{:S(2)}, u32[]{:S(2)}) %collective-permute-start.17) | collective-permute-done | bytes 524320 | tf_op jit(solution)/shard_map/ppermute | solution.py:334
  53.1 2.9 %shard_map.31 = (f32[256,256]{1,0:T(8,128)S(1)}, f32[256,256]{1,0:T(8,128)S(1)}, f32[256,256]{1,0:T(8,128)S(1)}, f32[256,256]{1,0:T(8,128)S(1)}) custom-call(f32[9,32]{1,0:T(8,128)S(1)} %bitcast.1, bf16[4096,256]{1,0:T(8,128)(2,1)S(1)} %get-tuple-element.29.refs_1_.refs_3_, bf16[512,256]{1,0:T(8,128)(2,1)S(1)} %collective-permute-done.13.refs_2_.refs_1_.refs_4_, ...), custom_call_target="tpu_custom_call" | custom-call | flops 1811939328 | bytes 2097152 | tf_op jit(solution)/shard_map/pallas_call | solution.py:278
  56.0 0.6 collective-permute-start.2
  56.6 2.9 %shard_map.32 = (bf16[3,256,256]{2,1,0:T(8,128)(2,1)S(1)}, f32[256,256]{1,0:T(8,128)S(1)}, f32[256,256]{1,0:T(8,128)S(1)}) custom-call(f32[9,32]{1,0:T(8,128)S(1)} %bitcast.2, bf16[4096,256]{1,0:T(8,128)(2,1)S(1)} %get-tuple-element.29.refs_1_.refs_3_, bf16[512,256]{1,0:T(8,128)(2,1)S(1)} %collective-permute-done.11.refs_5_.refs_2_, ...), custom_call_target="tpu_custom_call" | custom-call | flops 1811939328 | bytes 3801088 | tf_op jit(solution)/shard_map/pallas_call | solution.py:278
  59.5 0.1 collective-permute-start.6
  59.5 0.5 collective-permute-start.4
  60.0 2.9 %shard_map.33 = (bf16[3,256,256]{2,1,0:T(8,128)(2,1)S(1)}, f32[256,256]{1,0:T(8,128)S(1)}, f32[256,256]{1,0:T(8,128)S(1)}) custom-call(f32[9,32]{1,0:T(8,128)S(1)} %bitcast.3, bf16[4096,256]{1,0:T(8,128)(2,1)S(1)} %get-tuple-element.29.refs_1_.refs_3_, bf16[768,256]{1,0:T(8,128)(2,1)S(1)} %collective-permute-done.9.refs_5_.refs_2_, ...), custom_call_target="tpu_custom_call" | custom-call | flops 1811939328 | bytes 3801088 | tf_op jit(solution)/shard_map/pallas_call | solution.py:278
  62.9 2.2 %shard_map.34 = (bf16[2,256,256]{2,1,0:T(8,128)(2,1)S(1)}, f32[256,256]{1,0:T(8,128)S(1)}, f32[256,256]{1,0:T(8,128)S(1)}) custom-call(f32[9,32]{1,0:T(8,128)S(1)} %bitcast.4, bf16[4096,256]{1,0:T(8,128)(2,1)S(1)} %get-tuple-element.29.refs_1_.refs_3_, bf16[768,256]{1,0:T(8,128)(2,1)S(1)} %collective-permute-done.7.refs_5_.refs_2_, ...), custom_call_target="tpu_custom_call" | custom-call | flops 1207959552 | bytes 2883584 | tf_op jit(solution)/shard_map/pallas_call | solution.py:278
  65.2 3.4 %shard_map.37 = (bf16[2,256,256]{2,1,0:T(8,128)(2,1)S(1)}, f32[256,256]{1,0:T(8,128)S(1)}, f32[256,256]{1,0:T(8,128)S(1)}) custom-call(f32[9,32]{1,0:T(8,128)S(1)} %bitcast.5, bf16[1024,256]{1,0:T(8,128)(2,1)S(1)} %collective-permute-done.15.refs_1_, bf16[1024,256]{1,0:T(8,128)(2,1)S(1)} %collective-permute-done.16.refs_2_, ...), custom_call_target="tpu_custom_call" | custom-call | flops 1811939328 | bytes 4980736 | tf_op jit(solution)/shard_map/pallas_call | solution.py:278
  68.7 4.1 %shard_map.38 = bf16[4096,256]{1,0:T(8,128)(2,1)} custom-call(f32[9,32]{1,0:T(8,128)S(1)} %bitcast.6, bf16[4096,256]{1,0:T(8,128)(2,1)S(1)} %get-tuple-element.29.refs_1_.refs_3_, bf16[512,256]{1,0:T(8,128)(2,1)S(1)} %collective-permute-done.refs_5_.refs_2_, bf16[4096,256]{1,0:T(8,128)(2,1)S(1)} %shard_map.29.refs_3_.refs_5_, ...), custom_call_target="tpu_custom_call" | custom-call | flops 1811939328 | bytes 5505024 | tf_op jit(solution)/shard_map/pallas_call | solution.py:278
  (27 shorter events, 0.2 us)
Async XLA Ops:
  0.0 5.3 %copy-start = (bf16[4096,256]{1,0:T(8,128)(2,1)S(1)}, bf16[4096,256]{1,0:T(8,128)(2,1)}, u32[]{:S(2)}) copy-start(bf16[4096,256]{1,0:T(8,128)(2,1)} %source.3) | copy-start | bytes 6291460
  0.0 46.5 %collective-permute-start.1 = (bf16[4096,256]{1,0:T(8,128)(2,1)}, bf16[4096,256]{1,0:T(8,128)(2,1)}, u32[]{:S(2)}, u32[]{:S(2)}) collective-permute-start(bf16[4096,256]{1,0:T(8,128)(2,1)} %source.3), channel_id=1, source_target_pairs={{0,1},{1,0},{2,3},{3,2},{4,5},{5,4},{6,7},{7,6},{8,9},{9,8},{10,11... | collective-permute-start | bytes 6291464 | tf_op jit(solution)/shard_map/ppermute | solution.py:25
  2.6 5.3 %copy-start.4 = (bf16[512,256]{1,0:T(8,128)(2,1)S(1)}, bf16[512,256]{1,0:T(8,128)(2,1)}, u32[]{:S(2)}) copy-start(bf16[512,256]{1,0:T(8,128)(2,1)} %get-tuple-element.35) | copy-start | bytes 786436
  2.7 17.6 %copy-start.2 = (bf16[512,256]{1,0:T(8,128)(2,1)S(1)}, bf16[512,256]{1,0:T(8,128)(2,1)}, u32[]{:S(2)}) copy-start(bf16[512,256]{1,0:T(8,128)(2,1)} %get-tuple-element.32.refs_0_) | copy-start | bytes 786436
  2.7 17.6 %copy-start.1 = (bf16[512,256]{1,0:T(8,128)(2,1)S(1)}, bf16[512,256]{1,0:T(8,128)(2,1)}, u32[]{:S(2)}) copy-start(bf16[512,256]{1,0:T(8,128)(2,1)} %get-tuple-element.36.refs_0_) | copy-start | bytes 786436
  2.7 9.9 %collective-permute-start.13 = (bf16[512,256]{1,0:T(8,128)(2,1)}, bf16[512,256]{1,0:T(8,128)(2,1)S(1)}, u32[]{:S(2)}, u32[]{:S(2)}) collective-permute-start(bf16[512,256]{1,0:T(8,128)(2,1)} %get-tuple-element.36.refs_0_), channel_id=1, source_target_pairs={{0,2},{2,0},{1,3},{3,1},{4,6},{6,4},{5,7},{7,5},{8,10},{10,8},{9,1... | collective-permute-start | bytes 786440 | tf_op jit(solution)/shard_map/ppermute | solution.py:25
  5.2 13.0 %collective-permute-start.5 = (bf16[512,256]{1,0:T(8,128)(2,1)}, bf16[512,256]{1,0:T(8,128)(2,1)S(1)}, u32[]{:S(2)}, u32[]{:S(2)}) collective-permute-start(bf16[512,256]{1,0:T(8,128)(2,1)} %get-tuple-element.32.refs_0_), channel_id=1, source_target_pairs={{0,2},{2,0},{1,3},{3,1},{4,6},{6,4},{5,7},{7,5},{8,10},{10,8},{9,1... | collective-permute-start | bytes 786440 | tf_op jit(solution)/shard_map/ppermute | solution.py:25
  5.9 33.3 %collective-permute-start.9 = (bf16[768,256]{1,0:T(8,128)(2,1)S(1)}, bf16[768,256]{1,0:T(8,128)(2,1)S(1)}, u32[]{:S(2)}, u32[]{:S(2)}) collective-permute-start(bf16[768,256]{1,0:T(8,128)(2,1)S(1)} %get-tuple-element.34), channel_id=1, source_target_pairs={{0,2},{2,0},{1,3},{3,1},{4,6},{6,4},{5,7},{7,5},{8,10},{10,8},{9,1... | collective-permute-start | bytes 1179656 | tf_op jit(solution)/shard_map/ppermute | solution.py:25
  7.9 24.3 %collective-permute-start.11 = (bf16[512,256]{1,0:T(8,128)(2,1)S(1)}, bf16[512,256]{1,0:T(8,128)(2,1)S(1)}, u32[]{:S(2)}, u32[]{:S(2)}) collective-permute-start(bf16[512,256]{1,0:T(8,128)(2,1)S(1)} %copy-done.4), channel_id=1, source_target_pairs={{0,2},{2,0},{1,3},{3,1},{4,6},{6,4},{5,7},{7,5},{8,10},{10,8},{9,1... | collective-permute-start | bytes 786440 | tf_op jit(solution)/shard_map/ppermute | solution.py:25
  12.6 25.3 %collective-permute-start = (bf16[512,256]{1,0:T(8,128)(2,1)S(1)}, bf16[512,256]{1,0:T(8,128)(2,1)S(1)}, u32[]{:S(2)}, u32[]{:S(2)}) collective-permute-start(bf16[512,256]{1,0:T(8,128)(2,1)S(1)} %get-tuple-element.30), channel_id=1, source_target_pairs={{0,2},{2,0},{1,3},{3,1},{4,6},{6,4},{5,7},{7,5},{8,10},{10,8},{9,1... | collective-permute-start | bytes 786440 | tf_op jit(solution)/shard_map/ppermute | solution.py:25
  18.2 27.8 %collective-permute-start.7 = (bf16[768,256]{1,0:T(8,128)(2,1)S(1)}, bf16[768,256]{1,0:T(8,128)(2,1)S(1)}, u32[]{:S(2)}, u32[]{:S(2)}) collective-permute-start(bf16[768,256]{1,0:T(8,128)(2,1)S(1)} %get-tuple-element.33), channel_id=1, source_target_pairs={{0,2},{2,0},{1,3},{3,1},{4,6},{6,4},{5,7},{7,5},{8,10},{10,8},{9,1... | collective-permute-start | bytes 1179656 | tf_op jit(solution)/shard_map/ppermute | solution.py:25
  20.4 32.7 %copy-start.3 = (f32[32,9]{0,1:T(8,128)S(1)}, f32[32,9]{0,1:T(8,128)}, u32[]{:S(2)}) copy-start(f32[32,9]{0,1:T(8,128)} %param.3) | copy-start | bytes 3460
  32.3 17.7 %collective-permute-start.15 = (bf16[1024,256]{1,0:T(8,128)(2,1)S(1)}, bf16[1024,256]{1,0:T(8,128)(2,1)S(1)}, u32[]{:S(2)}, u32[]{:S(2)}) collective-permute-start(bf16[1024,256]{1,0:T(8,128)(2,1)S(1)} %shard_map.35), channel_id=1, source_target_pairs={{0,4},{4,8},{8,12},{1,5},{5,9},{9,13},{2,6},{6,10},{10,14},{3,7},{... | collective-permute-start | bytes 1572872 | tf_op jit(solution)/shard_map/ppermute | solution.py:333
  37.9 15.2 %collective-permute-start.17 = (bf16[1024,256]{1,0:T(8,128)(2,1)S(1)}, bf16[1024,256]{1,0:T(8,128)(2,1)S(1)}, u32[]{:S(2)}, u32[]{:S(2)}) collective-permute-start(bf16[1024,256]{1,0:T(8,128)(2,1)S(1)} %shard_map.36), channel_id=1, source_target_pairs={{4,0},{8,4},{12,8},{5,1},{9,5},{13,9},{6,2},{10,6},{14,10},{7,3},{... | collective-permute-start | bytes 1572872 | tf_op jit(solution)/shard_map/ppermute | solution.py:334
  39.2 6.8 %collective-permute-start.14 = (bf16[512,256]{1,0:T(8,128)(2,1)S(1)}, bf16[512,256]{1,0:T(8,128)(2,1)S(1)}, u32[]{:S(2)}, u32[]{:S(2)}) collective-permute-start(bf16[512,256]{1,0:T(8,128)(2,1)S(1)} %collective-permute-done.13.refs_2_.refs_1_.refs_4_), channel_id=1, source_target_pairs={{0,1},{1,0},{2,3},{3,2},{4,5},{5,4},{6,7},{7,6},{8,9},{9,8},{10,11... | collective-permute-start | bytes 786440 | tf_op jit(solution)/shard_map/ppermute | solution.py:25
  46.0 2.2 %collective-permute-start.12 = (bf16[512,256]{1,0:T(8,128)(2,1)S(1)}, bf16[512,256]{1,0:T(8,128)(2,1)S(1)}, u32[]{:S(2)}, u32[]{:S(2)}) collective-permute-start(bf16[512,256]{1,0:T(8,128)(2,1)S(1)} %collective-permute-done.11.refs_5_.refs_2_), channel_id=1, source_target_pairs={{0,1},{1,0},{2,3},{3,2},{4,5},{5,4},{6,7},{7,6},{8,9},{9,8},{10,11... | collective-permute-start | bytes 786440 | tf_op jit(solution)/shard_map/ppermute | solution.py:25
  46.0 10.0 %collective-permute-start.10 = (bf16[768,256]{1,0:T(8,128)(2,1)S(1)}, bf16[768,256]{1,0:T(8,128)(2,1)S(1)}, u32[]{:S(2)}, u32[]{:S(2)}) collective-permute-start(bf16[768,256]{1,0:T(8,128)(2,1)S(1)} %collective-permute-done.9.refs_5_.refs_2_), channel_id=1, source_target_pairs={{0,1},{1,0},{2,3},{3,2},{4,5},{5,4},{6,7},{7,6},{8,9},{9,8},{10,11... | collective-permute-start | bytes 1179656 | tf_op jit(solution)/shard_map/ppermute | solution.py:25
  46.5 13.0 %collective-permute-start.8 = (bf16[768,256]{1,0:T(8,128)(2,1)S(1)}, bf16[768,256]{1,0:T(8,128)(2,1)S(1)}, u32[]{:S(2)}, u32[]{:S(2)}) collective-permute-start(bf16[768,256]{1,0:T(8,128)(2,1)S(1)} %collective-permute-done.7.refs_5_.refs_2_), channel_id=1, source_target_pairs={{0,1},{1,0},{2,3},{3,2},{4,5},{5,4},{6,7},{7,6},{8,9},{9,8},{10,11... | collective-permute-start | bytes 1179656 | tf_op jit(solution)/shard_map/ppermute | solution.py:25
  48.2 11.3 %collective-permute-start.3 = (bf16[512,256]{1,0:T(8,128)(2,1)S(1)}, bf16[512,256]{1,0:T(8,128)(2,1)S(1)}, u32[]{:S(2)}, u32[]{:S(2)}) collective-permute-start(bf16[512,256]{1,0:T(8,128)(2,1)S(1)} %get-tuple-element.31), channel_id=1, source_target_pairs={{0,2},{2,0},{1,3},{3,1},{4,6},{6,4},{5,7},{7,5},{8,10},{10,8},{9,1... | collective-permute-start | bytes 786440 | tf_op jit(solution)/shard_map/ppermute | solution.py:25
  50.0 15.2 %collective-permute-start.16 = (bf16[1024,256]{1,0:T(8,128)(2,1)S(1)}, bf16[1024,256]{1,0:T(8,128)(2,1)S(1)}, u32[]{:S(2)}, u32[]{:S(2)}) collective-permute-start(bf16[1024,256]{1,0:T(8,128)(2,1)S(1)} %collective-permute-done.15.refs_1_), channel_id=1, source_target_pairs={{0,1},{1,0},{2,3},{3,2},{4,5},{5,4},{6,7},{7,6},{8,9},{9,8},{10,11... | collective-permute-start | bytes 1572872 | tf_op jit(solution)/shard_map/ppermute | solution.py:25
  53.0 12.1 %collective-permute-start.18 = (bf16[1024,256]{1,0:T(8,128)(2,1)S(1)}, bf16[1024,256]{1,0:T(8,128)(2,1)S(1)}, u32[]{:S(2)}, u32[]{:S(2)}) collective-permute-start(bf16[1024,256]{1,0:T(8,128)(2,1)S(1)} %collective-permute-done.17.refs_9_), channel_id=1, source_target_pairs={{0,1},{1,0},{2,3},{3,2},{4,5},{5,4},{6,7},{7,6},{8,9},{9,8},{10,11... | collective-permute-start | bytes 1572872 | tf_op jit(solution)/shard_map/ppermute | solution.py:25
  56.0 6.9 %collective-permute-start.2 = (bf16[512,256]{1,0:T(8,128)(2,1)S(1)}, bf16[512,256]{1,0:T(8,128)(2,1)S(1)}, u32[]{:S(2)}, u32[]{:S(2)}) collective-permute-start(bf16[512,256]{1,0:T(8,128)(2,1)S(1)} %collective-permute-done.refs_5_.refs_2_), channel_id=1, source_target_pairs={{0,1},{1,0},{2,3},{3,2},{4,5},{5,4},{6,7},{7,6},{8,9},{9,8},{10,11... | collective-permute-start | bytes 786440 | tf_op jit(solution)/shard_map/ppermute | solution.py:25
  59.5 5.7 %collective-permute-start.6 = (bf16[512,256]{1,0:T(8,128)(2,1)S(1)}, bf16[512,256]{1,0:T(8,128)(2,1)S(1)}, u32[]{:S(2)}, u32[]{:S(2)}) collective-permute-start(bf16[512,256]{1,0:T(8,128)(2,1)S(1)} %collective-permute-done.5.refs_1_.refs_7_), channel_id=1, source_target_pairs={{0,1},{1,0},{2,3},{3,2},{4,5},{5,4},{6,7},{7,6},{8,9},{9,8},{10,11... | collective-permute-start | bytes 786440 | tf_op jit(solution)/shard_map/ppermute | solution.py:25
  59.5 9.1 %collective-permute-start.4 = (bf16[512,256]{1,0:T(8,128)(2,1)S(1)}, bf16[512,256]{1,0:T(8,128)(2,1)S(1)}, u32[]{:S(2)}, u32[]{:S(2)}) collective-permute-start(bf16[512,256]{1,0:T(8,128)(2,1)S(1)} %collective-permute-done.3.refs_5_), channel_id=1, source_target_pairs={{0,1},{1,0},{2,3},{3,2},{4,5},{5,4},{6,7},{7,6},{8,9},{9,8},{10,11... | collective-permute-start | bytes 786440 | tf_op jit(solution)/shard_map/ppermute | solution.py:25

commit v7 on v6

--- a/solution.py
+++ b/solution.py
@@ -319,7 +319,7 @@
     chunks = chunk_bounds(pairs)
 
     top, bottom, start = cut_rows(
-        anomalies, [(0, NEAR), (pairs - NEAR, pairs), chunks[0]], 60 * 2**20
+        anomalies, [(0, NEAR), (pairs - NEAR, pairs), chunks[0]], 24 * 2**20
     )
     *cuts, inside = cut_rows(anomalies, chunks[1:] + [(0, pairs)])
     cuts = [start] + cuts
@@ -329,9 +329,10 @@
     for piece in cuts:
         middles.append(shifted(piece, "member"))
 
-    heads, tails = joined([top] + tops), joined([bottom] + bottoms)
+    heads = joined([top] + tops)
+    after = lax.ppermute(heads, "region", up)
+    tails = joined([bottom] + bottoms)
     before = lax.ppermute(tails, "region", down)
-    after = lax.ppermute(heads, "region", up)
 
     def run(array, first, count, start=0):
         return {first + n: (array, start + n) for n in range(count)}
@@ -352,7 +353,7 @@
         def passed(array):
             if id(array) not in sent:
                 if array is inside:
-                    moved = shifted(anomalies, "tile")[turn]
+                    moved = shifted(inside, "tile")[turn]
                     sent[id(array)] = staged(moved)
                 else:
                     sent[id(array)] = shifted(array, "tile")[turn]
@@ -380,8 +381,8 @@
     there, done = set(), set()
     low, high = list(range(NEAR)), list(range(pairs - NEAR, pairs))
     around = list(range(-NEAR, 0)) + list(range(pairs, pairs + NEAR))
-    batches = [low + list(range(*chunks[0])), list(range(*chunks[1])), high + around]
-    batches += [list(range(*c)) for c in chunks[2:]]
+    batches = [low + list(range(*chunks[0])), high + around]
+    batches += [list(range(*c)) for c in chunks[1:]]
     for n, fresh in enumerate(batches):
         steps, there = steps_for(fresh, there)
         ready = [

time: 72.9 us -> 73.1 us (level)
  Pallas kernels: 22.9 us -> 19.4 us
  waiting for transfers between devices: 31.3 us -> 33.7 us
  local copies, waits for them, and re-layouts: 0.02 us -> 1.6 us
    pallas_call x2, Pallas kernels: 2.74 us -> 0.68 us  [cut_rows(): pl.pallas_call(functools.partial(cut_kernel, tuple((first * ROWS for firs...]
    unnamed x10 -> x4, local copies, waits for them, and re-layouts: 0.02 us -> 1.6 us
    pallas_call x1, Pallas kernels: 1.6 us -> 0.15 us  [staged(): pl.pallas_call(stage_kernel, out_shape=jax.ShapeDtypeStruct(array.shape,...]
    ppermute x17, waiting for transfers between devices: 28.4 us -> 29.8 us  [shifted(): lax.ppermute(value, axis, [(i, (i + s) % count) for i in range(count)])]
    ppermute x1, waiting for transfers between devices: 2.89 us -> 3.92 us  [per_device(): after = lax.ppermute(heads, 'region', up)]
  transfers between devices with their start and end apart: 19 -> 19, of which waited for: 6 -> 7; matrix products, arithmetic and copies ran while one was open for 0% -> 0% of each run, Pallas kernels for 26% -> 20%
where the time goes in v7:
time: 73.1 us; the launch traced here: 73 us
  waiting for transfers between devices  33.7 us (46%)
  Pallas kernels  19.4 us (27%)
  starting transfers between devices  18.1 us (25%)
  local copies, waits for them, and re-layouts  1.6 us (2%)
    ppermute x17, waiting for transfers between devices, shifted(): lax.ppermute(value, axis, [(i, (i + s) % count) for i in range(count)])  29.8 us
    pallas_call x6, Pallas kernels, run_steps(): pl.pallas_call(functools.partial(update_kernel, job), out_shape=shapes, i...  18.4 us
    ppermute x17, starting transfers between devices, shifted(): lax.ppermute(value, axis, [(i, (i + s) % count) for i in range(count)])  12.8 us
    ppermute x1, starting transfers between devices, per_device(): before = lax.ppermute(tails, 'region', down)  4.03 us
    ppermute x1, waiting for transfers between devices, per_device(): after = lax.ppermute(heads, 'region', up)  3.92 us
    unnamed x4, local copies, waits for them, and re-layouts  1.6 us
  transfers between devices with their start and end apart: 19, of which 7 were waited for; matrix products, arithmetic and copies ran while one was open for 0% of the time, Pallas kernels for 20%

profile of v7, /device:TPU:0, one launch (start us, length us, event | category | flops | bytes accessed | tf_op | source)
XLA Modules:
  0.0 73.0 jit_solution(4378623302467166068)
XLA Ops:
  0.0 1.6 %copy-done = bf16[4096,256]{1,0:T(8,128)(2,1)S(1)} copy-done((bf16[4096,256]{1,0:T(8,128)(2,1)S(1)}, bf16[4096,256]{1,0:T(8,128)(2,1)}, u32[]{:S(2)}) %copy-start) | copy-done | bytes 2097176
  1.6 0.6 shard_map.28
  2.2 0.6 collective-permute-start.1
  2.8 0.1 shard_map.30
  2.8 2.6 %collective-permute-start.13 = (bf16[512,256]{1,0:T(8,128)(2,1)S(1)}, bf16[512,256]{1,0:T(8,128)(2,1)S(1)}, u32[]{:S(2)}, u32[]{:S(2)}) collective-permute-start(bf16[512,256]{1,0:T(8,128)(2,1)S(1)} %get-tuple-element.36.refs_0_), channel_id=1, source_target_pairs={{0,2},{2,0},{1,3},{3,1},{4,6},{6,4},{5,7},{7,5},{8,10},{10,8},{9,1... | collective-permute-start | bytes 786440 | tf_op jit(solution)/shard_map/ppermute | solution.py:25
  5.4 0.1 collective-permute-start.5
  5.5 1.9 %collective-permute-start.9 = (bf16[768,256]{1,0:T(8,128)(2,1)S(1)}, bf16[768,256]{1,0:T(8,128)(2,1)S(1)}, u32[]{:S(2)}, u32[]{:S(2)}) collective-permute-start(bf16[768,256]{1,0:T(8,128)(2,1)S(1)} %get-tuple-element.34), channel_id=1, source_target_pairs={{0,2},{2,0},{1,3},{3,1},{4,6},{6,4},{5,7},{7,5},{8,10},{10,8},{9,1... | collective-permute-start | bytes 1179656 | tf_op jit(solution)/shard_map/ppermute | solution.py:25
  7.4 0.1 collective-permute-start.11
  7.5 5.0 %collective-permute-done.13.refs_2_.refs_1_.refs_4_ = bf16[512,256]{1,0:T(8,128)(2,1)S(1)} collective-permute-done((bf16[512,256]{1,0:T(8,128)(2,1)S(1)}, bf16[512,256]{1,0:T(8,128)(2,1)S(1)}, u32[]{:S(2)}, u32[]{:S(2)}) %collective-permute-start.13) | collective-permute-done | bytes 262176 | tf_op jit(solution)/shard_map/ppermute | solution.py:25
  12.6 2.0 %collective-permute-start = (bf16[512,256]{1,0:T(8,128)(2,1)S(1)}, bf16[512,256]{1,0:T(8,128)(2,1)S(1)}, u32[]{:S(2)}, u32[]{:S(2)}) collective-permute-start(bf16[512,256]{1,0:T(8,128)(2,1)S(1)} %get-tuple-element.30), channel_id=1, source_target_pairs={{0,2},{2,0},{1,3},{3,1},{4,6},{6,4},{5,7},{7,5},{8,10},{10,8},{9,1... | collective-permute-start | bytes 786440 | tf_op jit(solution)/shard_map/ppermute | solution.py:25
  14.6 3.6 %collective-permute-done.5.refs_1_.refs_7_ = bf16[512,256]{1,0:T(8,128)(2,1)S(1)} collective-permute-done((bf16[512,256]{1,0:T(8,128)(2,1)S(1)}, bf16[512,256]{1,0:T(8,128)(2,1)S(1)}, u32[]{:S(2)}, u32[]{:S(2)}) %collective-permute-start.5) | collective-permute-done | bytes 262176 | tf_op jit(solution)/shard_map/ppermute | solution.py:25
  18.2 2.0 %collective-permute-start.7 = (bf16[768,256]{1,0:T(8,128)(2,1)S(1)}, bf16[768,256]{1,0:T(8,128)(2,1)S(1)}, u32[]{:S(2)}, u32[]{:S(2)}) collective-permute-start(bf16[768,256]{1,0:T(8,128)(2,1)S(1)} %get-tuple-element.33), channel_id=1, source_target_pairs={{0,2},{2,0},{1,3},{3,1},{4,6},{6,4},{5,7},{7,5},{8,10},{10,8},{9,1... | collective-permute-start | bytes 1179656 | tf_op jit(solution)/shard_map/ppermute | solution.py:25
  20.3 11.9 %collective-permute-done.11.refs_5_.refs_2_ = bf16[512,256]{1,0:T(8,128)(2,1)S(1)} collective-permute-done((bf16[512,256]{1,0:T(8,128)(2,1)S(1)}, bf16[512,256]{1,0:T(8,128)(2,1)S(1)}, u32[]{:S(2)}, u32[]{:S(2)}) %collective-permute-start.11) | collective-permute-done | bytes 262176 | tf_op jit(solution)/shard_map/ppermute | solution.py:25
  32.2 4.0 %collective-permute-start.15 = (bf16[1024,256]{1,0:T(8,128)(2,1)S(1)}, bf16[1024,256]{1,0:T(8,128)(2,1)S(1)}, u32[]{:S(2)}, u32[]{:S(2)}) collective-permute-start(bf16[1024,256]{1,0:T(8,128)(2,1)S(1)} %shard_map.35), channel_id=1, source_target_pairs={{0,4},{4,8},{8,12},{1,5},{5,9},{9,13},{2,6},{6,10},{10,14},{3,7},{... | collective-permute-start | bytes 1572872 | tf_op jit(solution)/shard_map/ppermute | solution.py:335
  36.3 1.6 %collective-permute-done.refs_5_.refs_2_ = bf16[512,256]{1,0:T(8,128)(2,1)S(1)} collective-permute-done((bf16[512,256]{1,0:T(8,128)(2,1)S(1)}, bf16[512,256]{1,0:T(8,128)(2,1)S(1)}, u32[]{:S(2)}, u32[]{:S(2)}) %collective-permute-start) | collective-permute-done | bytes 262176 | tf_op jit(solution)/shard_map/ppermute | solution.py:25
  37.8 1.3 %collective-permute-start.17 = (bf16[1024,256]{1,0:T(8,128)(2,1)S(1)}, bf16[1024,256]{1,0:T(8,128)(2,1)S(1)}, u32[]{:S(2)}, u32[]{:S(2)}) collective-permute-start(bf16[1024,256]{1,0:T(8,128)(2,1)S(1)} %shard_map.36), channel_id=1, source_target_pairs={{4,0},{8,4},{12,8},{5,1},{9,5},{13,9},{6,2},{10,6},{14,10},{7,3},{... | collective-permute-start | bytes 1572872 | tf_op jit(solution)/shard_map/ppermute | solution.py:333
  39.1 0.1 collective-permute-start.14
  39.2 6.9 %collective-permute-done.7.refs_5_.refs_2_ = bf16[768,256]{1,0:T(8,128)(2,1)S(1)} collective-permute-done((bf16[768,256]{1,0:T(8,128)(2,1)S(1)}, bf16[768,256]{1,0:T(8,128)(2,1)S(1)}, u32[]{:S(2)}, u32[]{:S(2)}) %collective-permute-start.7) | collective-permute-done | bytes 393248 | tf_op jit(solution)/shard_map/ppermute | solution.py:25
  46.1 0.5 collective-permute-start.10
  46.7 0.1 shard_map.29.refs_3_.refs_5_
  46.8 0.8 %collective-permute-done.12.refs_6_.refs_4_ = bf16[512,256]{1,0:T(8,128)(2,1)S(1)} collective-permute-done((bf16[512,256]{1,0:T(8,128)(2,1)S(1)}, bf16[512,256]{1,0:T(8,128)(2,1)S(1)}, u32[]{:S(2)}, u32[]{:S(2)}) %collective-permute-start.12) | collective-permute-done | bytes 262176 | tf_op jit(solution)/shard_map/ppermute | solution.py:25
  47.6 1.7 %collective-permute-start.3 = (bf16[512,256]{1,0:T(8,128)(2,1)S(1)}, bf16[512,256]{1,0:T(8,128)(2,1)S(1)}, u32[]{:S(2)}, u32[]{:S(2)}) collective-permute-start(bf16[512,256]{1,0:T(8,128)(2,1)S(1)} %get-tuple-element.31), channel_id=1, source_target_pairs={{0,2},{2,0},{1,3},{3,1},{4,6},{6,4},{5,7},{7,5},{8,10},{10,8},{9,1... | collective-permute-start | bytes 786440 | tf_op jit(solution)/shard_map/ppermute | solution.py:25
  49.4 3.9 %collective-permute-done.17.refs_9_ = bf16[1024,256]{1,0:T(8,128)(2,1)S(1)} collective-permute-done((bf16[1024,256]{1,0:T(8,128)(2,1)S(1)}, bf16[1024,256]{1,0:T(8,128)(2,1)S(1)}, u32[]{:S(2)}, u32[]{:S(2)}) %collective-permute-start.17) | collective-permute-done | bytes 524320 | tf_op jit(solution)/shard_map/ppermute | solution.py:333
  53.3 2.9 %shard_map.31 = (f32[256,256]{1,0:T(8,128)S(1)}, f32[256,256]{1,0:T(8,128)S(1)}, f32[256,256]{1,0:T(8,128)S(1)}, f32[256,256]{1,0:T(8,128)S(1)}) custom-call(f32[9,32]{1,0:T(8,128)S(1)} %bitcast.1, bf16[4096,256]{1,0:T(8,128)(2,1)S(1)} %get-tuple-element.29.refs_1_.refs_3_, bf16[512,256]{1,0:T(8,128)(2,1)S(1)} %collective-permute-done.13.refs_2_.refs_1_.refs_4_, ...), custom_call_target="tpu_custom_call" | custom-call | flops 1811939328 | bytes 2097152 | tf_op jit(solution)/shard_map/pallas_call | solution.py:278
  56.2 0.6 collective-permute-start.2
  56.8 2.9 %shard_map.32 = (bf16[3,256,256]{2,1,0:T(8,128)(2,1)S(1)}, f32[256,256]{1,0:T(8,128)S(1)}, f32[256,256]{1,0:T(8,128)S(1)}) custom-call(f32[9,32]{1,0:T(8,128)S(1)} %bitcast.2, bf16[4096,256]{1,0:T(8,128)(2,1)S(1)} %get-tuple-element.29.refs_1_.refs_3_, bf16[512,256]{1,0:T(8,128)(2,1)S(1)} %collective-permute-done.11.refs_5_.refs_2_, ...), custom_call_target="tpu_custom_call" | custom-call | flops 1811939328 | bytes 3801088 | tf_op jit(solution)/shard_map/pallas_call | solution.py:278
  59.7 0.1 collective-permute-start.6
  59.8 0.5 collective-permute-start.4
  60.3 2.9 %shard_map.33 = (bf16[3,256,256]{2,1,0:T(8,128)(2,1)S(1)}, f32[256,256]{1,0:T(8,128)S(1)}, f32[256,256]{1,0:T(8,128)S(1)}) custom-call(f32[9,32]{1,0:T(8,128)S(1)} %bitcast.3, bf16[4096,256]{1,0:T(8,128)(2,1)S(1)} %get-tuple-element.29.refs_1_.refs_3_, bf16[768,256]{1,0:T(8,128)(2,1)S(1)} %collective-permute-done.9.refs_5_.refs_2_, ...), custom_call_target="tpu_custom_call" | custom-call | flops 1811939328 | bytes 3801088 | tf_op jit(solution)/shard_map/pallas_call | solution.py:278
  63.2 2.2 %shard_map.34 = (bf16[2,256,256]{2,1,0:T(8,128)(2,1)S(1)}, f32[256,256]{1,0:T(8,128)S(1)}, f32[256,256]{1,0:T(8,128)S(1)}) custom-call(f32[9,32]{1,0:T(8,128)S(1)} %bitcast.4, bf16[4096,256]{1,0:T(8,128)(2,1)S(1)} %get-tuple-element.29.refs_1_.refs_3_, bf16[768,256]{1,0:T(8,128)(2,1)S(1)} %collective-permute-done.7.refs_5_.refs_2_, ...), custom_call_target="tpu_custom_call" | custom-call | flops 1207959552 | bytes 2883584 | tf_op jit(solution)/shard_map/pallas_call | solution.py:278
  65.5 3.4 %shard_map.37 = (bf16[2,256,256]{2,1,0:T(8,128)(2,1)S(1)}, f32[256,256]{1,0:T(8,128)S(1)}, f32[256,256]{1,0:T(8,128)S(1)}) custom-call(f32[9,32]{1,0:T(8,128)S(1)} %bitcast.5, bf16[1024,256]{1,0:T(8,128)(2,1)S(1)} %collective-permute-done.15.refs_1_, bf16[1024,256]{1,0:T(8,128)(2,1)S(1)} %collective-permute-done.16.refs_2_, ...), custom_call_target="tpu_custom_call" | custom-call | flops 1811939328 | bytes 4980736 | tf_op jit(solution)/shard_map/pallas_call | solution.py:278
  68.9 4.1 %shard_map.38 = bf16[4096,256]{1,0:T(8,128)(2,1)} custom-call(f32[9,32]{1,0:T(8,128)S(1)} %bitcast.6, bf16[4096,256]{1,0:T(8,128)(2,1)S(1)} %get-tuple-element.29.refs_1_.refs_3_, bf16[512,256]{1,0:T(8,128)(2,1)S(1)} %collective-permute-done.refs_5_.refs_2_, bf16[4096,256]{1,0:T(8,128)(2,1)S(1)} %shard_map.29.refs_3_.refs_5_, ...), custom_call_target="tpu_custom_call" | custom-call | flops 1811939328 | bytes 5505024 | tf_op jit(solution)/shard_map/pallas_call | solution.py:278
  (21 shorter events, 0.2 us)
Async XLA Ops:
  0.0 1.6 %copy-start = (bf16[4096,256]{1,0:T(8,128)(2,1)S(1)}, bf16[4096,256]{1,0:T(8,128)(2,1)}, u32[]{:S(2)}) copy-start(bf16[4096,256]{1,0:T(8,128)(2,1)} %source.3) | copy-start | bytes 6291460
  2.2 44.4 %collective-permute-start.1 = (bf16[4096,256]{1,0:T(8,128)(2,1)S(1)}, bf16[4096,256]{1,0:T(8,128)(2,1)S(1)}, u32[]{:S(2)}, u32[]{:S(2)}) collective-permute-start(bf16[4096,256]{1,0:T(8,128)(2,1)S(1)} %get-tuple-element.29.refs_1_.refs_3_), channel_id=1, source_target_pairs={{0,1},{1,0},{2,3},{3,2},{4,5},{5,4},{6,7},{7,6},{8,9},{9,8},{10,11... | collective-permute-start | bytes 6291464 | tf_op jit(solution)/shard_map/ppermute | solution.py:25
  2.8 9.7 %collective-permute-start.13 = (bf16[512,256]{1,0:T(8,128)(2,1)S(1)}, bf16[512,256]{1,0:T(8,128)(2,1)S(1)}, u32[]{:S(2)}, u32[]{:S(2)}) collective-permute-start(bf16[512,256]{1,0:T(8,128)(2,1)S(1)} %get-tuple-element.36.refs_0_), channel_id=1, source_target_pairs={{0,2},{2,0},{1,3},{3,1},{4,6},{6,4},{5,7},{7,5},{8,10},{10,8},{9,1... | collective-permute-start | bytes 786440 | tf_op jit(solution)/shard_map/ppermute | solution.py:25
  5.4 12.8 %collective-permute-start.5 = (bf16[512,256]{1,0:T(8,128)(2,1)S(1)}, bf16[512,256]{1,0:T(8,128)(2,1)S(1)}, u32[]{:S(2)}, u32[]{:S(2)}) collective-permute-start(bf16[512,256]{1,0:T(8,128)(2,1)S(1)} %get-tuple-element.32.refs_0_), channel_id=1, source_target_pairs={{0,2},{2,0},{1,3},{3,1},{4,6},{6,4},{5,7},{7,5},{8,10},{10,8},{9,1... | collective-permute-start | bytes 786440 | tf_op jit(solution)/shard_map/ppermute | solution.py:25
  5.5 33.6 %collective-permute-start.9 = (bf16[768,256]{1,0:T(8,128)(2,1)S(1)}, bf16[768,256]{1,0:T(8,128)(2,1)S(1)}, u32[]{:S(2)}, u32[]{:S(2)}) collective-permute-start(bf16[768,256]{1,0:T(8,128)(2,1)S(1)} %get-tuple-element.34), channel_id=1, source_target_pairs={{0,2},{2,0},{1,3},{3,1},{4,6},{6,4},{5,7},{7,5},{8,10},{10,8},{9,1... | collective-permute-start | bytes 1179656 | tf_op jit(solution)/shard_map/ppermute | solution.py:25
  7.4 24.8 %collective-permute-start.11 = (bf16[512,256]{1,0:T(8,128)(2,1)S(1)}, bf16[512,256]{1,0:T(8,128)(2,1)S(1)}, u32[]{:S(2)}, u32[]{:S(2)}) collective-permute-start(bf16[512,256]{1,0:T(8,128)(2,1)S(1)} %get-tuple-element.35), channel_id=1, source_target_pairs={{0,2},{2,0},{1,3},{3,1},{4,6},{6,4},{5,7},{7,5},{8,10},{10,8},{9,1... | collective-permute-start | bytes 786440 | tf_op jit(solution)/shard_map/ppermute | solution.py:25
  12.6 25.3 %collective-permute-start = (bf16[512,256]{1,0:T(8,128)(2,1)S(1)}, bf16[512,256]{1,0:T(8,128)(2,1)S(1)}, u32[]{:S(2)}, u32[]{:S(2)}) collective-permute-start(bf16[512,256]{1,0:T(8,128)(2,1)S(1)} %get-tuple-element.30), channel_id=1, source_target_pairs={{0,2},{2,0},{1,3},{3,1},{4,6},{6,4},{5,7},{7,5},{8,10},{10,8},{9,1... | collective-permute-start | bytes 786440 | tf_op jit(solution)/shard_map/ppermute | solution.py:25
  18.2 27.9 %collective-permute-start.7 = (bf16[768,256]{1,0:T(8,128)(2,1)S(1)}, bf16[768,256]{1,0:T(8,128)(2,1)S(1)}, u32[]{:S(2)}, u32[]{:S(2)}) collective-permute-start(bf16[768,256]{1,0:T(8,128)(2,1)S(1)} %get-tuple-element.33), channel_id=1, source_target_pairs={{0,2},{2,0},{1,3},{3,1},{4,6},{6,4},{5,7},{7,5},{8,10},{10,8},{9,1... | collective-permute-start | bytes 1179656 | tf_op jit(solution)/shard_map/ppermute | solution.py:25
  20.3 33.0 %copy-start.1 = (f32[32,9]{0,1:T(8,128)S(1)}, f32[32,9]{0,1:T(8,128)}, u32[]{:S(2)}) copy-start(f32[32,9]{0,1:T(8,128)} %param.3) | copy-start | bytes 3460
  32.2 17.1 %collective-permute-start.15 = (bf16[1024,256]{1,0:T(8,128)(2,1)S(1)}, bf16[1024,256]{1,0:T(8,128)(2,1)S(1)}, u32[]{:S(2)}, u32[]{:S(2)}) collective-permute-start(bf16[1024,256]{1,0:T(8,128)(2,1)S(1)} %shard_map.35), channel_id=1, source_target_pairs={{0,4},{4,8},{8,12},{1,5},{5,9},{9,13},{2,6},{6,10},{10,14},{3,7},{... | collective-permute-start | bytes 1572872 | tf_op jit(solution)/shard_map/ppermute | solution.py:335
  37.8 15.4 %collective-permute-start.17 = (bf16[1024,256]{1,0:T(8,128)(2,1)S(1)}, bf16[1024,256]{1,0:T(8,128)(2,1)S(1)}, u32[]{:S(2)}, u32[]{:S(2)}) collective-permute-start(bf16[1024,256]{1,0:T(8,128)(2,1)S(1)} %shard_map.36), channel_id=1, source_target_pairs={{4,0},{8,4},{12,8},{5,1},{9,5},{13,9},{6,2},{10,6},{14,10},{7,3},{... | collective-permute-start | bytes 1572872 | tf_op jit(solution)/shard_map/ppermute | solution.py:333
  39.1 6.9 %collective-permute-start.14 = (bf16[512,256]{1,0:T(8,128)(2,1)S(1)}, bf16[512,256]{1,0:T(8,128)(2,1)S(1)}, u32[]{:S(2)}, u32[]{:S(2)}) collective-permute-start(bf16[512,256]{1,0:T(8,128)(2,1)S(1)} %collective-permute-done.13.refs_2_.refs_1_.refs_4_), channel_id=1, source_target_pairs={{0,1},{1,0},{2,3},{3,2},{4,5},{5,4},{6,7},{7,6},{8,9},{9,8},{10,11... | collective-permute-start | bytes 786440 | tf_op jit(solution)/shard_map/ppermute | solution.py:25
  46.1 1.5 %collective-permute-start.12 = (bf16[512,256]{1,0:T(8,128)(2,1)S(1)}, bf16[512,256]{1,0:T(8,128)(2,1)S(1)}, u32[]{:S(2)}, u32[]{:S(2)}) collective-permute-start(bf16[512,256]{1,0:T(8,128)(2,1)S(1)} %collective-permute-done.11.refs_5_.refs_2_), channel_id=1, source_target_pairs={{0,1},{1,0},{2,3},{3,2},{4,5},{5,4},{6,7},{7,6},{8,9},{9,8},{10,11... | collective-permute-start | bytes 786440 | tf_op jit(solution)/shard_map/ppermute | solution.py:25
  46.1 10.1 %collective-permute-start.10 = (bf16[768,256]{1,0:T(8,128)(2,1)S(1)}, bf16[768,256]{1,0:T(8,128)(2,1)S(1)}, u32[]{:S(2)}, u32[]{:S(2)}) collective-permute-start(bf16[768,256]{1,0:T(8,128)(2,1)S(1)} %collective-permute-done.9.refs_5_.refs_2_), channel_id=1, source_target_pairs={{0,1},{1,0},{2,3},{3,2},{4,5},{5,4},{6,7},{7,6},{8,9},{9,8},{10,11... | collective-permute-start | bytes 1179656 | tf_op jit(solution)/shard_map/ppermute | solution.py:25
  46.6 13.2 %collective-permute-start.8 = (bf16[768,256]{1,0:T(8,128)(2,1)S(1)}, bf16[768,256]{1,0:T(8,128)(2,1)S(1)}, u32[]{:S(2)}, u32[]{:S(2)}) collective-permute-start(bf16[768,256]{1,0:T(8,128)(2,1)S(1)} %collective-permute-done.7.refs_5_.refs_2_), channel_id=1, source_target_pairs={{0,1},{1,0},{2,3},{3,2},{4,5},{5,4},{6,7},{7,6},{8,9},{9,8},{10,11... | collective-permute-start | bytes 1179656 | tf_op jit(solution)/shard_map/ppermute | solution.py:25
  47.6 12.1 %collective-permute-start.3 = (bf16[512,256]{1,0:T(8,128)(2,1)S(1)}, bf16[512,256]{1,0:T(8,128)(2,1)S(1)}, u32[]{:S(2)}, u32[]{:S(2)}) collective-permute-start(bf16[512,256]{1,0:T(8,128)(2,1)S(1)} %get-tuple-element.31), channel_id=1, source_target_pairs={{0,2},{2,0},{1,3},{3,1},{4,6},{6,4},{5,7},{7,5},{8,10},{10,8},{9,1... | collective-permute-start | bytes 786440 | tf_op jit(solution)/shard_map/ppermute | solution.py:25
  49.4 16.1 %collective-permute-start.16 = (bf16[1024,256]{1,0:T(8,128)(2,1)S(1)}, bf16[1024,256]{1,0:T(8,128)(2,1)S(1)}, u32[]{:S(2)}, u32[]{:S(2)}) collective-permute-start(bf16[1024,256]{1,0:T(8,128)(2,1)S(1)} %collective-permute-done.15.refs_1_), channel_id=1, source_target_pairs={{0,1},{1,0},{2,3},{3,2},{4,5},{5,4},{6,7},{7,6},{8,9},{9,8},{10,11... | collective-permute-start | bytes 1572872 | tf_op jit(solution)/shard_map/ppermute | solution.py:25
  53.3 12.2 %collective-permute-start.18 = (bf16[1024,256]{1,0:T(8,128)(2,1)S(1)}, bf16[1024,256]{1,0:T(8,128)(2,1)S(1)}, u32[]{:S(2)}, u32[]{:S(2)}) collective-permute-start(bf16[1024,256]{1,0:T(8,128)(2,1)S(1)} %collective-permute-done.17.refs_9_), channel_id=1, source_target_pairs={{0,1},{1,0},{2,3},{3,2},{4,5},{5,4},{6,7},{7,6},{8,9},{9,8},{10,11... | collective-permute-start | bytes 1572872 | tf_op jit(solution)/shard_map/ppermute | solution.py:25
  56.2 6.9 %collective-permute-start.2 = (bf16[512,256]{1,0:T(8,128)(2,1)S(1)}, bf16[512,256]{1,0:T(8,128)(2,1)S(1)}, u32[]{:S(2)}, u32[]{:S(2)}) collective-permute-start(bf16[512,256]{1,0:T(8,128)(2,1)S(1)} %collective-permute-done.refs_5_.refs_2_), channel_id=1, source_target_pairs={{0,1},{1,0},{2,3},{3,2},{4,5},{5,4},{6,7},{7,6},{8,9},{9,8},{10,11... | collective-permute-start | bytes 786440 | tf_op jit(solution)/shard_map/ppermute | solution.py:25
  59.7 5.7 %collective-permute-start.6 = (bf16[512,256]{1,0:T(8,128)(2,1)S(1)}, bf16[512,256]{1,0:T(8,128)(2,1)S(1)}, u32[]{:S(2)}, u32[]{:S(2)}) collective-permute-start(bf16[512,256]{1,0:T(8,128)(2,1)S(1)} %collective-permute-done.5.refs_1_.refs_7_), channel_id=1, source_target_pairs={{0,1},{1,0},{2,3},{3,2},{4,5},{5,4},{6,7},{7,6},{8,9},{9,8},{10,11... | collective-permute-start | bytes 786440 | tf_op jit(solution)/shard_map/ppermute | solution.py:25
  59.8 9.1 %collective-permute-start.4 = (bf16[512,256]{1,0:T(8,128)(2,1)S(1)}, bf16[512,256]{1,0:T(8,128)(2,1)S(1)}, u32[]{:S(2)}, u32[]{:S(2)}) collective-permute-start(bf16[512,256]{1,0:T(8,128)(2,1)S(1)} %collective-permute-done.3.refs_5_), channel_id=1, source_target_pairs={{0,1},{1,0},{2,3},{3,2},{4,5},{5,4},{6,7},{7,6},{8,9},{9,8},{10,11... | collective-permute-start | bytes 786440 | tf_op jit(solution)/shard_map/ppermute | solution.py:25

commit v8 on v7

--- a/solution.py
+++ b/solution.py
@@ -31,6 +31,72 @@
     return pl.ds(start * ROWS, count * ROWS)
 
 
+def gram_rows(held, j, near, begin=None):
+    left = jnp.concatenate([held(i) for i in near], axis=0)
+    half = left.shape[0] // 2
+    halves = []
+    for n in range(2):
+        part = lax.dot_general(
+            left[n * half : (n + 1) * half],
+            held(j),
+            (((1,), (1,)), ((), ())),
+            preferred_element_type=jnp.float32,
+        )
+        halves.append(part if begin is None else part + begin[pl.ds(n * half, half), :])
+    return jnp.concatenate(halves, axis=0)
+
+
+def partial_kernel(parts, plan, steps, arrays, *refs):
+    sources, begins, outs = refs[:arrays], refs[arrays : -len(steps)], refs[-len(steps) :]
+
+    def held(pair):
+        pieces = [plan[pair, part] for part in parts]
+        return jnp.concatenate([sources[n][tile_rows(start), :] for n, start in pieces], axis=1)
+
+    for k, (j, first, count) in enumerate(steps):
+        near = list(range(first, first + count))
+        outs[k][...] = gram_rows(held, j, near, begins[k] if begins else None)
+
+
+def planned(pieces, parts, pairs):
+    arrays, plan = [], {}
+    for pair in sorted(pairs):
+        for part in parts:
+            array, start = pieces[part][pair]
+            known = [n for n, other in enumerate(arrays) if other is array]
+            if not known:
+                arrays.append(array)
+                known = [len(arrays) - 1]
+            plan[pair, part] = (known[0], start)
+    return arrays, plan
+
+
+def touched_by(steps):
+    pairs = set()
+    for j, first, count in steps:
+        pairs |= {j} | set(range(first, first + count))
+    return pairs
+
+
+def partial_grams(pieces, parts, steps, begins):
+    arrays, plan = planned(pieces, parts, touched_by(steps))
+    inside = pl.BlockSpec(memory_space=pltpu.VMEM)
+    products = sum(n for _, _, n in steps)
+    members = arrays[0].shape[1]
+    return pl.pallas_call(
+        functools.partial(partial_kernel, parts, plan, steps, len(arrays)),
+        out_shape=[jax.ShapeDtypeStruct((n * ROWS, ROWS), jnp.float32) for _, _, n in steps],
+        in_specs=[inside] * (len(arrays) + len(begins)),
+        out_specs=[inside] * len(steps),
+        compiler_params=pltpu.CompilerParams(vmem_limit_bytes=VMEM_LIMIT),
+        cost_estimate=pl.CostEstimate(
+            flops=2 * products * ROWS * ROWS * members * len(parts),
+            bytes_accessed=4 * products * ROWS * ROWS,
+            transcendentals=0,
+        ),
+    )(*arrays, *begins)
+
+
 def update_kernel(job, *refs):
     parts = job["parts"]
     plan, steps, owned = job["plan"], job["steps"], job["owned"]
@@ -40,7 +106,8 @@
     taper = refs[0]
     sources = refs[1 : 1 + arrays]
     inputs = dict(zip(acc_in, refs[1 + arrays : 1 + arrays + len(acc_in)]))
-    earlier = refs[1 + arrays + len(acc_in) : job["operands"]]
+    begins = refs[1 + arrays + len(acc_in) : job["earlier"]]
+    earlier = refs[job["earlier"] : job["operands"]]
     outs = refs[job["operands"] :]
     if job["last"]:
         out, acc, obuf, out_sem = outs[0], *outs[-3:]
@@ -66,7 +133,7 @@
         return sources[array][tile_rows(start), :]
 
     def held(pair):
-        return jnp.concatenate([piece(pair, part) for part in range(parts)], axis=1)
+        return jnp.concatenate([piece(pair, part) for part in parts], axis=1)
 
     def own(pair):
         return piece(pair, 0)
@@ -95,22 +162,9 @@
             rows.append(jnp.concatenate(row, axis=1))
         return jnp.concatenate(rows, axis=0)
 
-    for j, first, count in steps:
+    for k, (j, first, count) in enumerate(steps):
         near = list(range(first, first + count))
-        left = jnp.concatenate([held(i) for i in near], axis=0)
-        half = count * ROWS // 2
-        gram = jnp.concatenate(
-            [
-                lax.dot_general(
-                    part,
-                    held(j),
-                    (((1,), (1,)), ((), ())),
-                    preferred_element_type=jnp.float32,
-                )
-                for part in (left[:half], left[half:])
-            ],
-            axis=0,
-        )
+        gram = gram_rows(held, j, near, begins[k] if begins else None)
         tiles = {i: gram[n * ROWS : (n + 1) * ROWS] for n, i in enumerate(near)}
         mine = [i for i in near if i in owned]
         if mine:
@@ -223,12 +277,11 @@
     )(*arrays)
 
 
-def run_steps(taper, pieces, steps, owned, state, finished, stored, rows, members, last):
-    parts = len(pieces)
-    needed = set()
-    for j, first, count in steps:
-        needed |= {j} | set(range(first, first + count))
-    needed |= set(finished)
+def run_steps(
+    taper, pieces, steps, owned, state, finished, stored, rows, members, last, parts=None, begins=()
+):
+    parts = tuple(range(len(pieces))) if parts is None else parts
+    needed = touched_by(steps) | set(finished)
     touched = set()
     for j, first, count in steps:
         near = set(range(first, first + count))
@@ -237,25 +290,19 @@
             touched.add(j)
     acc_in = [pair for pair in sorted(touched | set(finished)) if pair in state]
     acc_out = sorted(touched - set(finished))
-    arrays, plan = [], {}
-    for pair in sorted(needed):
-        for part in range(parts):
-            array, start = pieces[part][pair]
-            known = [n for n, other in enumerate(arrays) if other is array]
-            if not known:
-                arrays.append(array)
-                known = [len(arrays) - 1]
-            plan[pair, part] = (known[0], start)
+    arrays, plan = planned(pieces, sorted(set(parts) | {0}), needed)
     writes = []
     if last:
         for array, (pairs, _) in enumerate(stored):
             writes += [(array, n, pair) for n, pair in enumerate(pairs)]
-    operands = [taper.T] + arrays + [state[pair] for pair in acc_in]
+    operands = [taper.T] + arrays + [state[pair] for pair in acc_in] + list(begins)
+    earlier = len(operands)
     if last:
         operands += [block for _, block in stored]
     job = dict(
         parts=parts, plan=plan, steps=steps, owned=owned, acc_in=acc_in, acc_out=acc_out,
         finished=finished, arrays=len(arrays), writes=writes, operands=len(operands),
+        earlier=earlier,
         last=last,
     )
     inside = pl.BlockSpec(memory_space=pltpu.VMEM)
@@ -283,7 +330,7 @@
         scratch_shapes=scratch,
         compiler_params=pltpu.CompilerParams(vmem_limit_bytes=VMEM_LIMIT),
         cost_estimate=pl.CostEstimate(
-            flops=2 * products * ROWS * ROWS * members * (parts + 2),
+            flops=2 * products * ROWS * ROWS * members * (len(parts) + 2),
             bytes_accessed=2 * ROWS * members * (len(plan) + 3 * len(finished)),
             transcendentals=0,
         ),
@@ -319,7 +366,7 @@
     chunks = chunk_bounds(pairs)
 
     top, bottom, start = cut_rows(
-        anomalies, [(0, NEAR), (pairs - NEAR, pairs), chunks[0]], 24 * 2**20
+        anomalies, [(0, NEAR), (pairs - NEAR, pairs), chunks[0]], 52 * 2**20
     )
     *cuts, inside = cut_rows(anomalies, chunks[1:] + [(0, pairs)])
     cuts = [start] + cuts
@@ -390,9 +437,16 @@
             if i not in done and all(k in there for k in range(i - NEAR, i + NEAR + 1))
         ]
         done |= set(ready)
+        end = n == len(batches) - 1
+        parts, begins = None, ()
+        if end and len(pieces) == 2 * len(held):
+            near_parts, half = (0, len(held)), tuple(range(1, len(held)))
+            parts = tuple(len(held) + part for part in half)
+            begins = partial_grams(pieces, near_parts, steps, ())
+            begins = partial_grams(pieces, half, steps, begins)
         result, state = run_steps(
             taper, pieces, steps, owned, state, ready, stored, rows, members,
-            n == len(batches) - 1,
+            end, parts, begins,
         )
     return result
 

time: 73.1 us -> 82.6 us (1.13)
  waiting for transfers between devices: 33.7 us -> 42.9 us
  Pallas kernels: 19.4 us -> 20.6 us
  starting transfers between devices: 18.1 us -> 17 us
    ppermute x17, waiting for transfers between devices: 29.8 us -> 38 us  [shifted(): lax.ppermute(value, axis, [(i, (i + s) % count) for i in range(count)])]
    pallas_call x0 -> x2, Pallas kernels: none -> 1.5 us  [partial_grams(): pl.pallas_call(functools.partial(partial_kernel, parts, plan, steps, len(...]
    pallas_call x6, Pallas kernels: 18.4 us -> 17.1 us  [run_steps(): pl.pallas_call(functools.partial(update_kernel, job), out_shape=shapes, i...]
    pallas_call x2, Pallas kernels: 0.68 us -> 1.73 us  [cut_rows(): pl.pallas_call(functools.partial(cut_kernel, tuple((first * ROWS for firs...]
  transfers between devices with their start and end apart: 19 -> 19, of which waited for: 7 -> 7; matrix products, arithmetic and copies ran while one was open for 0% -> 0% of each run, Pallas kernels for 20% -> 21%
where the time goes in v8:
time: 82.6 us; the launch traced here: 82.4 us
  waiting for transfers between devices  42.9 us (52%)
  Pallas kernels  20.6 us (25%)
  starting transfers between devices  17 us (21%)
  local copies, waits for them, and re-layouts  1.59 us (2%)
    ppermute x17, waiting for transfers between devices, shifted(): lax.ppermute(value, axis, [(i, (i + s) % count) for i in range(count)])  38 us
    pallas_call x6, Pallas kernels, run_steps(): pl.pallas_call(functools.partial(update_kernel, job), out_shape=shapes, i...  17.1 us
    ppermute x17, starting transfers between devices, shifted(): lax.ppermute(value, axis, [(i, (i + s) % count) for i in range(count)])  12 us
    ppermute x1, waiting for transfers between devices, per_device(): after = lax.ppermute(heads, 'region', up)  4.15 us
    ppermute x1, starting transfers between devices, per_device(): before = lax.ppermute(tails, 'region', down)  3.75 us
    pallas_call x2, Pallas kernels, cut_rows(): pl.pallas_call(functools.partial(cut_kernel, tuple((first * ROWS for firs...  1.73 us
  transfers between devices with their start and end apart: 19, of which 7 were waited for; matrix products, arithmetic and copies ran while one was open for 0% of the time, Pallas kernels for 21%

profile of v8, /device:TPU:0, one launch (start us, length us, event | category | flops | bytes accessed | tf_op | source)
XLA Modules:
  0.0 82.4 jit_solution(18298695904406782958)
XLA Ops:
  0.0 1.6 %copy-done = bf16[4096,256]{1,0:T(8,128)(2,1)S(1)} copy-done((bf16[4096,256]{1,0:T(8,128)(2,1)S(1)}, bf16[4096,256]{1,0:T(8,128)(2,1)}, u32[]{:S(2)}) %copy-start) | copy-done | bytes 2097176
  1.6 0.6 shard_map.28
  2.2 0.6 collective-permute-start.7
  2.8 1.1 %shard_map.29 = (bf16[512,256]{1,0:T(8,128)(2,1)S(1)}, bf16[512,256]{1,0:T(8,128)(2,1)S(1)}, bf16[512,256]{1,0:T(8,128)(2,1)S(1)}) custom-call(bf16[4096,256]{1,0:T(8,128)(2,1)} %source.3), custom_call_target="tpu_custom_call" | custom-call | bytes 1572864 | tf_op jit(solution)/shard_map/pallas_call | solution.py:224
  3.9 2.6 %collective-permute-start.4 = (bf16[512,256]{1,0:T(8,128)(2,1)S(1)}, bf16[512,256]{1,0:T(8,128)(2,1)S(1)}, u32[]{:S(2)}, u32[]{:S(2)}) collective-permute-start(bf16[512,256]{1,0:T(8,128)(2,1)S(1)} %get-tuple-element.38.refs_0_), channel_id=1, source_target_pairs={{0,2},{2,0},{1,3},{3,1},{4,6},{6,4},{5,7},{7,5},{8,10},{10,8},{9,1... | collective-permute-start | bytes 786440 | tf_op jit(solution)/shard_map/ppermute | solution.py:25
  6.5 0.1 collective-permute-start.11
  6.5 1.9 %collective-permute-start.6 = (bf16[768,256]{1,0:T(8,128)(2,1)S(1)}, bf16[768,256]{1,0:T(8,128)(2,1)S(1)}, u32[]{:S(2)}, u32[]{:S(2)}) collective-permute-start(bf16[768,256]{1,0:T(8,128)(2,1)S(1)} %get-tuple-element.39), channel_id=1, source_target_pairs={{0,2},{2,0},{1,3},{3,1},{4,6},{6,4},{5,7},{7,5},{8,10},{10,8},{9,1... | collective-permute-start | bytes 1179656 | tf_op jit(solution)/shard_map/ppermute | solution.py:25
  8.5 0.1 collective-permute-start.13
  8.6 5.1 %collective-permute-done.4.refs_1_.refs_7_.refs_2_ = bf16[512,256]{1,0:T(8,128)(2,1)S(1)} collective-permute-done((bf16[512,256]{1,0:T(8,128)(2,1)S(1)}, bf16[512,256]{1,0:T(8,128)(2,1)S(1)}, u32[]{:S(2)}, u32[]{:S(2)}) %collective-permute-start.4) | collective-permute-done | bytes 262176 | tf_op jit(solution)/shard_map/ppermute | solution.py:25
  13.6 2.0 %collective-permute-start.9 = (bf16[768,256]{1,0:T(8,128)(2,1)S(1)}, bf16[768,256]{1,0:T(8,128)(2,1)S(1)}, u32[]{:S(2)}, u32[]{:S(2)}) collective-permute-start(bf16[768,256]{1,0:T(8,128)(2,1)S(1)} %get-tuple-element.40), channel_id=1, source_target_pairs={{0,2},{2,0},{1,3},{3,1},{4,6},{6,4},{5,7},{7,5},{8,10},{10,8},{9,1... | collective-permute-start | bytes 1179656 | tf_op jit(solution)/shard_map/ppermute | solution.py:25
  15.6 3.6 %collective-permute-done.11.refs_5_.refs_2_ = bf16[512,256]{1,0:T(8,128)(2,1)S(1)} collective-permute-done((bf16[512,256]{1,0:T(8,128)(2,1)S(1)}, bf16[512,256]{1,0:T(8,128)(2,1)S(1)}, u32[]{:S(2)}, u32[]{:S(2)}) %collective-permute-start.11) | collective-permute-done | bytes 262176 | tf_op jit(solution)/shard_map/ppermute | solution.py:25
  19.2 2.0 %collective-permute-start = (bf16[512,256]{1,0:T(8,128)(2,1)S(1)}, bf16[512,256]{1,0:T(8,128)(2,1)S(1)}, u32[]{:S(2)}, u32[]{:S(2)}) collective-permute-start(bf16[512,256]{1,0:T(8,128)(2,1)S(1)} %get-tuple-element.36), channel_id=1, source_target_pairs={{0,2},{2,0},{1,3},{3,1},{4,6},{6,4},{5,7},{7,5},{8,10},{10,8},{9,1... | collective-permute-start | bytes 786440 | tf_op jit(solution)/shard_map/ppermute | solution.py:25
  21.3 12.0 %collective-permute-done.13.refs_2_.refs_1_.refs_4_ = bf16[512,256]{1,0:T(8,128)(2,1)S(1)} collective-permute-done((bf16[512,256]{1,0:T(8,128)(2,1)S(1)}, bf16[512,256]{1,0:T(8,128)(2,1)S(1)}, u32[]{:S(2)}, u32[]{:S(2)}) %collective-permute-start.13) | collective-permute-done | bytes 262176 | tf_op jit(solution)/shard_map/ppermute | solution.py:25
  33.4 13.7 %collective-permute-done.refs_5_.refs_0_ = bf16[512,256]{1,0:T(8,128)(2,1)S(1)} collective-permute-done((bf16[512,256]{1,0:T(8,128)(2,1)S(1)}, bf16[512,256]{1,0:T(8,128)(2,1)S(1)}, u32[]{:S(2)}, u32[]{:S(2)}) %collective-permute-start) | collective-permute-done | bytes 262176 | tf_op jit(solution)/shard_map/ppermute | solution.py:25
  47.1 3.8 %collective-permute-start.15 = (bf16[1024,256]{1,0:T(8,128)(2,1)S(1)}, bf16[1024,256]{1,0:T(8,128)(2,1)S(1)}, u32[]{:S(2)}, u32[]{:S(2)}) collective-permute-start(bf16[1024,256]{1,0:T(8,128)(2,1)S(1)} %shard_map.35), channel_id=1, source_target_pairs={{0,4},{4,8},{8,12},{1,5},{5,9},{9,13},{2,6},{6,10},{10,14},{3,7},{... | collective-permute-start | bytes 1572872 | tf_op jit(solution)/shard_map/ppermute | solution.py:382
  50.9 1.3 %collective-permute-start.17 = (bf16[1024,256]{1,0:T(8,128)(2,1)S(1)}, bf16[1024,256]{1,0:T(8,128)(2,1)S(1)}, u32[]{:S(2)}, u32[]{:S(2)}) collective-permute-start(bf16[1024,256]{1,0:T(8,128)(2,1)S(1)} %shard_map.36), channel_id=1, source_target_pairs={{4,0},{8,4},{12,8},{5,1},{9,5},{13,9},{6,2},{10,6},{14,10},{7,3},{... | collective-permute-start | bytes 1572872 | tf_op jit(solution)/shard_map/ppermute | solution.py:380
  52.3 0.5 collective-permute-start.10
  52.8 1.5 %collective-permute-start.2 = (bf16[512,256]{1,0:T(8,128)(2,1)S(1)}, bf16[512,256]{1,0:T(8,128)(2,1)S(1)}, u32[]{:S(2)}, u32[]{:S(2)}) collective-permute-start(bf16[512,256]{1,0:T(8,128)(2,1)S(1)} %get-tuple-element.37), channel_id=1, source_target_pairs={{0,2},{2,0},{1,3},{3,1},{4,6},{6,4},{5,7},{7,5},{8,10},{10,8},{9,1... | collective-permute-start | bytes 786440 | tf_op jit(solution)/shard_map/ppermute | solution.py:25
  54.3 0.1 shard_map.30.refs_3_.refs_5_.refs_1_
  54.5 2.9 %shard_map.31 = (f32[256,256]{1,0:T(8,128)S(1)}, f32[256,256]{1,0:T(8,128)S(1)}, f32[256,256]{1,0:T(8,128)S(1)}, f32[256,256]{1,0:T(8,128)S(1)}) custom-call(f32[9,32]{1,0:T(8,128)S(1)} %bitcast.1, bf16[4096,256]{1,0:T(8,128)(2,1)S(1)} %get-tuple-element.35.refs_1_.refs_3_.refs_0_, bf16[512,256]{1,0:T(8,128)(2,1)S(1)} %collective-permute-done.13.refs_2_.refs_1_.refs_4_, ...), custom_call_target="tpu_custom_call" | custom-call | flops 1811939328 | bytes 2097152 | tf_op jit(solution)/shard_map/pallas_call | solution.py:325
  57.5 3.6 %collective-permute-done.2.refs_1_ = bf16[512,256]{1,0:T(8,128)(2,1)S(1)} collective-permute-done((bf16[512,256]{1,0:T(8,128)(2,1)S(1)}, bf16[512,256]{1,0:T(8,128)(2,1)S(1)}, u32[]{:S(2)}, u32[]{:S(2)}) %collective-permute-start.2) | collective-permute-done | bytes 262176 | tf_op jit(solution)/shard_map/ppermute | solution.py:25
  61.1 0.7 collective-permute-done.15.refs_1_
  61.8 4.2 %collective-permute-done.17.refs_9_ = bf16[1024,256]{1,0:T(8,128)(2,1)S(1)} collective-permute-done((bf16[1024,256]{1,0:T(8,128)(2,1)S(1)}, bf16[1024,256]{1,0:T(8,128)(2,1)S(1)}, u32[]{:S(2)}, u32[]{:S(2)}) %collective-permute-start.17) | collective-permute-done | bytes 524320 | tf_op jit(solution)/shard_map/ppermute | solution.py:380
  66.0 0.5 collective-permute-start.18
  66.5 2.9 %shard_map.32 = (bf16[3,256,256]{2,1,0:T(8,128)(2,1)S(1)}, f32[256,256]{1,0:T(8,128)S(1)}, f32[256,256]{1,0:T(8,128)S(1)}) custom-call(f32[9,32]{1,0:T(8,128)S(1)} %bitcast.2, bf16[4096,256]{1,0:T(8,128)(2,1)S(1)} %get-tuple-element.35.refs_1_.refs_3_.refs_0_, bf16[512,256]{1,0:T(8,128)(2,1)S(1)} %collective-permute-done.11.refs_5_.refs_2_, ...), custom_call_target="tpu_custom_call" | custom-call | flops 1811939328 | bytes 3801088 | tf_op jit(solution)/shard_map/pallas_call | solution.py:325
  69.4 0.9 %shard_map.38 = (f32[768,256]{1,0:T(8,128)S(1)}, f32[256,256]{1,0:T(8,128)S(1)}, f32[1280,256]{1,0:T(8,128)S(1)}) custom-call(bf16[4096,256]{1,0:T(8,128)(2,1)S(1)} %get-tuple-element.35.refs_1_.refs_3_.refs_0_, bf16[4096,256]{1,0:T(8,128)(2,1)S(1)} %shard_map.30.refs_3_.refs_5_.refs_1_), custom_call_target="tpu_custom_call" | custom-call | flops 603979776 | bytes 2359296 | tf_op jit(solution)/shard_map/pallas_call | solution.py:86
  70.3 0.6 shard_map.39
  70.9 0.1 collective-permute-start.5
  71.0 2.9 %shard_map.33 = (bf16[3,256,256]{2,1,0:T(8,128)(2,1)S(1)}, f32[256,256]{1,0:T(8,128)S(1)}, f32[256,256]{1,0:T(8,128)S(1)}) custom-call(f32[9,32]{1,0:T(8,128)S(1)} %bitcast.3, bf16[4096,256]{1,0:T(8,128)(2,1)S(1)} %get-tuple-element.35.refs_1_.refs_3_.refs_0_, bf16[768,256]{1,0:T(8,128)(2,1)S(1)} %collective-permute-done.9.refs_5_.refs_2_, ...), custom_call_target="tpu_custom_call" | custom-call | flops 1811939328 | bytes 3801088 | tf_op jit(solution)/shard_map/pallas_call | solution.py:325
  73.9 2.2 %shard_map.34 = (bf16[2,256,256]{2,1,0:T(8,128)(2,1)S(1)}, f32[256,256]{1,0:T(8,128)S(1)}, f32[256,256]{1,0:T(8,128)S(1)}) custom-call(f32[9,32]{1,0:T(8,128)S(1)} %bitcast.4, bf16[4096,256]{1,0:T(8,128)(2,1)S(1)} %get-tuple-element.35.refs_1_.refs_3_.refs_0_, bf16[768,256]{1,0:T(8,128)(2,1)S(1)} %collective-permute-done.6.refs_5_.refs_2_, ...), custom_call_target="tpu_custom_call" | custom-call | flops 1207959552 | bytes 2883584 | tf_op jit(solution)/shard_map/pallas_call | solution.py:325
  76.2 3.4 %shard_map.37 = (bf16[2,256,256]{2,1,0:T(8,128)(2,1)S(1)}, f32[256,256]{1,0:T(8,128)S(1)}, f32[256,256]{1,0:T(8,128)S(1)}) custom-call(f32[9,32]{1,0:T(8,128)S(1)} %bitcast.5, bf16[1024,256]{1,0:T(8,128)(2,1)S(1)} %collective-permute-done.15.refs_1_, bf16[1024,256]{1,0:T(8,128)(2,1)S(1)} %collective-permute-done.16.refs_2_, ...), custom_call_target="tpu_custom_call" | custom-call | flops 1811939328 | bytes 4980736 | tf_op jit(solution)/shard_map/pallas_call | solution.py:325
  79.6 2.8 %shard_map.40 = bf16[4096,256]{1,0:T(8,128)(2,1)} custom-call(f32[9,32]{1,0:T(8,128)S(1)} %bitcast.6, bf16[4096,256]{1,0:T(8,128)(2,1)S(1)} %get-tuple-element.35.refs_1_.refs_3_.refs_0_, bf16[512,256]{1,0:T(8,128)(2,1)S(1)} %collective-permute-done.1.refs_6_.refs_2_, bf16[512,256]{1,0:T(8,128)(2,1)S(1)} %collective-permute-done.3.refs_3_, ...), custom_call_target="tpu_custom_call" | custom-call | flops 905969664 | bytes 3932160 | tf_op jit(solution)/shard_map/pallas_call | solution.py:325
  (23 shorter events, 0.3 us)
Async XLA Ops:
  0.0 1.6 %copy-start = (bf16[4096,256]{1,0:T(8,128)(2,1)S(1)}, bf16[4096,256]{1,0:T(8,128)(2,1)}, u32[]{:S(2)}) copy-start(bf16[4096,256]{1,0:T(8,128)(2,1)} %source.3) | copy-start | bytes 6291460
  2.2 50.6 %collective-permute-start.7 = (bf16[4096,256]{1,0:T(8,128)(2,1)S(1)}, bf16[4096,256]{1,0:T(8,128)(2,1)S(1)}, u32[]{:S(2)}, u32[]{:S(2)}) collective-permute-start(bf16[4096,256]{1,0:T(8,128)(2,1)S(1)} %get-tuple-element.35.refs_1_.refs_3_.refs_0_), channel_id=1, source_target_pairs={{0,1},{1,0},{2,3},{3,2},{4,5},{5,4},{6,7},{7,6},{8,9},{9,8},{10,11... | collective-permute-start | bytes 6291464 | tf_op jit(solution)/shard_map/ppermute | solution.py:25
  3.9 9.7 %collective-permute-start.4 = (bf16[512,256]{1,0:T(8,128)(2,1)S(1)}, bf16[512,256]{1,0:T(8,128)(2,1)S(1)}, u32[]{:S(2)}, u32[]{:S(2)}) collective-permute-start(bf16[512,256]{1,0:T(8,128)(2,1)S(1)} %get-tuple-element.38.refs_0_), channel_id=1, source_target_pairs={{0,2},{2,0},{1,3},{3,1},{4,6},{6,4},{5,7},{7,5},{8,10},{10,8},{9,1... | collective-permute-start | bytes 786440 | tf_op jit(solution)/shard_map/ppermute | solution.py:25
  6.5 12.8 %collective-permute-start.11 = (bf16[512,256]{1,0:T(8,128)(2,1)S(1)}, bf16[512,256]{1,0:T(8,128)(2,1)S(1)}, u32[]{:S(2)}, u32[]{:S(2)}) collective-permute-start(bf16[512,256]{1,0:T(8,128)(2,1)S(1)} %get-tuple-element.41), channel_id=1, source_target_pairs={{0,2},{2,0},{1,3},{3,1},{4,6},{6,4},{5,7},{7,5},{8,10},{10,8},{9,1... | collective-permute-start | bytes 786440 | tf_op jit(solution)/shard_map/ppermute | solution.py:25
  6.5 44.4 %collective-permute-start.6 = (bf16[768,256]{1,0:T(8,128)(2,1)S(1)}, bf16[768,256]{1,0:T(8,128)(2,1)S(1)}, u32[]{:S(2)}, u32[]{:S(2)}) collective-permute-start(bf16[768,256]{1,0:T(8,128)(2,1)S(1)} %get-tuple-element.39), channel_id=1, source_target_pairs={{0,2},{2,0},{1,3},{3,1},{4,6},{6,4},{5,7},{7,5},{8,10},{10,8},{9,1... | collective-permute-start | bytes 1179656 | tf_op jit(solution)/shard_map/ppermute | solution.py:25
  8.5 24.8 %collective-permute-start.13 = (bf16[512,256]{1,0:T(8,128)(2,1)S(1)}, bf16[512,256]{1,0:T(8,128)(2,1)S(1)}, u32[]{:S(2)}, u32[]{:S(2)}) collective-permute-start(bf16[512,256]{1,0:T(8,128)(2,1)S(1)} %get-tuple-element.42.refs_0_), channel_id=1, source_target_pairs={{0,2},{2,0},{1,3},{3,1},{4,6},{6,4},{5,7},{7,5},{8,10},{10,8},{9,1... | collective-permute-start | bytes 786440 | tf_op jit(solution)/shard_map/ppermute | solution.py:25
  13.6 38.6 %collective-permute-start.9 = (bf16[768,256]{1,0:T(8,128)(2,1)S(1)}, bf16[768,256]{1,0:T(8,128)(2,1)S(1)}, u32[]{:S(2)}, u32[]{:S(2)}) collective-permute-start(bf16[768,256]{1,0:T(8,128)(2,1)S(1)} %get-tuple-element.40), channel_id=1, source_target_pairs={{0,2},{2,0},{1,3},{3,1},{4,6},{6,4},{5,7},{7,5},{8,10},{10,8},{9,1... | collective-permute-start | bytes 1179656 | tf_op jit(solution)/shard_map/ppermute | solution.py:25
  19.2 27.9 %collective-permute-start = (bf16[512,256]{1,0:T(8,128)(2,1)S(1)}, bf16[512,256]{1,0:T(8,128)(2,1)S(1)}, u32[]{:S(2)}, u32[]{:S(2)}) collective-permute-start(bf16[512,256]{1,0:T(8,128)(2,1)S(1)} %get-tuple-element.36), channel_id=1, source_target_pairs={{0,2},{2,0},{1,3},{3,1},{4,6},{6,4},{5,7},{7,5},{8,10},{10,8},{9,1... | collective-permute-start | bytes 786440 | tf_op jit(solution)/shard_map/ppermute | solution.py:25
  33.3 19.0 %collective-permute-start.12 = (bf16[512,256]{1,0:T(8,128)(2,1)S(1)}, bf16[512,256]{1,0:T(8,128)(2,1)S(1)}, u32[]{:S(2)}, u32[]{:S(2)}) collective-permute-start(bf16[512,256]{1,0:T(8,128)(2,1)S(1)} %collective-permute-done.11.refs_5_.refs_2_), channel_id=1, source_target_pairs={{0,1},{1,0},{2,3},{3,2},{4,5},{5,4},{6,7},{7,6},{8,9},{9,8},{10,11... | collective-permute-start | bytes 786440 | tf_op jit(solution)/shard_map/ppermute | solution.py:25
  47.1 14.7 %collective-permute-start.15 = (bf16[1024,256]{1,0:T(8,128)(2,1)S(1)}, bf16[1024,256]{1,0:T(8,128)(2,1)S(1)}, u32[]{:S(2)}, u32[]{:S(2)}) collective-permute-start(bf16[1024,256]{1,0:T(8,128)(2,1)S(1)} %shard_map.35), channel_id=1, source_target_pairs={{0,4},{4,8},{8,12},{1,5},{5,9},{9,13},{2,6},{6,10},{10,14},{3,7},{... | collective-permute-start | bytes 1572872 | tf_op jit(solution)/shard_map/ppermute | solution.py:382
  50.9 15.1 %collective-permute-start.17 = (bf16[1024,256]{1,0:T(8,128)(2,1)S(1)}, bf16[1024,256]{1,0:T(8,128)(2,1)S(1)}, u32[]{:S(2)}, u32[]{:S(2)}) collective-permute-start(bf16[1024,256]{1,0:T(8,128)(2,1)S(1)} %shard_map.36), channel_id=1, source_target_pairs={{4,0},{8,4},{12,8},{5,1},{9,5},{13,9},{6,2},{10,6},{14,10},{7,3},{... | collective-permute-start | bytes 1572872 | tf_op jit(solution)/shard_map/ppermute | solution.py:380
  52.2 2.2 %collective-permute-start.14 = (bf16[512,256]{1,0:T(8,128)(2,1)S(1)}, bf16[512,256]{1,0:T(8,128)(2,1)S(1)}, u32[]{:S(2)}, u32[]{:S(2)}) collective-permute-start(bf16[512,256]{1,0:T(8,128)(2,1)S(1)} %collective-permute-done.13.refs_2_.refs_1_.refs_4_), channel_id=1, source_target_pairs={{0,1},{1,0},{2,3},{3,2},{4,5},{5,4},{6,7},{7,6},{8,9},{9,8},{10,11... | collective-permute-start | bytes 786440 | tf_op jit(solution)/shard_map/ppermute | solution.py:25
  52.3 13.7 %collective-permute-start.10 = (bf16[768,256]{1,0:T(8,128)(2,1)S(1)}, bf16[768,256]{1,0:T(8,128)(2,1)S(1)}, u32[]{:S(2)}, u32[]{:S(2)}) collective-permute-start(bf16[768,256]{1,0:T(8,128)(2,1)S(1)} %collective-permute-done.9.refs_5_.refs_2_), channel_id=1, source_target_pairs={{0,1},{1,0},{2,3},{3,2},{4,5},{5,4},{6,7},{7,6},{8,9},{9,8},{10,11... | collective-permute-start | bytes 1179656 | tf_op jit(solution)/shard_map/ppermute | solution.py:25
  52.8 1.7 %copy-start.1 = (f32[32,9]{0,1:T(8,128)S(1)}, f32[32,9]{0,1:T(8,128)}, u32[]{:S(2)}) copy-start(f32[32,9]{0,1:T(8,128)} %param.3) | copy-start | bytes 3460
  52.8 8.3 %collective-permute-start.2 = (bf16[512,256]{1,0:T(8,128)(2,1)S(1)}, bf16[512,256]{1,0:T(8,128)(2,1)S(1)}, u32[]{:S(2)}, u32[]{:S(2)}) collective-permute-start(bf16[512,256]{1,0:T(8,128)(2,1)S(1)} %get-tuple-element.37), channel_id=1, source_target_pairs={{0,2},{2,0},{1,3},{3,1},{4,6},{6,4},{5,7},{7,5},{8,10},{10,8},{9,1... | collective-permute-start | bytes 786440 | tf_op jit(solution)/shard_map/ppermute | solution.py:25
  54.4 16.4 %collective-permute-start.8 = (bf16[768,256]{1,0:T(8,128)(2,1)S(1)}, bf16[768,256]{1,0:T(8,128)(2,1)S(1)}, u32[]{:S(2)}, u32[]{:S(2)}) collective-permute-start(bf16[768,256]{1,0:T(8,128)(2,1)S(1)} %collective-permute-done.6.refs_5_.refs_2_), channel_id=1, source_target_pairs={{0,1},{1,0},{2,3},{3,2},{4,5},{5,4},{6,7},{7,6},{8,9},{9,8},{10,11... | collective-permute-start | bytes 1179656 | tf_op jit(solution)/shard_map/ppermute | solution.py:25
  61.1 12.8 %collective-permute-start.1 = (bf16[512,256]{1,0:T(8,128)(2,1)S(1)}, bf16[512,256]{1,0:T(8,128)(2,1)S(1)}, u32[]{:S(2)}, u32[]{:S(2)}) collective-permute-start(bf16[512,256]{1,0:T(8,128)(2,1)S(1)} %collective-permute-done.refs_5_.refs_0_), channel_id=1, source_target_pairs={{0,1},{1,0},{2,3},{3,2},{4,5},{5,4},{6,7},{7,6},{8,9},{9,8},{10,11... | collective-permute-start | bytes 786440 | tf_op jit(solution)/shard_map/ppermute | solution.py:25
  61.8 17.8 %collective-permute-start.3 = (bf16[512,256]{1,0:T(8,128)(2,1)S(1)}, bf16[512,256]{1,0:T(8,128)(2,1)S(1)}, u32[]{:S(2)}, u32[]{:S(2)}) collective-permute-start(bf16[512,256]{1,0:T(8,128)(2,1)S(1)} %collective-permute-done.2.refs_1_), channel_id=1, source_target_pairs={{0,1},{1,0},{2,3},{3,2},{4,5},{5,4},{6,7},{7,6},{8,9},{9,8},{10,11... | collective-permute-start | bytes 786440 | tf_op jit(solution)/shard_map/ppermute | solution.py:25
  66.0 10.2 %collective-permute-start.16 = (bf16[1024,256]{1,0:T(8,128)(2,1)S(1)}, bf16[1024,256]{1,0:T(8,128)(2,1)S(1)}, u32[]{:S(2)}, u32[]{:S(2)}) collective-permute-start(bf16[1024,256]{1,0:T(8,128)(2,1)S(1)} %collective-permute-done.15.refs_1_), channel_id=1, source_target_pairs={{0,1},{1,0},{2,3},{3,2},{4,5},{5,4},{6,7},{7,6},{8,9},{9,8},{10,11... | collective-permute-start | bytes 1572872 | tf_op jit(solution)/shard_map/ppermute | solution.py:25
  66.0 10.2 %collective-permute-start.18 = (bf16[1024,256]{1,0:T(8,128)(2,1)S(1)}, bf16[1024,256]{1,0:T(8,128)(2,1)S(1)}, u32[]{:S(2)}, u32[]{:S(2)}) collective-permute-start(bf16[1024,256]{1,0:T(8,128)(2,1)S(1)} %collective-permute-done.17.refs_9_), channel_id=1, source_target_pairs={{0,1},{1,0},{2,3},{3,2},{4,5},{5,4},{6,7},{7,6},{8,9},{9,8},{10,11... | collective-permute-start | bytes 1572872 | tf_op jit(solution)/shard_map/ppermute | solution.py:25
  70.9 5.3 %collective-permute-start.5 = (bf16[512,256]{1,0:T(8,128)(2,1)S(1)}, bf16[512,256]{1,0:T(8,128)(2,1)S(1)}, u32[]{:S(2)}, u32[]{:S(2)}) collective-permute-start(bf16[512,256]{1,0:T(8,128)(2,1)S(1)} %collective-permute-done.4.refs_1_.refs_7_.refs_2_), channel_id=1, source_target_pairs={{0,1},{1,0},{2,3},{3,2},{4,5},{5,4},{6,7},{7,6},{8,9},{9,8},{10,11... | collective-permute-start | bytes 786440 | tf_op jit(solution)/shard_map/ppermute | solution.py:25

commit v9 on v8

--- a/solution.py
+++ b/solution.py
@@ -103,7 +103,10 @@
     acc_in, acc_out, finished = job["acc_in"], job["acc_out"], job["finished"]
     writes = job["writes"]
     arrays = job["arrays"]
-    taper = refs[0]
+    taper_source, taper, taper_sem = refs[0], *refs[-2:]
+    refs = refs[:-2]
+    taper_copy = pltpu.make_async_copy(taper_source, taper, taper_sem)
+    taper_copy.start()
     sources = refs[1 : 1 + arrays]
     inputs = dict(zip(acc_in, refs[1 + arrays : 1 + arrays + len(acc_in)]))
     begins = refs[1 + arrays + len(acc_in) : job["earlier"]]
@@ -162,9 +165,27 @@
             rows.append(jnp.concatenate(row, axis=1))
         return jnp.concatenate(rows, axis=0)
 
+    settled = set()
+
+    def finish(pairs):
+        for pair in pairs:
+            n = finished.index(pair)
+            update = (sums if pair in begun else inputs)[pair][...]
+            obuf[n] = (own(pair).astype(jnp.float32) - 0.5 * update).astype(jnp.bfloat16)
+            if job["last"]:
+                sent.append(
+                    pltpu.make_async_copy(obuf.at[n], out.at[tile_rows(pair)], out_sem.at[n])
+                )
+                sent[-1].start()
+            settled.add(pair)
+
     for k, (j, first, count) in enumerate(steps):
         near = list(range(first, first + count))
+        coming = touched_by(steps[k + 1 :])
+        ready = [pair for pair in finished if pair in near + [j] and pair not in coming]
         gram = gram_rows(held, j, near, begins[k] if begins else None)
+        if k == 0:
+            taper_copy.wait()
         tiles = {i: gram[n * ROWS : (n + 1) * ROWS] for n, i in enumerate(near)}
         mine = [i for i in near if i in owned]
         if mine:
@@ -176,6 +197,7 @@
             for n, i in enumerate(mine):
                 add(i, value[n * ROWS : (n + 1) * ROWS])
         others = [i for i in near if i != j]
+        finish([pair for pair in ready if pair != j])
         if j in owned and others:
             value = None
             for i in others:
@@ -184,15 +206,9 @@
                 )
                 value = term if value is None else value + term
             add(j, value)
-
-    for n, pair in enumerate(finished):
-        update = (sums if pair in begun else inputs)[pair][...]
-        obuf[n] = (own(pair).astype(jnp.float32) - 0.5 * update).astype(jnp.bfloat16)
-        if job["last"]:
-            sent.append(
-                pltpu.make_async_copy(obuf.at[n], out.at[tile_rows(pair)], out_sem.at[n])
-            )
-            sent[-1].start()
+        finish([pair for pair in ready if pair == j])
+
+    finish([pair for pair in finished if pair not in settled])
     if job["last"]:
         for copy in sent:
             copy.wait()
@@ -306,7 +322,7 @@
         last=last,
     )
     inside = pl.BlockSpec(memory_space=pltpu.VMEM)
-    specs = [pl.BlockSpec(memory_space=pltpu.SMEM)] + [inside] * (len(operands) - 1)
+    specs = [inside] * len(operands)
     products = sum(n for _, _, n in steps)
     count = max(len(finished), 1)
     carries = [jax.ShapeDtypeStruct((ROWS, members), jnp.float32)] * len(acc_out)
@@ -322,6 +338,7 @@
     else:
         shapes = [jax.ShapeDtypeStruct(block, jnp.bfloat16)] * int(bool(finished)) + carries
         out_specs = [inside] * len(shapes)
+    scratch += [pltpu.SMEM(operands[0].shape, jnp.float32), pltpu.SemaphoreType.DMA]
     outputs = pl.pallas_call(
         functools.partial(update_kernel, job),
         out_shape=shapes,
@@ -365,9 +382,8 @@
     up = [(i + 1, i) for i in range(ring - 1)]
     chunks = chunk_bounds(pairs)
 
-    top, bottom, start = cut_rows(
-        anomalies, [(0, NEAR), (pairs - NEAR, pairs), chunks[0]], 52 * 2**20
-    )
+    (top,) = cut_rows(anomalies, [(0, NEAR)], 52 * 2**20)
+    bottom, start = cut_rows(anomalies, [(pairs - NEAR, pairs), chunks[0]])
     *cuts, inside = cut_rows(anomalies, chunks[1:] + [(0, pairs)])
     cuts = [start] + cuts
     tops = shifted(top, "member")

time: 82.6 us -> 79.4 us (0.961)
  the two profiles are of different devices: /device:TPU:0 before, /device:TPU:1 now
where the time goes in v9:
time: 79.4 us; the launch traced here: 79.2 us
  waiting for transfers between devices  39.4 us (50%)
  starting transfers between devices  20 us (25%)
  Pallas kernels  18 us (23%)
  local copies, waits for them, and re-layouts  1.59 us (2%)
    ppermute x17, waiting for transfers between devices, shifted(): lax.ppermute(value, axis, [(i, (i + s) % count) for i in range(count)])  37.3 us
    ppermute x17, starting transfers between devices, shifted(): lax.ppermute(value, axis, [(i, (i + s) % count) for i in range(count)])  15.5 us
    pallas_call x6, Pallas kernels, run_steps(): pl.pallas_call(functools.partial(update_kernel, job), out_shape=shapes, i...  14.6 us
    ppermute x1, starting transfers between devices, per_device(): before = lax.ppermute(tails, 'region', down)  3.19 us
    ppermute x1, waiting for transfers between devices, per_device(): after = lax.ppermute(heads, 'region', up)  2.15 us
    pallas_call x3, Pallas kernels, cut_rows(): pl.pallas_call(functools.partial(cut_kernel, tuple((first * ROWS for firs...  1.61 us
    unnamed x4, local copies, waits for them, and re-layouts  1.59 us
  transfers between devices with their start and end apart: 19, of which 6 were waited for; matrix products, arithmetic and copies ran while one was open for 0% of the time, Pallas kernels for 19%

profile of v9, /device:TPU:1, one launch (start us, length us, event | category | flops | bytes accessed | tf_op | source)
XLA Modules:
  0.0 79.2 jit_solution(16404931307775820519)
XLA Ops:
  0.0 1.6 %copy-done = bf16[4096,256]{1,0:T(8,128)(2,1)S(1)} copy-done((bf16[4096,256]{1,0:T(8,128)(2,1)S(1)}, bf16[4096,256]{1,0:T(8,128)(2,1)}, u32[]{:S(2)}) %copy-start) | copy-done | bytes 2097176
  1.6 0.6 shard_map.28
  2.3 2.8 %collective-permute-start.4 = (bf16[512,256]{1,0:T(8,128)(2,1)S(1)}, bf16[512,256]{1,0:T(8,128)(2,1)S(1)}, u32[]{:S(2)}, u32[]{:S(2)}) collective-permute-start(bf16[512,256]{1,0:T(8,128)(2,1)S(1)} %get-tuple-element.37.refs_0_), channel_id=1, source_target_pairs={{0,2},{2,0},{1,3},{3,1},{4,6},{6,4},{5,7},{7,5},{8,10},{10,8},{9,1... | collective-permute-start | bytes 786440 | tf_op jit(solution)/shard_map/ppermute | solution.py:25
  5.2 1.4 %collective-permute-start.6 = (bf16[768,256]{1,0:T(8,128)(2,1)S(1)}, bf16[768,256]{1,0:T(8,128)(2,1)S(1)}, u32[]{:S(2)}, u32[]{:S(2)}) collective-permute-start(bf16[768,256]{1,0:T(8,128)(2,1)S(1)} %get-tuple-element.38), channel_id=1, source_target_pairs={{0,2},{2,0},{1,3},{3,1},{4,6},{6,4},{5,7},{7,5},{8,10},{10,8},{9,1... | collective-permute-start | bytes 1179656 | tf_op jit(solution)/shard_map/ppermute | solution.py:25
  6.6 1.0 %shard_map.31.refs_0_ = bf16[512,256]{1,0:T(8,128)(2,1)S(1)} custom-call(bf16[4096,256]{1,0:T(8,128)(2,1)} %source.5), custom_call_target="tpu_custom_call" | custom-call | bytes 524288 | tf_op jit(solution)/shard_map/pallas_call | solution.py:240
  7.7 4.1 %collective-permute-done.4.refs_1_.refs_7_.refs_2_ = bf16[512,256]{1,0:T(8,128)(2,1)S(1)} collective-permute-done((bf16[512,256]{1,0:T(8,128)(2,1)S(1)}, bf16[512,256]{1,0:T(8,128)(2,1)S(1)}, u32[]{:S(2)}, u32[]{:S(2)}) %collective-permute-start.4) | collective-permute-done | bytes 262176 | tf_op jit(solution)/shard_map/ppermute | solution.py:25
  11.8 1.2 %collective-permute-start.9 = (bf16[768,256]{1,0:T(8,128)(2,1)S(1)}, bf16[768,256]{1,0:T(8,128)(2,1)S(1)}, u32[]{:S(2)}, u32[]{:S(2)}) collective-permute-start(bf16[768,256]{1,0:T(8,128)(2,1)S(1)} %get-tuple-element.39), channel_id=1, source_target_pairs={{0,2},{2,0},{1,3},{3,1},{4,6},{6,4},{5,7},{7,5},{8,10},{10,8},{9,1... | collective-permute-start | bytes 1179656 | tf_op jit(solution)/shard_map/ppermute | solution.py:25
  12.9 4.4 %collective-permute-done.11.refs_5_.refs_2_ = bf16[512,256]{1,0:T(8,128)(2,1)S(1)} collective-permute-done((bf16[512,256]{1,0:T(8,128)(2,1)S(1)}, bf16[512,256]{1,0:T(8,128)(2,1)S(1)}, u32[]{:S(2)}, u32[]{:S(2)}) %collective-permute-start.11) | collective-permute-done | bytes 262176 | tf_op jit(solution)/shard_map/ppermute | solution.py:25
  17.4 1.2 %collective-permute-start = (bf16[512,256]{1,0:T(8,128)(2,1)S(1)}, bf16[512,256]{1,0:T(8,128)(2,1)S(1)}, u32[]{:S(2)}, u32[]{:S(2)}) collective-permute-start(bf16[512,256]{1,0:T(8,128)(2,1)S(1)} %get-tuple-element.35), channel_id=1, source_target_pairs={{0,2},{2,0},{1,3},{3,1},{4,6},{6,4},{5,7},{7,5},{8,10},{10,8},{9,1... | collective-permute-start | bytes 786440 | tf_op jit(solution)/shard_map/ppermute | solution.py:25
  18.6 12.9 %collective-permute-done.13.refs_2_.refs_1_.refs_4_ = bf16[512,256]{1,0:T(8,128)(2,1)S(1)} collective-permute-done((bf16[512,256]{1,0:T(8,128)(2,1)S(1)}, bf16[512,256]{1,0:T(8,128)(2,1)S(1)}, u32[]{:S(2)}, u32[]{:S(2)}) %collective-permute-start.13) | collective-permute-done | bytes 262176 | tf_op jit(solution)/shard_map/ppermute | solution.py:25
  31.4 0.8 collective-permute-start.12
  32.3 13.1 %collective-permute-done.refs_5_.refs_0_ = bf16[512,256]{1,0:T(8,128)(2,1)S(1)} collective-permute-done((bf16[512,256]{1,0:T(8,128)(2,1)S(1)}, bf16[512,256]{1,0:T(8,128)(2,1)S(1)}, u32[]{:S(2)}, u32[]{:S(2)}) %collective-permute-start) | collective-permute-done | bytes 262176 | tf_op jit(solution)/shard_map/ppermute | solution.py:25
  45.5 3.2 %collective-permute-start.15 = (bf16[1024,256]{1,0:T(8,128)(2,1)S(1)}, bf16[1024,256]{1,0:T(8,128)(2,1)S(1)}, u32[]{:S(2)}, u32[]{:S(2)}) collective-permute-start(bf16[1024,256]{1,0:T(8,128)(2,1)S(1)} %shard_map.36), channel_id=1, source_target_pairs={{0,4},{4,8},{8,12},{1,5},{5,9},{9,13},{2,6},{6,10},{10,14},{3,7},{... | collective-permute-start | bytes 1572872 | tf_op jit(solution)/shard_map/ppermute | solution.py:398
  48.7 1.3 %collective-permute-start.17 = (bf16[1024,256]{1,0:T(8,128)(2,1)S(1)}, bf16[1024,256]{1,0:T(8,128)(2,1)S(1)}, u32[]{:S(2)}, u32[]{:S(2)}) collective-permute-start(bf16[1024,256]{1,0:T(8,128)(2,1)S(1)} %shard_map.37), channel_id=1, source_target_pairs={{4,0},{8,4},{12,8},{5,1},{9,5},{13,9},{6,2},{10,6},{14,10},{7,3},{... | collective-permute-start | bytes 1572872 | tf_op jit(solution)/shard_map/ppermute | solution.py:396
  50.0 1.2 %collective-permute-start.14 = (bf16[512,256]{1,0:T(8,128)(2,1)S(1)}, bf16[512,256]{1,0:T(8,128)(2,1)S(1)}, u32[]{:S(2)}, u32[]{:S(2)}) collective-permute-start(bf16[512,256]{1,0:T(8,128)(2,1)S(1)} %collective-permute-done.13.refs_2_.refs_1_.refs_4_), channel_id=1, source_target_pairs={{0,1},{1,0},{2,3},{3,2},{4,5},{5,4},{6,7},{7,6},{8,9},{9,8},{10,11... | collective-permute-start | bytes 786440 | tf_op jit(solution)/shard_map/ppermute | solution.py:25
  51.3 1.2 %collective-permute-start.2 = (bf16[512,256]{1,0:T(8,128)(2,1)S(1)}, bf16[512,256]{1,0:T(8,128)(2,1)S(1)}, u32[]{:S(2)}, u32[]{:S(2)}) collective-permute-start(bf16[512,256]{1,0:T(8,128)(2,1)S(1)} %get-tuple-element.36), channel_id=1, source_target_pairs={{0,2},{2,0},{1,3},{3,1},{4,6},{6,4},{5,7},{7,5},{8,10},{10,8},{9,1... | collective-permute-start | bytes 786440 | tf_op jit(solution)/shard_map/ppermute | solution.py:25
  52.5 0.1 shard_map.30.refs_3_.refs_5_.refs_1_
  52.7 0.8 collective-permute-start.8
  53.5 2.5 %shard_map.32 = (f32[256,256]{1,0:T(8,128)S(1)}, f32[256,256]{1,0:T(8,128)S(1)}, f32[256,256]{1,0:T(8,128)S(1)}, f32[256,256]{1,0:T(8,128)S(1)}) custom-call(f32[9,32]{1,0:T(8,128)S(1)} %bitcast.1, bf16[4096,256]{1,0:T(8,128)(2,1)S(1)} %get-tuple-element.34.refs_1_.refs_3_.refs_0_, bf16[512,256]{1,0:T(8,128)(2,1)S(1)} %collective-permute-done.13.refs_2_.refs_1_.refs_4_, ...), custom_call_target="tpu_custom_call" | custom-call | flops 1811939328 | bytes 2097152 | tf_op jit(solution)/shard_map/pallas_call | solution.py:342
  56.0 2.7 %collective-permute-done.2.refs_1_ = bf16[512,256]{1,0:T(8,128)(2,1)S(1)} collective-permute-done((bf16[512,256]{1,0:T(8,128)(2,1)S(1)}, bf16[512,256]{1,0:T(8,128)(2,1)S(1)}, u32[]{:S(2)}, u32[]{:S(2)}) %collective-permute-start.2) | collective-permute-done | bytes 262176 | tf_op jit(solution)/shard_map/ppermute | solution.py:25
  58.7 1.3 %collective-permute-start.1 = (bf16[512,256]{1,0:T(8,128)(2,1)S(1)}, bf16[512,256]{1,0:T(8,128)(2,1)S(1)}, u32[]{:S(2)}, u32[]{:S(2)}) collective-permute-start(bf16[512,256]{1,0:T(8,128)(2,1)S(1)} %collective-permute-done.refs_5_.refs_0_), channel_id=1, source_target_pairs={{0,1},{1,0},{2,3},{3,2},{4,5},{5,4},{6,7},{7,6},{8,9},{9,8},{10,11... | collective-permute-start | bytes 786440 | tf_op jit(solution)/shard_map/ppermute | solution.py:25
  60.0 0.7 collective-permute-start.3
  60.8 2.1 %collective-permute-done.17.refs_9_ = bf16[1024,256]{1,0:T(8,128)(2,1)S(1)} collective-permute-done((bf16[1024,256]{1,0:T(8,128)(2,1)S(1)}, bf16[1024,256]{1,0:T(8,128)(2,1)S(1)}, u32[]{:S(2)}, u32[]{:S(2)}) %collective-permute-start.17) | collective-permute-done | bytes 524320 | tf_op jit(solution)/shard_map/ppermute | solution.py:396
  62.9 2.0 %collective-permute-start.16 = (bf16[1024,256]{1,0:T(8,128)(2,1)S(1)}, bf16[1024,256]{1,0:T(8,128)(2,1)S(1)}, u32[]{:S(2)}, u32[]{:S(2)}) collective-permute-start(bf16[1024,256]{1,0:T(8,128)(2,1)S(1)} %collective-permute-done.15.refs_1_), channel_id=1, source_target_pairs={{0,1},{1,0},{2,3},{3,2},{4,5},{5,4},{6,7},{7,6},{8,9},{9,8},{10,11... | collective-permute-start | bytes 1572872 | tf_op jit(solution)/shard_map/ppermute | solution.py:25
  64.9 2.4 %shard_map.33 = (bf16[3,256,256]{2,1,0:T(8,128)(2,1)S(1)}, f32[256,256]{1,0:T(8,128)S(1)}, f32[256,256]{1,0:T(8,128)S(1)}) custom-call(f32[9,32]{1,0:T(8,128)S(1)} %bitcast.2, bf16[4096,256]{1,0:T(8,128)(2,1)S(1)} %get-tuple-element.34.refs_1_.refs_3_.refs_0_, bf16[512,256]{1,0:T(8,128)(2,1)S(1)} %collective-permute-done.11.refs_5_.refs_2_, ...), custom_call_target="tpu_custom_call" | custom-call | flops 1811939328 | bytes 3801088 | tf_op jit(solution)/shard_map/pallas_call | solution.py:342
  67.4 0.9 %shard_map.39 = (f32[768,256]{1,0:T(8,128)S(1)}, f32[256,256]{1,0:T(8,128)S(1)}, f32[1280,256]{1,0:T(8,128)S(1)}) custom-call(bf16[4096,256]{1,0:T(8,128)(2,1)S(1)} %get-tuple-element.34.refs_1_.refs_3_.refs_0_, bf16[4096,256]{1,0:T(8,128)(2,1)S(1)} %shard_map.30.refs_3_.refs_5_.refs_1_), custom_call_target="tpu_custom_call" | custom-call | flops 603979776 | bytes 2359296 | tf_op jit(solution)/shard_map/pallas_call | solution.py:86
  68.3 0.6 shard_map.40
  68.9 0.6 collective-permute-start.5
  69.5 2.4 %shard_map.34 = (bf16[3,256,256]{2,1,0:T(8,128)(2,1)S(1)}, f32[256,256]{1,0:T(8,128)S(1)}, f32[256,256]{1,0:T(8,128)S(1)}) custom-call(f32[9,32]{1,0:T(8,128)S(1)} %bitcast.3, bf16[4096,256]{1,0:T(8,128)(2,1)S(1)} %get-tuple-element.34.refs_1_.refs_3_.refs_0_, bf16[768,256]{1,0:T(8,128)(2,1)S(1)} %collective-permute-done.9.refs_5_.refs_2_, ...), custom_call_target="tpu_custom_call" | custom-call | flops 1811939328 | bytes 3801088 | tf_op jit(solution)/shard_map/pallas_call | solution.py:342
  71.9 1.7 %shard_map.35 = (bf16[2,256,256]{2,1,0:T(8,128)(2,1)S(1)}, f32[256,256]{1,0:T(8,128)S(1)}, f32[256,256]{1,0:T(8,128)S(1)}) custom-call(f32[9,32]{1,0:T(8,128)S(1)} %bitcast.4, bf16[4096,256]{1,0:T(8,128)(2,1)S(1)} %get-tuple-element.34.refs_1_.refs_3_.refs_0_, bf16[768,256]{1,0:T(8,128)(2,1)S(1)} %collective-permute-done.6.refs_5_.refs_2_, ...), custom_call_target="tpu_custom_call" | custom-call | flops 1207959552 | bytes 2883584 | tf_op jit(solution)/shard_map/pallas_call | solution.py:342
  73.7 3.0 %shard_map.38 = (bf16[2,256,256]{2,1,0:T(8,128)(2,1)S(1)}, f32[256,256]{1,0:T(8,128)S(1)}, f32[256,256]{1,0:T(8,128)S(1)}) custom-call(f32[9,32]{1,0:T(8,128)S(1)} %bitcast.5, bf16[1024,256]{1,0:T(8,128)(2,1)S(1)} %collective-permute-done.15.refs_1_, bf16[1024,256]{1,0:T(8,128)(2,1)S(1)} %collective-permute-done.16.refs_2_, ...), custom_call_target="tpu_custom_call" | custom-call | flops 1811939328 | bytes 4980736 | tf_op jit(solution)/shard_map/pallas_call | solution.py:342
  76.7 2.5 %shard_map.41 = bf16[4096,256]{1,0:T(8,128)(2,1)} custom-call(f32[9,32]{1,0:T(8,128)S(1)} %bitcast.6, bf16[4096,256]{1,0:T(8,128)(2,1)S(1)} %get-tuple-element.34.refs_1_.refs_3_.refs_0_, bf16[512,256]{1,0:T(8,128)(2,1)S(1)} %collective-permute-done.1.refs_6_.refs_2_, bf16[512,256]{1,0:T(8,128)(2,1)S(1)} %collective-permute-done.3.refs_3_, ...), custom_call_target="tpu_custom_call" | custom-call | flops 905969664 | bytes 3932160 | tf_op jit(solution)/shard_map/pallas_call | solution.py:342
  (24 shorter events, 0.6 us)
Async XLA Ops:
  0.0 1.6 %copy-start = (bf16[4096,256]{1,0:T(8,128)(2,1)S(1)}, bf16[4096,256]{1,0:T(8,128)(2,1)}, u32[]{:S(2)}) copy-start(bf16[4096,256]{1,0:T(8,128)(2,1)} %source.5) | copy-start | bytes 6291460
  2.2 49.1 %collective-permute-start.7 = (bf16[4096,256]{1,0:T(8,128)(2,1)S(1)}, bf16[4096,256]{1,0:T(8,128)(2,1)S(1)}, u32[]{:S(2)}, u32[]{:S(2)}) collective-permute-start(bf16[4096,256]{1,0:T(8,128)(2,1)S(1)} %get-tuple-element.34.refs_1_.refs_3_.refs_0_), channel_id=1, source_target_pairs={{0,1},{1,0},{2,3},{3,2},{4,5},{5,4},{6,7},{7,6},{8,9},{9,8},{10,11... | collective-permute-start | bytes 6291464 | tf_op jit(solution)/shard_map/ppermute | solution.py:25
  2.3 9.4 %collective-permute-start.4 = (bf16[512,256]{1,0:T(8,128)(2,1)S(1)}, bf16[512,256]{1,0:T(8,128)(2,1)S(1)}, u32[]{:S(2)}, u32[]{:S(2)}) collective-permute-start(bf16[512,256]{1,0:T(8,128)(2,1)S(1)} %get-tuple-element.37.refs_0_), channel_id=1, source_target_pairs={{0,2},{2,0},{1,3},{3,1},{4,6},{6,4},{5,7},{7,5},{8,10},{10,8},{9,1... | collective-permute-start | bytes 786440 | tf_op jit(solution)/shard_map/ppermute | solution.py:25
  5.1 12.3 %collective-permute-start.11 = (bf16[512,256]{1,0:T(8,128)(2,1)S(1)}, bf16[512,256]{1,0:T(8,128)(2,1)S(1)}, u32[]{:S(2)}, u32[]{:S(2)}) collective-permute-start(bf16[512,256]{1,0:T(8,128)(2,1)S(1)} %get-tuple-element.40), channel_id=1, source_target_pairs={{0,2},{2,0},{1,3},{3,1},{4,6},{6,4},{5,7},{7,5},{8,10},{10,8},{9,1... | collective-permute-start | bytes 786440 | tf_op jit(solution)/shard_map/ppermute | solution.py:25
  5.2 43.5 %collective-permute-start.6 = (bf16[768,256]{1,0:T(8,128)(2,1)S(1)}, bf16[768,256]{1,0:T(8,128)(2,1)S(1)}, u32[]{:S(2)}, u32[]{:S(2)}) collective-permute-start(bf16[768,256]{1,0:T(8,128)(2,1)S(1)} %get-tuple-element.38), channel_id=1, source_target_pairs={{0,2},{2,0},{1,3},{3,1},{4,6},{6,4},{5,7},{7,5},{8,10},{10,8},{9,1... | collective-permute-start | bytes 1179656 | tf_op jit(solution)/shard_map/ppermute | solution.py:25
  7.5 23.9 %collective-permute-start.13 = (bf16[512,256]{1,0:T(8,128)(2,1)S(1)}, bf16[512,256]{1,0:T(8,128)(2,1)S(1)}, u32[]{:S(2)}, u32[]{:S(2)}) collective-permute-start(bf16[512,256]{1,0:T(8,128)(2,1)S(1)} %shard_map.31.refs_0_), channel_id=1, source_target_pairs={{0,2},{2,0},{1,3},{3,1},{4,6},{6,4},{5,7},{7,5},{8,10},{10,8},{9,1... | collective-permute-start | bytes 786440 | tf_op jit(solution)/shard_map/ppermute | solution.py:25
  11.8 38.2 %collective-permute-start.9 = (bf16[768,256]{1,0:T(8,128)(2,1)S(1)}, bf16[768,256]{1,0:T(8,128)(2,1)S(1)}, u32[]{:S(2)}, u32[]{:S(2)}) collective-permute-start(bf16[768,256]{1,0:T(8,128)(2,1)S(1)} %get-tuple-element.39), channel_id=1, source_target_pairs={{0,2},{2,0},{1,3},{3,1},{4,6},{6,4},{5,7},{7,5},{8,10},{10,8},{9,1... | collective-permute-start | bytes 1179656 | tf_op jit(solution)/shard_map/ppermute | solution.py:25
  17.4 28.1 %collective-permute-start = (bf16[512,256]{1,0:T(8,128)(2,1)S(1)}, bf16[512,256]{1,0:T(8,128)(2,1)S(1)}, u32[]{:S(2)}, u32[]{:S(2)}) collective-permute-start(bf16[512,256]{1,0:T(8,128)(2,1)S(1)} %get-tuple-element.35), channel_id=1, source_target_pairs={{0,2},{2,0},{1,3},{3,1},{4,6},{6,4},{5,7},{7,5},{8,10},{10,8},{9,1... | collective-permute-start | bytes 786440 | tf_op jit(solution)/shard_map/ppermute | solution.py:25
  31.4 19.8 %collective-permute-start.12 = (bf16[512,256]{1,0:T(8,128)(2,1)S(1)}, bf16[512,256]{1,0:T(8,128)(2,1)S(1)}, u32[]{:S(2)}, u32[]{:S(2)}) collective-permute-start(bf16[512,256]{1,0:T(8,128)(2,1)S(1)} %collective-permute-done.11.refs_5_.refs_2_), channel_id=1, source_target_pairs={{0,1},{1,0},{2,3},{3,2},{4,5},{5,4},{6,7},{7,6},{8,9},{9,8},{10,11... | collective-permute-start | bytes 786440 | tf_op jit(solution)/shard_map/ppermute | solution.py:25
  45.5 14.6 %collective-permute-start.15 = (bf16[1024,256]{1,0:T(8,128)(2,1)S(1)}, bf16[1024,256]{1,0:T(8,128)(2,1)S(1)}, u32[]{:S(2)}, u32[]{:S(2)}) collective-permute-start(bf16[1024,256]{1,0:T(8,128)(2,1)S(1)} %shard_map.36), channel_id=1, source_target_pairs={{0,4},{4,8},{8,12},{1,5},{5,9},{9,13},{2,6},{6,10},{10,14},{3,7},{... | collective-permute-start | bytes 1572872 | tf_op jit(solution)/shard_map/ppermute | solution.py:398
  48.7 14.2 %collective-permute-start.17 = (bf16[1024,256]{1,0:T(8,128)(2,1)S(1)}, bf16[1024,256]{1,0:T(8,128)(2,1)S(1)}, u32[]{:S(2)}, u32[]{:S(2)}) collective-permute-start(bf16[1024,256]{1,0:T(8,128)(2,1)S(1)} %shard_map.37), channel_id=1, source_target_pairs={{4,0},{8,4},{12,8},{5,1},{9,5},{13,9},{6,2},{10,6},{14,10},{7,3},{... | collective-permute-start | bytes 1572872 | tf_op jit(solution)/shard_map/ppermute | solution.py:396
  50.0 2.7 %collective-permute-start.14 = (bf16[512,256]{1,0:T(8,128)(2,1)S(1)}, bf16[512,256]{1,0:T(8,128)(2,1)S(1)}, u32[]{:S(2)}, u32[]{:S(2)}) collective-permute-start(bf16[512,256]{1,0:T(8,128)(2,1)S(1)} %collective-permute-done.13.refs_2_.refs_1_.refs_4_), channel_id=1, source_target_pairs={{0,1},{1,0},{2,3},{3,2},{4,5},{5,4},{6,7},{7,6},{8,9},{9,8},{10,11... | collective-permute-start | bytes 786440 | tf_op jit(solution)/shard_map/ppermute | solution.py:25
  51.2 13.7 %collective-permute-start.10 = (bf16[768,256]{1,0:T(8,128)(2,1)S(1)}, bf16[768,256]{1,0:T(8,128)(2,1)S(1)}, u32[]{:S(2)}, u32[]{:S(2)}) collective-permute-start(bf16[768,256]{1,0:T(8,128)(2,1)S(1)} %collective-permute-done.9.refs_5_.refs_2_), channel_id=1, source_target_pairs={{0,1},{1,0},{2,3},{3,2},{4,5},{5,4},{6,7},{7,6},{8,9},{9,8},{10,11... | collective-permute-start | bytes 1179656 | tf_op jit(solution)/shard_map/ppermute | solution.py:25
  51.3 2.2 %copy-start.1 = (f32[32,9]{0,1:T(8,128)S(1)}, f32[32,9]{0,1:T(8,128)}, u32[]{:S(2)}) copy-start(f32[32,9]{0,1:T(8,128)} %param.3) | copy-start | bytes 3460
  51.3 7.4 %collective-permute-start.2 = (bf16[512,256]{1,0:T(8,128)(2,1)S(1)}, bf16[512,256]{1,0:T(8,128)(2,1)S(1)}, u32[]{:S(2)}, u32[]{:S(2)}) collective-permute-start(bf16[512,256]{1,0:T(8,128)(2,1)S(1)} %get-tuple-element.36), channel_id=1, source_target_pairs={{0,2},{2,0},{1,3},{3,1},{4,6},{6,4},{5,7},{7,5},{8,10},{10,8},{9,1... | collective-permute-start | bytes 786440 | tf_op jit(solution)/shard_map/ppermute | solution.py:25
  52.7 16.2 %collective-permute-start.8 = (bf16[768,256]{1,0:T(8,128)(2,1)S(1)}, bf16[768,256]{1,0:T(8,128)(2,1)S(1)}, u32[]{:S(2)}, u32[]{:S(2)}) collective-permute-start(bf16[768,256]{1,0:T(8,128)(2,1)S(1)} %collective-permute-done.6.refs_5_.refs_2_), channel_id=1, source_target_pairs={{0,1},{1,0},{2,3},{3,2},{4,5},{5,4},{6,7},{7,6},{8,9},{9,8},{10,11... | collective-permute-start | bytes 1179656 | tf_op jit(solution)/shard_map/ppermute | solution.py:25
  58.7 13.2 %collective-permute-start.1 = (bf16[512,256]{1,0:T(8,128)(2,1)S(1)}, bf16[512,256]{1,0:T(8,128)(2,1)S(1)}, u32[]{:S(2)}, u32[]{:S(2)}) collective-permute-start(bf16[512,256]{1,0:T(8,128)(2,1)S(1)} %collective-permute-done.refs_5_.refs_0_), channel_id=1, source_target_pairs={{0,1},{1,0},{2,3},{3,2},{4,5},{5,4},{6,7},{7,6},{8,9},{9,8},{10,11... | collective-permute-start | bytes 786440 | tf_op jit(solution)/shard_map/ppermute | solution.py:25
  60.0 16.6 %collective-permute-start.3 = (bf16[512,256]{1,0:T(8,128)(2,1)S(1)}, bf16[512,256]{1,0:T(8,128)(2,1)S(1)}, u32[]{:S(2)}, u32[]{:S(2)}) collective-permute-start(bf16[512,256]{1,0:T(8,128)(2,1)S(1)} %collective-permute-done.2.refs_1_), channel_id=1, source_target_pairs={{0,1},{1,0},{2,3},{3,2},{4,5},{5,4},{6,7},{7,6},{8,9},{9,8},{10,11... | collective-permute-start | bytes 786440 | tf_op jit(solution)/shard_map/ppermute | solution.py:25
  62.9 10.8 %collective-permute-start.16 = (bf16[1024,256]{1,0:T(8,128)(2,1)S(1)}, bf16[1024,256]{1,0:T(8,128)(2,1)S(1)}, u32[]{:S(2)}, u32[]{:S(2)}) collective-permute-start(bf16[1024,256]{1,0:T(8,128)(2,1)S(1)} %collective-permute-done.15.refs_1_), channel_id=1, source_target_pairs={{0,1},{1,0},{2,3},{3,2},{4,5},{5,4},{6,7},{7,6},{8,9},{9,8},{10,11... | collective-permute-start | bytes 1572872 | tf_op jit(solution)/shard_map/ppermute | solution.py:25
  64.9 8.8 %collective-permute-start.18 = (bf16[1024,256]{1,0:T(8,128)(2,1)S(1)}, bf16[1024,256]{1,0:T(8,128)(2,1)S(1)}, u32[]{:S(2)}, u32[]{:S(2)}) collective-permute-start(bf16[1024,256]{1,0:T(8,128)(2,1)S(1)} %collective-permute-done.17.refs_9_), channel_id=1, source_target_pairs={{0,1},{1,0},{2,3},{3,2},{4,5},{5,4},{6,7},{7,6},{8,9},{9,8},{10,11... | collective-permute-start | bytes 1572872 | tf_op jit(solution)/shard_map/ppermute | solution.py:25
  68.9 4.8 %collective-permute-start.5 = (bf16[512,256]{1,0:T(8,128)(2,1)S(1)}, bf16[512,256]{1,0:T(8,128)(2,1)S(1)}, u32[]{:S(2)}, u32[]{:S(2)}) collective-permute-start(bf16[512,256]{1,0:T(8,128)(2,1)S(1)} %collective-permute-done.4.refs_1_.refs_7_.refs_2_), channel_id=1, source_target_pairs={{0,1},{1,0},{2,3},{3,2},{4,5},{5,4},{6,7},{7,6},{8,9},{9,8},{10,11... | collective-permute-start | bytes 786440 | tf_op jit(solution)/shard_map/ppermute | solution.py:25

commit v10 on v9

--- a/solution.py
+++ b/solution.py
@@ -367,7 +367,7 @@
 def chunk_bounds(pairs):
     first, last = NEAR, pairs - NEAR
     bulk = last - first - 6
-    sizes = [2, bulk // 2, bulk - bulk // 2, 2, 2]
+    sizes = [2, bulk // 2, bulk - bulk // 2, 2, 1, 1]
     bounds = [first]
     for size in sizes:
         bounds.append(bounds[-1] + size)
@@ -446,23 +446,32 @@
     around = list(range(-NEAR, 0)) + list(range(pairs, pairs + NEAR))
     batches = [low + list(range(*chunks[0])), high + around]
     batches += [list(range(*c)) for c in chunks[1:]]
-    for n, fresh in enumerate(batches):
+    work = []
+    for fresh in batches:
         steps, there = steps_for(fresh, there)
         ready = [
             i for i in range(pairs)
             if i not in done and all(k in there for k in range(i - NEAR, i + NEAR + 1))
         ]
         done |= set(ready)
-        end = n == len(batches) - 1
+        work.append((steps, ready))
+
+    tails = len(batches) - 2
+    split = len(pieces) == 2 * len(held)
+    received = tuple(range(1, len(held)))
+    if split:
+        sums = partial_grams(
+            pieces, (0, len(held)), work[tails][0] + work[tails + 1][0], ()
+        )
+    for n, (steps, ready) in enumerate(work):
         parts, begins = None, ()
-        if end and len(pieces) == 2 * len(held):
-            near_parts, half = (0, len(held)), tuple(range(1, len(held)))
-            parts = tuple(len(held) + part for part in half)
-            begins = partial_grams(pieces, near_parts, steps, ())
-            begins = partial_grams(pieces, half, steps, begins)
+        if split and n >= tails:
+            parts = tuple(len(held) + part for part in received)
+            begins, sums = sums[: len(steps)], sums[len(steps) :]
+            begins = partial_grams(pieces, received, steps, begins)
         result, state = run_steps(
             taper, pieces, steps, owned, state, ready, stored, rows, members,
-            end, parts, begins,
+            n == len(work) - 1, parts, begins,
         )
     return result
 

time: 79.4 us -> 84.1 us (1.059)
  the two profiles are of different devices: /device:TPU:1 before, /device:TPU:0 now
where the time goes in v10:
time: 84.1 us; the launch traced here: 83.9 us
  waiting for transfers between devices  43 us (51%)
  starting transfers between devices  19.6 us (23%)
  Pallas kernels  19.4 us (23%)
  local copies, waits for them, and re-layouts  1.6 us (2%)
    ppermute x19, waiting for transfers between devices, shifted(): lax.ppermute(value, axis, [(i, (i + s) % count) for i in range(count)])  33.1 us
    pallas_call x7, Pallas kernels, run_steps(): pl.pallas_call(functools.partial(update_kernel, job), out_shape=shapes, i...  15.6 us
    ppermute x19, starting transfers between devices, shifted(): lax.ppermute(value, axis, [(i, (i + s) % count) for i in range(count)])  14.6 us
    ppermute x1, waiting for transfers between devices, per_device(): before = lax.ppermute(tails, 'region', down)  5.77 us
    ppermute x1, waiting for transfers between devices, per_device(): after = lax.ppermute(heads, 'region', up)  4.15 us
    ppermute x1, starting transfers between devices, per_device(): before = lax.ppermute(tails, 'region', down)  3.75 us
    pallas_call x3, Pallas kernels, cut_rows(): pl.pallas_call(functools.partial(cut_kernel, tuple((first * ROWS for firs...  1.94 us
  transfers between devices with their start and end apart: 21, of which 7 were waited for; matrix products, arithmetic and copies ran while one was open for 0% of the time, Pallas kernels for 19%

profile of v10, /device:TPU:0, one launch (start us, length us, event | category | flops | bytes accessed | tf_op | source)
XLA Modules:
  0.0 83.9 jit_solution(16835841046842093414)
XLA Ops:
  0.0 1.6 %copy-done = bf16[4096,256]{1,0:T(8,128)(2,1)S(1)} copy-done((bf16[4096,256]{1,0:T(8,128)(2,1)S(1)}, bf16[4096,256]{1,0:T(8,128)(2,1)}, u32[]{:S(2)}) %copy-start) | copy-done | bytes 2097176
  1.6 0.9 %shard_map.28 = (bf16[768,256]{1,0:T(8,128)(2,1)S(1)}, bf16[768,256]{1,0:T(8,128)(2,1)S(1)}, bf16[512,256]{1,0:T(8,128)(2,1)S(1)}, bf16[256,256]{1,0:T(8,128)(2,...) custom-call(bf16[4096,256]{1,0:T(8,128)(2,1)S(1)} %copy-done), custom_call_target="tpu_custom_call" | custom-call | bytes 6815744 | tf_op jit(solution)/shard_map/pallas_call | solution.py:240
  2.5 0.6 collective-permute-start.9
  3.1 1.0 %shard_map.31.refs_0_ = bf16[512,256]{1,0:T(8,128)(2,1)S(1)} custom-call(bf16[4096,256]{1,0:T(8,128)(2,1)} %source.5), custom_call_target="tpu_custom_call" | custom-call | bytes 524288 | tf_op jit(solution)/shard_map/pallas_call | solution.py:240
  4.1 2.6 %collective-permute-start.15 = (bf16[512,256]{1,0:T(8,128)(2,1)S(1)}, bf16[512,256]{1,0:T(8,128)(2,1)S(1)}, u32[]{:S(2)}, u32[]{:S(2)}) collective-permute-start(bf16[512,256]{1,0:T(8,128)(2,1)S(1)} %shard_map.31.refs_0_), channel_id=1, source_target_pairs={{0,2},{2,0},{1,3},{3,1},{4,6},{6,4},{5,7},{7,5},{8,10},{10,8},{9,1... | collective-permute-start | bytes 786440 | tf_op jit(solution)/shard_map/ppermute | solution.py:25
  6.8 2.0 %collective-permute-start.11 = (bf16[768,256]{1,0:T(8,128)(2,1)S(1)}, bf16[768,256]{1,0:T(8,128)(2,1)S(1)}, u32[]{:S(2)}, u32[]{:S(2)}) collective-permute-start(bf16[768,256]{1,0:T(8,128)(2,1)S(1)} %get-tuple-element.44), channel_id=1, source_target_pairs={{0,2},{2,0},{1,3},{3,1},{4,6},{6,4},{5,7},{7,5},{8,10},{10,8},{9,1... | collective-permute-start | bytes 1179656 | tf_op jit(solution)/shard_map/ppermute | solution.py:25
  8.8 4.9 %collective-permute-done.15.refs_2_.refs_1_.refs_4_ = bf16[512,256]{1,0:T(8,128)(2,1)S(1)} collective-permute-done((bf16[512,256]{1,0:T(8,128)(2,1)S(1)}, bf16[512,256]{1,0:T(8,128)(2,1)S(1)}, u32[]{:S(2)}, u32[]{:S(2)}) %collective-permute-start.15) | collective-permute-done | bytes 262176 | tf_op jit(solution)/shard_map/ppermute | solution.py:25
  13.8 2.0 %collective-permute-start.8 = (bf16[768,256]{1,0:T(8,128)(2,1)S(1)}, bf16[768,256]{1,0:T(8,128)(2,1)S(1)}, u32[]{:S(2)}, u32[]{:S(2)}) collective-permute-start(bf16[768,256]{1,0:T(8,128)(2,1)S(1)} %get-tuple-element.43), channel_id=1, source_target_pairs={{0,2},{2,0},{1,3},{3,1},{4,6},{6,4},{5,7},{7,5},{8,10},{10,8},{9,1... | collective-permute-start | bytes 1179656 | tf_op jit(solution)/shard_map/ppermute | solution.py:25
  15.8 3.6 %collective-permute-done.6.refs_1_.refs_7_.refs_2_.refs_3_ = bf16[512,256]{1,0:T(8,128)(2,1)S(1)} collective-permute-done((bf16[512,256]{1,0:T(8,128)(2,1)S(1)}, bf16[512,256]{1,0:T(8,128)(2,1)S(1)}, u32[]{:S(2)}, u32[]{:S(2)}) %collective-permute-start.6) | collective-permute-done | bytes 262176 | tf_op jit(solution)/shard_map/ppermute | solution.py:25
  19.4 2.0 %collective-permute-start.2 = (bf16[256,256]{1,0:T(8,128)(2,1)S(1)}, bf16[256,256]{1,0:T(8,128)(2,1)S(1)}, u32[]{:S(2)}, u32[]{:S(2)}) collective-permute-start(bf16[256,256]{1,0:T(8,128)(2,1)S(1)} %get-tuple-element.40), channel_id=1, source_target_pairs={{0,2},{2,0},{1,3},{3,1},{4,6},{6,4},{5,7},{7,5},{8,10},{10,8},{9,1... | collective-permute-start | bytes 393224 | tf_op jit(solution)/shard_map/ppermute | solution.py:25
  21.5 22.9 %collective-permute-done.2.refs_1_ = bf16[256,256]{1,0:T(8,128)(2,1)S(1)} collective-permute-done((bf16[256,256]{1,0:T(8,128)(2,1)S(1)}, bf16[256,256]{1,0:T(8,128)(2,1)S(1)}, u32[]{:S(2)}, u32[]{:S(2)}) %collective-permute-start.2) | collective-permute-done | bytes 131104 | tf_op jit(solution)/shard_map/ppermute | solution.py:25
  44.5 3.8 %collective-permute-start.17 = (bf16[1024,256]{1,0:T(8,128)(2,1)S(1)}, bf16[1024,256]{1,0:T(8,128)(2,1)S(1)}, u32[]{:S(2)}, u32[]{:S(2)}) collective-permute-start(bf16[1024,256]{1,0:T(8,128)(2,1)S(1)} %shard_map.36), channel_id=1, source_target_pairs={{0,4},{4,8},{8,12},{1,5},{5,9},{9,13},{2,6},{6,10},{10,14},{3,7},{... | collective-permute-start | bytes 1572872 | tf_op jit(solution)/shard_map/ppermute | solution.py:398
  48.2 1.3 %collective-permute-start.19 = (bf16[1024,256]{1,0:T(8,128)(2,1)S(1)}, bf16[1024,256]{1,0:T(8,128)(2,1)S(1)}, u32[]{:S(2)}, u32[]{:S(2)}) collective-permute-start(bf16[1024,256]{1,0:T(8,128)(2,1)S(1)} %shard_map.37), channel_id=1, source_target_pairs={{4,0},{8,4},{12,8},{5,1},{9,5},{13,9},{6,2},{10,6},{14,10},{7,3},{... | collective-permute-start | bytes 1572872 | tf_op jit(solution)/shard_map/ppermute | solution.py:396
  49.6 0.5 collective-permute-start.14
  50.1 1.0 %collective-permute-done.16.refs_4_.refs_6_ = bf16[512,256]{1,0:T(8,128)(2,1)S(1)} collective-permute-done((bf16[512,256]{1,0:T(8,128)(2,1)S(1)}, bf16[512,256]{1,0:T(8,128)(2,1)S(1)}, u32[]{:S(2)}, u32[]{:S(2)}) %collective-permute-start.16) | collective-permute-done | bytes 262176 | tf_op jit(solution)/shard_map/ppermute | solution.py:25
  51.3 0.4 collective-permute-start.10
  51.8 1.6 %collective-permute-start = (bf16[512,256]{1,0:T(8,128)(2,1)S(1)}, bf16[512,256]{1,0:T(8,128)(2,1)S(1)}, u32[]{:S(2)}, u32[]{:S(2)}) collective-permute-start(bf16[512,256]{1,0:T(8,128)(2,1)S(1)} %get-tuple-element.39), channel_id=1, source_target_pairs={{0,2},{2,0},{1,3},{3,1},{4,6},{6,4},{5,7},{7,5},{8,10},{10,8},{9,1... | collective-permute-start | bytes 786440 | tf_op jit(solution)/shard_map/ppermute | solution.py:25
  53.4 5.8 %collective-permute-done.17.refs_1_ = bf16[1024,256]{1,0:T(8,128)(2,1)S(1)} collective-permute-done((bf16[1024,256]{1,0:T(8,128)(2,1)S(1)}, bf16[1024,256]{1,0:T(8,128)(2,1)S(1)}, u32[]{:S(2)}, u32[]{:S(2)}) %collective-permute-start.17) | collective-permute-done | bytes 524320 | tf_op jit(solution)/shard_map/ppermute | solution.py:398
  59.2 4.2 %collective-permute-done.19.refs_9_ = bf16[1024,256]{1,0:T(8,128)(2,1)S(1)} collective-permute-done((bf16[1024,256]{1,0:T(8,128)(2,1)S(1)}, bf16[1024,256]{1,0:T(8,128)(2,1)S(1)}, u32[]{:S(2)}, u32[]{:S(2)}) %collective-permute-start.19) | collective-permute-done | bytes 524320 | tf_op jit(solution)/shard_map/ppermute | solution.py:396
  63.3 2.5 %shard_map.32 = (f32[256,256]{1,0:T(8,128)S(1)}, f32[256,256]{1,0:T(8,128)S(1)}, f32[256,256]{1,0:T(8,128)S(1)}, f32[256,256]{1,0:T(8,128)S(1)}) custom-call(f32[9,32]{1,0:T(8,128)S(1)} %bitcast.1, bf16[4096,256]{1,0:T(8,128)(2,1)S(1)} %get-tuple-element.38.refs_1_.refs_3_.refs_0_, bf16[512,256]{1,0:T(8,128)(2,1)S(1)} %collective-permute-done.15.refs_2_.refs_1_.refs_4_, ...), custom_call_target="tpu_custom_call" | custom-call | flops 1811939328 | bytes 2097152 | tf_op jit(solution)/shard_map/pallas_call | solution.py:342
  65.9 0.6 collective-permute-start.7
  66.5 2.4 %shard_map.33 = (bf16[3,256,256]{2,1,0:T(8,128)(2,1)S(1)}, f32[256,256]{1,0:T(8,128)S(1)}, f32[256,256]{1,0:T(8,128)S(1)}) custom-call(f32[9,32]{1,0:T(8,128)S(1)} %bitcast.2, bf16[4096,256]{1,0:T(8,128)(2,1)S(1)} %get-tuple-element.38.refs_1_.refs_3_.refs_0_, bf16[512,256]{1,0:T(8,128)(2,1)S(1)} %collective-permute-done.13.refs_5_.refs_2_, ...), custom_call_target="tpu_custom_call" | custom-call | flops 1811939328 | bytes 3801088 | tf_op jit(solution)/shard_map/pallas_call | solution.py:342
  68.9 1.6 %collective-permute-start.4 = (bf16[256,256]{1,0:T(8,128)(2,1)S(1)}, bf16[256,256]{1,0:T(8,128)(2,1)S(1)}, u32[]{:S(2)}, u32[]{:S(2)}) collective-permute-start(bf16[256,256]{1,0:T(8,128)(2,1)S(1)} %get-tuple-element.41), channel_id=1, source_target_pairs={{0,2},{2,0},{1,3},{3,1},{4,6},{6,4},{5,7},{7,5},{8,10},{10,8},{9,1... | collective-permute-start | bytes 393224 | tf_op jit(solution)/shard_map/ppermute | solution.py:25
  70.5 2.4 %shard_map.34 = (bf16[3,256,256]{2,1,0:T(8,128)(2,1)S(1)}, f32[256,256]{1,0:T(8,128)S(1)}, f32[256,256]{1,0:T(8,128)S(1)}) custom-call(f32[9,32]{1,0:T(8,128)S(1)} %bitcast.3, bf16[4096,256]{1,0:T(8,128)(2,1)S(1)} %get-tuple-element.38.refs_1_.refs_3_.refs_0_, bf16[768,256]{1,0:T(8,128)(2,1)S(1)} %collective-permute-done.11.refs_5_.refs_2_, ...), custom_call_target="tpu_custom_call" | custom-call | flops 1811939328 | bytes 3801088 | tf_op jit(solution)/shard_map/pallas_call | solution.py:342
  72.9 0.9 %shard_map.39 = (f32[768,256]{1,0:T(8,128)S(1)}, f32[256,256]{1,0:T(8,128)S(1)}, f32[1280,256]{1,0:T(8,128)S(1)}) custom-call(bf16[4096,256]{1,0:T(8,128)(2,1)S(1)} %get-tuple-element.38.refs_1_.refs_3_.refs_0_, bf16[4096,256]{1,0:T(8,128)(2,1)S(1)} %shard_map.30.refs_3_.refs_5_.refs_1_), custom_call_target="tpu_custom_call" | custom-call | flops 603979776 | bytes 2359296 | tf_op jit(solution)/shard_map/pallas_call | solution.py:86
  73.8 0.6 collective-permute-done.4.refs_2_
  74.4 0.5 collective-permute-start.5
  74.9 3.0 %shard_map.38 = (bf16[2,256,256]{2,1,0:T(8,128)(2,1)S(1)}, f32[256,256]{1,0:T(8,128)S(1)}, f32[256,256]{1,0:T(8,128)S(1)}) custom-call(f32[9,32]{1,0:T(8,128)S(1)} %bitcast.4, bf16[1024,256]{1,0:T(8,128)(2,1)S(1)} %collective-permute-done.17.refs_1_, bf16[1024,256]{1,0:T(8,128)(2,1)S(1)} %collective-permute-done.18.refs_2_, ...), custom_call_target="tpu_custom_call" | custom-call | flops 1811939328 | bytes 4980736 | tf_op jit(solution)/shard_map/pallas_call | solution.py:342
  78.2 0.4 shard_map.42.refs_10_
  78.6 1.7 %shard_map.35 = (bf16[2,256,256]{2,1,0:T(8,128)(2,1)S(1)}, f32[256,256]{1,0:T(8,128)S(1)}, f32[256,256]{1,0:T(8,128)S(1)}) custom-call(f32[9,32]{1,0:T(8,128)S(1)} %bitcast.5, bf16[4096,256]{1,0:T(8,128)(2,1)S(1)} %get-tuple-element.38.refs_1_.refs_3_.refs_0_, bf16[768,256]{1,0:T(8,128)(2,1)S(1)} %collective-permute-done.8.refs_5_.refs_2_, ...), custom_call_target="tpu_custom_call" | custom-call | flops 1207959552 | bytes 2883584 | tf_op jit(solution)/shard_map/pallas_call | solution.py:342
  80.4 1.2 %shard_map.41 = (bf16[1,256,256]{2,1,0:T(8,128)(2,1)S(1)}, f32[256,256]{1,0:T(8,128)S(1)}, f32[256,256]{1,0:T(8,128)S(1)}, f32[256,256]{1,0:T(8,128)S(1)}) custom-call(f32[9,32]{1,0:T(8,128)S(1)} %bitcast.6, bf16[4096,256]{1,0:T(8,128)(2,1)S(1)} %get-tuple-element.38.refs_1_.refs_3_.refs_0_, bf16[512,256]{1,0:T(8,128)(2,1)S(1)} %collective-permute-done.1.refs_6_.refs_2_, ...), custom_call_target="tpu_custom_call" | custom-call | flops 402653184 | bytes 1441792 | tf_op jit(solution)/shard_map/pallas_call | solution.py:342
  81.6 2.3 %shard_map.43 = bf16[4096,256]{1,0:T(8,128)(2,1)} custom-call(f32[9,32]{1,0:T(8,128)S(1)} %bitcast.7, bf16[4096,256]{1,0:T(8,128)(2,1)S(1)} %get-tuple-element.38.refs_1_.refs_3_.refs_0_, bf16[512,256]{1,0:T(8,128)(2,1)S(1)} %collective-permute-done.1.refs_6_.refs_2_, bf16[256,256]{1,0:T(8,128)(2,1)S(1)} %collective-permute-done.3.refs_3_, ...), custom_call_target="tpu_custom_call" | custom-call | flops 503316480 | bytes 3276800 | tf_op jit(solution)/shard_map/pallas_call | solution.py:342
  (32 shorter events, 1.1 us)
Async XLA Ops:
  0.0 1.6 %copy-start = (bf16[4096,256]{1,0:T(8,128)(2,1)S(1)}, bf16[4096,256]{1,0:T(8,128)(2,1)}, u32[]{:S(2)}) copy-start(bf16[4096,256]{1,0:T(8,128)(2,1)} %source.5) | copy-start | bytes 6291460
  1.6 5.0 %copy-start.1 = (bf16[4096,256]{1,0:T(8,128)(2,1)S(1)}, bf16[4096,256]{1,0:T(8,128)(2,1)}, u32[]{:S(2)}) copy-start(bf16[4096,256]{1,0:T(8,128)(2,1)} %source.5) | copy-start | bytes 6291460
  2.5 48.8 %collective-permute-start.9 = (bf16[4096,256]{1,0:T(8,128)(2,1)S(1)}, bf16[4096,256]{1,0:T(8,128)(2,1)S(1)}, u32[]{:S(2)}, u32[]{:S(2)}) collective-permute-start(bf16[4096,256]{1,0:T(8,128)(2,1)S(1)} %get-tuple-element.38.refs_1_.refs_3_.refs_0_), channel_id=1, source_target_pairs={{0,1},{1,0},{2,3},{3,2},{4,5},{5,4},{6,7},{7,6},{8,9},{9,8},{10,11... | collective-permute-start | bytes 6291464 | tf_op jit(solution)/shard_map/ppermute | solution.py:25
  4.1 9.7 %collective-permute-start.15 = (bf16[512,256]{1,0:T(8,128)(2,1)S(1)}, bf16[512,256]{1,0:T(8,128)(2,1)S(1)}, u32[]{:S(2)}, u32[]{:S(2)}) collective-permute-start(bf16[512,256]{1,0:T(8,128)(2,1)S(1)} %shard_map.31.refs_0_), channel_id=1, source_target_pairs={{0,2},{2,0},{1,3},{3,1},{4,6},{6,4},{5,7},{7,5},{8,10},{10,8},{9,1... | collective-permute-start | bytes 786440 | tf_op jit(solution)/shard_map/ppermute | solution.py:25
  6.7 12.7 %collective-permute-start.6 = (bf16[512,256]{1,0:T(8,128)(2,1)S(1)}, bf16[512,256]{1,0:T(8,128)(2,1)S(1)}, u32[]{:S(2)}, u32[]{:S(2)}) collective-permute-start(bf16[512,256]{1,0:T(8,128)(2,1)S(1)} %get-tuple-element.42.refs_0_), channel_id=1, source_target_pairs={{0,2},{2,0},{1,3},{3,1},{4,6},{6,4},{5,7},{7,5},{8,10},{10,8},{9,1... | collective-permute-start | bytes 786440 | tf_op jit(solution)/shard_map/ppermute | solution.py:25
  6.8 42.8 %collective-permute-start.11 = (bf16[768,256]{1,0:T(8,128)(2,1)S(1)}, bf16[768,256]{1,0:T(8,128)(2,1)S(1)}, u32[]{:S(2)}, u32[]{:S(2)}) collective-permute-start(bf16[768,256]{1,0:T(8,128)(2,1)S(1)} %get-tuple-element.44), channel_id=1, source_target_pairs={{0,2},{2,0},{1,3},{3,1},{4,6},{6,4},{5,7},{7,5},{8,10},{10,8},{9,1... | collective-permute-start | bytes 1179656 | tf_op jit(solution)/shard_map/ppermute | solution.py:25
  8.8 39.5 %collective-permute-start.13 = (bf16[512,256]{1,0:T(8,128)(2,1)S(1)}, bf16[512,256]{1,0:T(8,128)(2,1)S(1)}, u32[]{:S(2)}, u32[]{:S(2)}) collective-permute-start(bf16[512,256]{1,0:T(8,128)(2,1)S(1)} %get-tuple-element.45), channel_id=1, source_target_pairs={{0,2},{2,0},{1,3},{3,1},{4,6},{6,4},{5,7},{7,5},{8,10},{10,8},{9,1... | collective-permute-start | bytes 786440 | tf_op jit(solution)/shard_map/ppermute | solution.py:25
  13.8 35.9 %collective-permute-start.8 = (bf16[768,256]{1,0:T(8,128)(2,1)S(1)}, bf16[768,256]{1,0:T(8,128)(2,1)S(1)}, u32[]{:S(2)}, u32[]{:S(2)}) collective-permute-start(bf16[768,256]{1,0:T(8,128)(2,1)S(1)} %get-tuple-element.43), channel_id=1, source_target_pairs={{0,2},{2,0},{1,3},{3,1},{4,6},{6,4},{5,7},{7,5},{8,10},{10,8},{9,1... | collective-permute-start | bytes 1179656 | tf_op jit(solution)/shard_map/ppermute | solution.py:25
  19.4 25.1 %collective-permute-start.2 = (bf16[256,256]{1,0:T(8,128)(2,1)S(1)}, bf16[256,256]{1,0:T(8,128)(2,1)S(1)}, u32[]{:S(2)}, u32[]{:S(2)}) collective-permute-start(bf16[256,256]{1,0:T(8,128)(2,1)S(1)} %get-tuple-element.40), channel_id=1, source_target_pairs={{0,2},{2,0},{1,3},{3,1},{4,6},{6,4},{5,7},{7,5},{8,10},{10,8},{9,1... | collective-permute-start | bytes 393224 | tf_op jit(solution)/shard_map/ppermute | solution.py:25
  21.5 41.8 %copy-start.2 = (f32[32,9]{0,1:T(8,128)S(1)}, f32[32,9]{0,1:T(8,128)}, u32[]{:S(2)}) copy-start(f32[32,9]{0,1:T(8,128)} %param.3) | copy-start | bytes 3460
  44.5 14.7 %collective-permute-start.17 = (bf16[1024,256]{1,0:T(8,128)(2,1)S(1)}, bf16[1024,256]{1,0:T(8,128)(2,1)S(1)}, u32[]{:S(2)}, u32[]{:S(2)}) collective-permute-start(bf16[1024,256]{1,0:T(8,128)(2,1)S(1)} %shard_map.36), channel_id=1, source_target_pairs={{0,4},{4,8},{8,12},{1,5},{5,9},{9,13},{2,6},{6,10},{10,14},{3,7},{... | collective-permute-start | bytes 1572872 | tf_op jit(solution)/shard_map/ppermute | solution.py:398
  48.2 15.1 %collective-permute-start.19 = (bf16[1024,256]{1,0:T(8,128)(2,1)S(1)}, bf16[1024,256]{1,0:T(8,128)(2,1)S(1)}, u32[]{:S(2)}, u32[]{:S(2)}) collective-permute-start(bf16[1024,256]{1,0:T(8,128)(2,1)S(1)} %shard_map.37), channel_id=1, source_target_pairs={{4,0},{8,4},{12,8},{5,1},{9,5},{13,9},{6,2},{10,6},{14,10},{7,3},{... | collective-permute-start | bytes 1572872 | tf_op jit(solution)/shard_map/ppermute | solution.py:396
  49.6 1.6 %collective-permute-start.16 = (bf16[512,256]{1,0:T(8,128)(2,1)S(1)}, bf16[512,256]{1,0:T(8,128)(2,1)S(1)}, u32[]{:S(2)}, u32[]{:S(2)}) collective-permute-start(bf16[512,256]{1,0:T(8,128)(2,1)S(1)} %collective-permute-done.15.refs_2_.refs_1_.refs_4_), channel_id=1, source_target_pairs={{0,1},{1,0},{2,3},{3,2},{4,5},{5,4},{6,7},{7,6},{8,9},{9,8},{10,11... | collective-permute-start | bytes 786440 | tf_op jit(solution)/shard_map/ppermute | solution.py:25
  49.6 2.2 %collective-permute-start.14 = (bf16[512,256]{1,0:T(8,128)(2,1)S(1)}, bf16[512,256]{1,0:T(8,128)(2,1)S(1)}, u32[]{:S(2)}, u32[]{:S(2)}) collective-permute-start(bf16[512,256]{1,0:T(8,128)(2,1)S(1)} %collective-permute-done.13.refs_5_.refs_2_), channel_id=1, source_target_pairs={{0,1},{1,0},{2,3},{3,2},{4,5},{5,4},{6,7},{7,6},{8,9},{9,8},{10,11... | collective-permute-start | bytes 786440 | tf_op jit(solution)/shard_map/ppermute | solution.py:25
  51.2 14.7 %collective-permute-start.12 = (bf16[768,256]{1,0:T(8,128)(2,1)S(1)}, bf16[768,256]{1,0:T(8,128)(2,1)S(1)}, u32[]{:S(2)}, u32[]{:S(2)}) collective-permute-start(bf16[768,256]{1,0:T(8,128)(2,1)S(1)} %collective-permute-done.11.refs_5_.refs_2_), channel_id=1, source_target_pairs={{0,1},{1,0},{2,3},{3,2},{4,5},{5,4},{6,7},{7,6},{8,9},{9,8},{10,11... | collective-permute-start | bytes 1179656 | tf_op jit(solution)/shard_map/ppermute | solution.py:25
  51.3 19.2 %collective-permute-start.10 = (bf16[768,256]{1,0:T(8,128)(2,1)S(1)}, bf16[768,256]{1,0:T(8,128)(2,1)S(1)}, u32[]{:S(2)}, u32[]{:S(2)}) collective-permute-start(bf16[768,256]{1,0:T(8,128)(2,1)S(1)} %collective-permute-done.8.refs_5_.refs_2_), channel_id=1, source_target_pairs={{0,1},{1,0},{2,3},{3,2},{4,5},{5,4},{6,7},{7,6},{8,9},{9,8},{10,11... | collective-permute-start | bytes 1179656 | tf_op jit(solution)/shard_map/ppermute | solution.py:25
  51.8 17.1 %collective-permute-start = (bf16[512,256]{1,0:T(8,128)(2,1)S(1)}, bf16[512,256]{1,0:T(8,128)(2,1)S(1)}, u32[]{:S(2)}, u32[]{:S(2)}) collective-permute-start(bf16[512,256]{1,0:T(8,128)(2,1)S(1)} %get-tuple-element.39), channel_id=1, source_target_pairs={{0,2},{2,0},{1,3},{3,1},{4,6},{6,4},{5,7},{7,5},{8,10},{10,8},{9,1... | collective-permute-start | bytes 786440 | tf_op jit(solution)/shard_map/ppermute | solution.py:25
  59.2 15.8 %collective-permute-start.18 = (bf16[1024,256]{1,0:T(8,128)(2,1)S(1)}, bf16[1024,256]{1,0:T(8,128)(2,1)S(1)}, u32[]{:S(2)}, u32[]{:S(2)}) collective-permute-start(bf16[1024,256]{1,0:T(8,128)(2,1)S(1)} %collective-permute-done.17.refs_1_), channel_id=1, source_target_pairs={{0,1},{1,0},{2,3},{3,2},{4,5},{5,4},{6,7},{7,6},{8,9},{9,8},{10,11... | collective-permute-start | bytes 1572872 | tf_op jit(solution)/shard_map/ppermute | solution.py:25
  63.3 11.6 %collective-permute-start.20 = (bf16[1024,256]{1,0:T(8,128)(2,1)S(1)}, bf16[1024,256]{1,0:T(8,128)(2,1)S(1)}, u32[]{:S(2)}, u32[]{:S(2)}) collective-permute-start(bf16[1024,256]{1,0:T(8,128)(2,1)S(1)} %collective-permute-done.19.refs_9_), channel_id=1, source_target_pairs={{0,1},{1,0},{2,3},{3,2},{4,5},{5,4},{6,7},{7,6},{8,9},{9,8},{10,11... | collective-permute-start | bytes 1572872 | tf_op jit(solution)/shard_map/ppermute | solution.py:25
  65.9 8.5 %collective-permute-start.7 = (bf16[512,256]{1,0:T(8,128)(2,1)S(1)}, bf16[512,256]{1,0:T(8,128)(2,1)S(1)}, u32[]{:S(2)}, u32[]{:S(2)}) collective-permute-start(bf16[512,256]{1,0:T(8,128)(2,1)S(1)} %collective-permute-done.6.refs_1_.refs_7_.refs_2_.refs_3_), channel_id=1, source_target_pairs={{0,1},{1,0},{2,3},{3,2},{4,5},{5,4},{6,7},{7,6},{8,9},{9,8},{10,11... | collective-permute-start | bytes 786440 | tf_op jit(solution)/shard_map/ppermute | solution.py:25
  68.9 5.5 %collective-permute-start.4 = (bf16[256,256]{1,0:T(8,128)(2,1)S(1)}, bf16[256,256]{1,0:T(8,128)(2,1)S(1)}, u32[]{:S(2)}, u32[]{:S(2)}) collective-permute-start(bf16[256,256]{1,0:T(8,128)(2,1)S(1)} %get-tuple-element.41), channel_id=1, source_target_pairs={{0,2},{2,0},{1,3},{3,1},{4,6},{6,4},{5,7},{7,5},{8,10},{10,8},{9,1... | collective-permute-start | bytes 393224 | tf_op jit(solution)/shard_map/ppermute | solution.py:25
  70.5 8.2 %collective-permute-start.1 = (bf16[512,256]{1,0:T(8,128)(2,1)S(1)}, bf16[512,256]{1,0:T(8,128)(2,1)S(1)}, u32[]{:S(2)}, u32[]{:S(2)}) collective-permute-start(bf16[512,256]{1,0:T(8,128)(2,1)S(1)} %collective-permute-done.refs_5_.refs_0_), channel_id=1, source_target_pairs={{0,1},{1,0},{2,3},{3,2},{4,5},{5,4},{6,7},{7,6},{8,9},{9,8},{10,11... | collective-permute-start | bytes 786440 | tf_op jit(solution)/shard_map/ppermute | solution.py:25
  74.4 6.0 %collective-permute-start.3 = (bf16[256,256]{1,0:T(8,128)(2,1)S(1)}, bf16[256,256]{1,0:T(8,128)(2,1)S(1)}, u32[]{:S(2)}, u32[]{:S(2)}) collective-permute-start(bf16[256,256]{1,0:T(8,128)(2,1)S(1)} %collective-permute-done.2.refs_1_), channel_id=1, source_target_pairs={{0,1},{1,0},{2,3},{3,2},{4,5},{5,4},{6,7},{7,6},{8,9},{9,8},{10,11... | collective-permute-start | bytes 393224 | tf_op jit(solution)/shard_map/ppermute | solution.py:25
  74.4 7.2 %collective-permute-start.5 = (bf16[256,256]{1,0:T(8,128)(2,1)S(1)}, bf16[256,256]{1,0:T(8,128)(2,1)S(1)}, u32[]{:S(2)}, u32[]{:S(2)}) collective-permute-start(bf16[256,256]{1,0:T(8,128)(2,1)S(1)} %collective-permute-done.4.refs_2_), channel_id=1, source_target_pairs={{0,1},{1,0},{2,3},{3,2},{4,5},{5,4},{6,7},{7,6},{8,9},{9,8},{10,11... | collective-permute-start | bytes 393224 | tf_op jit(solution)/shard_map/ppermute | solution.py:25

commit v11 on v9

--- a/solution.py
+++ b/solution.py
@@ -112,8 +112,9 @@
     begins = refs[1 + arrays + len(acc_in) : job["earlier"]]
     earlier = refs[job["earlier"] : job["operands"]]
     outs = refs[job["operands"] :]
-    if job["last"]:
-        out, acc, obuf, out_sem = outs[0], *outs[-3:]
+    sent = []
+    if job["writer"]:
+        out, outs, out_sem = outs[0], outs[1:-1], outs[-1]
         sent = [
             pltpu.make_async_copy(
                 earlier[array].at[n], out.at[tile_rows(pair)], out_sem.at[len(finished) + k]
@@ -122,10 +123,11 @@
         ]
         for copy in sent:
             copy.start()
-    else:
-        outs, acc = outs[:-1], outs[-1]
-        if finished:
-            obuf, outs = outs[0], outs[1:]
+    if job["last"]:
+        obuf, outs = outs[-1], outs[:-1]
+    acc, outs = outs[-1], outs[:-1]
+    if finished and not job["last"]:
+        obuf, outs = outs[0], outs[1:]
     carried = outs
     sums = {pair: carried[n] for n, pair in enumerate(acc_out)}
     sums |= {pair: acc.at[n] for n, pair in enumerate(finished)}
@@ -209,9 +211,8 @@
         finish([pair for pair in ready if pair == j])
 
     finish([pair for pair in finished if pair not in settled])
-    if job["last"]:
-        for copy in sent:
-            copy.wait()
+    for copy in sent:
+        copy.wait()
 
 
 def stage_kernel(source, target, sem):
@@ -294,7 +295,8 @@
 
 
 def run_steps(
-    taper, pieces, steps, owned, state, finished, stored, rows, members, last, parts=None, begins=()
+    taper, pieces, steps, owned, state, finished, stored, rows, members, last, parts=None, begins=(),
+    writer=False, result=None,
 ):
     parts = tuple(range(len(pieces))) if parts is None else parts
     needed = touched_by(steps) | set(finished)
@@ -308,36 +310,44 @@
     acc_out = sorted(touched - set(finished))
     arrays, plan = planned(pieces, sorted(set(parts) | {0}), needed)
     writes = []
-    if last:
+    writer = writer or last
+    if writer:
         for array, (pairs, _) in enumerate(stored):
             writes += [(array, n, pair) for n, pair in enumerate(pairs)]
     operands = [taper.T] + arrays + [state[pair] for pair in acc_in] + list(begins)
     earlier = len(operands)
-    if last:
+    aliases = {}
+    if writer:
         operands += [block for _, block in stored]
+        stored.clear()
+        if result is not None:
+            aliases = {len(operands): 0}
+            operands.append(result)
     job = dict(
         parts=parts, plan=plan, steps=steps, owned=owned, acc_in=acc_in, acc_out=acc_out,
         finished=finished, arrays=len(arrays), writes=writes, operands=len(operands),
         earlier=earlier,
-        last=last,
+        last=last, writer=writer,
     )
     inside = pl.BlockSpec(memory_space=pltpu.VMEM)
-    specs = [inside] * len(operands)
+    specs = [pl.BlockSpec(memory_space=pl.ANY) if n in aliases else inside for n in range(len(operands))]
     products = sum(n for _, _, n in steps)
     count = max(len(finished), 1)
     carries = [jax.ShapeDtypeStruct((ROWS, members), jnp.float32)] * len(acc_out)
     block = (len(finished), ROWS, members)
     scratch = [pltpu.VMEM((count, ROWS, members), jnp.float32)]
+    shapes, out_specs = [], []
+    if writer:
+        shapes.append(jax.ShapeDtypeStruct((rows, members), jnp.bfloat16))
+        out_specs.append(pl.BlockSpec(memory_space=pl.ANY))
     if last:
-        shapes = [jax.ShapeDtypeStruct((rows, members), jnp.bfloat16)]
-        out_specs = [pl.BlockSpec(memory_space=pl.ANY)]
-        scratch += [
-            pltpu.VMEM(block, jnp.bfloat16),
-            pltpu.SemaphoreType.DMA((len(finished) + len(writes),)),
-        ]
+        scratch.append(pltpu.VMEM(block, jnp.bfloat16))
     else:
-        shapes = [jax.ShapeDtypeStruct(block, jnp.bfloat16)] * int(bool(finished)) + carries
-        out_specs = [inside] * len(shapes)
+        held_here = [jax.ShapeDtypeStruct(block, jnp.bfloat16)] * int(bool(finished)) + carries
+        shapes += held_here
+        out_specs += [inside] * len(held_here)
+    if writer:
+        scratch.append(pltpu.SemaphoreType.DMA((len(finished) + len(writes),)))
     scratch += [pltpu.SMEM(operands[0].shape, jnp.float32), pltpu.SemaphoreType.DMA]
     outputs = pl.pallas_call(
         functools.partial(update_kernel, job),
@@ -345,6 +355,7 @@
         in_specs=specs,
         out_specs=out_specs,
         scratch_shapes=scratch,
+        input_output_aliases=aliases,
         compiler_params=pltpu.CompilerParams(vmem_limit_bytes=VMEM_LIMIT),
         cost_estimate=pl.CostEstimate(
             flops=2 * products * ROWS * ROWS * members * (len(parts) + 2),
@@ -352,8 +363,10 @@
             transcendentals=0,
         ),
     )(*operands)
+    if writer:
+        result, outputs = outputs[0], outputs[1:]
     if last:
-        return outputs[0], state
+        return result, state
     if finished:
         stored.append((finished, outputs[0]))
         outputs = outputs[1:]
@@ -361,7 +374,7 @@
     state.update(zip(acc_out, outputs))
     for pair in finished:
         state.pop(pair, None)
-    return None, state
+    return result, state
 
 
 def chunk_bounds(pairs):
@@ -426,7 +439,7 @@
             pieces.append({pair: (passed(array), n) for pair, (array, n) in listed.items()})
 
     owned = set(range(pairs))
-    state, stored = {}, []
+    state, stored, result = {}, [], None
 
     def steps_for(fresh, before):
         there, steps = set(before), []
@@ -462,7 +475,7 @@
             begins = partial_grams(pieces, half, steps, begins)
         result, state = run_steps(
             taper, pieces, steps, owned, state, ready, stored, rows, members,
-            end, parts, begins,
+            end, parts, begins, n >= len(batches) - 3, result,
         )
     return result
 

time: 79.4 us -> 67.6 us (0.85)
  the two profiles are of different devices: /device:TPU:1 before, /device:TPU:0 now
where the time goes in v11:
time: 67.6 us; the launch traced here: 67.4 us
  waiting for transfers between devices  29 us (43%)
  starting transfers between devices  18.6 us (28%)
  Pallas kernels  18.1 us (27%)
  local copies, waits for them, and re-layouts  1.59 us (2%)
    ppermute x17, waiting for transfers between devices, shifted(): lax.ppermute(value, axis, [(i, (i + s) % count) for i in range(count)])  29 us
    pallas_call x6, Pallas kernels, run_steps(): pl.pallas_call(functools.partial(update_kernel, job), out_shape=shapes, i...  14.7 us
    ppermute x17, starting transfers between devices, shifted(): lax.ppermute(value, axis, [(i, (i + s) % count) for i in range(count)])  13.2 us
    ppermute x1, starting transfers between devices, per_device(): before = lax.ppermute(tails, 'region', down)  4.04 us
    pallas_call x3, Pallas kernels, cut_rows(): pl.pallas_call(functools.partial(cut_kernel, tuple((first * ROWS for firs...  1.61 us
    unnamed x4, local copies, waits for them, and re-layouts  1.59 us
    pallas_call x2, Pallas kernels, partial_grams(): pl.pallas_call(functools.partial(partial_kernel, parts, plan, steps, len(...  1.51 us
  transfers between devices with their start and end apart: 19, of which 7 were waited for; matrix products, arithmetic and copies ran while one was open for 0% of the time, Pallas kernels for 22%

profile of v11, /device:TPU:0, one launch (start us, length us, event | category | flops | bytes accessed | tf_op | source)
XLA Modules:
  0.0 67.4 jit_solution(3972578907017918848)
XLA Ops:
  0.0 1.6 %copy-done = bf16[4096,256]{1,0:T(8,128)(2,1)S(1)} copy-done((bf16[4096,256]{1,0:T(8,128)(2,1)S(1)}, bf16[4096,256]{1,0:T(8,128)(2,1)}, u32[]{:S(2)}) %copy-start) | copy-done | bytes 2097176
  1.6 0.6 shard_map.28
  2.2 0.6 collective-permute-start.7
  2.8 2.6 %collective-permute-start.4 = (bf16[512,256]{1,0:T(8,128)(2,1)S(1)}, bf16[512,256]{1,0:T(8,128)(2,1)S(1)}, u32[]{:S(2)}, u32[]{:S(2)}) collective-permute-start(bf16[512,256]{1,0:T(8,128)(2,1)S(1)} %get-tuple-element.39.refs_0_), channel_id=1, source_target_pairs={{0,2},{2,0},{1,3},{3,1},{4,6},{6,4},{5,7},{7,5},{8,10},{10,8},{9,1... | collective-permute-start | bytes 786440 | tf_op jit(solution)/shard_map/ppermute | solution.py:25
  5.4 1.0 %shard_map.31.refs_0_ = bf16[512,256]{1,0:T(8,128)(2,1)S(1)} custom-call(bf16[4096,256]{1,0:T(8,128)(2,1)} %source.5), custom_call_target="tpu_custom_call" | custom-call | bytes 524288 | tf_op jit(solution)/shard_map/pallas_call | solution.py:241
  6.3 0.1 collective-permute-start.13
  6.4 2.0 %collective-permute-start.11 = (bf16[512,256]{1,0:T(8,128)(2,1)S(1)}, bf16[512,256]{1,0:T(8,128)(2,1)S(1)}, u32[]{:S(2)}, u32[]{:S(2)}) collective-permute-start(bf16[512,256]{1,0:T(8,128)(2,1)S(1)} %get-tuple-element.42), channel_id=1, source_target_pairs={{0,2},{2,0},{1,3},{3,1},{4,6},{6,4},{5,7},{7,5},{8,10},{10,8},{9,1... | collective-permute-start | bytes 786440 | tf_op jit(solution)/shard_map/ppermute | solution.py:25
  8.5 4.0 %collective-permute-done.4.refs_1_.refs_7_.refs_2_ = bf16[512,256]{1,0:T(8,128)(2,1)S(1)} collective-permute-done((bf16[512,256]{1,0:T(8,128)(2,1)S(1)}, bf16[512,256]{1,0:T(8,128)(2,1)S(1)}, u32[]{:S(2)}, u32[]{:S(2)}) %collective-permute-start.4) | collective-permute-done | bytes 262176 | tf_op jit(solution)/shard_map/ppermute | solution.py:25
  12.6 4.0 %collective-permute-start.15 = (bf16[1024,256]{1,0:T(8,128)(2,1)S(1)}, bf16[1024,256]{1,0:T(8,128)(2,1)S(1)}, u32[]{:S(2)}, u32[]{:S(2)}) collective-permute-start(bf16[1024,256]{1,0:T(8,128)(2,1)S(1)} %shard_map.34), channel_id=1, source_target_pairs={{0,4},{4,8},{8,12},{1,5},{5,9},{9,13},{2,6},{6,10},{10,14},{3,7},{... | collective-permute-start | bytes 1572872 | tf_op jit(solution)/shard_map/ppermute | solution.py:411
  16.6 1.5 %collective-permute-done.13.refs_2_.refs_1_.refs_4_ = bf16[512,256]{1,0:T(8,128)(2,1)S(1)} collective-permute-done((bf16[512,256]{1,0:T(8,128)(2,1)S(1)}, bf16[512,256]{1,0:T(8,128)(2,1)S(1)}, u32[]{:S(2)}, u32[]{:S(2)}) %collective-permute-start.13) | collective-permute-done | bytes 262176 | tf_op jit(solution)/shard_map/ppermute | solution.py:25
  18.2 1.3 %collective-permute-start.17 = (bf16[1024,256]{1,0:T(8,128)(2,1)S(1)}, bf16[1024,256]{1,0:T(8,128)(2,1)S(1)}, u32[]{:S(2)}, u32[]{:S(2)}) collective-permute-start(bf16[1024,256]{1,0:T(8,128)(2,1)S(1)} %shard_map.35), channel_id=1, source_target_pairs={{4,0},{8,4},{12,8},{5,1},{9,5},{13,9},{6,2},{10,6},{14,10},{7,3},{... | collective-permute-start | bytes 1572872 | tf_op jit(solution)/shard_map/ppermute | solution.py:409
  19.5 4.3 %collective-permute-done.11.refs_5_.refs_2_ = bf16[512,256]{1,0:T(8,128)(2,1)S(1)} collective-permute-done((bf16[512,256]{1,0:T(8,128)(2,1)S(1)}, bf16[512,256]{1,0:T(8,128)(2,1)S(1)}, u32[]{:S(2)}, u32[]{:S(2)}) %collective-permute-start.11) | collective-permute-done | bytes 262176 | tf_op jit(solution)/shard_map/ppermute | solution.py:25
  23.8 2.0 %collective-permute-start.6 = (bf16[768,256]{1,0:T(8,128)(2,1)S(1)}, bf16[768,256]{1,0:T(8,128)(2,1)S(1)}, u32[]{:S(2)}, u32[]{:S(2)}) collective-permute-start(bf16[768,256]{1,0:T(8,128)(2,1)S(1)} %get-tuple-element.40), channel_id=1, source_target_pairs={{0,2},{2,0},{1,3},{3,1},{4,6},{6,4},{5,7},{7,5},{8,10},{10,8},{9,1... | collective-permute-start | bytes 1179656 | tf_op jit(solution)/shard_map/ppermute | solution.py:25
  25.8 3.6 %collective-permute-done.refs_5_.refs_0_ = bf16[512,256]{1,0:T(8,128)(2,1)S(1)} collective-permute-done((bf16[512,256]{1,0:T(8,128)(2,1)S(1)}, bf16[512,256]{1,0:T(8,128)(2,1)S(1)}, u32[]{:S(2)}, u32[]{:S(2)}) %collective-permute-start) | collective-permute-done | bytes 262176 | tf_op jit(solution)/shard_map/ppermute | solution.py:25
  29.4 2.0 %collective-permute-start.9 = (bf16[768,256]{1,0:T(8,128)(2,1)S(1)}, bf16[768,256]{1,0:T(8,128)(2,1)S(1)}, u32[]{:S(2)}, u32[]{:S(2)}) collective-permute-start(bf16[768,256]{1,0:T(8,128)(2,1)S(1)} %get-tuple-element.41), channel_id=1, source_target_pairs={{0,2},{2,0},{1,3},{3,1},{4,6},{6,4},{5,7},{7,5},{8,10},{10,8},{9,1... | collective-permute-start | bytes 1179656 | tf_op jit(solution)/shard_map/ppermute | solution.py:25
  31.4 6.4 %collective-permute-done.6.refs_5_.refs_2_ = bf16[768,256]{1,0:T(8,128)(2,1)S(1)} collective-permute-done((bf16[768,256]{1,0:T(8,128)(2,1)S(1)}, bf16[768,256]{1,0:T(8,128)(2,1)S(1)}, u32[]{:S(2)}, u32[]{:S(2)}) %collective-permute-start.6) | collective-permute-done | bytes 393248 | tf_op jit(solution)/shard_map/ppermute | solution.py:25
  37.8 8.2 %collective-permute-done.9.refs_5_.refs_2_ = bf16[768,256]{1,0:T(8,128)(2,1)S(1)} collective-permute-done((bf16[768,256]{1,0:T(8,128)(2,1)S(1)}, bf16[768,256]{1,0:T(8,128)(2,1)S(1)}, u32[]{:S(2)}, u32[]{:S(2)}) %collective-permute-start.9) | collective-permute-done | bytes 393248 | tf_op jit(solution)/shard_map/ppermute | solution.py:25
  46.1 0.5 collective-permute-start.10
  46.6 0.4 collective-permute-start.18
  47.1 0.1 shard_map.30.refs_3_.refs_5_.refs_1_
  47.2 1.8 %collective-permute-start.2 = (bf16[512,256]{1,0:T(8,128)(2,1)S(1)}, bf16[512,256]{1,0:T(8,128)(2,1)S(1)}, u32[]{:S(2)}, u32[]{:S(2)}) collective-permute-start(bf16[512,256]{1,0:T(8,128)(2,1)S(1)} %get-tuple-element.38), channel_id=1, source_target_pairs={{0,2},{2,0},{1,3},{3,1},{4,6},{6,4},{5,7},{7,5},{8,10},{10,8},{9,1... | collective-permute-start | bytes 786440 | tf_op jit(solution)/shard_map/ppermute | solution.py:25
  49.1 2.6 %shard_map.32 = (f32[256,256]{1,0:T(8,128)S(1)}, f32[256,256]{1,0:T(8,128)S(1)}, f32[256,256]{1,0:T(8,128)S(1)}, f32[256,256]{1,0:T(8,128)S(1)}) custom-call(f32[9,32]{1,0:T(8,128)S(1)} %bitcast.1, bf16[4096,256]{1,0:T(8,128)(2,1)S(1)} %get-tuple-element.36.refs_1_.refs_3_.refs_0_, bf16[512,256]{1,0:T(8,128)(2,1)S(1)} %collective-permute-done.13.refs_2_.refs_1_.refs_4_, ...), custom_call_target="tpu_custom_call" | custom-call | flops 1811939328 | bytes 2097152 | tf_op jit(solution)/shard_map/pallas_call | solution.py:352
  51.6 0.6 collective-permute-start.8
  52.2 2.4 %shard_map.33 = (bf16[3,256,256]{2,1,0:T(8,128)(2,1)S(1)}, f32[256,256]{1,0:T(8,128)S(1)}, f32[256,256]{1,0:T(8,128)S(1)}) custom-call(f32[9,32]{1,0:T(8,128)S(1)} %bitcast.2, bf16[4096,256]{1,0:T(8,128)(2,1)S(1)} %get-tuple-element.36.refs_1_.refs_3_.refs_0_, bf16[512,256]{1,0:T(8,128)(2,1)S(1)} %collective-permute-done.11.refs_5_.refs_2_, ...), custom_call_target="tpu_custom_call" | custom-call | flops 1811939328 | bytes 3801088 | tf_op jit(solution)/shard_map/pallas_call | solution.py:352
  54.6 1.0 %collective-permute-done.2.refs_1_ = bf16[512,256]{1,0:T(8,128)(2,1)S(1)} collective-permute-done((bf16[512,256]{1,0:T(8,128)(2,1)S(1)}, bf16[512,256]{1,0:T(8,128)(2,1)S(1)}, u32[]{:S(2)}, u32[]{:S(2)}) %collective-permute-start.2) | collective-permute-done | bytes 262176 | tf_op jit(solution)/shard_map/ppermute | solution.py:25
  55.6 0.5 collective-permute-start.3
  56.1 3.0 %shard_map.36 = (bf16[2,256,256]{2,1,0:T(8,128)(2,1)S(1)}, f32[256,256]{1,0:T(8,128)S(1)}, f32[256,256]{1,0:T(8,128)S(1)}) custom-call(f32[9,32]{1,0:T(8,128)S(1)} %bitcast.3, bf16[1024,256]{1,0:T(8,128)(2,1)S(1)} %collective-permute-done.15.refs_1_, bf16[1024,256]{1,0:T(8,128)(2,1)S(1)} %collective-permute-done.16.refs_2_, ...), custom_call_target="tpu_custom_call" | custom-call | flops 1811939328 | bytes 4980736 | tf_op jit(solution)/shard_map/pallas_call | solution.py:352
  59.1 0.9 %shard_map.39 = (f32[768,256]{1,0:T(8,128)S(1)}, f32[256,256]{1,0:T(8,128)S(1)}, f32[1280,256]{1,0:T(8,128)S(1)}) custom-call(bf16[4096,256]{1,0:T(8,128)(2,1)S(1)} %get-tuple-element.36.refs_1_.refs_3_.refs_0_, bf16[4096,256]{1,0:T(8,128)(2,1)S(1)} %shard_map.30.refs_3_.refs_5_.refs_1_), custom_call_target="tpu_custom_call" | custom-call | flops 603979776 | bytes 2359296 | tf_op jit(solution)/shard_map/pallas_call | solution.py:86
  60.0 0.6 shard_map.40
  60.6 2.5 %shard_map.37 = (bf16[4096,256]{1,0:T(8,128)(2,1)}, bf16[3,256,256]{2,1,0:T(8,128)(2,1)S(1)}, f32[256,256]{1,0:T(8,128)S(1)}, f32[256,256]{1,0:T(8,128)S(1)}) custom-call(f32[9,32]{1,0:T(8,128)S(1)} %bitcast.4, bf16[4096,256]{1,0:T(8,128)(2,1)S(1)} %get-tuple-element.36.refs_1_.refs_3_.refs_0_, bf16[768,256]{1,0:T(8,128)(2,1)S(1)} %collective-permute-done.9.refs_5_.refs_2_, ...), custom_call_target="tpu_custom_call" | custom-call | flops 1811939328 | bytes 3801088 | tf_op jit(solution)/shard_map/pallas_call | solution.py:352
  63.2 1.8 %shard_map.38 = (bf16[4096,256]{1,0:T(8,128)(2,1)}, bf16[2,256,256]{2,1,0:T(8,128)(2,1)S(1)}, f32[256,256]{1,0:T(8,128)S(1)}, f32[256,256]{1,0:T(8,128)S(1)}) custom-call(f32[9,32]{1,0:T(8,128)S(1)} %bitcast.5, bf16[4096,256]{1,0:T(8,128)(2,1)S(1)} %get-tuple-element.36.refs_1_.refs_3_.refs_0_, ...), custom_call_target="tpu_custom_call", output_to_operand_aliasing={{0}: (10, {})} | custom-call | flops 1207959552 | bytes 2883584 | tf_op jit(solution)/shard_map/pallas_call | solution.py:352
  65.0 2.4 %shard_map.41 = bf16[4096,256]{1,0:T(8,128)(2,1)} custom-call(f32[9,32]{1,0:T(8,128)S(1)} %bitcast.6, bf16[4096,256]{1,0:T(8,128)(2,1)S(1)} %get-tuple-element.36.refs_1_.refs_3_.refs_0_, bf16[512,256]{1,0:T(8,128)(2,1)S(1)} %collective-permute-done.1.refs_6_.refs_2_, ...), custom_call_target="tpu_custom_call", output_to_operand_aliasing={{}: (13, {})} | custom-call | flops 905969664 | bytes 3932160 | tf_op jit(solution)/shard_map/pallas_call | solution.py:352
  (24 shorter events, 0.4 us)
Async XLA Ops:
  0.0 1.6 %copy-start = (bf16[4096,256]{1,0:T(8,128)(2,1)S(1)}, bf16[4096,256]{1,0:T(8,128)(2,1)}, u32[]{:S(2)}) copy-start(bf16[4096,256]{1,0:T(8,128)(2,1)} %source.5) | copy-start | bytes 6291460
  2.2 44.4 %collective-permute-start.7 = (bf16[4096,256]{1,0:T(8,128)(2,1)S(1)}, bf16[4096,256]{1,0:T(8,128)(2,1)S(1)}, u32[]{:S(2)}, u32[]{:S(2)}) collective-permute-start(bf16[4096,256]{1,0:T(8,128)(2,1)S(1)} %get-tuple-element.36.refs_1_.refs_3_.refs_0_), channel_id=1, source_target_pairs={{0,1},{1,0},{2,3},{3,2},{4,5},{5,4},{6,7},{7,6},{8,9},{9,8},{10,11... | collective-permute-start | bytes 6291464 | tf_op jit(solution)/shard_map/ppermute | solution.py:25
  2.8 9.7 %collective-permute-start.4 = (bf16[512,256]{1,0:T(8,128)(2,1)S(1)}, bf16[512,256]{1,0:T(8,128)(2,1)S(1)}, u32[]{:S(2)}, u32[]{:S(2)}) collective-permute-start(bf16[512,256]{1,0:T(8,128)(2,1)S(1)} %get-tuple-element.39.refs_0_), channel_id=1, source_target_pairs={{0,2},{2,0},{1,3},{3,1},{4,6},{6,4},{5,7},{7,5},{8,10},{10,8},{9,1... | collective-permute-start | bytes 786440 | tf_op jit(solution)/shard_map/ppermute | solution.py:25
  6.3 11.8 %collective-permute-start.13 = (bf16[512,256]{1,0:T(8,128)(2,1)S(1)}, bf16[512,256]{1,0:T(8,128)(2,1)S(1)}, u32[]{:S(2)}, u32[]{:S(2)}) collective-permute-start(bf16[512,256]{1,0:T(8,128)(2,1)S(1)} %shard_map.31.refs_0_), channel_id=1, source_target_pairs={{0,2},{2,0},{1,3},{3,1},{4,6},{6,4},{5,7},{7,5},{8,10},{10,8},{9,1... | collective-permute-start | bytes 786440 | tf_op jit(solution)/shard_map/ppermute | solution.py:25
  6.4 17.3 %collective-permute-start.11 = (bf16[512,256]{1,0:T(8,128)(2,1)S(1)}, bf16[512,256]{1,0:T(8,128)(2,1)S(1)}, u32[]{:S(2)}, u32[]{:S(2)}) collective-permute-start(bf16[512,256]{1,0:T(8,128)(2,1)S(1)} %get-tuple-element.42), channel_id=1, source_target_pairs={{0,2},{2,0},{1,3},{3,1},{4,6},{6,4},{5,7},{7,5},{8,10},{10,8},{9,1... | collective-permute-start | bytes 786440 | tf_op jit(solution)/shard_map/ppermute | solution.py:25
  8.4 21.0 %collective-permute-start = (bf16[512,256]{1,0:T(8,128)(2,1)S(1)}, bf16[512,256]{1,0:T(8,128)(2,1)S(1)}, u32[]{:S(2)}, u32[]{:S(2)}) collective-permute-start(bf16[512,256]{1,0:T(8,128)(2,1)S(1)} %get-tuple-element.37), channel_id=1, source_target_pairs={{0,2},{2,0},{1,3},{3,1},{4,6},{6,4},{5,7},{7,5},{8,10},{10,8},{9,1... | collective-permute-start | bytes 786440 | tf_op jit(solution)/shard_map/ppermute | solution.py:25
  12.6 33.5 %collective-permute-start.15 = (bf16[1024,256]{1,0:T(8,128)(2,1)S(1)}, bf16[1024,256]{1,0:T(8,128)(2,1)S(1)}, u32[]{:S(2)}, u32[]{:S(2)}) collective-permute-start(bf16[1024,256]{1,0:T(8,128)(2,1)S(1)} %shard_map.34), channel_id=1, source_target_pairs={{0,4},{4,8},{8,12},{1,5},{5,9},{9,13},{2,6},{6,10},{10,14},{3,7},{... | collective-permute-start | bytes 1572872 | tf_op jit(solution)/shard_map/ppermute | solution.py:411
  18.2 28.3 %collective-permute-start.17 = (bf16[1024,256]{1,0:T(8,128)(2,1)S(1)}, bf16[1024,256]{1,0:T(8,128)(2,1)S(1)}, u32[]{:S(2)}, u32[]{:S(2)}) collective-permute-start(bf16[1024,256]{1,0:T(8,128)(2,1)S(1)} %shard_map.35), channel_id=1, source_target_pairs={{4,0},{8,4},{12,8},{5,1},{9,5},{13,9},{6,2},{10,6},{14,10},{7,3},{... | collective-permute-start | bytes 1572872 | tf_op jit(solution)/shard_map/ppermute | solution.py:409
  23.8 14.0 %collective-permute-start.6 = (bf16[768,256]{1,0:T(8,128)(2,1)S(1)}, bf16[768,256]{1,0:T(8,128)(2,1)S(1)}, u32[]{:S(2)}, u32[]{:S(2)}) collective-permute-start(bf16[768,256]{1,0:T(8,128)(2,1)S(1)} %get-tuple-element.40), channel_id=1, source_target_pairs={{0,2},{2,0},{1,3},{3,1},{4,6},{6,4},{5,7},{7,5},{8,10},{10,8},{9,1... | collective-permute-start | bytes 1179656 | tf_op jit(solution)/shard_map/ppermute | solution.py:25
  29.4 19.7 %copy-start.1 = (f32[32,9]{0,1:T(8,128)S(1)}, f32[32,9]{0,1:T(8,128)}, u32[]{:S(2)}) copy-start(f32[32,9]{0,1:T(8,128)} %param.3) | copy-start | bytes 3460
  29.4 16.7 %collective-permute-start.9 = (bf16[768,256]{1,0:T(8,128)(2,1)S(1)}, bf16[768,256]{1,0:T(8,128)(2,1)S(1)}, u32[]{:S(2)}, u32[]{:S(2)}) collective-permute-start(bf16[768,256]{1,0:T(8,128)(2,1)S(1)} %get-tuple-element.41), channel_id=1, source_target_pairs={{0,2},{2,0},{1,3},{3,1},{4,6},{6,4},{5,7},{7,5},{8,10},{10,8},{9,1... | collective-permute-start | bytes 1179656 | tf_op jit(solution)/shard_map/ppermute | solution.py:25
  37.8 9.4 %collective-permute-start.14 = (bf16[512,256]{1,0:T(8,128)(2,1)S(1)}, bf16[512,256]{1,0:T(8,128)(2,1)S(1)}, u32[]{:S(2)}, u32[]{:S(2)}) collective-permute-start(bf16[512,256]{1,0:T(8,128)(2,1)S(1)} %collective-permute-done.13.refs_2_.refs_1_.refs_4_), channel_id=1, source_target_pairs={{0,1},{1,0},{2,3},{3,2},{4,5},{5,4},{6,7},{7,6},{8,9},{9,8},{10,11... | collective-permute-start | bytes 786440 | tf_op jit(solution)/shard_map/ppermute | solution.py:25
  46.0 3.0 %collective-permute-start.12 = (bf16[512,256]{1,0:T(8,128)(2,1)S(1)}, bf16[512,256]{1,0:T(8,128)(2,1)S(1)}, u32[]{:S(2)}, u32[]{:S(2)}) collective-permute-start(bf16[512,256]{1,0:T(8,128)(2,1)S(1)} %collective-permute-done.11.refs_5_.refs_2_), channel_id=1, source_target_pairs={{0,1},{1,0},{2,3},{3,2},{4,5},{5,4},{6,7},{7,6},{8,9},{9,8},{10,11... | collective-permute-start | bytes 786440 | tf_op jit(solution)/shard_map/ppermute | solution.py:25
  46.1 5.6 %collective-permute-start.10 = (bf16[768,256]{1,0:T(8,128)(2,1)S(1)}, bf16[768,256]{1,0:T(8,128)(2,1)S(1)}, u32[]{:S(2)}, u32[]{:S(2)}) collective-permute-start(bf16[768,256]{1,0:T(8,128)(2,1)S(1)} %collective-permute-done.9.refs_5_.refs_2_), channel_id=1, source_target_pairs={{0,1},{1,0},{2,3},{3,2},{4,5},{5,4},{6,7},{7,6},{8,9},{9,8},{10,11... | collective-permute-start | bytes 1179656 | tf_op jit(solution)/shard_map/ppermute | solution.py:25
  46.6 9.5 %collective-permute-start.16 = (bf16[1024,256]{1,0:T(8,128)(2,1)S(1)}, bf16[1024,256]{1,0:T(8,128)(2,1)S(1)}, u32[]{:S(2)}, u32[]{:S(2)}) collective-permute-start(bf16[1024,256]{1,0:T(8,128)(2,1)S(1)} %collective-permute-done.15.refs_1_), channel_id=1, source_target_pairs={{0,1},{1,0},{2,3},{3,2},{4,5},{5,4},{6,7},{7,6},{8,9},{9,8},{10,11... | collective-permute-start | bytes 1572872 | tf_op jit(solution)/shard_map/ppermute | solution.py:25
  46.6 9.5 %collective-permute-start.18 = (bf16[1024,256]{1,0:T(8,128)(2,1)S(1)}, bf16[1024,256]{1,0:T(8,128)(2,1)S(1)}, u32[]{:S(2)}, u32[]{:S(2)}) collective-permute-start(bf16[1024,256]{1,0:T(8,128)(2,1)S(1)} %collective-permute-done.17.refs_9_), channel_id=1, source_target_pairs={{0,1},{1,0},{2,3},{3,2},{4,5},{5,4},{6,7},{7,6},{8,9},{9,8},{10,11... | collective-permute-start | bytes 1572872 | tf_op jit(solution)/shard_map/ppermute | solution.py:25
  47.2 8.3 %collective-permute-start.2 = (bf16[512,256]{1,0:T(8,128)(2,1)S(1)}, bf16[512,256]{1,0:T(8,128)(2,1)S(1)}, u32[]{:S(2)}, u32[]{:S(2)}) collective-permute-start(bf16[512,256]{1,0:T(8,128)(2,1)S(1)} %get-tuple-element.38), channel_id=1, source_target_pairs={{0,2},{2,0},{1,3},{3,1},{4,6},{6,4},{5,7},{7,5},{8,10},{10,8},{9,1... | collective-permute-start | bytes 786440 | tf_op jit(solution)/shard_map/ppermute | solution.py:25
  49.1 6.5 %collective-permute-start.5 = (bf16[512,256]{1,0:T(8,128)(2,1)S(1)}, bf16[512,256]{1,0:T(8,128)(2,1)S(1)}, u32[]{:S(2)}, u32[]{:S(2)}) collective-permute-start(bf16[512,256]{1,0:T(8,128)(2,1)S(1)} %collective-permute-done.4.refs_1_.refs_7_.refs_2_), channel_id=1, source_target_pairs={{0,1},{1,0},{2,3},{3,2},{4,5},{5,4},{6,7},{7,6},{8,9},{9,8},{10,11... | collective-permute-start | bytes 786440 | tf_op jit(solution)/shard_map/ppermute | solution.py:25
  51.6 9.0 %collective-permute-start.8 = (bf16[768,256]{1,0:T(8,128)(2,1)S(1)}, bf16[768,256]{1,0:T(8,128)(2,1)S(1)}, u32[]{:S(2)}, u32[]{:S(2)}) collective-permute-start(bf16[768,256]{1,0:T(8,128)(2,1)S(1)} %collective-permute-done.6.refs_5_.refs_2_), channel_id=1, source_target_pairs={{0,1},{1,0},{2,3},{3,2},{4,5},{5,4},{6,7},{7,6},{8,9},{9,8},{10,11... | collective-permute-start | bytes 1179656 | tf_op jit(solution)/shard_map/ppermute | solution.py:25
  55.6 7.6 %collective-permute-start.1 = (bf16[512,256]{1,0:T(8,128)(2,1)S(1)}, bf16[512,256]{1,0:T(8,128)(2,1)S(1)}, u32[]{:S(2)}, u32[]{:S(2)}) collective-permute-start(bf16[512,256]{1,0:T(8,128)(2,1)S(1)} %collective-permute-done.refs_5_.refs_0_), channel_id=1, source_target_pairs={{0,1},{1,0},{2,3},{3,2},{4,5},{5,4},{6,7},{7,6},{8,9},{9,8},{10,11... | collective-permute-start | bytes 786440 | tf_op jit(solution)/shard_map/ppermute | solution.py:25
  55.6 9.4 %collective-permute-start.3 = (bf16[512,256]{1,0:T(8,128)(2,1)S(1)}, bf16[512,256]{1,0:T(8,128)(2,1)S(1)}, u32[]{:S(2)}, u32[]{:S(2)}) collective-permute-start(bf16[512,256]{1,0:T(8,128)(2,1)S(1)} %collective-permute-done.2.refs_1_), channel_id=1, source_target_pairs={{0,1},{1,0},{2,3},{3,2},{4,5},{5,4},{6,7},{7,6},{8,9},{9,8},{10,11... | collective-permute-start | bytes 786440 | tf_op jit(solution)/shard_map/ppermute | solution.py:25
